TPU v7x, 32 devices: a whole 2x2x4 slice. The times are simulated.
32 devices in a mesh: row: 8 (over z, y), col: 4 (over x, core).
Axes of the slice: x: 2, y: 2, z: 4, core: 2. Of those that a mesh axis runs over, the one named last changes fastest.
Arguments:
- latents: bfloat16 [4, 1152, 4096], P(None, 'col', 'row'), may hold values from -6 to 6
- cond: bfloat16 [4, 1, 1152], P(None, None, 'row'), may hold values from -6 to 6
- w_ada: bfloat16 [2, 1152, 6, 1152], P(None, 'row', None, 'col'), may hold values from -0.1875 to 0.1875
- b_ada: bfloat16 [2, 6, 1152], P(None, None, 'col'), may hold values from -3 to 3
- w_qkv: bfloat16 [2, 1152, 3, 1152], P(None, 'row', None, 'col'), may hold values from -0.1875 to 0.1875
- b_qv: bfloat16 [2, 2, 1152], P(None, None, 'col'), may hold values from -3 to 3
- w_out: bfloat16 [2, 1152, 1152], P(None, 'row', 'col'), may hold values from -0.5 to 0.5
- b_out: bfloat16 [2, 1152], P(None, 'col'), may hold values from -2 to 2
- w_fc1: bfloat16 [2, 1152, 4608], P(None, 'row', 'col'), may hold values from -0.1875 to 0.1875
- b_fc1: bfloat16 [2, 4608], P(None, 'col'), may hold values from -3 to 3
- w_fc2: bfloat16 [2, 1152, 4608], P(None, 'row', 'col'), may hold values from -0.09375 to 0.09375
- b_fc2: bfloat16 [2, 1152], P(None, 'col'), may hold values from -2 to 2
- cotangent: bfloat16 [4, 1152, 4096], P(None, 'col', 'row'), may hold values from -6 to 6
Outputs:
- output: bfloat16 [4, 1152, 4096], P(None, 'col', 'row')
- grad_latents: float32 [4, 1152, 4096], P(None, 'col', 'row')
- grad_cond: float32 [4, 1, 1152], P(None, None, 'row')
- grad_w_ada: float32 [2, 1152, 6, 1152], P(None, 'row', None, 'col')
- grad_b_ada: float32 [2, 6, 1152], P(None, None, 'col')
- grad_w_qkv: float32 [2, 1152, 3, 1152], P(None, 'row', None, 'col')
- grad_b_qv: float32 [2, 2, 1152], P(None, None, 'col')
- grad_w_out: float32 [2, 1152, 1152], P(None, 'row', 'col')
- grad_b_out: float32 [2, 1152], P(None, 'col')
- grad_w_fc1: float32 [2, 1152, 4608], P(None, 'row', 'col')
- grad_b_fc1: float32 [2, 4608], P(None, 'col')
- grad_w_fc2: float32 [2, 1152, 4608], P(None, 'row', 'col')
- grad_b_fc2: float32 [2, 1152], P(None, 'col')
All inputs are finite; a program needn't handle non-finite values.
Results may differ from a plain program's by a relative error of at most 0.03.
Values may be sent and summed in bfloat16 or wider, within the bound.
No kernel may reach another device: no remote copies, remote signals or barrier semaphores. Data moves between devices by JAX's collectives and lax.ppermute only.
A program may use at most 320 MiB of HBM per device.

v0:
```python
import jax
import jax.numpy as jnp
from jax import lax
from jax.sharding import PartitionSpec as P

D = 1152
HD = 72
P_SIZE = 256
NF = 16


epsilon = 1e-06


def gelu_tanh(value):
    return jax.nn.gelu(value, approximate=True)


def contract_rows(left, right):
    return lax.dot_general(
        left, right, (((0,), (0,)), ((), ())), preferred_element_type=jnp.float32
    )


def contract_last(left, right):
    return lax.dot_general(
        left, right, (((1,), (1,)), ((), ())), preferred_element_type=jnp.float32
    )


def gather_features(value):
    return lax.all_gather(value, "col", axis=1, tiled=True)


def feature_sums(partial_value):
    return lax.psum_scatter(partial_value, "col", scatter_dimension=1, tiled=True)


def row_totals(first, second):
    return lax.psum((first, second), "col")


def fold_product(left, weight):
    return jnp.dot(
        left, lax.all_gather(weight, "row", axis=0, tiled=True), preferred_element_type=jnp.float32
    )


def map_product(left, weight):
    return contract_last(left, lax.all_gather(weight, "row", axis=0, tiled=True))


def norm_forward(stream):
    first, second = row_totals(jnp.sum(stream, 1), jnp.sum(stream * stream, 1))
    row_mean = first / D
    inverse = lax.rsqrt(second / D - row_mean * row_mean + epsilon)
    return ((stream - row_mean[:, None]) * inverse[:, None], inverse)


def norm_backward(grad_normed, normed, inverse):
    first, second = row_totals(jnp.sum(grad_normed, 1), jnp.sum(grad_normed * normed, 1))
    return inverse[:, None] * (grad_normed - first[:, None] / D - normed * second[:, None] / D)


def spread(vector, groups, tokens):
    width = vector.shape[-1]
    return jnp.broadcast_to(vector[:, None, :], (groups, tokens // groups, width)).reshape(
        tokens, width
    )


def group_sum(value, groups):
    return jnp.sum(value.reshape(groups, -1, value.shape[-1]), 1)


def split_heads(value, layout):
    return value.reshape(layout + (value.shape[1] // HD, HD))


def attention_scores(query_split, key_split):
    return jnp.einsum(
        "sqehd,skehd->sehqk", query_split, key_split, preferred_element_type=jnp.float32
    ) * HD ** (-0.5)


def attend_forward(queries, key_heads, value_heads, layout):
    tokens, width = queries.shape
    scores = attention_scores(split_heads(queries, layout), split_heads(key_heads, layout))
    largest = jnp.max(scores, -1, keepdims=True)
    powered = jnp.exp(scores - largest)
    total = jnp.sum(powered, -1, keepdims=True)
    soft_weights = (powered / total).astype(jnp.bfloat16)
    attended = jnp.einsum(
        "sehqk,skehd->sqehd",
        soft_weights,
        split_heads(value_heads, layout),
        preferred_element_type=jnp.float32,
    )
    return (attended.reshape(tokens, width), largest + jnp.log(total))


def attend_backward(queries, key_heads, value_heads, log_total, grad_out, layout):
    tokens, width = queries.shape
    query_split = split_heads(queries, layout)
    key_split = split_heads(key_heads, layout)
    value_split = split_heads(value_heads, layout)
    grad_split = split_heads(grad_out, layout)
    soft_weights = jnp.exp(attention_scores(query_split, key_split) - log_total)
    grad_weights = jnp.einsum(
        "sqehd,skehd->sehqk", grad_split, value_split, preferred_element_type=jnp.float32
    )
    grad_scores = (
        soft_weights * (grad_weights - jnp.sum(grad_weights * soft_weights, -1, keepdims=True))
    ).astype(jnp.bfloat16)
    factor = HD ** (-0.5)
    grad_query = (
        jnp.einsum("sehqk,skehd->sqehd", grad_scores, key_split, preferred_element_type=jnp.float32)
        * factor
    )
    grad_keys = (
        jnp.einsum(
            "sehqk,sqehd->skehd", grad_scores, query_split, preferred_element_type=jnp.float32
        )
        * factor
    )
    grad_values = jnp.einsum(
        "sehqk,sqehd->skehd",
        soft_weights.astype(jnp.bfloat16),
        grad_split,
        preferred_element_type=jnp.float32,
    )
    return (
        grad_query.reshape(tokens, width),
        grad_keys.reshape(tokens, width),
        grad_values.reshape(tokens, width),
    )


def block_forward(stream, modulate, weights, groups, layout):
    w_qkv, b_qv, w_out, b_out, w_fc1, b_fc1, w_fc2, b_fc2, out_local = weights
    tokens, width = stream.shape
    pieces = [spread(modulate[:, column], groups, tokens) for column in range(6)]
    normed, inverse = norm_forward(stream)
    hidden = (normed * (1.0 + pieces[1]) + pieces[0]).astype(jnp.bfloat16)
    hidden_all = gather_features(hidden)
    qv_bias = b_qv.astype(jnp.float32)
    biases = jnp.concatenate([qv_bias[0], jnp.zeros((width,), jnp.float32), qv_bias[1]])
    projected = (fold_product(hidden_all, w_qkv) + biases).astype(jnp.bfloat16)
    queries = projected[:, :width]
    key_heads = projected[:, width : 2 * width]
    value_heads = projected[:, 2 * width :]
    attended, log_total = attend_forward(queries, key_heads, value_heads, layout)
    attended_low = attended.astype(jnp.bfloat16)
    branch = feature_sums(map_product(attended_low, w_out)) + b_out.astype(jnp.float32)
    middle = stream + pieces[2] * branch
    normed_two, inverse_two = norm_forward(middle)
    hidden_two = (normed_two * (1.0 + pieces[4]) + pieces[3]).astype(jnp.bfloat16)
    hidden_two_all = gather_features(hidden_two)
    preact = fold_product(hidden_two_all, w_fc1) + b_fc1.astype(jnp.float32)
    activated = gelu_tanh(preact).astype(jnp.bfloat16)
    branch_two = feature_sums(map_product(activated, w_fc2)) + b_fc2.astype(jnp.float32)
    result = middle + pieces[5] * branch_two
    kept = (
        normed,
        inverse,
        hidden_all,
        queries,
        key_heads,
        value_heads,
        log_total,
        attended_low,
        branch,
        normed_two,
        inverse_two,
        hidden_two_all,
        preact,
        activated,
        branch_two,
    )
    return (result, kept)


def block_backward(grad, kept, modulate, weights, groups, layout):
    (
        normed,
        inverse,
        hidden_all,
        queries,
        key_heads,
        value_heads,
        log_total,
        attended_low,
        branch,
        normed_two,
        inverse_two,
        hidden_two_all,
        preact,
        activated,
        branch_two,
    ) = kept
    w_qkv, b_qv, w_out, b_out, w_fc1, b_fc1, w_fc2, b_fc2, out_local = weights
    tokens, width = grad.shape
    pieces = [spread(modulate[:, column], groups, tokens) for column in range(6)]
    grad_branch_two = (pieces[5] * grad).astype(jnp.bfloat16)
    grad_two_all = gather_features(grad_branch_two)
    grad_activated = fold_product(grad_two_all, w_fc2)
    grad_preact = jax.vjp(gelu_tanh, preact)[1](grad_activated)[0].astype(jnp.bfloat16)
    grad_hidden_two = feature_sums(map_product(grad_preact, w_fc1))
    grad_middle = grad + norm_backward(grad_hidden_two * (1.0 + pieces[4]), normed_two, inverse_two)
    grad_branch = (pieces[2] * grad_middle).astype(jnp.bfloat16)
    grad_branch_all = gather_features(grad_branch)
    grad_attended = fold_product(grad_branch_all, w_out).astype(jnp.bfloat16)
    grad_query, grad_keys, grad_values = attend_backward(
        queries, key_heads, value_heads, log_total, grad_attended, layout
    )
    grad_mixed = jnp.concatenate([grad_query, grad_keys, grad_values], 1).astype(jnp.bfloat16)
    grad_hidden = feature_sums(map_product(grad_mixed, w_qkv))
    grad_stream = grad_middle + norm_backward(grad_hidden * (1.0 + pieces[1]), normed, inverse)
    modulate_grad = jnp.stack(
        [
            group_sum(grad_hidden, groups),
            group_sum(grad_hidden * normed, groups),
            group_sum(grad_middle * branch, groups),
            group_sum(grad_hidden_two, groups),
            group_sum(grad_hidden_two * normed_two, groups),
            group_sum(grad * branch_two, groups),
        ],
        1,
    )
    weight_grads = (
        contract_rows(hidden_all, grad_mixed),
        contract_rows(grad_branch_all, attended_low),
        contract_rows(hidden_two_all, grad_preact),
        contract_rows(grad_two_all, activated),
    )
    mixed_float = grad_mixed.astype(jnp.float32)
    bias_grads = (
        jnp.stack([jnp.sum(mixed_float[:, :width], 0), jnp.sum(mixed_float[:, 2 * width :], 0)]),
        jnp.sum(grad_branch.astype(jnp.float32), 0),
        jnp.sum(grad_preact.astype(jnp.float32), 0),
        jnp.sum(grad_branch_two.astype(jnp.float32), 0),
    )
    return (grad_stream, weight_grads, bias_grads, modulate_grad)


def to_positions(value, frames_dev, row_count, pos_block):
    tokens, width = value.shape
    shaped = value.reshape(frames_dev, row_count, pos_block, width)
    moved = lax.all_to_all(shaped, "row", split_axis=1, concat_axis=0, tiled=True)
    return moved.reshape(tokens, width)


def to_frames(value, frames_dev, row_count, pos_block):
    tokens, width = value.shape
    shaped = value.reshape(frames_dev * row_count, 1, pos_block, width)
    moved = lax.all_to_all(
        shaped.astype(jnp.bfloat16), "row", split_axis=0, concat_axis=1, tiled=True
    ).astype(shaped.dtype)
    return moved.reshape(tokens, width)


def shards(
    latents, cond, w_ada, b_ada, w_qkv, b_qv, w_out, b_out, w_fc1, b_fc1, w_fc2, b_fc2, cotangent
):
    batches, width, tokens = latents.shape
    lat_count = cond.shape[1]
    row_count = lax.axis_size("row")
    frames_dev = tokens // P_SIZE
    pos_block = tokens // (lat_count * NF)
    spatial = (frames_dev, P_SIZE, 1)
    temporal = (lat_count, NF, pos_block)
    cond_float = cond.astype(jnp.float32)
    cond_low = jax.nn.silu(cond_float).astype(jnp.bfloat16)
    mod_partial = jnp.einsum("mlr,brjk->mlbjk", cond_low, w_ada, preferred_element_type=jnp.float32)
    mod_all = lax.psum(mod_partial, "row") + b_ada.astype(jnp.float32)[None, None]
    qkv_weight, out_weight, fc1_weight, fc2_weight = (w_qkv, w_out, w_fc1, w_fc2)
    out_locals = [None, None]
    block_weights = [
        (
            qkv_weight[which].reshape(qkv_weight.shape[1], -1),
            b_qv[which],
            out_weight[which],
            b_out[which],
            fc1_weight[which],
            b_fc1[which],
            fc2_weight[which],
            b_fc2[which],
            out_locals[which],
        )
        for which in range(2)
    ]
    lat_here = lax.axis_index("row") * frames_dev // NF
    onehot = (jnp.arange(lat_count) == lat_here).astype(jnp.float32)
    outputs = []
    grad_inputs = []
    mod_grads = []
    weight_totals = None
    bias_totals = None
    for batch_index in range(batches):
        mod_batch = mod_all[batch_index]
        mod_space = lax.dynamic_slice_in_dim(mod_batch[:, 0], lat_here, 1, 0)
        mod_time = mod_batch[:, 1]
        first_out, kept_space = block_forward(
            latents[batch_index].T.astype(jnp.float32), mod_space, block_weights[0], 1, spatial
        )
        second_in = to_positions(first_out, frames_dev, row_count, pos_block)
        second_out, kept_time = block_forward(
            second_in, mod_time, block_weights[1], lat_count, temporal
        )
        outputs.append(
            to_frames(second_out, frames_dev, row_count, pos_block).astype(jnp.bfloat16).T
        )
        grad_top = to_positions(
            cotangent[batch_index].T.astype(jnp.float32), frames_dev, row_count, pos_block
        )
        grad_mid, weights_time, biases_time, mod_grad_time = block_backward(
            grad_top, kept_time, mod_time, block_weights[1], lat_count, temporal
        )
        grad_low = to_frames(grad_mid, frames_dev, row_count, pos_block)
        grad_first, weights_space, biases_space, mod_grad_space = block_backward(
            grad_low, kept_space, mod_space, block_weights[0], 1, spatial
        )
        grad_inputs.append(grad_first.T)
        mod_grads.append(jnp.stack([onehot[:, None, None] * mod_grad_space, mod_grad_time], 1))
        terms = tuple(
            (jnp.stack([weights_space[column], weights_time[column]]) for column in range(4))
        )
        bias_terms = tuple(
            (jnp.stack([biases_space[column], biases_time[column]]) for column in range(4))
        )
        terms = (
            lax.psum_scatter(
                terms[0].astype(jnp.bfloat16), "row", scatter_dimension=1, tiled=True
            ).astype(jnp.float32),
            lax.psum_scatter(
                terms[1].astype(jnp.bfloat16), "row", scatter_dimension=1, tiled=True
            ).astype(jnp.float32),
            lax.psum_scatter(
                terms[2].astype(jnp.bfloat16), "row", scatter_dimension=1, tiled=True
            ).astype(jnp.float32),
            lax.psum_scatter(
                terms[3].astype(jnp.bfloat16), "row", scatter_dimension=1, tiled=True
            ).astype(jnp.float32),
        )
        if weight_totals is None:
            weight_totals = terms
            bias_totals = bias_terms
        else:
            weight_totals = jax.tree.map(jnp.add, weight_totals, terms)
            bias_totals = jax.tree.map(jnp.add, bias_totals, bias_terms)
    mod_grad_all, grad_bias_qv, grad_bias_out, grad_bias_fc1, grad_bias_fc2 = lax.psum(
        (jnp.stack(mod_grads), bias_totals[0], bias_totals[1], bias_totals[2], bias_totals[3]),
        "row",
    )
    mod_grad_low = mod_grad_all.astype(jnp.bfloat16)
    grad_bias_ada = jnp.sum(mod_grad_low.astype(jnp.float32), (0, 1))
    grad_weight_ada = jnp.einsum(
        "mlr,mlbjk->brjk", cond_low, mod_grad_low, preferred_element_type=jnp.float32
    )
    cond_partial = jnp.einsum(
        "mlbjk,brjk->mlr", mod_grad_low, w_ada, preferred_element_type=jnp.float32
    )
    cond_total = lax.psum(cond_partial, "col")
    sigmoid_cond = jax.nn.sigmoid(cond_float)
    grad_condition = cond_total * sigmoid_cond * (1.0 + cond_float * (1.0 - sigmoid_cond))
    grad_weight_qkv = weight_totals[0].reshape(2, weight_totals[0].shape[1], 3, width)
    return (
        jnp.stack(outputs),
        jnp.stack(grad_inputs),
        grad_condition,
        grad_weight_ada,
        grad_bias_ada,
        grad_weight_qkv,
        grad_bias_qv,
        weight_totals[1],
        grad_bias_out,
        weight_totals[2],
        grad_bias_fc1,
        weight_totals[3],
        grad_bias_fc2,
    )


def solution(mesh):
    placed = (
        P(None, "col", "row"),
        P(None, None, "row"),
        P(None, "row", None, "col"),
        P(None, None, "col"),
        P(None, "row", None, "col"),
        P(None, None, "col"),
        P(None, "row", "col"),
        P(None, "col"),
        P(None, "row", "col"),
        P(None, "col"),
        P(None, "row", "col"),
        P(None, "col"),
        P(None, "col", "row"),
    )
    return jax.shard_map(
        shards,
        mesh=mesh,
        in_specs=placed,
        out_specs=(
            P(None, "col", "row"),
            P(None, "col", "row"),
            P(None, None, "row"),
            P(None, "row", None, "col"),
            P(None, None, "col"),
            P(None, "row", None, "col"),
            P(None, None, "col"),
            P(None, "row", "col"),
            P(None, "col"),
            P(None, "row", "col"),
            P(None, "col"),
            P(None, "row", "col"),
            P(None, "col"),
        ),
        check_vma=False,
    )
```

profile of v0, /device:TPU:0, one launch (start us, length us, event | category | flops | bytes accessed | tf_op | source)
XLA Modules:
  0.0 4143.2 jit_solution(4381274286340281583)
XLA Ops:
  12.1 39.9 psum.497
  64.3 34.9 all-gather
  99.2 31.0 all-gather.47.cloned.1.call-done
  144.6 29.0 reduce-scatter.41.cloned.1.call-done
  187.7 43.8 %all-gather.113.cloned.1.call-done = bf16[1,1152,1152]{2,1,0:T(8,128)(2,1)} async-done(((bf16[1,144,1152]{2,1,0:T(8,128)(2,1)}), bf16[1,1152,1152]{2,1,0:T(8,128)(2,1)}) %all-gather.113.cloned.1.call-update) | async-done | bytes 2654224 | tf_op jit(solution)/shard_map/all_gather | solution.py:45
  231.5 18.1 all-gather.49.cloned.1.call-done
  255.0 52.5 %all-gather.115.cloned.1.call-done = bf16[1,1152,1152]{2,1,0:T(8,128)(2,1)} async-done(((bf16[1,144,1152]{2,1,0:T(8,128)(2,1)}), bf16[1,1152,1152]{2,1,0:T(8,128)(2,1)}) %all-gather.115.cloned.1.call-update) | async-done | bytes 2654224 | tf_op jit(solution)/shard_map/all_gather | solution.py:50
  318.6 26.4 reduce-scatter.43.cloned.1.call-done
  358.9 25.9 all-to-all-done
  402.4 34.4 all-gather.3
  463.7 30.7 reduce-scatter.45.cloned.1.call-done
  509.7 37.8 all_to_all.228
  558.8 17.8 all-gather.55.cloned.1.call-done
  581.9 14.3 all-gather.81.cloned.1.call-done
  596.2 57.3 %all-gather.119.cloned.1.call-done = bf16[1,1152,1152]{2,1,0:T(8,128)(2,1)} async-done(((bf16[1,144,1152]{2,1,0:T(8,128)(2,1)}), bf16[1,1152,1152]{2,1,0:T(8,128)(2,1)}) %all-gather.119.cloned.1.call-update) | async-done | bytes 2654224 | tf_op jit(solution)/shard_map/all_gather | solution.py:50
  670.4 25.9 reduce-scatter.73.cloned.1.call-done
  704.2 27.6 reduce-scatter.47.cloned.1.call-done
  736.6 16.5 all-gather.83.cloned.1.call-done
  782.4 33.2 reduce-scatter.75.cloned.1.call-done
  827.7 17.7 all_to_all.229
  851.7 14.9 all-gather.85.cloned.1.call-done
  877.7 33.1 reduce-scatter.77.cloned.1.call-done
  921.9 18.6 all-gather.87.cloned.1.call-done
  955.0 32.3 reduce-scatter.79.cloned.1.call-done
  1002.5 17.1 all-gather.65.cloned.1.call-done
  1074.7 19.5 reduce-scatter.57.cloned.1.call-done
  1094.2 35.6 reduce-scatter.65.cloned.1.call-done
  1129.8 35.6 reduce-scatter.49.cloned.1.call-done
  1183.6 15.5 all-gather.59.cloned.1.call-done
  1247.2 27.0 reduce-scatter.51.cloned.1.call-done
  1274.2 35.5 reduce-scatter.59.cloned.1.call-done
  1309.7 35.8 reduce-scatter.67.cloned.1.call-done
  1358.5 17.9 all-to-all-done.2
  1384.2 16.1 all-to-all-done.4
  1406.0 18.4 all-to-all-done.6
  1529.6 35.7 reduce-scatter.61.cloned.1.call-done
  1565.3 35.6 reduce-scatter.53.cloned.1.call-done
  1621.5 25.5 all_to_all.230
  1656.9 23.3 all_to_all.231
  1690.1 23.2 all_to_all.232
  1787.8 26.8 reduce-scatter.89.cloned.1.call-done
  1816.8 33.5 reduce-scatter.81.cloned.1.call-done
  1865.0 20.9 reduce-scatter.63.cloned.1.call-done
  1890.2 31.4 reduce-scatter.71.cloned.1.call-done
  1921.5 35.6 reduce-scatter.55.cloned.1.call-done
  2053.9 32.4 reduce-scatter.83.cloned.1.call-done
  2088.3 33.7 reduce-scatter.99.cloned.1.call-done
  2254.9 24.5 reduce-scatter.93.cloned.1.call-done
  2281.4 33.7 reduce-scatter.85.cloned.1.call-done
  2317.0 33.5 reduce-scatter.101.cloned.1.call-done
  2612.9 18.5 all-to-all-done.1
  2657.6 14.4 all-to-all-done.3
  2679.0 19.5 all-to-all-done.7
  2715.0 52.4 %reduce-scatter.115.cloned.1.call-done = bf16[2,144,1152]{2,1,0:T(8,128)(2,1)} async-done(((bf16[2,1152,1152]{2,1,0:T(8,128)(2,1)}), bf16[2,144,1152]{2,1,0:T(8,128)(2,1)}) %reduce-scatter.115.cloned.1.call-update) | async-done | bytes 663568 | tf_op jit(solution)/shard_map/reduce_scatter | solution.py:341
  2767.4 107.2 %reduce-scatter.117.cloned.1.call-done = bf16[2,144,1152]{2,1,0:T(8,128)(2,1)} async-done(((bf16[2,1152,1152]{2,1,0:T(8,128)(2,1)}), bf16[2,144,1152]{2,1,0:T(8,128)(2,1)}) %reduce-scatter.117.cloned.1.call-update) | async-done | bytes 663568 | tf_op jit(solution)/shard_map/reduce_scatter | solution.py:341
  2877.7 104.0 %reduce-scatter.105.cloned.1.call-done = bf16[2,144,1152]{2,1,0:T(8,128)(2,1)} async-done(((bf16[2,1152,1152]{2,1,0:T(8,128)(2,1)}), bf16[2,144,1152]{2,1,0:T(8,128)(2,1)}) %reduce-scatter.105.cloned.1.call-update) | async-done | bytes 663568 | tf_op jit(solution)/shard_map/reduce_scatter | solution.py:338
  2981.7 107.1 %reduce-scatter.109.cloned.1.call-done = bf16[2,144,1152]{2,1,0:T(8,128)(2,1)} async-done(((bf16[2,1152,1152]{2,1,0:T(8,128)(2,1)}), bf16[2,144,1152]{2,1,0:T(8,128)(2,1)}) %reduce-scatter.109.cloned.1.call-update) | async-done | bytes 663568 | tf_op jit(solution)/shard_map/reduce_scatter | solution.py:338
  3088.8 107.1 %reduce-scatter.107.cloned.1.call-done = bf16[2,144,1152]{2,1,0:T(8,128)(2,1)} async-done(((bf16[2,1152,1152]{2,1,0:T(8,128)(2,1)}), bf16[2,144,1152]{2,1,0:T(8,128)(2,1)}) %reduce-scatter.107.cloned.1.call-update) | async-done | bytes 663568 | tf_op jit(solution)/shard_map/reduce_scatter | solution.py:338
  3195.9 107.2 %reduce-scatter.111.cloned.1.call-done = bf16[2,144,1152]{2,1,0:T(8,128)(2,1)} async-done(((bf16[2,1152,1152]{2,1,0:T(8,128)(2,1)}), bf16[2,144,1152]{2,1,0:T(8,128)(2,1)}) %reduce-scatter.111.cloned.1.call-update) | async-done | bytes 663568 | tf_op jit(solution)/shard_map/reduce_scatter | solution.py:338
  3306.3 32.2 reduce-scatter.95.cloned.1.call-done
  3338.4 36.2 reduce-scatter.87.cloned.1.call-done
  3374.7 35.8 reduce-scatter.103.cloned.1.call-done
  3413.4 40.3 all-reduce.8
  3473.0 650.4 %all-reduce.27.cloned.1.call-done = (bf16[2,1152,864]{2,0,1:T(2,128)(2,1)}, bf16[2,1152,864]{2,0,1:T(2,128)(2,1)}, bf16[2,1152,864]{2,0,1:T(2,128)(2,1)}, bf16[2...) async-done(((bf16[2,1152,864]{2,0,1:T(2,128)(2,1)}, ...) | async-done | bytes 21233680
  (1706 shorter events, 1252.0 us)
Async XLA Ops:
  7.2 92.0 %all-gather.45.cloned.1.call-start = ((), (), s32[]{:S(2)}) async-start(), calls=%async_computation.56 | async-start | bytes 1474560 | tf_op jit(solution)/shard_map/all_gather | solution.py:32
  61.4 68.8 %all-gather.47.cloned.1.call-start = ((), (), s32[]{:S(2)}) async-start(), calls=%async_computation.57 | async-start | bytes 2322432 | tf_op jit(solution)/shard_map/all_gather | solution.py:45
  63.4 110.1 %reduce-scatter.41.cloned.1.call-start = ((), (), s32[]{:S(2)}) async-start(), calls=%async_computation.58 | async-start | bytes 2949120 | tf_op jit(solution)/shard_map/reduce_scatter | solution.py:36
  141.8 89.6 %all-gather.113.cloned.1.call-start = ((), (), s32[]{:S(2)}) async-start(), calls=%async_computation.130 | async-start | bytes 2985984 | tf_op jit(solution)/shard_map/all_gather | solution.py:45
  143.9 105.7 %all-gather.49.cloned.1.call-start = ((), (), s32[]{:S(2)}) async-start(), calls=%async_computation.59 | async-start | bytes 1474560 | tf_op jit(solution)/shard_map/all_gather | solution.py:32
  184.7 122.8 %all-gather.115.cloned.1.call-start = ((), (), s32[]{:S(2)}) async-start(), calls=%async_computation.131 | async-start | bytes 2985984 | tf_op jit(solution)/shard_map/all_gather | solution.py:50
  186.8 158.2 %reduce-scatter.43.cloned.1.call-start = ((), (), s32[]{:S(2)}) async-start(), calls=%async_computation.60 | async-start | bytes 2949120 | tf_op jit(solution)/shard_map/reduce_scatter | solution.py:36
  313.2 123.6 %all-gather.53.cloned.1.call-start = ((), (), s32[]{:S(2)}) async-start(), calls=%async_computation.62 | async-start | bytes 2322432 | tf_op jit(solution)/shard_map/all_gather | solution.py:45
  357.0 79.8 %all-gather.51.cloned.1.call-start = ((), (), s32[]{:S(2)}) async-start(), calls=%async_computation.61 | async-start | bytes 1474560 | tf_op jit(solution)/shard_map/all_gather | solution.py:32
  402.4 92.1 %reduce-scatter.45.cloned.1.call-start = ((), (), s32[]{:S(2)}) async-start(), calls=%async_computation.63 | async-start | bytes 2949120 | tf_op jit(solution)/shard_map/reduce_scatter | solution.py:36
  462.9 95.9 %all-gather.117.cloned.1.call-start = ((), (), s32[]{:S(2)}) async-start(), calls=%async_computation.132 | async-start | bytes 2985984 | tf_op jit(solution)/shard_map/all_gather | solution.py:45
  463.6 112.9 %all-gather.55.cloned.1.call-start = ((), (), s32[]{:S(2)}) async-start(), calls=%async_computation.64 | async-start | bytes 1474560 | tf_op jit(solution)/shard_map/all_gather | solution.py:32
  504.4 91.9 %all-gather.81.cloned.1.call-start = ((), (), s32[]{:S(2)}) async-start(), calls=%async_computation.90 | async-start | bytes 1474560 | tf_op jit(solution)/shard_map/all_gather | solution.py:32
  551.7 101.9 %all-gather.119.cloned.1.call-start = ((), (), s32[]{:S(2)}) async-start(), calls=%async_computation.133 | async-start | bytes 2985984 | tf_op jit(solution)/shard_map/all_gather | solution.py:50
  552.2 144.1 %reduce-scatter.73.cloned.1.call-start = ((), (), s32[]{:S(2)}) async-start(), calls=%async_computation.91 | async-start | bytes 2949120 | tf_op jit(solution)/shard_map/reduce_scatter | solution.py:36
  664.6 67.2 %reduce-scatter.47.cloned.1.call-start = ((), (), s32[]{:S(2)}) async-start(), calls=%async_computation.65 | async-start | bytes 2949120 | tf_op jit(solution)/shard_map/reduce_scatter | solution.py:36
  670.4 82.6 %all-gather.83.cloned.1.call-start = ((), (), s32[]{:S(2)}) async-start(), calls=%async_computation.92 | async-start | bytes 1474560 | tf_op jit(solution)/shard_map/all_gather | solution.py:32
  735.4 80.1 %reduce-scatter.75.cloned.1.call-start = ((), (), s32[]{:S(2)}) async-start(), calls=%async_computation.93 | async-start | bytes 2949120 | tf_op jit(solution)/shard_map/reduce_scatter | solution.py:36
  782.4 84.2 %all-gather.85.cloned.1.call-start = ((), (), s32[]{:S(2)}) async-start(), calls=%async_computation.94 | async-start | bytes 1474560 | tf_op jit(solution)/shard_map/all_gather | solution.py:32
  1002.3 91.9 %reduce-scatter.57.cloned.1.call-start = ((), (), s32[]{:S(2)}) async-start(), calls=%async_computation.75 | async-start | bytes 2949120 | tf_op jit(solution)/shard_map/reduce_scatter | solution.py:36
  1029.2 100.6 %reduce-scatter.65.cloned.1.call-start = ((), (), s32[]{:S(2)}) async-start(), calls=%async_computation.83 | async-start | bytes 2949120 | tf_op jit(solution)/shard_map/reduce_scatter | solution.py:36
  1054.8 110.6 %reduce-scatter.49.cloned.1.call-start = ((), (), s32[]{:S(2)}) async-start(), calls=%async_computation.67 | async-start | bytes 2949120 | tf_op jit(solution)/shard_map/reduce_scatter | solution.py:36
  1074.5 124.7 %all-gather.59.cloned.1.call-start = ((), (), s32[]{:S(2)}) async-start(), calls=%async_computation.68 | async-start | bytes 1474560 | tf_op jit(solution)/shard_map/all_gather | solution.py:32
  1183.6 90.7 %reduce-scatter.51.cloned.1.call-start = ((), (), s32[]{:S(2)}) async-start(), calls=%async_computation.69 | async-start | bytes 2949120 | tf_op jit(solution)/shard_map/reduce_scatter | solution.py:36
  1208.0 101.7 %reduce-scatter.59.cloned.1.call-start = ((), (), s32[]{:S(2)}) async-start(), calls=%async_computation.77 | async-start | bytes 2949120 | tf_op jit(solution)/shard_map/reduce_scatter | solution.py:36
  1227.5 118.0 %reduce-scatter.67.cloned.1.call-start = ((), (), s32[]{:S(2)}) async-start(), calls=%async_computation.85 | async-start | bytes 2949120 | tf_op jit(solution)/shard_map/reduce_scatter | solution.py:36
  1443.4 86.2 %reduce-scatter.69.cloned.1.call-start = ((), (), s32[]{:S(2)}) async-start(), calls=%async_computation.87 | async-start | bytes 2949120 | tf_op jit(solution)/shard_map/reduce_scatter | solution.py:36
  1472.8 92.5 %reduce-scatter.61.cloned.1.call-start = ((), (), s32[]{:S(2)}) async-start(), calls=%async_computation.79 | async-start | bytes 2949120 | tf_op jit(solution)/shard_map/reduce_scatter | solution.py:36
  1500.4 100.5 %reduce-scatter.53.cloned.1.call-start = ((), (), s32[]{:S(2)}) async-start(), calls=%async_computation.71 | async-start | bytes 2949120 | tf_op jit(solution)/shard_map/reduce_scatter | solution.py:36
  1521.7 196.3 %all-gather.79.cloned.1.call-start = ((), (), s32[]{:S(2)}) async-start(), calls=%async_computation.88 | async-start | bytes 1474560 | tf_op jit(solution)/shard_map/all_gather | solution.py:32
  1618.4 105.0 %all-gather.105.cloned.1.call-start = ((), (), s32[]{:S(2)}) async-start(), calls=%async_computation.114 | async-start | bytes 1474560 | tf_op jit(solution)/shard_map/all_gather | solution.py:32
  1651.1 83.3 %all-gather.71.cloned.1.call-start = ((), (), s32[]{:S(2)}) async-start(), calls=%async_computation.80 | async-start | bytes 1474560 | tf_op jit(solution)/shard_map/all_gather | solution.py:32
  1653.9 86.0 %all-gather.97.cloned.1.call-start = ((), (), s32[]{:S(2)}) async-start(), calls=%async_computation.106 | async-start | bytes 1474560 | tf_op jit(solution)/shard_map/all_gather | solution.py:32
  1687.1 69.5 %all-gather.89.cloned.1.call-start = ((), (), s32[]{:S(2)}) async-start(), calls=%async_computation.98 | async-start | bytes 1474560 | tf_op jit(solution)/shard_map/all_gather | solution.py:32
  1717.5 68.1 %reduce-scatter.97.cloned.1.call-start = ((), (), s32[]{:S(2)}) async-start(), calls=%async_computation.115 | async-start | bytes 2949120 | tf_op jit(solution)/shard_map/reduce_scatter | solution.py:36
  1734.4 80.2 %reduce-scatter.89.cloned.1.call-start = ((), (), s32[]{:S(2)}) async-start(), calls=%async_computation.107 | async-start | bytes 2949120 | tf_op jit(solution)/shard_map/reduce_scatter | solution.py:36
  1750.9 99.4 %reduce-scatter.81.cloned.1.call-start = ((), (), s32[]{:S(2)}) async-start(), calls=%async_computation.99 | async-start | bytes 2949120 | tf_op jit(solution)/shard_map/reduce_scatter | solution.py:36
  1767.6 118.3 %reduce-scatter.63.cloned.1.call-start = ((), (), s32[]{:S(2)}) async-start(), calls=%async_computation.81 | async-start | bytes 2949120 | tf_op jit(solution)/shard_map/reduce_scatter | solution.py:36
  1773.4 148.1 %reduce-scatter.71.cloned.1.call-start = ((), (), s32[]{:S(2)}) async-start(), calls=%async_computation.89 | async-start | bytes 2949120 | tf_op jit(solution)/shard_map/reduce_scatter | solution.py:36
  1779.2 177.9 %reduce-scatter.55.cloned.1.call-start = ((), (), s32[]{:S(2)}) async-start(), calls=%async_computation.73 | async-start | bytes 2949120 | tf_op jit(solution)/shard_map/reduce_scatter | solution.py:36
  1785.1 191.6 %all-gather.99.cloned.1.call-start = ((), (), s32[]{:S(2)}) async-start(), calls=%async_computation.108 | async-start | bytes 1474560 | tf_op jit(solution)/shard_map/all_gather | solution.py:32
  1889.4 116.9 %all-gather.91.cloned.1.call-start = ((), (), s32[]{:S(2)}) async-start(), calls=%async_computation.100 | async-start | bytes 1474560 | tf_op jit(solution)/shard_map/all_gather | solution.py:32
  1962.0 69.4 %all-gather.107.cloned.1.call-start = ((), (), s32[]{:S(2)}) async-start(), calls=%async_computation.116 | async-start | bytes 1474560 | tf_op jit(solution)/shard_map/all_gather | solution.py:32
  1965.7 85.4 %reduce-scatter.91.cloned.1.call-start = ((), (), s32[]{:S(2)}) async-start(), calls=%async_computation.109 | async-start | bytes 2949120 | tf_op jit(solution)/shard_map/reduce_scatter | solution.py:36
  2005.4 81.0 %reduce-scatter.83.cloned.1.call-start = ((), (), s32[]{:S(2)}) async-start(), calls=%async_computation.101 | async-start | bytes 2949120 | tf_op jit(solution)/shard_map/reduce_scatter | solution.py:36
  2030.6 91.5 %reduce-scatter.99.cloned.1.call-start = ((), (), s32[]{:S(2)}) async-start(), calls=%async_computation.117 | async-start | bytes 2949120 | tf_op jit(solution)/shard_map/reduce_scatter | solution.py:36
  2190.8 88.6 %reduce-scatter.93.cloned.1.call-start = ((), (), s32[]{:S(2)}) async-start(), calls=%async_computation.111 | async-start | bytes 2949120 | tf_op jit(solution)/shard_map/reduce_scatter | solution.py:36
  2216.2 98.9 %reduce-scatter.85.cloned.1.call-start = ((), (), s32[]{:S(2)}) async-start(), calls=%async_computation.103 | async-start | bytes 2949120 | tf_op jit(solution)/shard_map/reduce_scatter | solution.py:36
  2235.8 114.7 %reduce-scatter.101.cloned.1.call-start = ((), (), s32[]{:S(2)}) async-start(), calls=%async_computation.119 | async-start | bytes 2949120 | tf_op jit(solution)/shard_map/reduce_scatter | solution.py:36
  2254.9 188.9 %all-gather.103.cloned.1.call-start = ((), (), s32[]{:S(2)}) async-start(), calls=%async_computation.112 | async-start | bytes 1474560 | tf_op jit(solution)/shard_map/all_gather | solution.py:32
  2365.6 92.7 %all-gather.95.cloned.1.call-start = ((), (), s32[]{:S(2)}) async-start(), calls=%async_computation.104 | async-start | bytes 1474560 | tf_op jit(solution)/shard_map/all_gather | solution.py:32
  2368.7 136.1 %all-gather.111.cloned.1.call-start = ((), (), s32[]{:S(2)}) async-start(), calls=%async_computation.120 | async-start | bytes 1474560 | tf_op jit(solution)/shard_map/all_gather | solution.py:32
  2371.7 343.2 %reduce-scatter.113.cloned.1.call-start = ((), (), s32[]{:S(2)}) async-start(), calls=%async_computation.126 | async-start | bytes 5971968 | tf_op jit(solution)/shard_map/reduce_scatter | solution.py:341
  2380.7 334.3 %reduce-scatter.119.cloned.1.call-start = ((), (), s32[]{:S(2)}) async-start(), calls=%async_computation.129 | async-start | bytes 5971968 | tf_op jit(solution)/shard_map/reduce_scatter | solution.py:341
  2390.4 377.0 %reduce-scatter.115.cloned.1.call-start = ((), (), s32[]{:S(2)}) async-start(), calls=%async_computation.127 | async-start | bytes 5971968 | tf_op jit(solution)/shard_map/reduce_scatter | solution.py:341
  2400.2 474.4 %reduce-scatter.117.cloned.1.call-start = ((), (), s32[]{:S(2)}) async-start(), calls=%async_computation.128 | async-start | bytes 5971968 | tf_op jit(solution)/shard_map/reduce_scatter | solution.py:341
  2409.9 571.9 %reduce-scatter.105.cloned.1.call-start = ((), (), s32[]{:S(2)}) async-start(), calls=%async_computation.122 | async-start | bytes 5971968 | tf_op jit(solution)/shard_map/reduce_scatter | solution.py:338
  2418.1 670.7 %reduce-scatter.109.cloned.1.call-start = ((), (), s32[]{:S(2)}) async-start(), calls=%async_computation.124 | async-start | bytes 5971968 | tf_op jit(solution)/shard_map/reduce_scatter | solution.py:338
  2426.4 769.5 %reduce-scatter.107.cloned.1.call-start = ((), (), s32[]{:S(2)}) async-start(), calls=%async_computation.123 | async-start | bytes 5971968 | tf_op jit(solution)/shard_map/reduce_scatter | solution.py:338
  2434.9 868.2 %reduce-scatter.111.cloned.1.call-start = ((), (), s32[]{:S(2)}) async-start(), calls=%async_computation.125 | async-start | bytes 5971968 | tf_op jit(solution)/shard_map/reduce_scatter | solution.py:338
  2443.1 895.3 %reduce-scatter.95.cloned.1.call-start = ((), (), s32[]{:S(2)}) async-start(), calls=%async_computation.113 | async-start | bytes 2949120 | tf_op jit(solution)/shard_map/reduce_scatter | solution.py:36
  2457.5 917.1 %reduce-scatter.87.cloned.1.call-start = ((), (), s32[]{:S(2)}) async-start(), calls=%async_computation.105 | async-start | bytes 2949120 | tf_op jit(solution)/shard_map/reduce_scatter | solution.py:36
  2472.0 938.4 %reduce-scatter.103.cloned.1.call-start = ((), (), s32[]{:S(2)}) async-start(), calls=%async_computation.121 | async-start | bytes 2949120 | tf_op jit(solution)/shard_map/reduce_scatter | solution.py:36
  2518.6 1604.8 %all-reduce.27.cloned.1.call-start = ((), (), s32[]{:S(2)}) async-start(), calls=%async_computation.134 | async-start | bytes 47185920
  (439 other events, 18386.4 us)
Sparse Core Ops, SparseCore 0:
  79.3 50.9 all-gather.46
  142.0 31.5 reduce-scatter.40
  176.4 55.0 all-gather.112
  252.4 55.0 all-gather.114
  313.3 31.6 reduce-scatter.42
  347.8 60.2 all-gather.52
  463.0 31.3 reduce-scatter.44
  496.8 61.8 all-gather.116
  578.7 17.4 all-gather.80
  598.5 55.0 all-gather.118
  664.7 31.6 reduce-scatter.72
  698.8 33.0 reduce-scatter.46
  735.5 17.4 all-gather.82
  782.5 33.0 reduce-scatter.74
  877.7 33.0 reduce-scatter.76
  922.0 18.5 all-gather.86
  954.3 33.0 reduce-scatter.78
  1001.1 18.4 all-gather.64
  1021.6 17.4 all-gather.72
  1041.2 17.4 all-gather.56
  1061.1 33.0 reduce-scatter.56
  1096.7 33.0 reduce-scatter.64
  1132.3 33.0 reduce-scatter.48
  1180.6 18.4 all-gather.58
  1220.9 17.4 all-gather.74
  1241.1 33.0 reduce-scatter.50
  1276.6 33.0 reduce-scatter.58
  1312.4 33.0 reduce-scatter.66
  1476.5 17.4 all-gather.60
  1496.5 33.0 reduce-scatter.68
  1532.2 33.0 reduce-scatter.60
  1567.8 33.0 reduce-scatter.52
  1618.6 18.8 all-gather.78
  1687.4 17.4 all-gather.96
  1726.0 17.4 all-gather.88
  1746.0 33.0 reduce-scatter.96
  1781.5 33.0 reduce-scatter.88
  1817.2 33.0 reduce-scatter.80
  1852.8 33.0 reduce-scatter.62
  1888.4 33.0 reduce-scatter.70
  1924.0 33.0 reduce-scatter.54
  1959.2 17.4 all-gather.98
  2017.6 33.0 reduce-scatter.90
  2053.3 33.0 reduce-scatter.82
  2088.9 33.0 reduce-scatter.98
  2226.3 17.4 all-gather.108
  2246.3 33.0 reduce-scatter.92
  2281.9 33.0 reduce-scatter.84
  2317.4 33.0 reduce-scatter.100
  2365.7 18.4 all-gather.102
  2385.7 17.4 all-gather.94
  2404.7 17.4 all-gather.110
  2426.3 103.6 reduce-scatter.112
  2534.2 116.8 reduce-scatter.118
  2655.0 112.3 reduce-scatter.114
  2771.6 103.0 reduce-scatter.116
  2878.6 103.0 reduce-scatter.104
  2985.7 103.0 reduce-scatter.108
  3092.8 103.0 reduce-scatter.106
  3200.0 103.0 reduce-scatter.110
  3306.2 32.1 reduce-scatter.94
  3341.5 33.0 reduce-scatter.86
  3377.4 33.0 reduce-scatter.102
  3416.1 707.1 all-reduce.26
  (15 shorter events, 247.1 us)
where the time goes:
time: 4160 us; the launch traced here: 4140 us
  waiting for transfers between devices  2730 us (66%)
  blocking collectives  403 us (10%)
  matrix products  393 us (9%)
  local copies, waits for them, and re-layouts  330 us (8%)
  other arithmetic  212 us (5%)
  starting transfers between devices  57.4 us (1%)
    reduce_scatter x32, waiting for transfers between devices, feature_sums(): lax.psum_scatter(partial_value, 'col', scatter_dimension=1, tiled=True)  917 us
    unnamed x80, waiting for transfers between devices  655 us
    reduce_scatter x4, waiting for transfers between devices, shards(): lax.psum_scatter(terms[2].astype(jnp.bfloat16), 'row', scatter_dimension=...  425 us
    all_gather x32, waiting for transfers between devices, gather_features(): return lax.all_gather(value, 'col', axis=1, tiled=True)  221 us
    reduce_scatter x4, waiting for transfers between devices, shards(): lax.psum_scatter(terms[3].astype(jnp.bfloat16), 'row', scatter_dimension=...  160 us
    dot_general x32, matrix products, fold_product(): jnp.dot(left, lax.all_gather(weight, 'row', axis=0, tiled=True), preferre...  143 us
    psum x15, blocking collectives, row_totals(): return lax.psum((first, second), 'col')  126 us
    dot_general x32, matrix products, contract_last(): lax.dot_general(left, right, (((1,), (1,)), ((), ())), preferred_element_...  116 us
  transfers between devices with their start and end apart: 90, of which 71 were waited for; matrix products, arithmetic and copies ran while one was open for 17% of the time, Pallas kernels for 0%

commit v1 on v0

v1 whole, which is shorter than its diff:
```python
import functools

import jax
import jax.numpy as jnp
import numpy as np
from jax import lax
from jax.experimental import pallas as pl
from jax.experimental.pallas import tpu as pltpu
from jax.sharding import Mesh
from jax.sharding import PartitionSpec as P

D = 1152
HD = 72
P_SIZE = 256
NF = 16
SCALE = HD ** (-0.5)
EPSILON = 1e-06


f32 = jnp.float32
bf16 = jnp.bfloat16


def bits_of(count):
    found = []
    bit = count // 2
    while bit:
        found.append(bit)
        bit //= 2
    return found


def swap(value, axis, bit):
    count = lax.axis_size(axis)
    return lax.ppermute(value, axis, [(i, i ^ bit) for i in range(count)])


def row_order(rows):
    order = [0]
    for bit in bits_of(rows):
        order = order + [j ^ bit for j in order]
    return order


def step_plan(rows, parts, kind):
    by_row = [("row", bit) for bit in bits_of(rows)]
    by_part = [("m", bit) for bit in bits_of(parts)]
    if kind == 0 or not by_row or len(by_part) < 2:
        return by_row + by_part
    return by_row[:-1] + by_part[:-1] + by_row[-1:] + by_part[-1:]


def moved(label, axis, bit):
    return (label[0] ^ bit, label[1]) if axis == "row" else (label[0], label[1] ^ bit)


def gather_blocks(shard, rows, parts, kind):
    buffers = [([(0, 0)], shard[None])]
    plan = step_plan(rows, parts, kind)
    for number, (axis, bit) in enumerate(plan):
        fresh = []
        for labels, value in buffers:
            other = swap(value, axis, bit)
            other_labels = [moved(label, axis, bit) for label in labels]
            if number < len(plan) - 2:
                fresh.append((labels + other_labels, jnp.concatenate([value, other], 0)))
            else:
                fresh.append((labels, value))
                fresh.append((other_labels, other))
        buffers = fresh
    depth, width = shard.shape
    blocks = []
    for part in range(parts):
        wanted = [(j, part) for j in row_order(rows)]
        pieces = []
        for labels, value in buffers:
            hits = [place for place, label in enumerate(labels) if label[1] == part]
            if hits:
                rank = wanted.index(labels[hits[0]])
                pieces.append((rank, value[hits[0] : hits[-1] + 1]))
                assert [labels[h] for h in hits] == wanted[rank : rank + len(hits)]
        pieces = [piece for _, piece in sorted(pieces, key=lambda item: item[0])]
        whole = pieces[0] if len(pieces) == 1 else jnp.concatenate(pieces, 0)
        blocks.append(whole.reshape(rows * depth, width))
    return blocks


def total(terms):
    result = terms[0].astype(f32)
    for term in terms[1:]:
        result = result + term.astype(f32)
    return result


def scatter_blocks(blocks, rows, parts, kind):
    order = row_order(rows)
    height = blocks[0].shape[0] // rows
    live = {part: [blocks[part]] for part in range(parts)}
    span = rows
    for axis, bit in reversed(step_plan(rows, parts, kind)):
        if axis == "m":
            for part in [p for p in live if p & bit]:
                terms = live.pop(part)
                sent = terms[0] if len(terms) == 1 else total(terms).astype(bf16)
                live[part ^ bit].append(swap(sent, axis, bit))
        else:
            half = span // 2
            assert all(order[half + p] == order[p] ^ bit for p in range(half))
            names = sorted(live)
            sent = jnp.stack(
                [total([t[half * height :] for t in live[n]]).astype(bf16) for n in names]
            )
            got = swap(sent, axis, bit)
            for place, name in enumerate(names):
                live[name] = [t[: half * height] for t in live[name]] + [got[place]]
            span = half
    return total(live[0])


def all_sum(value, axis):
    for bit in bits_of(lax.axis_size(axis)):
        value = value + swap(value, axis, bit)
    return value


def over_u(value):
    return lax.psum(value, "u") if lax.axis_size("u") > 1 else value


def features_all(value):
    return lax.all_gather(value, "u", axis=1, tiled=True) if lax.axis_size("u") > 1 else value


def features_sum(value):
    if lax.axis_size("u") > 1:
        return lax.psum_scatter(value, "u", scatter_dimension=1, tiled=True)
    return value


def dot_nn(left, right):
    return lax.dot_general(left, right, (((1,), (0,)), ((), ())), preferred_element_type=f32)


def dot_nt(left, right):
    return lax.dot_general(left, right, (((1,), (1,)), ((), ())), preferred_element_type=f32)


def dot_tn(left, right):
    return lax.dot_general(left, right, (((0,), (0,)), ((), ())), preferred_element_type=f32)


def apart(value):
    return lax.optimization_barrier(value)


def gelu_tanh(value):
    return jax.nn.gelu(value, approximate=True)


def probabilities(query, key, allowed):
    scores = dot_nt(query, key) * SCALE
    if allowed is not None:
        scores = jnp.where(allowed, scores, -jnp.inf)
    powered = jnp.exp(scores - jnp.max(scores, -1, keepdims=True))
    return powered / jnp.sum(powered, -1, keepdims=True)


def allowed_pairs(temporal, span, tokens):
    if not temporal:
        return None
    first = lax.broadcasted_iota(jnp.int32, (tokens, tokens), 0)
    second = lax.broadcasted_iota(jnp.int32, (tokens, tokens), 1)
    return lax.rem(first, span) == lax.rem(second, span)


def forward_kernel(parts, temporal, span, *refs):
    ins, out = refs[:parts], refs[parts]
    width = ins[0].shape[-1] // 3
    tokens = int(np.prod(ins[0].shape[:-1]))
    allowed = allowed_pairs(temporal, span, tokens)
    for part in range(parts):
        block = ins[part][...].reshape(tokens, 3 * width)
        done = []
        for start in range(0, width, HD):
            query, key, value = [block[:, c * width + start : c * width + start + HD] for c in range(3)]
            weights = probabilities(query, key, allowed).astype(bf16)
            done.append(dot_nn(weights, value).astype(bf16))
        joined = done[0] if len(done) == 1 else jnp.concatenate(done, 1)
        where = (Ellipsis, slice(part * width, (part + 1) * width))
        out[where] = joined.reshape(out.shape[:-1] + (width,))


def backward_kernel(parts, temporal, span, *refs):
    ins, grad, outs = refs[:parts], refs[parts], refs[parts + 1 :]
    width = ins[0].shape[-1] // 3
    tokens = int(np.prod(ins[0].shape[:-1]))
    allowed = allowed_pairs(temporal, span, tokens)
    for part in range(parts):
        block = ins[part][...].reshape(tokens, 3 * width)
        outer = grad[..., part * width : (part + 1) * width].reshape(tokens, width)
        pieces = [[], [], []]
        for start in range(0, width, HD):
            query, key, value = [block[:, c * width + start : c * width + start + HD] for c in range(3)]
            above = outer[:, start : start + HD]
            weights = probabilities(query, key, allowed)
            grad_weights = dot_nt(above, value)
            inner = jnp.sum(grad_weights * weights, -1, keepdims=True)
            grad_scores = (weights * (grad_weights - inner)).astype(bf16)
            pieces[0].append((dot_nn(grad_scores, key) * SCALE).astype(bf16))
            pieces[1].append((dot_tn(grad_scores, query) * SCALE).astype(bf16))
            pieces[2].append(dot_tn(weights.astype(bf16), above).astype(bf16))
        joined = jnp.concatenate(pieces[0] + pieces[1] + pieces[2], 1)
        outs[part][...] = joined.reshape(outs[part].shape)


def attention_specs(layout, width):
    if len(layout) == 2:
        return (layout[0],), pl.BlockSpec((1, layout[1], width), lambda g: (g, 0, 0))
    chunk = 16
    assert layout[2] % chunk == 0
    return (
        (layout[0], layout[2] // chunk),
        pl.BlockSpec((1, layout[1], chunk, width), lambda g, c: (g, 0, c, 0)),
    )


def attend_forward(qkv, layout):
    parts = len(qkv)
    tokens, triple = qkv[0].shape
    width = triple // 3
    grid, in_spec = attention_specs(layout, triple)
    out_spec = attention_specs(layout, parts * width)[1]
    temporal = len(layout) == 3
    heads = parts * width // HD
    attended = pl.pallas_call(
        functools.partial(forward_kernel, parts, temporal, 16),
        grid=grid,
        in_specs=[in_spec] * parts,
        out_specs=out_spec,
        out_shape=jax.ShapeDtypeStruct(layout + (parts * width,), bf16),
        cost_estimate=pl.CostEstimate(
            flops=tokens * heads * 256 * 128 * 4,
            transcendentals=tokens * heads * 256,
            bytes_accessed=tokens * width * parts * 8,
        ),
        name="attend_forward",
    )(*[block.reshape(layout + (triple,)) for block in qkv])
    return attended.reshape(tokens, parts * width)


def attend_backward(qkv, grad, layout):
    parts = len(qkv)
    tokens, triple = qkv[0].shape
    width = triple // 3
    grid, in_spec = attention_specs(layout, triple)
    grad_spec = attention_specs(layout, parts * width)[1]
    temporal = len(layout) == 3
    heads = parts * width // HD
    grads = pl.pallas_call(
        functools.partial(backward_kernel, parts, temporal, 16),
        grid=grid,
        in_specs=[in_spec] * parts + [grad_spec],
        out_specs=[in_spec] * parts,
        out_shape=[jax.ShapeDtypeStruct(layout + (triple,), bf16)] * parts,
        cost_estimate=pl.CostEstimate(
            flops=tokens * heads * 256 * 128 * 10,
            transcendentals=tokens * heads * 256,
            bytes_accessed=tokens * width * parts * 14,
        ),
        name="attend_backward",
    )(*[block.reshape(layout + (triple,)) for block in qkv], grad.reshape(layout + (parts * width,)))
    return [block.reshape(tokens, triple) for block in grads]


def norm_forward(stream):
    center = stream - over_u(jnp.sum(stream, 1, keepdims=True)) / D
    inverse = lax.rsqrt(over_u(jnp.sum(center * center, 1, keepdims=True)) / D + EPSILON)
    return center * inverse, inverse


def norm_backward(grad_normed, normed, inverse):
    first, second = over_u(
        (
            jnp.sum(grad_normed, 1, keepdims=True),
            jnp.sum(grad_normed * normed, 1, keepdims=True),
        )
    )
    return inverse * (grad_normed - first / D - normed * (second / D))


def spread(vector, tokens):
    groups, width = vector.shape
    if groups == 1:
        return vector
    return jnp.broadcast_to(vector[:, None, :], (groups, tokens // groups, width)).reshape(tokens, width)


def group_sum(value, groups):
    return jnp.sum(value.reshape(groups, -1, value.shape[-1]), 1)


def block_forward(stream, modulate, weights, layout):
    w_qkv, w_out, w_fc1, w_fc2, b_qkv, b_out, b_fc1, b_fc2 = weights
    tokens = stream.shape[0]
    pieces = [spread(modulate[:, column], tokens) for column in range(6)]
    normed, inverse = norm_forward(stream)
    hidden = features_all((normed * (1.0 + pieces[1]) + pieces[0]).astype(bf16))
    qkv = [(dot_nn(hidden, w) + b).astype(bf16) for w, b in zip(w_qkv, b_qkv)]
    attended = attend_forward(qkv, layout)
    branch = apart(features_sum(dot_nt(attended, w_out))) + b_out
    middle = stream + pieces[2] * branch
    normed_two, inverse_two = norm_forward(middle)
    hidden_two = features_all((normed_two * (1.0 + pieces[4]) + pieces[3]).astype(bf16))
    preact = [dot_nn(hidden_two, w) + b for w, b in zip(w_fc1, b_fc1)]
    activated = [gelu_tanh(p).astype(bf16) for p in preact]
    branch_two = apart(features_sum(total([dot_nt(a, w) for a, w in zip(activated, w_fc2)]))) + b_fc2
    result = middle + pieces[5] * branch_two
    kept = (
        pieces, normed, inverse, hidden, qkv, attended, branch,
        normed_two, inverse_two, hidden_two, preact, activated, branch_two,
    )
    return result, kept


def block_backward(grad, kept, groups, weights, layout, place):
    (
        pieces, normed, inverse, hidden, qkv, attended, branch,
        normed_two, inverse_two, hidden_two, preact, activated, branch_two,
    ) = kept
    w_qkv, w_out, w_fc1, w_fc2 = weights[:4]
    width = w_out.shape[1] // len(w_qkv)
    grad_branch_two = (pieces[5] * grad).astype(bf16)
    grad_two_all = features_all(grad_branch_two)
    d_fc2 = [dot_tn(grad_two_all, a).astype(bf16) for a in activated]
    sum_fc2 = place(d_fc2, 1)
    grad_preact = [
        jax.vjp(gelu_tanh, p)[1](dot_nn(grad_two_all, w))[0].astype(bf16) for p, w in zip(preact, w_fc2)
    ]
    d_fc1 = [dot_tn(hidden_two, g).astype(bf16) for g in grad_preact]
    sum_fc1 = place(d_fc1, 0)
    grad_hidden_two = apart(features_sum(total([dot_nt(g, w) for g, w in zip(grad_preact, w_fc1)])))
    grad_middle = grad + norm_backward(grad_hidden_two * (1.0 + pieces[4]), normed_two, inverse_two)
    grad_branch = (pieces[2] * grad_middle).astype(bf16)
    grad_branch_all = features_all(grad_branch)
    grad_attended = dot_nn(grad_branch_all, w_out).astype(bf16)
    d_out = dot_tn(grad_branch_all, attended).astype(bf16)
    grad_qkv = attend_backward(qkv, grad_attended, layout)
    d_mixed = [
        jnp.concatenate(
            [dot_tn(hidden, g).astype(bf16), d_out[:, part * width : (part + 1) * width]], 1
        )
        for part, g in enumerate(grad_qkv)
    ]
    sum_mixed = place(d_mixed, 1)
    grad_hidden = apart(features_sum(total([dot_nt(g, w) for g, w in zip(grad_qkv, w_qkv)])))
    grad_stream = grad_middle + norm_backward(grad_hidden * (1.0 + pieces[1]), normed, inverse)
    modulate_grad = jnp.stack(
        [
            group_sum(grad_hidden, groups),
            group_sum(grad_hidden * normed, groups),
            group_sum(grad_middle * branch, groups),
            group_sum(grad_hidden_two, groups),
            group_sum(grad_hidden_two * normed_two, groups),
            group_sum(grad * branch_two, groups),
        ],
        1,
    )
    summed = lambda value: jnp.sum(value.astype(f32), 0)
    bias_grads = (
        jnp.stack([summed(g[:, :width]) for g in grad_qkv]),
        jnp.stack([summed(g[:, 2 * width :]) for g in grad_qkv]),
        summed(grad_branch),
        jnp.stack([summed(g) for g in grad_preact]),
        summed(grad_branch_two),
    )
    return grad_stream, (sum_mixed, sum_fc1, sum_fc2), bias_grads, modulate_grad


def shards(
    latents, cond, w_ada, b_ada, w_qkv, b_qv, w_out, b_out, w_fc1, b_fc1, w_fc2, b_fc2, cotangent
):
    batches, width, tokens = latents.shape
    lat_count = cond.shape[1]
    rows = lax.axis_size("row")
    parts = lax.axis_size("m")
    split = lax.axis_size("u")
    row = lax.axis_index("row")
    part_here = lax.axis_index("m")
    span = parts * width
    order = jnp.asarray(row_order(rows), jnp.int32)
    inverse_order = jnp.asarray(np.argsort(row_order(rows)), jnp.int32)
    part_ids = part_here ^ jnp.arange(parts)
    frames_dev = tokens // P_SIZE
    pos_block = tokens // (lat_count * NF)
    spatial = (frames_dev, P_SIZE)
    temporal = (lat_count, NF, pos_block)

    relative = split == 1
    depth = D // rows
    if relative:
        slot = jnp.arange(D)
        source = (row ^ order[slot // depth]) * depth + slot % depth
        exchange = (jnp.arange(D)[:, None] == source[None, :]).astype(bf16)

    def vector_rel(value):
        if not relative:
            return value
        shaped = value.reshape(value.shape[:-1] + (rows, depth))
        return jnp.take(shaped, row ^ order, axis=-2).reshape(value.shape)

    def vector_plain(value):
        if not relative:
            return value
        shaped = value.reshape(value.shape[:-1] + (rows, depth))
        return jnp.take(shaped, inverse_order[row ^ jnp.arange(rows)], axis=-2).reshape(value.shape)

    def stream_plain(value):
        return dot_nt(value, exchange).astype(bf16) if relative else value

    def stream_rel(value):
        return dot_nn(value, exchange) if relative else value.astype(f32)

    def to_positions(value):
        shaped = stream_plain(value.astype(bf16)).reshape(frames_dev, rows, pos_block, span)
        got = lax.all_to_all(shaped, "row", split_axis=1, concat_axis=0, tiled=True)
        return stream_rel(got.reshape(tokens, span))

    def to_frames(value):
        shaped = stream_plain(value.astype(bf16)).reshape(frames_dev * rows, 1, pos_block, span)
        got = lax.all_to_all(shaped, "row", split_axis=0, concat_axis=1, tiled=True)
        return got.reshape(tokens, span)

    def whole(shard, kind):
        blocks = gather_blocks(shard, rows, parts, kind)
        if relative:
            return blocks
        places = inverse_order[row ^ jnp.arange(rows)]
        return [jnp.take(b.reshape(rows, depth, -1), places, axis=0).reshape(b.shape) for b in blocks]

    def place(blocks, kind):
        if not relative:
            blocks = [
                jnp.take(b.reshape(rows, depth, -1), row ^ order, axis=0).reshape(b.shape)
                for b in blocks
            ]
        return scatter_blocks(blocks, rows, parts, kind)

    cond_float = cond.astype(f32)
    cond_low = jax.nn.silu(cond_float).astype(bf16)
    mod_partial = jnp.einsum("mlr,brjk->mlbjk", cond_low, w_ada, preferred_element_type=f32)
    mod_partial = mod_partial + jnp.where(row == 0, b_ada.astype(f32), 0.0)[None, None]
    small = jnp.concatenate(
        [b.astype(f32).reshape(-1) for b in (b_qv, b_out, b_fc1, b_fc2)]
    )
    packed = jnp.concatenate(
        [mod_partial.reshape(batches, -1), jnp.broadcast_to(small, (parts,) + small.shape)], 1
    )
    packed = lax.all_to_all(packed, "m", split_axis=0, concat_axis=0, tiled=True)
    mod_size = lat_count * 12 * width
    mod_here = all_sum(packed[:, :mod_size], "row").reshape(parts, lat_count, 2, 6, width)
    mod_here = vector_rel(jnp.moveaxis(mod_here, 0, -2).reshape(lat_count, 2, 6, span))
    small = packed[:, mod_size:]
    sizes = np.cumsum([0, 4 * width, 2 * width, 2 * b_fc1.shape[1], 2 * width])
    all_qv, all_out, all_fc1, all_fc2 = [small[:, a:b] for a, b in zip(sizes[:-1], sizes[1:])]
    all_qv = jnp.take(all_qv.reshape(parts, 2, 2, width), part_ids, axis=0)
    all_fc1 = jnp.take(all_fc1.reshape(parts, 2, -1), part_ids, axis=0)
    all_out = vector_rel(jnp.moveaxis(all_out.reshape(parts, 2, width), 0, 1).reshape(2, span))
    all_fc2 = vector_rel(jnp.moveaxis(all_fc2.reshape(parts, 2, width), 0, 1).reshape(2, span))

    block_weights = []
    for which in range(2):
        mixed = jnp.concatenate([w_qkv[which].reshape(depth, 3 * width), w_out[which]], 1)
        mixed = whole(mixed, 0)
        zeros = jnp.zeros((width,), f32)
        block_weights.append(
            (
                [b[:, : 3 * width] for b in mixed],
                jnp.concatenate([b[:, 3 * width :] for b in mixed], 1),
                whole(w_fc1[which], 1),
                whole(w_fc2[which], 0),
                [jnp.concatenate([all_qv[i, which, 0], zeros, all_qv[i, which, 1]]) for i in range(parts)],
                all_out[which],
                [all_fc1[i, which] for i in range(parts)],
                all_fc2[which],
            )
        )

    def own_batch(value):
        return lax.all_to_all(value, "m", split_axis=0, concat_axis=1, tiled=True)[0]

    def to_stream(value):
        return dot_tn(value, exchange) if relative else value.T.astype(f32)

    def to_argument(value):
        return lax.all_to_all(value[None], "m", split_axis=1, concat_axis=0, tiled=True)

    lat_here = row * frames_dev // NF
    mod_space = lax.dynamic_slice_in_dim(mod_here[:, 0], lat_here, 1, 0)
    mod_time = mod_here[:, 1]
    first_in = to_stream(own_batch(latents))
    grad_top = own_batch(cotangent).T
    shaped = grad_top.reshape(frames_dev, rows, pos_block, span)
    grad_top = stream_rel(
        lax.all_to_all(shaped, "row", split_axis=1, concat_axis=0, tiled=True).reshape(tokens, span)
    )
    first_out, kept_space = block_forward(first_in, mod_space, block_weights[0], spatial)
    second_in = to_positions(first_out)
    second_out, kept_time = block_forward(second_in, mod_time, block_weights[1], temporal)
    output = to_argument(to_frames(second_out).T)

    grad_mid, weights_time, biases_time, mod_grad_time = block_backward(
        grad_top, kept_time, lat_count, block_weights[1], temporal, place
    )
    grad_low = stream_rel(to_frames(grad_mid))
    grad_first, weights_space, biases_space, mod_grad_space = block_backward(
        grad_low, kept_space, 1, block_weights[0], spatial, place
    )
    grad_first = grad_first.astype(bf16)
    grad_first = dot_nt(exchange, grad_first).astype(bf16) if relative else grad_first.T
    grad_latents = to_argument(grad_first).astype(f32)

    onehot = (jnp.arange(lat_count) == lat_here).astype(f32)
    mod_grads = jnp.stack([onehot[:, None, None] * mod_grad_space, mod_grad_time], 1)
    mod_grads = vector_plain(mod_grads).reshape(lat_count, 2, 6, parts, width)
    mod_grads = jnp.moveaxis(mod_grads, -2, 0).reshape(parts, -1)

    def by_part(value):
        return jnp.take(value, part_ids, axis=0)

    def by_stream(value):
        return vector_plain(value).reshape(parts, width)

    pieces = [mod_grads]
    for space, time in zip(biases_space, biases_time):
        for value in (space, time):
            pieces.append(by_part(value) if value.ndim == 2 else by_stream(value))
    counts = np.cumsum([0] + [piece.shape[1] for piece in pieces])
    packed = jnp.concatenate(pieces, 1)
    packed = lax.all_to_all(packed, "m", split_axis=0, concat_axis=0, tiled=True)
    mod_part = packed[:, : counts[1]]
    bias_part = jnp.sum(packed[:, counts[1] :], 0, keepdims=True)
    flat = jnp.concatenate([mod_part.reshape(1, -1), bias_part], 1)
    flat = all_sum(flat, "row")[0]
    mod_grad_low = flat[: batches * counts[1]].reshape(batches, lat_count, 2, 6, width).astype(bf16)
    bias_part = flat[batches * counts[1] :]
    bias_out = [bias_part[a - counts[1] : b - counts[1]] for a, b in zip(counts[1:-1], counts[2:])]
    grad_bias_qv = jnp.stack(
        [jnp.stack([bias_out[0], bias_out[2]]), jnp.stack([bias_out[1], bias_out[3]])]
    )
    grad_bias_out = jnp.stack(bias_out[4:6])
    grad_bias_fc1 = jnp.stack(bias_out[6:8])
    grad_bias_fc2 = jnp.stack(bias_out[8:10])
    grad_bias_ada = jnp.sum(mod_grad_low.astype(f32), (0, 1))
    grad_weight_ada = jnp.einsum("mlr,mlbjk->brjk", cond_low, mod_grad_low, preferred_element_type=f32)
    cond_partial = jnp.einsum("mlbjk,brjk->mlr", mod_grad_low, w_ada, preferred_element_type=f32)
    cond_total = over_u(all_sum(cond_partial, "m"))
    sigmoid_cond = jax.nn.sigmoid(cond_float)
    grad_condition = cond_total * sigmoid_cond * (1.0 + cond_float * (1.0 - sigmoid_cond))
    grad_weight_qkv, grad_weight_out, grad_weight_fc1, grad_weight_fc2 = [], [], [], []
    for mixed, first, second in (weights_space, weights_time):
        grad_weight_qkv.append(mixed[:, : 3 * width].reshape(depth, 3, width))
        grad_weight_out.append(mixed[:, 3 * width :])
        grad_weight_fc1.append(first)
        grad_weight_fc2.append(second)
    return (
        output,
        grad_latents,
        grad_condition,
        grad_weight_ada,
        grad_bias_ada,
        jnp.stack(grad_weight_qkv),
        grad_bias_qv,
        jnp.stack(grad_weight_out),
        grad_bias_out,
        jnp.stack(grad_weight_fc1),
        grad_bias_fc1,
        jnp.stack(grad_weight_fc2),
        grad_bias_fc2,
    )


def solution(mesh):
    rows, columns = mesh.devices.shape

    def placed(latents, *rest):
        parts = latents.shape[0]
        inner = Mesh(mesh.devices.reshape(rows, columns // parts, parts), ("row", "u", "m"))
        col = ("u", "m")
        in_specs = (
            P(None, col, "row"),
            P(None, None, "row"),
            P(None, "row", None, col),
            P(None, None, col),
            P(None, "row", None, col),
            P(None, None, col),
            P(None, "row", col),
            P(None, col),
            P(None, "row", col),
            P(None, col),
            P(None, "row", col),
            P(None, col),
            P(None, col, "row"),
        )
        out_specs = (P(None, col, "row"),) + in_specs[:1] + in_specs[1:-1]
        return jax.shard_map(
            shards, mesh=inner, in_specs=in_specs, out_specs=out_specs, check_vma=False
        )(latents, *rest)

    return placed
```

time: 4160 us -> 1500 us (0.36)
  waiting for transfers between devices: 2730 us -> 487 us
  blocking collectives: 403 us -> 0 us
  matrix products: 393 us -> 286 us
  Pallas kernels: 0 us -> 80.9 us
  starting transfers between devices: 57.4 us -> 118 us
  local copies, waits for them, and re-layouts: 330 us -> 277 us
    reduce_scatter x40 -> x0, waiting for transfers between devices: 1500 us -> none  [the longest x32 917 us: feature_sums(): lax.psum_scatter(partial_value, 'col', scatter_dimension=1, tiled=True)]
    unnamed x80 -> x0, waiting for transfers between devices: 655 us -> none
    ppermute x0 -> x80, waiting for transfers between devices: none -> 475 us  [swap(): return lax.ppermute(value, axis, [(i, i ^ bit) for i in range(count)])]
    all_gather x38 -> x0, waiting for transfers between devices: 412 us -> none  [the longest x32 221 us: gather_features(): return lax.all_gather(value, 'col', axis=1, tiled=True)]
    psum x17 -> x0, blocking collectives: 206 us -> none  [the longest x15 126 us: row_totals(): return lax.psum((first, second), 'col')]
    all_to_all x11 -> x10, waiting for transfers between devices: 158 us -> 11.4 us  [the longest x2 11.2 us: own_batch(): lax.all_to_all(value, 'm', split_axis=0, concat_axis=1, tiled=True)[0]]
    all_to_all x5 -> x0, blocking collectives: 127 us -> none  [the longest x4 110 us: to_positions(): lax.all_to_all(shaped, 'row', split_axis=1, concat_axis=0, tiled=True)]
    dot_general x145 -> x87, matrix products: 390 us -> 284 us  [the longest x29 99.2 us: dot_nn(): lax.dot_general(left, right, (((1,), (0,)), ((), ())), preferred_element_...]
  transfers between devices with their start and end apart: 90 -> 90, of which waited for: 71 -> 29; matrix products, arithmetic and copies ran while one was open for 17% -> 47% of each run, Pallas kernels for 0% -> 4%
where the time goes in v1:
time: 1500 us; the launch traced here: 1480 us
  waiting for transfers between devices  487 us (32%)
  matrix products  286 us (19%)
  local copies, waits for them, and re-layouts  277 us (18%)
  other arithmetic  230 us (15%)
  starting transfers between devices  118 us (8%)
  Pallas kernels  80.9 us (5%)
    ppermute x80, waiting for transfers between devices, swap(): return lax.ppermute(value, axis, [(i, i ^ bit) for i in range(count)])  475 us
    dot_general x29, matrix products, dot_nn(): lax.dot_general(left, right, (((1,), (0,)), ((), ())), preferred_element_...  99.2 us
    dot_general x30, matrix products, dot_nt(): lax.dot_general(left, right, (((1,), (1,)), ((), ())), preferred_element_...  95 us
    dot_general x27, matrix products, dot_tn(): lax.dot_general(left, right, (((0,), (0,)), ((), ())), preferred_element_...  88.8 us
    unnamed x475, local copies, waits for them, and re-layouts  83.9 us
    another operation x26, other arithmetic, scatter_blocks(): jnp.stack([total([t[half * height:] for t in live[n]]).astype(bf16) for n...  75.3 us
    ppermute x80, starting transfers between devices, swap(): return lax.ppermute(value, axis, [(i, i ^ bit) for i in range(count)])  72.2 us
    pallas_call x2, Pallas kernels, attend_backward(): pl.pallas_call(functools.partial(backward_kernel, parts, temporal, 16), g...  45.9 us
  transfers between devices with their start and end apart: 90, of which 29 were waited for; matrix products, arithmetic and copies ran while one was open for 47% of the time, Pallas kernels for 4%

profile of v1, /device:TPU:0, one launch (start us, length us, event | category | flops | bytes accessed | tf_op | source)
XLA Modules:
  0.0 1483.8 jit_solution(1917832131237067858)
XLA Ops:
  7.0 4.2 all-to-all-start.1
  30.6 4.3 all-to-all-start
  49.0 28.3 %collective-permute-done = f32[4,3456]{1,0:T(4,128)} collective-permute-done((f32[4,3456]{1,0:T(4,128)}, f32[4,3456]{1,0:T(4,128)}, u32[]{:S(2)}, u32[]{:S(2)}) %collective-permute-start) | collective-permute-done | bytes 55328 | tf_op jit(solution)/shard_map/ppermute | solution.py:35
  106.8 7.4 collective-permute-done.27
  121.6 4.3 all-to-all-start.5
  130.6 11.2 all-to-all-done.5
  146.6 5.1 all-to-all-start.6
  162.4 15.5 %collective-permute-done.22 = bf16[2,144,1152]{2,1,0:T(8,128)(2,1)} collective-permute-done((bf16[2,144,1152]{2,1,0:T(8,128)(2,1)}, bf16[2,144,1152]{2,1,0:T(8,128)(2,1)}, u32[]{:S(2)}, u32[]{:S(2)}) %collective-permute-start.22) | collective-permute-done | bytes 663584 | tf_op jit(solution)/shard_map/ppermute | solution.py:35
  179.8 18.5 %collective-permute-done.28 = bf16[2,144,1152]{2,1,0:T(8,128)(2,1)S(1)} collective-permute-done((bf16[2,144,1152]{2,1,0:T(8,128)(2,1)}, bf16[2,144,1152]{2,1,0:T(8,128)(2,1)S(1)}, u32[]{:S(2)}, u32[]{:S(2)}) %collective-permute-start.28) | collective-permute-done | bytes 663584 | tf_op jit(solution)/shard_map/ppermute | solution.py:35
  200.0 15.6 %collective-permute-done.32 = bf16[2,144,1152]{2,1,0:T(8,128)(2,1)S(1)} collective-permute-done((bf16[2,144,1152]{2,1,0:T(8,128)(2,1)S(1)}, bf16[2,144,1152]{2,1,0:T(8,128)(2,1)S(1)}, u32[]{:S(2)}, u32[]{:S(2)}) %collective-permute-start.32) | collective-permute-done | bytes 663584 | tf_op jit(solution)/shard_map/ppermute | solution.py:35
  230.4 17.2 %collective-permute-done.29 = bf16[4,144,1152]{2,1,0:T(8,128)(2,1)S(1)} collective-permute-done((bf16[4,144,1152]{2,1,0:T(8,128)(2,1)S(1)}, bf16[4,144,1152]{2,1,0:T(8,128)(2,1)S(1)}, u32[]{:S(2)}, u32[]{:S(2)}) %collective-permute-start.29) | collective-permute-done | bytes 1327136 | tf_op jit(solution)/shard_map/ppermute | solution.py:35
  250.4 4.9 collective-permute-done.23
  271.9 12.0 collective-permute-done.33
  286.8 5.0 convert_reduce_fusion
  293.1 47.7 %collective-permute-done.12 = bf16[8,144,1152]{2,1,0:T(8,128)(2,1)} collective-permute-done((bf16[8,144,1152]{2,1,0:T(8,128)(2,1)}, bf16[8,144,1152]{2,1,0:T(8,128)(2,1)}, u32[]{:S(2)}, u32[]{:S(2)}) %collective-permute-start.12) | collective-permute-done | bytes 2654240 | tf_op jit(solution)/shard_map/ppermute | solution.py:35
  354.6 41.8 %collective-permute-done.30 = bf16[8,144,1152]{2,1,0:T(8,128)(2,1)} collective-permute-done((bf16[8,144,1152]{2,1,0:T(8,128)(2,1)}, bf16[8,144,1152]{2,1,0:T(8,128)(2,1)}, u32[]{:S(2)}, u32[]{:S(2)}) %collective-permute-start.30) | collective-permute-done | bytes 2654240 | tf_op jit(solution)/shard_map/ppermute | solution.py:35
  426.0 5.8 concatenate.190
  431.8 17.4 %attend_forward.2 = bf16[2,256,1152]{2,1,0:T(8,128)(2,1)} custom-call(bf16[2,256,864]{2,1,0:T(8,128)(2,1)} %bitcast.553, bf16[2,256,864]{2,1,0:T(8,128)(2,1)} %bitcast.557, bf16[2,256,864]{2,1,0:T(8,128)(2,1)} %bitcast.555, bf16[2,256,864]{2,1,0:T(8,128)(2,1)} %bitcast.559), custom_call_target="tpu_custom_call" | custom-call | flops 1073741824 | bytes 4718592 | tf_op jit(solution)/shard_map/attend_forward/pallas_call | solution.py:235
  449.2 5.4 fusion.269
  492.8 4.8 all-to-all-start.2
  505.6 26.8 %collective-permute-done.37 = bf16[8,144,1152]{2,1,0:T(8,128)(2,1)} collective-permute-done((bf16[8,144,1152]{2,1,0:T(8,128)(2,1)}, bf16[8,144,1152]{2,1,0:T(8,128)(2,1)}, u32[]{:S(2)}, u32[]{:S(2)}) %collective-permute-start.37) | collective-permute-done | bytes 2654240 | tf_op jit(solution)/shard_map/ppermute | solution.py:35
  538.0 5.8 concatenate.209
  571.6 17.6 %attend_forward.3 = bf16[1,16,32,1152]{3,2,1,0:T(8,128)(2,1)} custom-call(bf16[1,16,32,864]{3,2,1,0:T(8,128)(2,1)} %bitcast.567, bf16[1,16,32,864]{3,2,1,0:T(8,128)(2,1)} %bitcast.565, bf16[1,16,32,864]{3,2,1,0:T(8,128)(2,1)} %bitcast.563, bf16[1,16,32,864]{3,2,1,0:T(8,128)(2,1)} %bitcast.561), custom_call_target="tpu_custom_call" | custom-call | flops 1073741824 | bytes 4718592 | tf_op jit(solution)/shard_map/attend_forward/pallas_call | solution.py:235
  606.1 4.8 fusion.235
  610.9 4.5 fusion.236
  615.4 4.4 convert_reduce_fusion.5
  621.8 4.4 convert_reduce_fusion.4
  629.1 4.4 convert_reduce_fusion.3
  635.5 4.6 convert_reduce_fusion.2
  647.1 4.1 convolution_add_fusion.12
  657.6 23.0 %attend_backward.2 = (bf16[1,16,32,864]{3,2,1,0:T(8,128)(2,1)}, bf16[1,16,32,864]{3,2,1,0:T(8,128)(2,1)}, bf16[1,16,32,864]{3,2,1,0:T(8,128)(2,1)}, bf16[1,16,32,864]{3,2,1,0:T(8,128)(2,1)}) custom-call(bf16[1,16,32,864]{3,2,1,0:T(8,128)(2,1)} %bitcast.568, bf16[1,16,32,864]{3,2,1,0:T(8,128)(2,1)} %bitcast.566, bf16[1,16,32,864]{3,2,1,0:T(8,128)(2,1)} %bitcast.564, ...), custom_call_target="tpu_custom_call" | custom-call | flops 2684354560 | bytes 8257536 | tf_op jit(solution)/shard_map/attend_backward/pallas_call | solution.py:259
  724.7 5.1 all-to-all-start.7
  760.4 4.7 convert_reduce_fusion.1
  768.5 5.5 convert_reduce_fusion.7
  774.0 5.5 convert_reduce_fusion.8
  779.6 5.7 convert_reduce_fusion.9
  799.3 22.9 %attend_backward.3 = (bf16[2,256,864]{2,1,0:T(8,128)(2,1)}, bf16[2,256,864]{2,1,0:T(8,128)(2,1)}, bf16[2,256,864]{2,1,0:T(8,128)(2,1)}, bf16[2,256,864]{2,1,0:T(8,128)(2,1)}) custom-call(bf16[2,256,864]{2,1,0:T(8,128)(2,1)} %bitcast.554, bf16[2,256,864]{2,1,0:T(8,128)(2,1)} %bitcast.558, bf16[2,256,864]{2,1,0:T(8,128)(2,1)} %bitcast.556, ...), custom_call_target="tpu_custom_call" | custom-call | flops 2684354560 | bytes 8257536 | tf_op jit(solution)/shard_map/attend_backward/pallas_call | solution.py:259
  823.5 4.8 fusion.106
  907.0 6.0 all-to-all-start.3
  916.3 4.8 convolution_convert_fusion.15
  921.1 24.2 %collective-permute-done.39 = f32[1,18432]{1,0:T(1,128)S(1)} collective-permute-done((f32[1,18432]{1,0:T(1,128)S(1)}, f32[1,18432]{1,0:T(1,128)S(1)}, u32[]{:S(2)}, u32[]{:S(2)}) %collective-permute-start.39) | collective-permute-done | bytes 73760 | tf_op jit(solution)/shard_map/ppermute | solution.py:35
  954.1 10.7 copy.287
  965.4 9.7 reduce.113
  978.9 4.7 all-to-all-start.8
  986.0 6.2 copy.182
  992.2 9.7 reduce.112
  1019.1 4.1 fusion.123
  1023.3 4.2 fusion.124
  1030.7 4.5 all-to-all-start.4
  1040.9 4.7 copy.218
  1046.1 5.7 add_convert_fusion
  1075.2 4.7 copy.204
  1089.6 5.0 add_convert_fusion.1
  1094.6 35.6 %collective-permute-done.76 = bf16[2,576,1152]{2,1,0:T(8,128)(2,1)} collective-permute-done((bf16[2,576,1152]{2,1,0:T(8,128)(2,1)}, bf16[2,576,1152]{2,1,0:T(8,128)(2,1)}, u32[]{:S(2)}, u32[]{:S(2)}) %collective-permute-start.76) | collective-permute-done | bytes 2654240 | tf_op jit(solution)/shard_map/ppermute | solution.py:35
  1134.1 52.9 %collective-permute-done.52 = bf16[2,576,1152]{2,1,0:T(8,128)(2,1)S(1)} collective-permute-done((bf16[2,576,1152]{2,1,0:T(8,128)(2,1)}, bf16[2,576,1152]{2,1,0:T(8,128)(2,1)S(1)}, u32[]{:S(2)}, u32[]{:S(2)}) %collective-permute-start.52) | collective-permute-done | bytes 2654240 | tf_op jit(solution)/shard_map/ppermute | solution.py:35
  1213.5 5.9 collective-permute-done.77
  1224.3 23.5 %collective-permute-done.53 = bf16[576,1152]{1,0:T(8,128)(2,1)} collective-permute-done((bf16[576,1152]{1,0:T(8,128)(2,1)}, bf16[576,1152]{1,0:T(8,128)(2,1)}, u32[]{:S(2)}, u32[]{:S(2)}) %collective-permute-start.53) | collective-permute-done | bytes 1327136 | tf_op jit(solution)/shard_map/ppermute | solution.py:35
  1258.8 13.3 collective-permute-done.65
  1281.3 7.6 collective-permute-done.54
  1303.6 5.5 collective-permute-done.66
  1323.0 24.5 %collective-permute-done.46 = bf16[2,576,1152]{2,1,0:T(8,128)(2,1)} collective-permute-done((bf16[2,576,1152]{2,1,0:T(8,128)(2,1)}, bf16[2,576,1152]{2,1,0:T(8,128)(2,1)}, u32[]{:S(2)}, u32[]{:S(2)}) %collective-permute-start.46) | collective-permute-done | bytes 2654240 | tf_op jit(solution)/shard_map/ppermute | solution.py:35
  1392.4 6.8 collective-permute-done.47
  1420.9 16.2 %collective-permute-done.48 = bf16[1,288,1152]{2,1,0:T(8,128)(2,1)} collective-permute-done((bf16[1,288,1152]{2,1,0:T(8,128)(2,1)}, bf16[1,288,1152]{2,1,0:T(8,128)(2,1)}, u32[]{:S(2)}, u32[]{:S(2)}) %collective-permute-start.48) | collective-permute-done | bytes 663584 | tf_op jit(solution)/shard_map/ppermute | solution.py:35
  1453.7 14.8 collective-permute-done.49
  (1035 shorter events, 728.7 us)
Async XLA Ops:
  13.5 81.6 %collective-permute-start.3 = (bf16[1,144,1152]{2,1,0:T(8,128)(2,1)S(1)}, bf16[1,144,1152]{2,1,0:T(8,128)(2,1)}, u32[]{:S(2)}, u32[]{:S(2)}) collective-permute-start(bf16[1,144,1152]{2,1,0:T(8,128)(2,1)S(1)} %maximum_bitcast_fusion), channel_id=1, source_target_pairs={{0,16},{4,20},{8,24},{12,28},{16,0},{20,4},{24,8},{28,12},{1,17},{... | collective-permute-start | bytes 995336 | tf_op jit(solution)/shard_map/ppermute | solution.py:35
  17.8 80.0 %collective-permute-start.9 = (bf16[1,144,1152]{2,1,0:T(8,128)(2,1)S(1)}, bf16[1,144,1152]{2,1,0:T(8,128)(2,1)}, u32[]{:S(2)}, u32[]{:S(2)}) collective-permute-start(bf16[1,144,1152]{2,1,0:T(8,128)(2,1)S(1)} %get-tuple-element.225), channel_id=1, source_target_pairs={{0,16},{4,20},{8,24},{12,28},{16,0},{20,4},{24,8},{28,12},{1,17},{... | collective-permute-start | bytes 995336 | tf_op jit(solution)/shard_map/ppermute | solution.py:35
  19.1 81.7 %collective-permute-start.13 = (bf16[1,144,1152]{2,1,0:T(8,128)(2,1)S(1)}, bf16[1,144,1152]{2,1,0:T(8,128)(2,1)}, u32[]{:S(2)}, u32[]{:S(2)}) collective-permute-start(bf16[1,144,1152]{2,1,0:T(8,128)(2,1)S(1)} %get-tuple-element.227), channel_id=1, source_target_pairs={{0,16},{4,20},{8,24},{12,28},{16,0},{20,4},{24,8},{28,12},{1,17},{... | collective-permute-start | bytes 995336 | tf_op jit(solution)/shard_map/ppermute | solution.py:35
  26.1 77.6 %collective-permute-start.21 = (bf16[1,144,1152]{2,1,0:T(8,128)(2,1)S(1)}, bf16[1,144,1152]{2,1,0:T(8,128)(2,1)}, u32[]{:S(2)}, u32[]{:S(2)}) collective-permute-start(bf16[1,144,1152]{2,1,0:T(8,128)(2,1)S(1)} %maximum_bitcast_fusion.1), channel_id=1, source_target_pairs={{0,16},{4,20},{8,24},{12,28},{16,0},{20,4},{24,8},{28,12},{1,17},{... | collective-permute-start | bytes 995336 | tf_op jit(solution)/shard_map/ppermute | solution.py:35
  30.6 91.0 %all-to-all-start = ((bf16[4,288,512]{2,1,0:T(8,128)(2,1)}), bf16[4,288,512]{2,1,0:T(8,128)(2,1)}, u32[]{:S(2)}, u32[]{:S(2)}) async-start(bf16[4,288,512]{2,1,0:T(8,128)(2,1)} %param.25), calls=%async_computation | async-start | bytes 2359296 | tf_op jit(solution)/shard_map/all_to_all | solution.py:489
  97.8 59.4 %collective-permute-start.4 = (bf16[2,144,1152]{2,1,0:T(8,128)(2,1)}, bf16[2,144,1152]{2,1,0:T(8,128)(2,1)}, u32[]{:S(2)}, u32[]{:S(2)}) collective-permute-start(bf16[2,144,1152]{2,1,0:T(8,128)(2,1)} %pad_maximum_fusion.35), channel_id=1, source_target_pairs={{0,8},{4,12},{8,0},{12,4},{16,24},{20,28},{24,16},{28,20},{1,9},{5... | collective-permute-start | bytes 1990664 | tf_op jit(solution)/shard_map/ppermute | solution.py:35
  100.8 53.1 %collective-permute-start.10 = (bf16[2,144,1152]{2,1,0:T(8,128)(2,1)}, bf16[2,144,1152]{2,1,0:T(8,128)(2,1)S(1)}, u32[]{:S(2)}, u32[]{:S(2)}) collective-permute-start(bf16[2,144,1152]{2,1,0:T(8,128)(2,1)} %pad_maximum_fusion.36), channel_id=1, source_target_pairs={{0,8},{4,12},{8,0},{12,4},{16,24},{20,28},{24,16},{28,20},{1,9},{5... | collective-permute-start | bytes 1990664 | tf_op jit(solution)/shard_map/ppermute | solution.py:35
  103.7 55.2 %collective-permute-start.14 = (bf16[2,144,1152]{2,1,0:T(8,128)(2,1)}, bf16[2,144,1152]{2,1,0:T(8,128)(2,1)}, u32[]{:S(2)}, u32[]{:S(2)}) collective-permute-start(bf16[2,144,1152]{2,1,0:T(8,128)(2,1)} %pad_maximum_fusion.37), channel_id=1, source_target_pairs={{0,8},{4,12},{8,0},{12,4},{16,24},{20,28},{24,16},{28,20},{1,9},{5... | collective-permute-start | bytes 1990664 | tf_op jit(solution)/shard_map/ppermute | solution.py:35
  114.2 63.7 %collective-permute-start.22 = (bf16[2,144,1152]{2,1,0:T(8,128)(2,1)}, bf16[2,144,1152]{2,1,0:T(8,128)(2,1)}, u32[]{:S(2)}, u32[]{:S(2)}) collective-permute-start(bf16[2,144,1152]{2,1,0:T(8,128)(2,1)} %pad_maximum_fusion.38), channel_id=1, source_target_pairs={{0,8},{4,12},{8,0},{12,4},{16,24},{20,28},{24,16},{28,20},{1,9},{5... | collective-permute-start | bytes 1990664 | tf_op jit(solution)/shard_map/ppermute | solution.py:35
  119.9 78.4 %collective-permute-start.28 = (bf16[2,144,1152]{2,1,0:T(8,128)(2,1)}, bf16[2,144,1152]{2,1,0:T(8,128)(2,1)S(1)}, u32[]{:S(2)}, u32[]{:S(2)}) collective-permute-start(bf16[2,144,1152]{2,1,0:T(8,128)(2,1)} %pad_maximum_fusion.39), channel_id=1, source_target_pairs={{0,8},{4,12},{8,0},{12,4},{16,24},{20,28},{24,16},{28,20},{1,9},{5... | collective-permute-start | bytes 1990664 | tf_op jit(solution)/shard_map/ppermute | solution.py:35
  146.6 140.2 %all-to-all-start.6 = ((bf16[2,8,32,1152]{3,2,0,1:T(8,128)(2,1)}), bf16[2,8,32,1152]{3,2,0,1:T(8,128)(2,1)}, u32[]{:S(2)}, u32[]{:S(2)}) async-start(bf16[2,8,32,1152]{3,2,0,1:T(8,128)(2,1)} %copy.184), calls=%async_computation.6 | async-start | bytes 2359296 | tf_op jit(solution)/shard_map/all_to_all | solution.py:504
  153.9 61.7 %collective-permute-start.32 = (bf16[2,144,1152]{2,1,0:T(8,128)(2,1)S(1)}, bf16[2,144,1152]{2,1,0:T(8,128)(2,1)S(1)}, u32[]{:S(2)}, u32[]{:S(2)}) collective-permute-start(bf16[2,144,1152]{2,1,0:T(8,128)(2,1)S(1)} %copy-done.127), channel_id=1, source_target_pairs={{0,8},{4,12},{8,0},{12,4},{16,24},{20,28},{24,16},{28,20},{1,9},{5... | collective-permute-start | bytes 1990664 | tf_op jit(solution)/shard_map/ppermute | solution.py:35
  157.2 61.3 %collective-permute-start.11 = (bf16[4,144,1152]{2,1,0:T(8,128)(2,1)S(1)}, bf16[4,144,1152]{2,1,0:T(8,128)(2,1)S(1)}, u32[]{:S(2)}, u32[]{:S(2)}) collective-permute-start(bf16[4,144,1152]{2,1,0:T(8,128)(2,1)S(1)} %pad_maximum_fusion.27), channel_id=1, source_target_pairs={{0,2},{1,3},{2,0},{3,1},{4,6},{5,7},{6,4},{7,5},{8,10},{9,11},{10,... | collective-permute-start | bytes 3981320 | tf_op jit(solution)/shard_map/ppermute | solution.py:35
  159.0 62.7 %collective-permute-start.5 = (bf16[4,144,1152]{2,1,0:T(8,128)(2,1)S(1)}, bf16[4,144,1152]{2,1,0:T(8,128)(2,1)S(1)}, u32[]{:S(2)}, u32[]{:S(2)}) collective-permute-start(bf16[4,144,1152]{2,1,0:T(8,128)(2,1)S(1)} %pad_maximum_fusion.26), channel_id=1, source_target_pairs={{0,4},{4,0},{8,12},{12,8},{16,20},{20,16},{24,28},{28,24},{1,5},{5... | collective-permute-start | bytes 3981320 | tf_op jit(solution)/shard_map/ppermute | solution.py:35
  177.9 49.0 %collective-permute-start.15 = (bf16[4,144,1152]{2,1,0:T(8,128)(2,1)S(1)}, bf16[4,144,1152]{2,1,0:T(8,128)(2,1)S(1)}, u32[]{:S(2)}, u32[]{:S(2)}) collective-permute-start(bf16[4,144,1152]{2,1,0:T(8,128)(2,1)S(1)} %pad_maximum_fusion.28), channel_id=1, source_target_pairs={{0,4},{4,0},{8,12},{12,8},{16,20},{20,16},{24,28},{28,24},{1,5},{5... | collective-permute-start | bytes 3981320 | tf_op jit(solution)/shard_map/ppermute | solution.py:35
  198.3 57.0 %collective-permute-start.23 = (bf16[4,144,1152]{2,1,0:T(8,128)(2,1)S(1)}, bf16[4,144,1152]{2,1,0:T(8,128)(2,1)S(1)}, u32[]{:S(2)}, u32[]{:S(2)}) collective-permute-start(bf16[4,144,1152]{2,1,0:T(8,128)(2,1)S(1)} %pad_maximum_fusion.29), channel_id=1, source_target_pairs={{0,4},{4,0},{8,12},{12,8},{16,20},{20,16},{24,28},{28,24},{1,5},{5... | collective-permute-start | bytes 3981320 | tf_op jit(solution)/shard_map/ppermute | solution.py:35
  218.5 65.4 %collective-permute-start.33 = (bf16[4,144,1152]{2,1,0:T(8,128)(2,1)}, bf16[4,144,1152]{2,1,0:T(8,128)(2,1)}, u32[]{:S(2)}, u32[]{:S(2)}) collective-permute-start(bf16[4,144,1152]{2,1,0:T(8,128)(2,1)} %pad_maximum_fusion.31), channel_id=1, source_target_pairs={{0,4},{4,0},{8,12},{12,8},{16,20},{20,16},{24,28},{28,24},{1,5},{5... | collective-permute-start | bytes 3981320 | tf_op jit(solution)/shard_map/ppermute | solution.py:35
  221.7 119.1 %collective-permute-start.12 = (bf16[8,144,1152]{2,1,0:T(8,128)(2,1)}, bf16[8,144,1152]{2,1,0:T(8,128)(2,1)}, u32[]{:S(2)}, u32[]{:S(2)}) collective-permute-start(bf16[8,144,1152]{2,1,0:T(8,128)(2,1)} %pad_maximum_fusion.3), channel_id=1, source_target_pairs={{0,4},{4,0},{8,12},{12,8},{16,20},{20,16},{24,28},{28,24},{1,5},{5... | collective-permute-start | bytes 7962632 | tf_op jit(solution)/shard_map/ppermute | solution.py:35
  226.9 115.8 %collective-permute-start.7 = (bf16[8,144,1152]{2,1,0:T(8,128)(2,1)}, bf16[8,144,1152]{2,1,0:T(8,128)(2,1)}, u32[]{:S(2)}, u32[]{:S(2)}) collective-permute-start(bf16[8,144,1152]{2,1,0:T(8,128)(2,1)} %pad_maximum_fusion.2), channel_id=1, source_target_pairs={{0,2},{1,3},{2,0},{3,1},{4,6},{5,7},{6,4},{7,5},{8,10},{9,11},{10,... | collective-permute-start | bytes 7962632 | tf_op jit(solution)/shard_map/ppermute | solution.py:35
  247.7 99.8 %collective-permute-start.6 = (bf16[8,144,1152]{2,1,0:T(8,128)(2,1)}, bf16[8,144,1152]{2,1,0:T(8,128)(2,1)}, u32[]{:S(2)}, u32[]{:S(2)}) collective-permute-start(bf16[8,144,1152]{2,1,0:T(8,128)(2,1)} %pad_maximum_fusion.2), channel_id=1, source_target_pairs={{0,1},{1,0},{2,3},{3,2},{4,5},{5,4},{6,7},{7,6},{8,9},{9,8},{10,11... | collective-permute-start | bytes 7962632 | tf_op jit(solution)/shard_map/ppermute | solution.py:35
  255.3 141.0 %collective-permute-start.30 = (bf16[8,144,1152]{2,1,0:T(8,128)(2,1)}, bf16[8,144,1152]{2,1,0:T(8,128)(2,1)}, u32[]{:S(2)}, u32[]{:S(2)}) collective-permute-start(bf16[8,144,1152]{2,1,0:T(8,128)(2,1)} %pad_maximum_fusion.11), channel_id=1, source_target_pairs={{0,4},{4,0},{8,12},{12,8},{16,20},{20,16},{24,28},{28,24},{1,5},{5... | collective-permute-start | bytes 7962632 | tf_op jit(solution)/shard_map/ppermute | solution.py:35
  283.9 129.0 %collective-permute-start.16 = (bf16[8,144,1152]{2,1,0:T(8,128)(2,1)}, bf16[8,144,1152]{2,1,0:T(8,128)(2,1)}, u32[]{:S(2)}, u32[]{:S(2)}) collective-permute-start(bf16[8,144,1152]{2,1,0:T(8,128)(2,1)} %pad_maximum_fusion.3), channel_id=1, source_target_pairs={{0,1},{1,0},{2,3},{3,2},{4,5},{5,4},{6,7},{7,6},{8,9},{9,8},{10,11... | collective-permute-start | bytes 7962632 | tf_op jit(solution)/shard_map/ppermute | solution.py:35
  340.8 131.5 %collective-permute-start.18 = (bf16[8,144,1152]{2,1,0:T(8,128)(2,1)}, bf16[8,144,1152]{2,1,0:T(8,128)(2,1)}, u32[]{:S(2)}, u32[]{:S(2)}) collective-permute-start(bf16[8,144,1152]{2,1,0:T(8,128)(2,1)} %pad_maximum_fusion.6), channel_id=1, source_target_pairs={{0,1},{1,0},{2,3},{3,2},{4,5},{5,4},{6,7},{7,6},{8,9},{9,8},{10,11... | collective-permute-start | bytes 7962632 | tf_op jit(solution)/shard_map/ppermute | solution.py:35
  342.7 118.0 %collective-permute-start.19 = (bf16[8,144,1152]{2,1,0:T(8,128)(2,1)}, bf16[8,144,1152]{2,1,0:T(8,128)(2,1)}, u32[]{:S(2)}, u32[]{:S(2)}) collective-permute-start(bf16[8,144,1152]{2,1,0:T(8,128)(2,1)} %pad_maximum_fusion.6), channel_id=1, source_target_pairs={{0,2},{1,3},{2,0},{3,1},{4,6},{5,7},{6,4},{7,5},{8,10},{9,11},{10,... | collective-permute-start | bytes 7962632 | tf_op jit(solution)/shard_map/ppermute | solution.py:35
  347.5 69.6 %collective-permute-start.8 = (bf16[8,144,1152]{2,1,0:T(8,128)(2,1)}, bf16[8,144,1152]{2,1,0:T(8,128)(2,1)}, u32[]{:S(2)}, u32[]{:S(2)}) collective-permute-start(bf16[8,144,1152]{2,1,0:T(8,128)(2,1)} %collective-permute-done.7), channel_id=1, source_target_pairs={{0,1},{1,0},{2,3},{3,2},{4,5},{5,4},{6,7},{7,6},{8,9},{9,8},{10,11... | collective-permute-start | bytes 7962632 | tf_op jit(solution)/shard_map/ppermute | solution.py:35
  396.3 64.7 %collective-permute-start.17 = (bf16[8,144,1152]{2,1,0:T(8,128)(2,1)}, bf16[8,144,1152]{2,1,0:T(8,128)(2,1)}, u32[]{:S(2)}, u32[]{:S(2)}) collective-permute-start(bf16[8,144,1152]{2,1,0:T(8,128)(2,1)} %collective-permute-done.12), channel_id=1, source_target_pairs={{0,1},{1,0},{2,3},{3,2},{4,5},{5,4},{6,7},{7,6},{8,9},{9,8},{10,11... | collective-permute-start | bytes 7962632 | tf_op jit(solution)/shard_map/ppermute | solution.py:35
  412.9 71.6 %collective-permute-start.25 = (bf16[8,144,1152]{2,1,0:T(8,128)(2,1)}, bf16[8,144,1152]{2,1,0:T(8,128)(2,1)}, u32[]{:S(2)}, u32[]{:S(2)}) collective-permute-start(bf16[8,144,1152]{2,1,0:T(8,128)(2,1)} %pad_maximum_fusion.10), channel_id=1, source_target_pairs={{0,2},{1,3},{2,0},{3,1},{4,6},{5,7},{6,4},{7,5},{8,10},{9,11},{10,... | collective-permute-start | bytes 7962632 | tf_op jit(solution)/shard_map/ppermute | solution.py:35
  417.2 86.0 %collective-permute-start.24 = (bf16[8,144,1152]{2,1,0:T(8,128)(2,1)}, bf16[8,144,1152]{2,1,0:T(8,128)(2,1)}, u32[]{:S(2)}, u32[]{:S(2)}) collective-permute-start(bf16[8,144,1152]{2,1,0:T(8,128)(2,1)} %pad_maximum_fusion.10), channel_id=1, source_target_pairs={{0,1},{1,0},{2,3},{3,2},{4,5},{5,4},{6,7},{7,6},{8,9},{9,8},{10,11... | collective-permute-start | bytes 7962632 | tf_op jit(solution)/shard_map/ppermute | solution.py:35
  460.7 71.8 %collective-permute-start.34 = (bf16[8,144,1152]{2,1,0:T(8,128)(2,1)}, bf16[8,144,1152]{2,1,0:T(8,128)(2,1)}, u32[]{:S(2)}, u32[]{:S(2)}) collective-permute-start(bf16[8,144,1152]{2,1,0:T(8,128)(2,1)} %pad_maximum_fusion.11), channel_id=1, source_target_pairs={{0,1},{1,0},{2,3},{3,2},{4,5},{5,4},{6,7},{7,6},{8,9},{9,8},{10,11... | collective-permute-start | bytes 7962632 | tf_op jit(solution)/shard_map/ppermute | solution.py:35
  472.3 60.2 %collective-permute-start.37 = (bf16[8,144,1152]{2,1,0:T(8,128)(2,1)}, bf16[8,144,1152]{2,1,0:T(8,128)(2,1)}, u32[]{:S(2)}, u32[]{:S(2)}) collective-permute-start(bf16[8,144,1152]{2,1,0:T(8,128)(2,1)} %pad_maximum_fusion.14), channel_id=1, source_target_pairs={{0,2},{1,3},{2,0},{3,1},{4,6},{5,7},{6,4},{7,5},{8,10},{9,11},{10,... | collective-permute-start | bytes 7962632 | tf_op jit(solution)/shard_map/ppermute | solution.py:35
  484.5 59.3 %collective-permute-start.35 = (bf16[8,144,1152]{2,1,0:T(8,128)(2,1)}, bf16[8,144,1152]{2,1,0:T(8,128)(2,1)}, u32[]{:S(2)}, u32[]{:S(2)}) collective-permute-start(bf16[8,144,1152]{2,1,0:T(8,128)(2,1)} %collective-permute-done.30), channel_id=1, source_target_pairs={{0,1},{1,0},{2,3},{3,2},{4,5},{5,4},{6,7},{7,6},{8,9},{9,8},{10,11... | collective-permute-start | bytes 7962632 | tf_op jit(solution)/shard_map/ppermute | solution.py:35
  484.7 50.7 %collective-permute-start.26 = (bf16[8,144,1152]{2,1,0:T(8,128)(2,1)}, bf16[8,144,1152]{2,1,0:T(8,128)(2,1)}, u32[]{:S(2)}, u32[]{:S(2)}) collective-permute-start(bf16[8,144,1152]{2,1,0:T(8,128)(2,1)} %collective-permute-done.25), channel_id=1, source_target_pairs={{0,1},{1,0},{2,3},{3,2},{4,5},{5,4},{6,7},{7,6},{8,9},{9,8},{10,11... | collective-permute-start | bytes 7962632 | tf_op jit(solution)/shard_map/ppermute | solution.py:35
  492.8 56.7 %all-to-all-start.2 = ((bf16[2,8,32,1152]{3,2,0,1:T(8,128)(2,1)}), bf16[2,8,32,1152]{3,2,0,1:T(8,128)(2,1)}, u32[]{:S(2)}, u32[]{:S(2)}) async-start(bf16[2,8,32,1152]{3,2,0,1:T(8,128)(2,1)} %copy.174), calls=%async_computation.2 | async-start | bytes 2359296 | tf_op jit(solution)/shard_map/all_to_all | solution.py:425
  503.1 103.0 %collective-permute-start.36 = (bf16[8,144,1152]{2,1,0:T(8,128)(2,1)}, bf16[8,144,1152]{2,1,0:T(8,128)(2,1)}, u32[]{:S(2)}, u32[]{:S(2)}) collective-permute-start(bf16[8,144,1152]{2,1,0:T(8,128)(2,1)} %pad_maximum_fusion.14), channel_id=1, source_target_pairs={{0,1},{1,0},{2,3},{3,2},{4,5},{5,4},{6,7},{7,6},{8,9},{9,8},{10,11... | collective-permute-start | bytes 7962632 | tf_op jit(solution)/shard_map/ppermute | solution.py:35
  532.5 103.0 %collective-permute-start.38 = (bf16[8,144,1152]{2,1,0:T(8,128)(2,1)}, bf16[8,144,1152]{2,1,0:T(8,128)(2,1)}, u32[]{:S(2)}, u32[]{:S(2)}) collective-permute-start(bf16[8,144,1152]{2,1,0:T(8,128)(2,1)} %collective-permute-done.37), channel_id=1, source_target_pairs={{0,1},{1,0},{2,3},{3,2},{4,5},{5,4},{6,7},{7,6},{8,9},{9,8},{10,11... | collective-permute-start | bytes 7962632 | tf_op jit(solution)/shard_map/ppermute | solution.py:35
  734.3 281.6 %collective-permute-start.74 = (bf16[1152,1152]{1,0:T(8,128)(2,1)}, bf16[1152,1152]{1,0:T(8,128)(2,1)}, u32[]{:S(2)}, u32[]{:S(2)}) collective-permute-start(bf16[1152,1152]{1,0:T(8,128)(2,1)} %convolution_convert_fusion.2), channel_id=1, source_target_pairs={{0,1},{1,0},{2,3},{3,2},{4,5},{5,4},{6,7},{7,6},{8,9},{9,8},{10,11... | collective-permute-start | bytes 7962632 | tf_op jit(solution)/shard_map/ppermute | solution.py:35
  734.6 292.8 %collective-permute-start.75 = (bf16[1152,1152]{1,0:T(8,128)(2,1)}, bf16[1152,1152]{1,0:T(8,128)(2,1)}, u32[]{:S(2)}, u32[]{:S(2)}) collective-permute-start(bf16[1152,1152]{1,0:T(8,128)(2,1)} %convolution_convert_fusion), channel_id=1, source_target_pairs={{0,1},{1,0},{2,3},{3,2},{4,5},{5,4},{6,7},{7,6},{8,9},{9,8},{10,11... | collective-permute-start | bytes 7962632 | tf_op jit(solution)/shard_map/ppermute | solution.py:35
  739.6 279.0 %collective-permute-start.50 = (bf16[1152,1152]{0,1:T(8,128)(2,1)}, bf16[1152,1152]{0,1:T(8,128)(2,1)}, u32[]{:S(2)}, u32[]{:S(2)}) collective-permute-start(bf16[1152,1152]{0,1:T(8,128)(2,1)} %pad_maximum_fusion.20), channel_id=1, source_target_pairs={{0,1},{1,0},{2,3},{3,2},{4,5},{5,4},{6,7},{7,6},{8,9},{9,8},{10,11... | collective-permute-start | bytes 7962632 | tf_op jit(solution)/shard_map/ppermute | solution.py:35
  742.1 281.1 %collective-permute-start.51 = (bf16[1152,1152]{0,1:T(8,128)(2,1)}, bf16[1152,1152]{0,1:T(8,128)(2,1)}, u32[]{:S(2)}, u32[]{:S(2)}) collective-permute-start(bf16[1152,1152]{0,1:T(8,128)(2,1)} %pad_maximum_fusion.21), channel_id=1, source_target_pairs={{0,1},{1,0},{2,3},{3,2},{4,5},{5,4},{6,7},{7,6},{8,9},{9,8},{10,11... | collective-permute-start | bytes 7962632 | tf_op jit(solution)/shard_map/ppermute | solution.py:35
  907.0 71.9 %all-to-all-start.3 = ((bf16[16,1,32,1152]{3,2,1,0:T(8,128)(2,1)}), bf16[16,1,32,1152]{3,2,1,0:T(8,128)(2,1)}, u32[]{:S(2)}, u32[]{:S(2)}) async-start(bf16[16,1,32,1152]{3,2,1,0:T(8,128)(2,1)} %bitcast.581), calls=%async_computation.3 | async-start | bytes 2359296 | tf_op jit(solution)/shard_map/all_to_all | solution.py:430
  949.9 55.8 %collective-permute-start.41 = (f32[1,18432]{1,0:T(1,128)S(1)}, f32[1,18432]{1,0:T(1,128)}, u32[]{:S(2)}, u32[]{:S(2)}) collective-permute-start(f32[1,18432]{1,0:T(1,128)S(1)} %add.995), channel_id=1, source_target_pairs={{0,4},{4,0},{8,12},{12,8},{16,20},{20,16},{24,28},{28,24},{1,5},{5... | collective-permute-start | bytes 221192 | tf_op jit(solution)/shard_map/ppermute | solution.py:35
  978.9 51.8 %all-to-all-start.8 = ((bf16[4,2,73728]{2,1,0:T(2,128)(2,1)}), bf16[4,2,73728]{2,1,0:T(2,128)(2,1)}, u32[]{:S(2)}, u32[]{:S(2)}) async-start(bf16[4,2,73728]{2,1,0:T(2,128)(2,1)} %reshape.1294), calls=%async_computation.8 | async-start | bytes 2359296 | tf_op jit(solution)/shard_map/all_to_all | solution.py:495
  1015.9 64.0 %collective-permute-start.68 = (bf16[1152,1152]{1,0:T(8,128)(2,1)}, bf16[1152,1152]{1,0:T(8,128)(2,1)}, u32[]{:S(2)}, u32[]{:S(2)}) collective-permute-start(bf16[1152,1152]{1,0:T(8,128)(2,1)} %convolution_convert_fusion.6), channel_id=1, source_target_pairs={{0,1},{1,0},{2,3},{3,2},{4,5},{5,4},{6,7},{7,6},{8,9},{9,8},{10,11... | collective-permute-start | bytes 7962632 | tf_op jit(solution)/shard_map/ppermute | solution.py:35
  1018.6 47.8 %collective-permute-start.44 = (bf16[1152,1152]{0,1:T(8,128)(2,1)}, bf16[1152,1152]{0,1:T(8,128)(2,1)}, u32[]{:S(2)}, u32[]{:S(2)}) collective-permute-start(bf16[1152,1152]{0,1:T(8,128)(2,1)} %pad_maximum_fusion.18), channel_id=1, source_target_pairs={{0,1},{1,0},{2,3},{3,2},{4,5},{5,4},{6,7},{7,6},{8,9},{9,8},{10,11... | collective-permute-start | bytes 7962632 | tf_op jit(solution)/shard_map/ppermute | solution.py:35
  1023.2 46.3 %collective-permute-start.45 = (bf16[1152,1152]{0,1:T(8,128)(2,1)}, bf16[1152,1152]{0,1:T(8,128)(2,1)}, u32[]{:S(2)}, u32[]{:S(2)}) collective-permute-start(bf16[1152,1152]{0,1:T(8,128)(2,1)} %pad_maximum_fusion.19), channel_id=1, source_target_pairs={{0,1},{1,0},{2,3},{3,2},{4,5},{5,4},{6,7},{7,6},{8,9},{9,8},{10,11... | collective-permute-start | bytes 7962632 | tf_op jit(solution)/shard_map/ppermute | solution.py:35
  1027.4 55.9 %collective-permute-start.69 = (bf16[1152,1152]{1,0:T(8,128)(2,1)}, bf16[1152,1152]{1,0:T(8,128)(2,1)}, u32[]{:S(2)}, u32[]{:S(2)}) collective-permute-start(bf16[1152,1152]{1,0:T(8,128)(2,1)} %convolution_convert_fusion.4), channel_id=1, source_target_pairs={{0,1},{1,0},{2,3},{3,2},{4,5},{5,4},{6,7},{7,6},{8,9},{9,8},{10,11... | collective-permute-start | bytes 7962632 | tf_op jit(solution)/shard_map/ppermute | solution.py:35
  1045.6 154.0 %collective-permute-start.62 = (bf16[1152,1152]{1,0:T(8,128)(2,1)}, bf16[1152,1152]{1,0:T(8,128)(2,1)}, u32[]{:S(2)}, u32[]{:S(2)}) collective-permute-start(bf16[1152,1152]{1,0:T(8,128)(2,1)} %convolution_convert_fusion.10), channel_id=1, source_target_pairs={{0,1},{1,0},{2,3},{3,2},{4,5},{5,4},{6,7},{7,6},{8,9},{9,8},{10,11... | collective-permute-start | bytes 7962632 | tf_op jit(solution)/shard_map/ppermute | solution.py:35
  1069.5 60.7 %collective-permute-start.76 = (bf16[2,576,1152]{2,1,0:T(8,128)(2,1)}, bf16[2,576,1152]{2,1,0:T(8,128)(2,1)}, u32[]{:S(2)}, u32[]{:S(2)}) collective-permute-start(bf16[2,576,1152]{2,1,0:T(8,128)(2,1)} %pad_maximum_fusion.23), channel_id=1, source_target_pairs={{0,4},{4,0},{8,12},{12,8},{16,20},{20,16},{24,28},{28,24},{1,5},{5... | collective-permute-start | bytes 7962632 | tf_op jit(solution)/shard_map/ppermute | solution.py:35
  1079.8 107.2 %collective-permute-start.52 = (bf16[2,576,1152]{2,1,0:T(8,128)(2,1)}, bf16[2,576,1152]{2,1,0:T(8,128)(2,1)S(1)}, u32[]{:S(2)}, u32[]{:S(2)}) collective-permute-start(bf16[2,576,1152]{2,1,0:T(8,128)(2,1)} %copy.218), channel_id=1, source_target_pairs={{0,4},{4,0},{8,12},{12,8},{16,20},{20,16},{24,28},{28,24},{1,5},{5... | collective-permute-start | bytes 7962632 | tf_op jit(solution)/shard_map/ppermute | solution.py:35
  1083.3 117.7 %collective-permute-start.64 = (bf16[1152,1152]{1,0:T(8,128)(2,1)}, bf16[1152,1152]{1,0:T(8,128)(2,1)}, u32[]{:S(2)}, u32[]{:S(2)}) collective-permute-start(bf16[1152,1152]{1,0:T(8,128)(2,1)} %add_convert_fusion), channel_id=1, source_target_pairs={{0,2},{1,3},{2,0},{3,1},{4,6},{5,7},{6,4},{7,5},{8,10},{9,11},{10,... | collective-permute-start | bytes 7962632 | tf_op jit(solution)/shard_map/ppermute | solution.py:35
  1088.9 228.7 %collective-permute-start.56 = (bf16[1152,1152]{1,0:T(8,128)(2,1)}, bf16[1152,1152]{1,0:T(8,128)(2,1)}, u32[]{:S(2)}, u32[]{:S(2)}) collective-permute-start(bf16[1152,1152]{1,0:T(8,128)(2,1)} %convolution_convert_fusion.14), channel_id=1, source_target_pairs={{0,1},{1,0},{2,3},{3,2},{4,5},{5,4},{6,7},{7,6},{8,9},{9,8},{10,11... | collective-permute-start | bytes 7962632 | tf_op jit(solution)/shard_map/ppermute | solution.py:35
  1130.3 182.3 %collective-permute-start.70 = (bf16[2,576,1152]{2,1,0:T(8,128)(2,1)}, bf16[2,576,1152]{2,1,0:T(8,128)(2,1)}, u32[]{:S(2)}, u32[]{:S(2)}) collective-permute-start(bf16[2,576,1152]{2,1,0:T(8,128)(2,1)} %pad_maximum_fusion.22), channel_id=1, source_target_pairs={{0,4},{4,0},{8,12},{12,8},{16,20},{20,16},{24,28},{28,24},{1,5},{5... | collective-permute-start | bytes 7962632 | tf_op jit(solution)/shard_map/ppermute | solution.py:35
  1199.5 48.3 %collective-permute-start.53 = (bf16[576,1152]{1,0:T(8,128)(2,1)}, bf16[576,1152]{1,0:T(8,128)(2,1)}, u32[]{:S(2)}, u32[]{:S(2)}) collective-permute-start(bf16[576,1152]{1,0:T(8,128)(2,1)} %copy.221), channel_id=1, source_target_pairs={{0,2},{1,3},{2,0},{3,1},{4,6},{5,7},{6,4},{7,5},{8,10},{9,11},{10,... | collective-permute-start | bytes 3981320 | tf_op jit(solution)/shard_map/ppermute | solution.py:35
  1204.7 67.4 %collective-permute-start.65 = (bf16[1,576,1152]{2,1,0:T(8,128)(2,1)}, bf16[1,576,1152]{2,1,0:T(8,128)(2,1)}, u32[]{:S(2)}, u32[]{:S(2)}) collective-permute-start(bf16[1,576,1152]{2,1,0:T(8,128)(2,1)} %fusion.142), channel_id=1, source_target_pairs={{0,4},{4,0},{8,12},{12,8},{16,20},{20,16},{24,28},{28,24},{1,5},{5... | collective-permute-start | bytes 3981320 | tf_op jit(solution)/shard_map/ppermute | solution.py:35
  1219.5 99.3 %collective-permute-start.58 = (bf16[1152,1152]{1,0:T(8,128)(2,1)}, bf16[1152,1152]{1,0:T(8,128)(2,1)}, u32[]{:S(2)}, u32[]{:S(2)}) collective-permute-start(bf16[1152,1152]{1,0:T(8,128)(2,1)} %add_convert_fusion.1), channel_id=1, source_target_pairs={{0,2},{1,3},{2,0},{3,1},{4,6},{5,7},{6,4},{7,5},{8,10},{9,11},{10,... | collective-permute-start | bytes 7962632 | tf_op jit(solution)/shard_map/ppermute | solution.py:35
  1247.9 45.6 %collective-permute-start.78 = (bf16[1,288,1152]{2,1,0:T(8,128)(2,1)}, bf16[1,288,1152]{2,1,0:T(8,128)(2,1)}, u32[]{:S(2)}, u32[]{:S(2)}) collective-permute-start(bf16[1,288,1152]{2,1,0:T(8,128)(2,1)} %fusion.180), channel_id=1, source_target_pairs={{0,8},{4,12},{8,0},{12,4},{16,24},{20,28},{24,16},{28,20},{1,9},{5... | collective-permute-start | bytes 1990664 | tf_op jit(solution)/shard_map/ppermute | solution.py:35
  1288.9 58.6 %collective-permute-start.46 = (bf16[2,576,1152]{2,1,0:T(8,128)(2,1)}, bf16[2,576,1152]{2,1,0:T(8,128)(2,1)}, u32[]{:S(2)}, u32[]{:S(2)}) collective-permute-start(bf16[2,576,1152]{2,1,0:T(8,128)(2,1)} %copy.204), channel_id=1, source_target_pairs={{0,4},{4,0},{8,12},{12,8},{16,20},{20,16},{24,28},{28,24},{1,5},{5... | collective-permute-start | bytes 7962632 | tf_op jit(solution)/shard_map/ppermute | solution.py:35
  1309.1 68.7 %collective-permute-start.79 = (bf16[1,144,1152]{2,1,0:T(8,128)(2,1)}, bf16[1,144,1152]{2,1,0:T(8,128)(2,1)}, u32[]{:S(2)}, u32[]{:S(2)}) collective-permute-start(bf16[1,144,1152]{2,1,0:T(8,128)(2,1)} %fusion.198), channel_id=1, source_target_pairs={{0,16},{4,20},{8,24},{12,28},{16,0},{20,4},{24,8},{28,12},{1,17},{... | collective-permute-start | bytes 995336 | tf_op jit(solution)/shard_map/ppermute | solution.py:35
  1312.6 67.8 %collective-permute-start.67 = (bf16[1,144,1152]{2,1,0:T(8,128)(2,1)}, bf16[1,144,1152]{2,1,0:T(8,128)(2,1)}, u32[]{:S(2)}, u32[]{:S(2)}) collective-permute-start(bf16[1,144,1152]{2,1,0:T(8,128)(2,1)} %fusion.196), channel_id=1, source_target_pairs={{0,16},{4,20},{8,24},{12,28},{16,0},{20,4},{24,8},{28,12},{1,17},{... | collective-permute-start | bytes 995336 | tf_op jit(solution)/shard_map/ppermute | solution.py:35
  1317.6 52.7 %collective-permute-start.55 = (bf16[1,144,1152]{2,1,0:T(8,128)(2,1)}, bf16[1,144,1152]{2,1,0:T(8,128)(2,1)}, u32[]{:S(2)}, u32[]{:S(2)}) collective-permute-start(bf16[1,144,1152]{2,1,0:T(8,128)(2,1)} %copy.230), channel_id=1, source_target_pairs={{0,16},{4,20},{8,24},{12,28},{16,0},{20,4},{24,8},{28,12},{1,17},{... | collective-permute-start | bytes 995336 | tf_op jit(solution)/shard_map/ppermute | solution.py:35
  1318.8 65.9 %collective-permute-start.71 = (bf16[576,1152]{1,0:T(8,128)(2,1)}, bf16[576,1152]{1,0:T(8,128)(2,1)}, u32[]{:S(2)}, u32[]{:S(2)}) collective-permute-start(bf16[576,1152]{1,0:T(8,128)(2,1)} %fusion.21), channel_id=1, source_target_pairs={{0,2},{1,3},{2,0},{3,1},{4,6},{5,7},{6,4},{7,5},{8,10},{9,11},{10,... | collective-permute-start | bytes 3981320 | tf_op jit(solution)/shard_map/ppermute | solution.py:35
  1347.5 40.5 %collective-permute-start.59 = (bf16[1,576,1152]{2,1,0:T(8,128)(2,1)}, bf16[1,576,1152]{2,1,0:T(8,128)(2,1)}, u32[]{:S(2)}, u32[]{:S(2)}) collective-permute-start(bf16[1,576,1152]{2,1,0:T(8,128)(2,1)} %fusion.141), channel_id=1, source_target_pairs={{0,4},{4,0},{8,12},{12,8},{16,20},{20,16},{24,28},{28,24},{1,5},{5... | collective-permute-start | bytes 3981320 | tf_op jit(solution)/shard_map/ppermute | solution.py:35
  1391.0 55.8 %collective-permute-start.60 = (bf16[1,288,1152]{2,1,0:T(8,128)(2,1)}, bf16[1,288,1152]{2,1,0:T(8,128)(2,1)}, u32[]{:S(2)}, u32[]{:S(2)}) collective-permute-start(bf16[1,288,1152]{2,1,0:T(8,128)(2,1)} %fusion.177), channel_id=1, source_target_pairs={{0,8},{4,12},{8,0},{12,4},{16,24},{20,28},{24,16},{28,20},{1,9},{5... | collective-permute-start | bytes 1990664 | tf_op jit(solution)/shard_map/ppermute | solution.py:35
  1418.5 54.3 %collective-permute-start.73 = (bf16[1,144,1152]{2,1,0:T(8,128)(2,1)}, bf16[1,144,1152]{2,1,0:T(8,128)(2,1)}, u32[]{:S(2)}, u32[]{:S(2)}) collective-permute-start(bf16[1,144,1152]{2,1,0:T(8,128)(2,1)} %fusion.197), channel_id=1, source_target_pairs={{0,16},{4,20},{8,24},{12,28},{16,0},{20,4},{24,8},{28,12},{1,17},{... | collective-permute-start | bytes 995336 | tf_op jit(solution)/shard_map/ppermute | solution.py:35
  (242 other events, 2959.4 us)

commit v2 on v1

v2 whole, which is shorter than its diff:
```python
import functools

import jax
import jax.numpy as jnp
import numpy as np
from jax import lax
from jax.experimental import pallas as pl
from jax.experimental.pallas import tpu as pltpu
from jax.sharding import Mesh
from jax.sharding import PartitionSpec as P

D = 1152
HD = 72
P_SIZE = 256
NF = 16
SCALE = HD ** (-0.5)
EPSILON = 1e-06


KINDS = ({"mixed": 0, "fc1": 1, "fc2": 0}, {"mixed": 1, "fc1": 0, "fc2": 1})

f32 = jnp.float32
bf16 = jnp.bfloat16


def bits_of(count):
    found = []
    bit = count // 2
    while bit:
        found.append(bit)
        bit //= 2
    return found


def swap(value, axis, bit):
    count = lax.axis_size(axis)
    return lax.ppermute(value, axis, [(i, i ^ bit) for i in range(count)])


def row_order(rows):
    order = [0]
    for bit in bits_of(rows):
        order = order + [j ^ bit for j in order]
    return order


def step_plan(rows, parts, kind):
    by_row = [("row", bit) for bit in bits_of(rows)]
    by_part = [("m", bit) for bit in bits_of(parts)]
    if kind == 0:
        return by_row + by_part
    return by_row[:-1] + by_part[:-1] + by_row[-1:] + by_part[-1:]


def moved(label, axis, bit):
    return (label[0] ^ bit, label[1]) if axis == "row" else (label[0], label[1] ^ bit)


def total(terms):
    result = terms[0].astype(f32)
    for term in terms[1:]:
        result = result + term.astype(f32)
    return result


class Gather:
    def __init__(self, shard, rows, parts, kind):
        self.rows, self.parts, self.depth = rows, parts, shard.shape[0]
        self.plan = step_plan(rows, parts, kind)
        self.labels = [[(0, 0)]]
        self.arrays = [shard]
        self.done = 0

    def step(self):
        axis, bit = self.plan[self.done]
        merge = self.done < len(self.plan) - 2
        labels, arrays = [], []
        for names, value in zip(self.labels, self.arrays):
            other = swap(value, axis, bit)
            other_names = [moved(name, axis, bit) for name in names]
            if merge:
                labels.append(names + other_names)
                arrays.append(jnp.concatenate([value, other], 0))
            else:
                labels += [names, other_names]
                arrays += [value, other]
        self.labels, self.arrays = labels, arrays
        self.done += 1

    def pieces(self):
        order, depth = row_order(self.rows), self.depth
        found = []
        for part in range(self.parts):
            entries = []
            for number, names in enumerate(self.labels):
                hits = [place for place, name in enumerate(names) if name[1] == part]
                if hits:
                    rank = order.index(names[hits[0]][0])
                    assert [names[h][0] for h in hits] == order[rank : rank + len(hits)]
                    assert hits == list(range(hits[0], hits[0] + len(hits)))
                    entries.append((number, hits[0] * depth, len(hits) * depth, rank * depth))
            found.append(entries)
        return found


class Scatter:
    def __init__(self, sent, kept, rows, parts, kind):
        self.plan = step_plan(rows, parts, kind)[::-1]
        self.order = row_order(rows)
        self.depth = kept.shape[1] // rows
        self.span = rows
        self.arrays = [sent, kept]
        evens = [part for part in range(parts) if not part & 1]
        self.live = {part: [(1, place, 0)] for place, part in enumerate(evens)}
        self.done = 0

    def take(self, term, first, count):
        number, lead, start = term
        return self.arrays[number][lead, start + first : start + first + count]

    def sums(self, names, first, count):
        return [total([self.take(t, first, count) for t in self.live[n]]).astype(bf16) for n in names]

    def step(self):
        axis, bit = self.plan[self.done]
        if self.done == 0:
            assert (axis, bit) == ("m", 1)
            self.arrays.append(swap(self.arrays[0], axis, bit))
            for place, name in enumerate(sorted(self.live)):
                self.live[name].append((len(self.arrays) - 1, place, 0))
        elif axis == "m":
            names = [name for name in sorted(self.live) if name & bit]
            sent = self.sums(names, 0, self.span * self.depth)
            for name in names:
                self.live.pop(name)
            self.arrays.append(swap(jnp.stack(sent), axis, bit))
            for place, name in enumerate(names):
                self.live[name ^ bit].append((len(self.arrays) - 1, place, 0))
        else:
            half = self.span // 2
            order = self.order
            assert all(order[half + p] == order[p] ^ bit for p in range(half))
            names = sorted(self.live)
            sent = self.sums(names, half * self.depth, half * self.depth)
            self.arrays.append(swap(jnp.stack(sent), axis, bit))
            for place, name in enumerate(names):
                self.live[name].append((len(self.arrays) - 1, place, 0))
            self.span = half
        self.done += 1

    def result(self):
        return total([self.take(t, 0, self.depth) for t in self.live[0]])


def fence(objects, values):
    arrays, values = lax.optimization_barrier(([o.arrays for o in objects], values))
    for o, fresh in zip(objects, arrays):
        o.arrays = list(fresh)
    return values


def all_sum(value, axis):
    for bit in bits_of(lax.axis_size(axis)):
        value = value + swap(value, axis, bit)
    return value


def over_u(value):
    return lax.psum(value, "u") if lax.axis_size("u") > 1 else value


def features_all(value):
    return lax.all_gather(value, "u", axis=1, tiled=True) if lax.axis_size("u") > 1 else value


def features_sum(value):
    if lax.axis_size("u") > 1:
        return lax.psum_scatter(value, "u", scatter_dimension=1, tiled=True)
    return value


def dot_nn(left, right):
    return lax.dot_general(left, right, (((1,), (0,)), ((), ())), preferred_element_type=f32)


def dot_nt(left, right):
    return lax.dot_general(left, right, (((1,), (1,)), ((), ())), preferred_element_type=f32)


def dot_tn(left, right):
    return lax.dot_general(left, right, (((0,), (0,)), ((), ())), preferred_element_type=f32)


LIMIT = 56 * 1024 * 1024


class Weight:
    def __init__(self, arrays, pieces):
        self.arrays = [value.reshape(-1, value.shape[-1]) for value in arrays]
        self.places = pieces
        self.parts = len(pieces)
        self.height = sum(rows for _, _, rows, _ in pieces[0])
        self.width = self.arrays[0].shape[1]

    def scratch(self):
        pieces = len(self.places[0])
        return [
            pltpu.VMEM((self.parts, self.height, self.width), bf16),
            pltpu.SemaphoreType.DMA((self.parts, pieces)),
        ]

    def copies(self, part, refs, held, sems):
        return [
            pltpu.make_async_copy(
                refs[number].at[pl.ds(start, rows)], held.at[part, pl.ds(to, rows)], sems.at[part, place]
            )
            for place, (number, start, rows, to) in enumerate(self.places[part])
        ]

    def arrive(self, step, refs, held, sems):
        @pl.when(step == 0)
        def _():
            for part in range(self.parts):
                for copy in self.copies(part, refs, held, sems):
                    copy.start()

        for part in range(self.parts):

            @pl.when(step == part)
            def _(part=part):
                for copy in self.copies(part, refs, held, sems):
                    copy.wait()


def cut_last(load, low, high):
    base = low // 128 * 128
    value = load(base, high)
    return value if base == low else value[:, low - base :]


def whole_spec(shape):
    return pl.BlockSpec(shape, lambda s: (0,) * len(shape))


def part_spec(shape):
    return pl.BlockSpec((1,) + shape, lambda s: (s,) + (0,) * len(shape))


def project(x, weight, columns, extras, epilogue, out_types, name):
    tokens, depth = x.shape
    low, high = columns
    n = high - low
    count = len(weight.arrays)

    def body(*refs):
        x_ref, refs = refs[0], refs[1:]
        w_refs, refs = refs[:count], refs[count:]
        extra_refs, refs = refs[: len(extras)], refs[len(extras) :]
        outs, (held, sems) = refs[: len(out_types)], refs[len(out_types) :]
        step = pl.program_id(0)
        weight.arrive(step, w_refs, held, sems)
        left = x_ref[...]
        right = cut_last(lambda a, b: held[step, :, a:b], low, high)
        made = epilogue(dot_nn(left, right), *[e[0] for e in extra_refs])
        for out, piece in zip(outs, made):
            out[0] = piece.astype(out.dtype)

    return pl.pallas_call(
        body,
        grid=(weight.parts,),
        in_specs=[whole_spec((tokens, depth))]
        + [pl.BlockSpec(memory_space=pl.ANY)] * count
        + [part_spec(e.shape[1:]) for e in extras],
        out_specs=[part_spec((tokens, n))] * len(out_types),
        out_shape=[jax.ShapeDtypeStruct((weight.parts, tokens, n), t) for t in out_types],
        scratch_shapes=weight.scratch(),
        compiler_params=pltpu.CompilerParams(vmem_limit_bytes=LIMIT),
        cost_estimate=pl.CostEstimate(
            flops=2 * tokens * depth * n * weight.parts,
            transcendentals=0,
            bytes_accessed=2 * weight.parts * n * (depth + 2 * tokens),
        ),
        name=name,
    )(x, *weight.arrays, *extras)


def contract(xs, weight, columns, name):
    parts, tokens, n = xs.shape
    low, high = columns
    count = len(weight.arrays)
    height = weight.height

    def body(*refs):
        x_ref, refs = refs[0], refs[1:]
        w_refs, (out, held, sems) = refs[:count], refs[count:]
        step = pl.program_id(0)
        weight.arrive(step, w_refs, held, sems)
        left = x_ref[0]
        right = cut_last(lambda a, b: held[step, :, a:b], low, high)
        value = dot_nt(left, right)

        @pl.when(step == 0)
        def _():
            out[...] = value

        @pl.when(step > 0)
        def _():
            out[...] += value

    return pl.pallas_call(
        body,
        grid=(parts,),
        in_specs=[part_spec((tokens, n))] + [pl.BlockSpec(memory_space=pl.ANY)] * count,
        out_specs=whole_spec((tokens, height)),
        out_shape=jax.ShapeDtypeStruct((tokens, height), f32),
        scratch_shapes=weight.scratch(),
        compiler_params=pltpu.CompilerParams(vmem_limit_bytes=LIMIT),
        cost_estimate=pl.CostEstimate(
            flops=2 * tokens * height * n * parts,
            transcendentals=0,
            bytes_accessed=2 * parts * n * (height + tokens) + 4 * tokens * height,
        ),
        name=name,
    )(xs, *weight.arrays)


def weight_grads(pairs, name):
    tokens, depth = pairs[0][0].shape
    parts = pairs[0][1].shape[0]
    half = parts // 2
    widths = [g.shape[2] for _, g in pairs]
    full = sum(widths)
    count = len(pairs)

    def which(step):
        return jnp.where(step < half, 2 * step + 1, 2 * (step - half))

    def body(*refs):
        x_refs, refs = refs[:count], refs[count:]
        g_refs, refs = refs[:count], refs[count:]
        (sent, kept), refs = refs[:2], refs[2:]
        x_sums, refs = refs[:count], refs[count:]
        g_sums, turned = refs[:count], refs[count:]
        step = pl.program_id(0)

        @pl.when(step == 0)
        def _():
            for x_ref, x_sum, t_ref in zip(x_refs, x_sums, turned):
                value = x_ref[...].astype(f32)
                x_sum[...] = jnp.sum(value, 0, keepdims=True)
                t_ref[...] = value.T.astype(bf16)

        rights = [g_ref[0] for g_ref in g_refs]
        for right, g_sum in zip(rights, g_sums):
            g_sum[0] = jnp.sum(right.astype(f32), 0, keepdims=True)

        def fill(out):
            made = [dot_nn(t_ref[...], r).astype(bf16) for t_ref, r in zip(turned, rights)]
            out[0] = made[0] if count == 1 else jnp.concatenate(made, 1)

        @pl.when(step < half)
        def _():
            fill(sent)

        @pl.when(step >= half)
        def _():
            fill(kept)

    outs = pl.pallas_call(
        body,
        grid=(parts,),
        in_specs=[whole_spec((tokens, depth))] * count
        + [pl.BlockSpec((1, tokens, n), lambda s: (which(s), 0, 0)) for n in widths],
        out_specs=[
            pl.BlockSpec((1, depth, full), lambda s: (jnp.minimum(s, half - 1), 0, 0)),
            pl.BlockSpec((1, depth, full), lambda s: (jnp.maximum(s - half, 0), 0, 0)),
        ]
        + [whole_spec((1, depth))] * count
        + [pl.BlockSpec((1, 1, n), lambda s: (which(s), 0, 0)) for n in widths],
        out_shape=[jax.ShapeDtypeStruct((half, depth, full), bf16)] * 2
        + [jax.ShapeDtypeStruct((1, depth), f32)] * count
        + [jax.ShapeDtypeStruct((parts, 1, n), f32) for n in widths],
        scratch_shapes=[pltpu.VMEM((depth, tokens), bf16)] * count,
        compiler_params=pltpu.CompilerParams(vmem_limit_bytes=LIMIT),
        cost_estimate=pl.CostEstimate(
            flops=2 * tokens * depth * full * parts,
            transcendentals=0,
            bytes_accessed=2 * parts * full * (depth + tokens),
        ),
        name=name,
    )(*[x for x, _ in pairs], *[g for _, g in pairs])
    return outs[:2], outs[2 : 2 + count], outs[2 + count :]


def gelu_pair(value, bias):
    v = value + bias
    slope = 0.7978845608028654
    inner = jnp.tanh(slope * (v + 0.044715 * v * v * v))
    outer = 0.5 * (1.0 + inner)
    change = outer + 0.5 * v * (1.0 - inner * inner) * (slope * (1.0 + 3.0 * 0.044715 * v * v))
    return v * outer, change


POWER = SCALE * 1.4426950408889634


def allowed_pairs(temporal, span, tokens):
    if not temporal:
        return None
    first = lax.broadcasted_iota(jnp.int32, (tokens, tokens), 0)
    second = lax.broadcasted_iota(jnp.int32, (tokens, tokens), 1)
    return lax.rem(first, span) == lax.rem(second, span)


def head_columns(block, start, width):
    return [block[:, c * width + start : c * width + start + HD] for c in range(3)]


def forward_kernel(temporal, span, qkv, out, logs):
    width = qkv.shape[-1] // 3
    tokens = int(np.prod(qkv.shape[:-1]))
    allowed = allowed_pairs(temporal, span, tokens)
    block = qkv[...].reshape(tokens, 3 * width)
    done, kept = [], []
    for start in range(0, width, HD):
        query, key, value = head_columns(block, start, width)
        scores = dot_nt(key, query)
        if allowed is not None:
            scores = jnp.where(allowed, scores, -jnp.inf)
        largest = jnp.max(scores, 0, keepdims=True)
        powered = jnp.exp2((scores - largest) * POWER)
        summed = jnp.sum(powered, 0, keepdims=True)
        done.append(dot_tn(value, powered.astype(bf16)) / summed)
        kept.append(largest * POWER + jnp.log2(summed))
    out[...] = jnp.concatenate(done, 0).T.astype(bf16).reshape(out.shape)
    logs[...] = jnp.concatenate(kept, 0).reshape(logs.shape)


def backward_kernel(temporal, span, qkv, grad, attended, logs, out):
    width = qkv.shape[-1] // 3
    tokens = int(np.prod(qkv.shape[:-1]))
    allowed = allowed_pairs(temporal, span, tokens)
    block = qkv[...].reshape(tokens, 3 * width)
    outer = grad[...].reshape(tokens, width)
    turned = outer.astype(f32).T * attended[...].reshape(tokens, width).astype(f32).T
    log_rows = logs[...].reshape(width // HD, tokens)
    pieces = [[], [], []]
    for place, start in enumerate(range(0, width, HD)):
        query, key, value = head_columns(block, start, width)
        above = outer[:, start : start + HD]
        inner = jnp.sum(turned[start : start + HD], 0, keepdims=True)
        weights = jnp.exp2(dot_nt(key, query) * POWER - log_rows[place : place + 1])
        if allowed is not None:
            weights = jnp.where(allowed, weights, 0.0)
        grad_scores = (weights * (dot_nt(value, above) - inner)).astype(bf16)
        pieces[0].append(dot_tn(key, grad_scores) * SCALE)
        pieces[1].append((dot_nn(grad_scores, query) * SCALE).astype(bf16))
        pieces[2].append(dot_nn(weights.astype(bf16), above).astype(bf16))
    first = jnp.concatenate(pieces[0], 0).T.astype(bf16)
    out[...] = jnp.concatenate([first] + pieces[1] + pieces[2], 1).reshape(out.shape)


def attention_call(kernel, values, logs, layout, out_width, work, name):
    parts, tokens, triple = values[0].shape
    heads = triple // 3 // HD
    temporal = len(layout) == 3
    chunk = 16
    grid = (parts, layout[0])
    if temporal:
        assert layout[2] % chunk == 0
        grid = grid + (layout[2] // chunk,)
    groups = tokens // P_SIZE

    def spec(width):
        if temporal:
            return pl.BlockSpec((1, 1, layout[1], chunk, width), lambda p, g, c: (p, g, 0, c, 0))
        return pl.BlockSpec((1, 1, layout[1], width), lambda p, g: (p, g, 0, 0))

    if temporal:
        log_spec = pl.BlockSpec((1, 1, heads, P_SIZE), lambda p, g, c: (p, g * grid[2] + c, 0, 0))
    else:
        log_spec = pl.BlockSpec((1, 1, heads, P_SIZE), lambda p, g: (p, g, 0, 0))
    out_shape = [jax.ShapeDtypeStruct((parts,) + layout + (out_width,), bf16)]
    out_specs = [spec(out_width)]
    in_specs = [spec(v.shape[-1]) for v in values]
    given = [v.reshape((parts,) + layout + (v.shape[-1],)) for v in values]
    if logs is None:
        out_shape.append(jax.ShapeDtypeStruct((parts, groups, heads, P_SIZE), f32))
        out_specs.append(log_spec)
    else:
        in_specs.append(log_spec)
        given.append(logs)
    result = pl.pallas_call(
        functools.partial(kernel, temporal, chunk),
        grid=grid,
        in_specs=in_specs,
        out_specs=out_specs,
        out_shape=out_shape,
        cost_estimate=pl.CostEstimate(
            flops=tokens * parts * heads * P_SIZE * 128 * work,
            transcendentals=tokens * parts * heads * P_SIZE,
            bytes_accessed=tokens * parts * out_width * 8,
        ),
        name=name,
    )(*given)
    return [result[0].reshape(parts, tokens, out_width)] + list(result[1:])


def norm_forward(stream):
    center = stream - over_u(jnp.sum(stream, 1, keepdims=True)) / D
    inverse = lax.rsqrt(over_u(jnp.sum(center * center, 1, keepdims=True)) / D + EPSILON)
    return center * inverse, inverse


def norm_backward(grad_normed, normed, inverse):
    first, second = over_u(
        (
            jnp.sum(grad_normed, 1, keepdims=True),
            jnp.sum(grad_normed * normed, 1, keepdims=True),
        )
    )
    return inverse * (grad_normed - first / D - normed * (second / D))


def spread(vector, tokens):
    groups, width = vector.shape
    if groups == 1:
        return vector
    return jnp.broadcast_to(vector[:, None, :], (groups, tokens // groups, width)).reshape(tokens, width)


def group_sum(value, groups):
    return jnp.sum(value.reshape(groups, -1, value.shape[-1]), 1)


def shards(
    latents, cond, w_ada, b_ada, w_qkv, b_qv, w_out, b_out, w_fc1, b_fc1, w_fc2, b_fc2, cotangent
):
    batches, width, tokens = latents.shape
    lat_count = cond.shape[1]
    rows = lax.axis_size("row")
    parts = lax.axis_size("m")
    split = lax.axis_size("u")
    row = lax.axis_index("row")
    part_here = lax.axis_index("m")
    span = parts * width
    order = jnp.asarray(row_order(rows), jnp.int32)
    inverse_order = jnp.asarray(np.argsort(row_order(rows)), jnp.int32)
    part_ids = part_here ^ jnp.arange(parts)
    frames_dev = tokens // P_SIZE
    pos_block = tokens // (lat_count * NF)
    spatial = (frames_dev, P_SIZE)
    temporal = (lat_count, NF, pos_block)

    relative = split == 1
    depth = D // rows
    if relative:
        slot = jnp.arange(D)
        source = (row ^ order[slot // depth]) * depth + slot % depth
        exchange = (jnp.arange(D)[:, None] == source[None, :]).astype(bf16)

    def vector_rel(value):
        if not relative:
            return value
        shaped = value.reshape(value.shape[:-1] + (rows, depth))
        return jnp.take(shaped, row ^ order, axis=-2).reshape(value.shape)

    def vector_plain(value):
        if not relative:
            return value
        shaped = value.reshape(value.shape[:-1] + (rows, depth))
        return jnp.take(shaped, inverse_order[row ^ jnp.arange(rows)], axis=-2).reshape(value.shape)

    def stream_plain(value):
        return dot_nt(value, exchange).astype(bf16) if relative else value

    def stream_rel(value):
        return dot_nn(value, exchange) if relative else value.astype(f32)

    def to_positions(value):
        return stream_rel(send_positions(stream_plain(value.astype(bf16))))

    def send_positions(value):
        shaped = value.reshape(frames_dev, rows, pos_block, span).swapaxes(0, 1)
        return lax.all_to_all(shaped, "row", 0, 0).reshape(tokens, span)

    def to_frames(value):
        shaped = stream_plain(value.astype(bf16)).reshape(rows, frames_dev, pos_block, span)
        return lax.all_to_all(shaped, "row", 0, 0).swapaxes(0, 1).reshape(tokens, span)

    def gathered(gather):
        pieces = gather.pieces()
        arrays = [value.reshape(-1, value.shape[-1]) for value in gather.arrays]
        if relative:
            return Weight(arrays, pieces)
        places = inverse_order[row ^ jnp.arange(rows)]
        blocks = []
        for entries in pieces:
            entries = sorted(entries, key=lambda entry: entry[3])
            block = jnp.concatenate([arrays[n][a : a + count] for n, a, count, _ in entries], 0)
            blocks.append(jnp.take(block.reshape(rows, depth, -1), places, axis=0).reshape(block.shape))
        return Weight(blocks, [[(part, 0, D, 0)] for part in range(parts)])

    def scatter(stacks, kind):
        if not relative:
            stacks = [
                jnp.take(s.reshape(s.shape[0], rows, depth, -1), row ^ order, axis=1).reshape(s.shape)
                for s in stacks
            ]
        return Scatter(stacks[0], stacks[1], rows, parts, kind)

    def own_share(value):
        return value if relative else lax.dynamic_slice_in_dim(value, lax.axis_index("u") * span, span, 1)

    cond_float = cond.astype(f32)
    cond_low = jax.nn.silu(cond_float).astype(bf16)
    mod_partial = jnp.einsum("mlr,brjk->mlbjk", cond_low, w_ada, preferred_element_type=f32)
    mod_partial = mod_partial + jnp.where(row == 0, b_ada.astype(f32), 0.0)[None, None]
    small = jnp.concatenate(
        [b.astype(f32).reshape(-1) for b in (b_qv, b_out, b_fc1, b_fc2)]
    )
    packed = jnp.concatenate(
        [mod_partial.reshape(batches, -1), jnp.broadcast_to(small, (parts,) + small.shape)], 1
    )
    packed = lax.all_to_all(packed, "m", split_axis=0, concat_axis=0, tiled=True)
    mod_size = lat_count * 12 * width
    mod_here = all_sum(packed[:, :mod_size], "row").reshape(parts, lat_count, 2, 6, width)
    mod_here = vector_rel(jnp.moveaxis(mod_here, 0, -2).reshape(lat_count, 2, 6, span))
    small = packed[:, mod_size:]
    sizes = np.cumsum([0, 4 * width, 2 * width, 2 * b_fc1.shape[1], 2 * width])
    all_qv, all_out, all_fc1, all_fc2 = [small[:, a:b] for a, b in zip(sizes[:-1], sizes[1:])]
    all_qv = jnp.take(all_qv.reshape(parts, 2, 2, width), part_ids, axis=0)
    all_fc1 = jnp.take(all_fc1.reshape(parts, 2, -1), part_ids, axis=0)
    all_out = vector_rel(jnp.moveaxis(all_out.reshape(parts, 2, width), 0, 1).reshape(2, span))
    all_fc2 = vector_rel(jnp.moveaxis(all_fc2.reshape(parts, 2, width), 0, 1).reshape(2, span))

    zeros = jnp.zeros((parts, width), f32)
    bias_qkv = [
        jnp.concatenate([all_qv[:, b, 0], zeros, all_qv[:, b, 1]], 1)[:, None, :] for b in range(2)
    ]
    bias_fc1 = [all_fc1[:, b][:, None, :] for b in range(2)]
    hidden_width = w_fc1.shape[2]
    mixed_cols, out_cols, hidden_cols = (0, 3 * width), (3 * width, 4 * width), (0, hidden_width)
    layouts = (spatial, temporal)
    groups_of = (1, lat_count)

    def shard_of(b, name):
        if name == "mixed":
            return jnp.concatenate([w_qkv[b].reshape(depth, 3 * width), w_out[b]], 1)
        return (w_fc1 if name == "fc1" else w_fc2)[b]

    def own_batch(value):
        return lax.all_to_all(value, "m", 0, 0).reshape(span, tokens)

    def to_stream(value):
        return dot_tn(value, exchange) if relative else value.T.astype(f32)

    def to_argument(value):
        return lax.all_to_all(value.reshape(parts, width, tokens), "m", 0, 0)

    lat_here = row * frames_dev // NF
    mod_space = lax.dynamic_slice_in_dim(mod_here[:, 0], lat_here, 1, 0)
    mods = [
        [spread(m[:, column], tokens) for column in range(6)] for m in (mod_space, mod_here[:, 1])
    ]

    def open_stage(b, stream):
        normed, inverse = norm_forward(stream)
        hidden = features_all((normed * (1.0 + mods[b][1]) + mods[b][0]).astype(bf16))
        return {"stream": stream, "normed": normed, "inverse": inverse, "hidden": hidden}

    def attention_stage(b, k):
        qkv = project(
            k["hidden"], weights[b]["mixed"], mixed_cols, [bias_qkv[b]], lambda v, c: (v + c,), [bf16], "qkv"
        )[0]
        attended, logs = attention_call(forward_kernel, [qkv], None, layouts[b], width, 4, "attend")
        return {**k, "qkv": qkv, "attended": attended, "logs": logs}

    def middle_stage(b, k):
        branch = features_sum(contract(k["attended"], weights[b]["mixed"], out_cols, "out")) + all_out[b]
        middle = k["stream"] + mods[b][2] * branch
        normed, inverse = norm_forward(middle)
        hidden = features_all((normed * (1.0 + mods[b][4]) + mods[b][3]).astype(bf16))
        return {**k, "branch": branch, "middle": middle, "normed2": normed, "inverse2": inverse, "hidden2": hidden}

    def up_stage(b, k):
        act, slope = project(
            k["hidden2"], weights[b]["fc1"], hidden_cols, [bias_fc1[b]], gelu_pair, [bf16, bf16], "up"
        )
        return {**k, "act": act, "slope": slope}

    def down_stage(b, k):
        branch = features_sum(contract(k["act"], weights[b]["fc2"], hidden_cols, "down")) + all_fc2[b]
        return k["middle"] + mods[b][5] * branch, {**k, "branch2": branch}

    def fc2_grads(b, k, grad):
        low = features_all((mods[b][5] * grad).astype(bf16))
        stacks, (total_low,), _ = weight_grads([(low, k["act"])], "grad_fc2")
        return {**k, "grad": grad, "low2": low, "sum_b2": own_share(total_low)}, scatter(stacks, KINDS[b]["fc2"])

    def up_back(b, k):
        grad_pre = project(
            k["low2"], weights[b]["fc2"], hidden_cols, [k["slope"]],
            lambda v, s: (v * s.astype(f32),), [bf16], "up_back",
        )[0]
        stacks, _, (total_pre,) = weight_grads([(k["hidden2"], grad_pre)], "grad_fc1")
        return {**k, "pre": grad_pre, "sum_b1": total_pre[:, 0]}, scatter(stacks, KINDS[b]["fc1"])

    def hidden2_back(b, k):
        grad_hidden = features_sum(contract(k["pre"], weights[b]["fc1"], hidden_cols, "hidden2_back"))
        return {**k, "g_hidden2": grad_hidden}

    def attention_back(b, k):
        grad_hidden = k["g_hidden2"]
        back = norm_backward(grad_hidden * (1.0 + mods[b][4]), k["normed2"], k["inverse2"])
        middle = k["grad"] + back
        low = features_all((mods[b][2] * middle).astype(bf16))
        grad_att = project(low, weights[b]["mixed"], out_cols, [], lambda v: (v,), [bf16], "out_back")[0]
        grad_qkv = attention_call(
            backward_kernel, [k["qkv"], grad_att, k["attended"]], k["logs"], layouts[b], 3 * width, 10, "attend_back"
        )[0]
        return {**k, "g_middle": middle, "low1": low, "g_qkv": grad_qkv}

    def mixed_grads(b, k):
        stacks, (_, total_low), (total_qkv, _) = weight_grads(
            [(k["hidden"], k["g_qkv"]), (k["low1"], k["attended"])], "grad_mixed"
        )
        return {**k, "sum_bo": own_share(total_low), "sum_qkv": total_qkv[:, 0]}, scatter(stacks, KINDS[b]["mixed"])

    def stream_back(b, k):
        grad_hidden = features_sum(contract(k["g_qkv"], weights[b]["mixed"], mixed_cols, "hidden_back"))
        back = norm_backward(grad_hidden * (1.0 + mods[b][1]), k["normed"], k["inverse"])
        groups = groups_of[b]
        modulate_grad = jnp.stack(
            [
                group_sum(grad_hidden, groups),
                group_sum(grad_hidden * k["normed"], groups),
                group_sum(k["g_middle"] * k["branch"], groups),
                group_sum(k["g_hidden2"], groups),
                group_sum(k["g_hidden2"] * k["normed2"], groups),
                group_sum(k["grad"] * k["branch2"], groups),
            ],
            1,
        )
        biases = (
            k["sum_qkv"][:, :width], k["sum_qkv"][:, 2 * width :], k["sum_bo"], k["sum_b1"], k["sum_b2"],
        )
        return k["g_middle"] + back, (modulate_grad, biases)

    names = ("mixed", "fc1", "fc2")
    gathers = [Gather(shard_of(b, n), rows, parts, KINDS[b][n]) for b in range(2) for n in names]
    weights = [{}, {}]
    depth_of = len(gathers[0].plan)

    def move(*pairs):
        for item, until in pairs:
            while item.done < min(until, depth_of):
                item.step()

    def ready(number):
        weights[number // 3][names[number % 3]] = gathered(gathers[number])

    last = depth_of
    g = gathers
    first = depth_of - 3
    move((g[0], first - 1), (g[1], first - 1))
    first_in, grad_top = fence(g, (own_batch(latents), own_batch(cotangent)))
    move((g[0], first), (g[1], first))
    grad_top = send_positions(grad_top.T)
    grad_top, mods = fence(g, (grad_top, mods))
    move((g[0], last - 2), (g[1], last - 2), (g[2], first - 1), (g[3], first - 1))
    first_in, grad_top = to_stream(first_in), stream_rel(grad_top)
    first_in, grad_top = fence(g, (first_in, grad_top))
    move((g[0], last - 1), (g[1], last - 1), (g[2], first), (g[3], first))
    fence(g, ())
    move((g[0], last), (g[1], last), (g[2], last - 2), (g[3], last - 2), (g[4], first - 1), (g[5], first - 1))
    k0 = open_stage(0, first_in)
    k0 = fence(g, k0)
    ready(0)
    ready(1)
    move((g[2], last - 1), (g[3], last - 1), (g[4], first), (g[5], first))
    k0 = middle_stage(0, attention_stage(0, k0))
    k0, grad_top = fence(g, (k0, grad_top))
    move((g[2], last), (g[3], last), (g[4], last - 2), (g[5], last - 2))
    k0 = up_stage(0, k0)
    k0 = fence(g, k0)
    ready(2)
    ready(3)
    move((g[4], last - 1), (g[5], last - 1))
    first_out, k0 = down_stage(0, k0)
    k1 = open_stage(1, to_positions(first_out))
    k1 = attention_stage(1, k1)
    k0, k1 = fence(g, (k0, k1))
    move((g[4], last))
    k1 = middle_stage(1, k1)
    k0, k1 = fence(g, (k0, k1))
    ready(4)
    move((g[5], last))
    k1 = up_stage(1, k1)
    k1, s5 = fc2_grads(1, k1, grad_top)
    k0, k1 = fence(g + [s5], (k0, k1))
    ready(5)
    move((s5, 1))
    second_out, k1 = down_stage(1, k1)
    k1, s4 = up_back(1, k1)
    k0, k1, second_out = fence([s4, s5], (k0, k1, second_out))
    move((s4, 1))
    k1 = hidden2_back(1, k1)
    output = to_argument(to_frames(second_out).T)
    k0, k1 = fence([s4, s5], (k0, k1))
    move((s5, 2), (s4, 2))
    k1 = attention_back(1, k1)
    k1, s3 = mixed_grads(1, k1)
    k0, k1 = fence([s3, s4, s5], (k0, k1))
    move((s5, 3), (s4, 3), (s3, 1))
    grad_mid, small_time = stream_back(1, k1)
    grad_low = to_frames(grad_mid)
    k0, grad_low, small_time, output = fence([s3, s4, s5], (k0, grad_low, small_time, output))
    move((s3, 2), (s5, 4), (s4, 4))
    k0, s2 = fc2_grads(0, k0, stream_rel(grad_low))
    k0, s1 = up_back(0, k0)
    k0 = hidden2_back(0, k0)
    k0 = fence([s1, s2, s3, s4, s5], k0)
    move((s3, 3), (s5, last), (s4, last), (s2, 1), (s1, 1))
    k0 = attention_back(0, k0)
    k0 = fence([s1, s2, s3, s4, s5], k0)
    move((s2, 2), (s1, 2), (s3, 4))
    k0, s0 = mixed_grads(0, k0)
    grad_first, small_space = stream_back(0, k0)
    grad_first, small_space, small_time = fence(
        [s0, s1, s2, s3], (grad_first, small_space, small_time)
    )
    move((s2, 3), (s1, 3), (s0, 1), (s3, last))
    fence([s0, s1, s2, s3], ())
    move((s0, 2), (s2, 4), (s1, 4))
    fence([s0, s1, s2], ())
    move((s0, 3), (s2, last), (s1, last))
    for item in (s0, s1, s2, s3, s4, s5):
        move((item, last))
    mod_grad_space, biases_space = small_space
    mod_grad_time, biases_time = small_time
    weights_space = [item.result() for item in (s0, s1, s2)]
    weights_time = [item.result() for item in (s3, s4, s5)]
    grad_first = grad_first.astype(bf16)
    grad_first = dot_nt(exchange, grad_first).astype(bf16) if relative else grad_first.T
    grad_latents = to_argument(grad_first).astype(f32)

    onehot = (jnp.arange(lat_count) == lat_here).astype(f32)
    mod_grads = jnp.stack([onehot[:, None, None] * mod_grad_space, mod_grad_time], 1)
    mod_grads = vector_plain(mod_grads).reshape(lat_count, 2, 6, parts, width)
    mod_grads = jnp.moveaxis(mod_grads, -2, 0).reshape(parts, -1)

    def by_part(value):
        return jnp.take(value, part_ids, axis=0)

    def by_stream(value):
        return vector_plain(value).reshape(parts, width)

    pieces = [mod_grads]
    for space, time in zip(biases_space, biases_time):
        for value in (space, time):
            pieces.append(by_part(value) if value.shape[0] == parts else by_stream(value))
    counts = np.cumsum([0] + [piece.shape[1] for piece in pieces])
    packed = jnp.concatenate(pieces, 1)
    packed = lax.all_to_all(packed, "m", split_axis=0, concat_axis=0, tiled=True)
    mod_part = packed[:, : counts[1]]
    bias_part = jnp.sum(packed[:, counts[1] :], 0, keepdims=True)
    flat = jnp.concatenate([mod_part.reshape(1, -1), bias_part], 1)
    flat = all_sum(flat, "row")[0]
    mod_grad_low = flat[: batches * counts[1]].reshape(batches, lat_count, 2, 6, width).astype(bf16)
    bias_part = flat[batches * counts[1] :]
    bias_out = [bias_part[a - counts[1] : b - counts[1]] for a, b in zip(counts[1:-1], counts[2:])]
    grad_bias_qv = jnp.stack(
        [jnp.stack([bias_out[0], bias_out[2]]), jnp.stack([bias_out[1], bias_out[3]])]
    )
    grad_bias_out = jnp.stack(bias_out[4:6])
    grad_bias_fc1 = jnp.stack(bias_out[6:8])
    grad_bias_fc2 = jnp.stack(bias_out[8:10])
    grad_bias_ada = jnp.sum(mod_grad_low.astype(f32), (0, 1))
    grad_weight_ada = jnp.einsum("mlr,mlbjk->brjk", cond_low, mod_grad_low, preferred_element_type=f32)
    cond_partial = jnp.einsum("mlbjk,brjk->mlr", mod_grad_low, w_ada, preferred_element_type=f32)
    cond_total = over_u(all_sum(cond_partial, "m"))
    sigmoid_cond = jax.nn.sigmoid(cond_float)
    grad_condition = cond_total * sigmoid_cond * (1.0 + cond_float * (1.0 - sigmoid_cond))
    grad_weight_qkv, grad_weight_out, grad_weight_fc1, grad_weight_fc2 = [], [], [], []
    for mixed, first, second in (weights_space, weights_time):
        grad_weight_qkv.append(mixed[:, : 3 * width].reshape(depth, 3, width))
        grad_weight_out.append(mixed[:, 3 * width :])
        grad_weight_fc1.append(first)
        grad_weight_fc2.append(second)
    return (
        output,
        grad_latents,
        grad_condition,
        grad_weight_ada,
        grad_bias_ada,
        jnp.stack(grad_weight_qkv),
        grad_bias_qv,
        jnp.stack(grad_weight_out),
        grad_bias_out,
        jnp.stack(grad_weight_fc1),
        grad_bias_fc1,
        jnp.stack(grad_weight_fc2),
        grad_bias_fc2,
    )


def solution(mesh):
    rows, columns = mesh.devices.shape

    def placed(latents, *rest):
        parts = latents.shape[0]
        inner = Mesh(mesh.devices.reshape(rows, columns // parts, parts), ("row", "u", "m"))
        col = ("u", "m")
        in_specs = (
            P(None, col, "row"),
            P(None, None, "row"),
            P(None, "row", None, col),
            P(None, None, col),
            P(None, "row", None, col),
            P(None, None, col),
            P(None, "row", col),
            P(None, col),
            P(None, "row", col),
            P(None, col),
            P(None, "row", col),
            P(None, col),
            P(None, col, "row"),
        )
        out_specs = (P(None, col, "row"),) + in_specs[:1] + in_specs[1:-1]
        return jax.shard_map(
            shards, mesh=inner, in_specs=in_specs, out_specs=out_specs, check_vma=False
        )(latents, *rest)

    return placed
```

time: 1500 us -> 1180 us (0.79)
  matrix products: 286 us -> 29.4 us
  Pallas kernels: 80.9 us -> 318 us
  local copies, waits for them, and re-layouts: 277 us -> 64.2 us
  other arithmetic: 230 us -> 183 us
  waiting for transfers between devices: 487 us -> 452 us
    pallas_call x4 -> x26, Pallas kernels: 80.9 us -> 318 us  [the longest x8 94.4 us: contract(): pl.pallas_call(body, grid=(parts,), in_specs=[part_spec((tokens, n))] + [...]
    dot_general x29 -> x3, matrix products: 99.2 us -> 10.3 us  [dot_nn(): lax.dot_general(left, right, (((1,), (0,)), ((), ())), preferred_element_...]
    ppermute x80 -> x74, waiting for transfers between devices: 475 us -> 390 us  [swap(): return lax.ppermute(value, axis, [(i, i ^ bit) for i in range(count)])]
    dot_general x27 -> x1, matrix products: 88.8 us -> 4.72 us  [dot_tn(): lax.dot_general(left, right, (((0,), (0,)), ((), ())), preferred_element_...]
    dot_general x30 -> x4, matrix products: 95 us -> 10.9 us  [dot_nt(): lax.dot_general(left, right, (((1,), (1,)), ((), ())), preferred_element_...]
    another operation x32 -> x3, other arithmetic: 75.4 us -> 3.88 us  [step(): self.arrays.append(swap(jnp.stack(sent), axis, bit))]
    convert_element_type x8 -> x30, other arithmetic: 17.9 us -> 86.6 us  [the longest x24 70 us: sums(): total([self.take(t, first, count) for t in self.live[n]]).astype(bf16)]
    slice x37 -> x8, local copies, waits for them, and re-layouts: 68.6 us -> 1.29 us  [the longest x1 0.64 us: shards(): bias_fc1 = [all_fc1[:, b][:, None, :] for b in range(2)]]
  transfers between devices with their start and end apart: 90 -> 84, of which waited for: 29 -> 40; matrix products, arithmetic and copies ran while one was open for 47% -> 18% of each run, Pallas kernels for 4% -> 25%
where the time goes in v2:
time: 1180 us; the launch traced here: 1170 us
  waiting for transfers between devices  452 us (38%)
  Pallas kernels  318 us (27%)
  other arithmetic  183 us (16%)
  starting transfers between devices  120 us (10%)
  local copies, waits for them, and re-layouts  64.2 us (5%)
  matrix products  29.4 us (2%)
    ppermute x74, waiting for transfers between devices, swap(): return lax.ppermute(value, axis, [(i, i ^ bit) for i in range(count)])  390 us
    pallas_call x8, Pallas kernels, contract(): pl.pallas_call(body, grid=(parts,), in_specs=[part_spec((tokens, n))] + [...  94.4 us
    pallas_call x8, Pallas kernels, project(): pl.pallas_call(body, grid=(weight.parts,), in_specs=[whole_spec((tokens,...  88.8 us
    pallas_call x6, Pallas kernels, weight_grads(): pl.pallas_call(body, grid=(parts,), in_specs=[whole_spec((tokens, depth))...  81 us
    ppermute x74, starting transfers between devices, swap(): return lax.ppermute(value, axis, [(i, i ^ bit) for i in range(count)])  77.3 us
    convert_element_type x24, other arithmetic, sums(): total([self.take(t, first, count) for t in self.live[n]]).astype(bf16)  70 us
    pallas_call x4, Pallas kernels, attention_call(): pl.pallas_call(functools.partial(kernel, temporal, chunk), grid=grid, in_...  53.8 us
    concatenate x18, other arithmetic, step(): arrays.append(jnp.concatenate([value, other], 0))  27.8 us
  transfers between devices with their start and end apart: 84, of which 40 were waited for; matrix products, arithmetic and copies ran while one was open for 18% of the time, Pallas kernels for 25%

profile of v2, /device:TPU:0, one launch (start us, length us, event | category | flops | bytes accessed | tf_op | source)
XLA Modules:
  0.0 1170.2 jit_solution(17485681400710325594)
XLA Ops:
  28.5 9.8 all-to-all-done
  41.8 6.9 collective-permute-done.4
  65.3 6.3 all-to-all-start.2
  75.3 33.2 %collective-permute-done.3 = bf16[288,1152]{1,0:T(8,128)(2,1)S(1)} collective-permute-done((bf16[288,1152]{1,0:T(8,128)(2,1)S(1)}, bf16[288,1152]{1,0:T(8,128)(2,1)S(1)}, u32[]{:S(2)}, u32[]{:S(2)}) %collective-permute-start.3) | collective-permute-done | bytes 663584 | tf_op jit(solution)/shard_map/ppermute | solution.py:37
  109.7 9.8 collective-permute-done.2
  122.7 4.7 fusion.7
  131.8 4.6 fusion.6
  136.4 13.9 %collective-permute-done.10 = bf16[144,1152]{1,0:T(8,128)(2,1)S(1)} collective-permute-done((bf16[144,1152]{1,0:T(8,128)(2,1)S(1)}, bf16[144,1152]{1,0:T(8,128)(2,1)S(1)}, u32[]{:S(2)}, u32[]{:S(2)}) %collective-permute-start.10) | collective-permute-done | bytes 331808 | tf_op jit(solution)/shard_map/ppermute | solution.py:37
  150.3 6.1 collective-permute-done.9
  166.4 15.7 %collective-permute-done.14 = bf16[288,1152]{1,0:T(8,128)(2,1)S(1)} collective-permute-done((bf16[288,1152]{1,0:T(8,128)(2,1)S(1)}, bf16[288,1152]{1,0:T(8,128)(2,1)S(1)}, u32[]{:S(2)}, u32[]{:S(2)}) %collective-permute-start.14) | collective-permute-done | bytes 663584 | tf_op jit(solution)/shard_map/ppermute | solution.py:37
  182.2 12.5 %collective-permute-done.13 = bf16[288,1152]{1,0:T(8,128)(2,1)S(1)} collective-permute-done((bf16[288,1152]{1,0:T(8,128)(2,1)}, bf16[288,1152]{1,0:T(8,128)(2,1)S(1)}, u32[]{:S(2)}, u32[]{:S(2)}) %collective-permute-start.13) | collective-permute-done | bytes 663584 | tf_op jit(solution)/shard_map/ppermute | solution.py:37
  197.0 22.7 %collective-permute-done.11.refs_3_ = bf16[1152,1152]{1,0:T(8,128)(2,1)} collective-permute-done((bf16[1152,1152]{1,0:T(8,128)(2,1)}, bf16[1152,1152]{1,0:T(8,128)(2,1)}, u32[]{:S(2)}, u32[]{:S(2)}) %collective-permute-start.11) | collective-permute-done | bytes 2654240 | tf_op jit(solution)/shard_map/ppermute | solution.py:37
  236.5 18.0 %collective-permute-done.22 = bf16[144,1152]{1,0:T(8,128)(2,1)S(1)} collective-permute-done((bf16[144,1152]{1,0:T(8,128)(2,1)S(1)}, bf16[144,1152]{1,0:T(8,128)(2,1)S(1)}, u32[]{:S(2)}, u32[]{:S(2)}) %collective-permute-start.22) | collective-permute-done | bytes 331808 | tf_op jit(solution)/shard_map/ppermute | solution.py:37
  254.5 7.0 collective-permute-done.21
  269.5 23.9 %collective-permute-done.19 = bf16[576,1152]{1,0:T(8,128)(2,1)S(1)} collective-permute-done((bf16[576,1152]{1,0:T(8,128)(2,1)}, bf16[576,1152]{1,0:T(8,128)(2,1)S(1)}, u32[]{:S(2)}, u32[]{:S(2)}) %collective-permute-start.19) | collective-permute-done | bytes 1327136 | tf_op jit(solution)/shard_map/ppermute | solution.py:37
  300.8 10.0 qkv.2
  310.8 13.3 %attend.2 = (bf16[4,2,256,288]{3,2,1,0:T(8,128)(2,1)}, f32[4,2,4,256]{3,2,1,0:T(4,128)}) custom-call(bf16[4,2,256,864]{3,2,1,0:T(8,128)(2,1)} %bitcast.196), custom_call_target="tpu_custom_call" | custom-call | flops 1073741824 | bytes 4718592 | tf_op jit(solution)/shard_map/attend/pallas_call | solution.py:493
  324.1 9.3 out.2
  343.3 14.4 %collective-permute-done.23.refs_3_ = bf16[1152,1152]{1,0:T(8,128)(2,1)} collective-permute-done((bf16[1152,1152]{1,0:T(8,128)(2,1)}, bf16[1152,1152]{1,0:T(8,128)(2,1)}, u32[]{:S(2)}, u32[]{:S(2)}) %collective-permute-start.23) | collective-permute-done | bytes 2654240 | tf_op jit(solution)/shard_map/ppermute | solution.py:37
  361.5 25.6 %collective-permute-done.32 = bf16[576,1152]{1,0:T(8,128)(2,1)} collective-permute-done((bf16[576,1152]{1,0:T(8,128)(2,1)S(1)}, bf16[576,1152]{1,0:T(8,128)(2,1)}, u32[]{:S(2)}, u32[]{:S(2)}) %collective-permute-start.32) | collective-permute-done | bytes 1327136 | tf_op jit(solution)/shard_map/ppermute | solution.py:37
  389.4 14.9 %up.2 = (bf16[4,512,1152]{2,1,0:T(8,128)(2,1)}, bf16[4,512,1152]{2,1,0:T(8,128)(2,1)}) custom-call(bf16[512,1152]{1,0:T(8,128)(2,1)} %get-tuple-element.788.refs_0_, bf16[1152,1152]{1,0:T(8,128)(2,1)} %pad_maximum_fusion.1.refs_1_, bf16[1152,1152]{1,0:T(8,128)(2,1)} %copy-done.91, bf16[1152,1152]{1,0:T(8,128)(2,1)} %collective-permute-done.12.refs_3_, ...), custom_call_target="tpu_custom_call" | custom-call | flops 5435817984 | bytes 20054016 | tf_op jit(solution)/shard_map/up/pallas_call | solution.py:268
  407.4 8.1 collective-permute-done.31
  418.6 13.0 %down.2 = f32[512,1152]{1,0:T(8,128)} custom-call(bf16[4,512,1152]{2,1,0:T(8,128)(2,1)} %get-tuple-element.793.refs_0_.refs_1_, bf16[1152,1152]{1,0:T(8,128)(2,1)} %pad_maximum_fusion.2.refs_1_, bf16[1152,1152]{1,0:T(8,128)(2,1)} %collective-permute-done.27.refs_2_, bf16[1152,1152]{1,0:T(8,128)(2,1)} %collective-permute-done.23.refs_3_, ...), custom_call_target="tpu_custom_call" | custom-call | flops 5435817984 | bytes 17694720 | tf_op jit(solution)/shard_map/down/pallas_call | solution.py:310
  445.3 21.2 %all-to-all-done.4 = bf16[8,2,32,1152]{3,2,1,0:T(8,128)(2,1)S(1)} async-done(((bf16[8,2,32,1152]{3,2,1,0:T(8,128)(2,1)}), bf16[8,2,32,1152]{3,2,1,0:T(8,128)(2,1)S(1)}, u32[]{:S(2)}, u32[]{:S(2)}) %all-to-all-start.4) | async-done | bytes 1179680 | tf_op jit(solution)/shard_map/all_to_all | solution.py:585
  471.2 10.0 qkv.3
  481.2 13.4 %attend.3 = (bf16[4,1,16,32,288]{4,3,2,1,0:T(8,128)(2,1)}, f32[4,2,4,256]{3,2,1,0:T(4,128)}) custom-call(bf16[4,1,16,32,864]{4,3,2,1,0:T(8,128)(2,1)} %bitcast.198), custom_call_target="tpu_custom_call" | custom-call | flops 1073741824 | bytes 4718592 | tf_op jit(solution)/shard_map/attend/pallas_call | solution.py:493
  497.1 12.5 %collective-permute-done.34.refs_3_ = bf16[1152,1152]{1,0:T(8,128)(2,1)} collective-permute-done((bf16[1152,1152]{1,0:T(8,128)(2,1)}, bf16[1152,1152]{1,0:T(8,128)(2,1)}, u32[]{:S(2)}, u32[]{:S(2)}) %collective-permute-start.34) | collective-permute-done | bytes 2654240 | tf_op jit(solution)/shard_map/ppermute | solution.py:37
  510.3 9.2 out.3
  529.2 14.9 %up.3 = (bf16[4,512,1152]{2,1,0:T(8,128)(2,1)}, bf16[4,512,1152]{2,1,0:T(8,128)(2,1)}) custom-call(bf16[512,1152]{1,0:T(8,128)(2,1)} %get-tuple-element.648.refs_0_, bf16[1152,1152]{1,0:T(8,128)(2,1)} %pad_maximum_fusion.4.refs_1_, bf16[1152,1152]{1,0:T(8,128)(2,1)} %collective-permute-done.35.refs_2_, bf16[1152,1152]{1,0:T(8,128)(2,1)} %collective-permute-done.33.refs_3_, ...), custom_call_target="tpu_custom_call" | custom-call | flops 5435817984 | bytes 20054016 | tf_op jit(solution)/shard_map/up/pallas_call | solution.py:268
  544.1 13.2 %grad_fc2.2 = (bf16[2,1152,1152]{2,1,0:T(8,128)(2,1)}, bf16[2,1152,1152]{2,1,0:T(8,128)(2,1)}, f32[1,1152]{1,0:T(1,128)}, f32[4,1,1152]{2,1,0:T(1,128)}) custom-call(bf16[512,1152]{1,0:T(8,128)(2,1)} %multiply_convert_fusion.3.refs_0_, bf16[4,512,1152]{2,1,0:T(8,128)(2,1)} %get-tuple-element.672.refs_1_.refs_0_), custom_call_target="tpu_custom_call" | custom-call | flops 5435817984 | bytes 15335424 | tf_op jit(solution)/shard_map/grad_fc2/pallas_call | solution.py:369
  557.5 12.0 %up_back.2.refs_1_.refs_0_ = bf16[4,512,1152]{2,1,0:T(8,128)(2,1)} custom-call(bf16[512,1152]{1,0:T(8,128)(2,1)} %multiply_convert_fusion.3.refs_0_, bf16[1152,1152]{1,0:T(8,128)(2,1)} %pad_maximum_fusion.5.refs_1_, bf16[1152,1152]{1,0:T(8,128)(2,1)} %collective-permute-done.37.refs_2_, bf16[1152,1152]{1,0:T(8,128)(2,1)} %collective-permute-done.34.refs_3_, ...), custom_call_target="tpu_custom_call" | custom-call | flops 5435817984 | bytes 20054016 | tf_op jit(solution)/shard_map/up_back/pallas_call | solution.py:268
  569.5 12.7 %grad_fc1.2 = (bf16[2,1152,1152]{2,1,0:T(8,128)(2,1)}, bf16[2,1152,1152]{2,1,0:T(8,128)(2,1)}, f32[1,1152]{1,0:T(1,128)}, f32[4,1,1152]{2,1,0:T(1,128)}) custom-call(bf16[512,1152]{1,0:T(8,128)(2,1)} %get-tuple-element.648.refs_0_, bf16[4,512,1152]{2,1,0:T(8,128)(2,1)} %up_back.2.refs_1_.refs_0_), custom_call_target="tpu_custom_call" | custom-call | flops 5435817984 | bytes 15335424 | tf_op jit(solution)/shard_map/grad_fc1/pallas_call | solution.py:369
  582.9 13.1 %down.3 = f32[512,1152]{1,0:T(8,128)} custom-call(bf16[4,512,1152]{2,1,0:T(8,128)(2,1)} %get-tuple-element.672.refs_1_.refs_0_, bf16[1152,1152]{1,0:T(8,128)(2,1)} %pad_maximum_fusion.5.refs_1_, bf16[1152,1152]{1,0:T(8,128)(2,1)} %collective-permute-done.37.refs_2_, bf16[1152,1152]{1,0:T(8,128)(2,1)} %collective-permute-done.34.refs_3_, ...), custom_call_target="tpu_custom_call" | custom-call | flops 5435817984 | bytes 17694720 | tf_op jit(solution)/shard_map/down/pallas_call | solution.py:310
  602.8 4.9 all-to-all-start.6
  607.7 13.2 %hidden2_back.2 = f32[512,1152]{1,0:T(8,128)} custom-call(bf16[4,512,1152]{2,1,0:T(8,128)(2,1)} %up_back.2.refs_1_.refs_0_, bf16[1152,1152]{1,0:T(8,128)(2,1)} %pad_maximum_fusion.4.refs_1_, bf16[1152,1152]{1,0:T(8,128)(2,1)} %collective-permute-done.35.refs_2_, bf16[1152,1152]{1,0:T(8,128)(2,1)} %collective-permute-done.33.refs_3_, ...), custom_call_target="tpu_custom_call" | custom-call | flops 5435817984 | bytes 17694720 | tf_op jit(solution)/shard_map/hidden2_back/pallas_call | solution.py:310
  627.1 4.7 add_convert_fusion.2
  643.2 4.6 multiply_convert_fusion.2
  647.8 7.6 out_back.2
  655.3 13.6 %attend_back.2 = bf16[4,1,16,32,864]{4,3,2,1,0:T(8,128)(2,1)} custom-call(bf16[4,1,16,32,864]{4,3,2,1,0:T(8,128)(2,1)} %bitcast.199, bf16[4,1,16,32,288]{4,3,2,1,0:T(8,128)(2,1)} %bitcast.208, bf16[4,1,16,32,288]{4,3,2,1,0:T(8,128)(2,1)} %get-tuple-element.582, f32[4,2,4,256]{3,2,1,0:T(4,128)} %get-tuple-element.724.logs), custom_call_target="tpu_custom_call" | custom-call | flops 2684354560 | bytes 14155776 | tf_op jit(solution)/shard_map/attend_back/pallas_call | solution.py:493
  669.0 14.9 %grad_mixed.2 = (bf16[2,1152,1152]{2,1,0:T(8,128)(2,1)}, bf16[2,1152,1152]{2,1,0:T(8,128)(2,1)}, f32[1,1152]{1,0:T(1,128)}, f32[1,1152]{1,0:T(1,128)}, f32[4,1,864]{2,1,0:T(1,128)}, /*index=5*/f32[4,1,288]{2,1,0:T(1,128)}) custom-call(bf16[512,1152]{1,0:T(8,128)(2,1)} %get-tuple-element.717.refs_0_, bf16[512,1152]{1,0:T(8,128)(2,1)} %get-tuple-element.1022.refs_0_.refs_1_, ...), custom_call_target="tpu_custom_call" | custom-call | flops 5435817984 | bytes 15335424 | tf_op jit(solution)/shard_map/grad_mixed/pallas_call | solution.py:369
  686.0 4.8 collective-permute-done.41
  690.8 11.8 %hidden_back.2 = f32[512,1152]{1,0:T(8,128)} custom-call(bf16[4,512,864]{2,1,0:T(8,128)(2,1)} %bitcast.203, bf16[1152,1152]{1,0:T(8,128)(2,1)} %pad_maximum_fusion.3.refs_1_, bf16[1152,1152]{1,0:T(8,128)(2,1)} %collective-permute-done.29.refs_2_, bf16[1152,1152]{1,0:T(8,128)(2,1)} %collective-permute-done.24.refs_3_, ...), custom_call_target="tpu_custom_call" | custom-call | flops 4076863488 | bytes 13860864 | tf_op jit(solution)/shard_map/hidden_back/pallas_call | solution.py:310
  709.1 4.5 all-to-all-start.5
  727.3 15.5 %all-to-all-done.5 = bf16[8,2,32,1152]{3,2,1,0:T(8,128)(2,1)S(1)} async-done(((bf16[8,2,32,1152]{3,2,1,0:T(8,128)(2,1)}), bf16[8,2,32,1152]{3,2,1,0:T(8,128)(2,1)S(1)}, u32[]{:S(2)}, u32[]{:S(2)}) %all-to-all-start.5) | async-done | bytes 1179680 | tf_op jit(solution)/shard_map/all_to_all | solution.py:589
  751.7 11.9 %all-to-all-done.7 = bf16[4,288,512]{2,1,0:T(8,128)(2,1)S(1)} async-done(((bf16[4,288,512]{2,1,0:T(8,128)(2,1)}), bf16[4,288,512]{2,1,0:T(8,128)(2,1)S(1)}, u32[]{:S(2)}, u32[]{:S(2)}) %all-to-all-start.7) | async-done | bytes 1179680 | tf_op jit(solution)/shard_map/all_to_all | solution.py:659
  778.8 12.0 %up_back.3.refs_1_.refs_0_ = bf16[4,512,1152]{2,1,0:T(8,128)(2,1)} custom-call(bf16[512,1152]{1,0:T(8,128)(2,1)} %get-tuple-element.1108.refs_0_, bf16[1152,1152]{1,0:T(8,128)(2,1)} %pad_maximum_fusion.2.refs_1_, bf16[1152,1152]{1,0:T(8,128)(2,1)} %collective-permute-done.27.refs_2_, bf16[1152,1152]{1,0:T(8,128)(2,1)} %collective-permute-done.23.refs_3_, ...), custom_call_target="tpu_custom_call" | custom-call | flops 5435817984 | bytes 20054016 | tf_op jit(solution)/shard_map/up_back/pallas_call | solution.py:268
  790.8 12.9 %hidden2_back.3 = f32[512,1152]{1,0:T(8,128)} custom-call(bf16[4,512,1152]{2,1,0:T(8,128)(2,1)} %up_back.3.refs_1_.refs_0_, bf16[1152,1152]{1,0:T(8,128)(2,1)} %pad_maximum_fusion.1.refs_1_, bf16[1152,1152]{1,0:T(8,128)(2,1)} %copy-done.91, bf16[1152,1152]{1,0:T(8,128)(2,1)} %collective-permute-done.12.refs_3_, bf16[1152,1152]{1,0:T(8,128)(2,1)} %copy-done.92), custom_call_target="tpu_custom_call" | custom-call | flops 5435817984 | bytes 17694720 | tf_op jit(solution)/shard_map/hidden2_back/pallas_call | solution.py:310
  803.8 12.7 %grad_fc1.3 = (bf16[2,1152,1152]{2,1,0:T(8,128)(2,1)}, bf16[2,1152,1152]{2,1,0:T(8,128)(2,1)}, f32[1,1152]{1,0:T(1,128)}, f32[4,1,1152]{2,1,0:T(1,128)}) custom-call(bf16[512,1152]{1,0:T(8,128)(2,1)} %get-tuple-element.788.refs_0_, bf16[4,512,1152]{2,1,0:T(8,128)(2,1)} %up_back.3.refs_1_.refs_0_), custom_call_target="tpu_custom_call" | custom-call | flops 5435817984 | bytes 15335424 | tf_op jit(solution)/shard_map/grad_fc1/pallas_call | solution.py:369
  817.2 12.8 %grad_fc2.3 = (bf16[2,1152,1152]{2,1,0:T(8,128)(2,1)}, bf16[2,1152,1152]{2,1,0:T(8,128)(2,1)}, f32[1,1152]{1,0:T(1,128)}, f32[4,1,1152]{2,1,0:T(1,128)}) custom-call(bf16[512,1152]{1,0:T(8,128)(2,1)} %get-tuple-element.1108.refs_0_, bf16[4,512,1152]{2,1,0:T(8,128)(2,1)} %get-tuple-element.793.refs_0_.refs_1_), custom_call_target="tpu_custom_call" | custom-call | flops 5435817984 | bytes 15335424 | tf_op jit(solution)/shard_map/grad_fc2/pallas_call | solution.py:369
  846.7 7.5 out_back.3
  854.2 13.4 %attend_back.3 = bf16[4,2,256,864]{3,2,1,0:T(8,128)(2,1)} custom-call(bf16[4,2,256,864]{3,2,1,0:T(8,128)(2,1)} %bitcast.197, bf16[4,2,256,288]{3,2,1,0:T(8,128)(2,1)} %bitcast.209, bf16[4,2,256,288]{3,2,1,0:T(8,128)(2,1)} %get-tuple-element.528, f32[4,2,4,256]{3,2,1,0:T(4,128)} %get-tuple-element.843.logs), custom_call_target="tpu_custom_call" | custom-call | flops 2684354560 | bytes 14155776 | tf_op jit(solution)/shard_map/attend_back/pallas_call | solution.py:493
  870.5 11.8 %hidden_back.3 = f32[512,1152]{1,0:T(8,128)} custom-call(bf16[4,512,864]{2,1,0:T(8,128)(2,1)} %bitcast.200, bf16[1152,1152]{1,0:T(8,128)(2,1)} %pad_maximum_fusion.refs_1_, bf16[1152,1152]{1,0:T(8,128)(2,1)} %copy-done.3, bf16[1152,1152]{1,0:T(8,128)(2,1)} %collective-permute-done.11.refs_3_, bf16[1152,1152]{1,0:T(8,128)(2,1)} %collective-permute-done.16.refs_4_), custom_call_target="tpu_custom_call" | custom-call | flops 4076863488 | bytes 13860864 | tf_op jit(solution)/shard_map/hidden_back/pallas_call | solution.py:310
  888.3 4.7 add_convert_fusion.1
  899.2 14.8 %grad_mixed.3 = (bf16[2,1152,1152]{2,1,0:T(8,128)(2,1)}, bf16[2,1152,1152]{2,1,0:T(8,128)(2,1)}, f32[1,1152]{1,0:T(1,128)}, f32[1,1152]{1,0:T(1,128)}, f32[4,1,864]{2,1,0:T(1,128)}, /*index=5*/f32[4,1,288]{2,1,0:T(1,128)}) custom-call(bf16[512,1152]{1,0:T(8,128)(2,1)} %get-tuple-element.849.refs_0_, bf16[512,1152]{1,0:T(8,128)(2,1)} %get-tuple-element.850.refs_0_.refs_1_, ...), custom_call_target="tpu_custom_call" | custom-call | flops 5435817984 | bytes 15335424 | tf_op jit(solution)/shard_map/grad_mixed/pallas_call | solution.py:369
  926.3 25.3 %collective-permute-done.55 = bf16[1,1152,1152]{2,1,0:T(8,128)(2,1)} collective-permute-done((bf16[1,1152,1152]{2,1,0:T(8,128)(2,1)}, bf16[1,1152,1152]{2,1,0:T(8,128)(2,1)}, u32[]{:S(2)}, u32[]{:S(2)}) %collective-permute-start.55) | collective-permute-done | bytes 2654240 | tf_op jit(solution)/shard_map/ppermute | solution.py:37
  951.6 5.0 collective-permute-done.54
  1000.2 12.4 %collective-permute-done.59 = f32[1,18432]{1,0:T(1,128)S(1)} collective-permute-done((f32[1,18432]{1,0:T(1,128)S(1)}, f32[1,18432]{1,0:T(1,128)S(1)}, u32[]{:S(2)}, u32[]{:S(2)}) %collective-permute-start.59) | collective-permute-done | bytes 73760 | tf_op jit(solution)/shard_map/ppermute | solution.py:37
  1018.0 4.7 add_convert_fusion
  1039.8 8.5 collective-permute-done.68
  1048.3 11.6 collective-permute-done.67
  1059.9 27.1 %collective-permute-done.66 = bf16[1,1152,1152]{2,1,0:T(8,128)(2,1)} collective-permute-done((bf16[1,1152,1152]{2,1,0:T(8,128)(2,1)}, bf16[1,1152,1152]{2,1,0:T(8,128)(2,1)}, u32[]{:S(2)}, u32[]{:S(2)}) %collective-permute-start.66) | collective-permute-done | bytes 2654240 | tf_op jit(solution)/shard_map/ppermute | solution.py:37
  1102.6 18.9 %collective-permute-done.69 = bf16[1,576,1152]{2,1,0:T(8,128)(2,1)} collective-permute-done((bf16[1,576,1152]{2,1,0:T(8,128)(2,1)}, bf16[1,576,1152]{2,1,0:T(8,128)(2,1)}, u32[]{:S(2)}, u32[]{:S(2)}) %collective-permute-start.69) | collective-permute-done | bytes 1327136 | tf_op jit(solution)/shard_map/ppermute | solution.py:37
  1130.9 12.5 %collective-permute-done.70 = bf16[1,288,1152]{2,1,0:T(8,128)(2,1)S(1)} collective-permute-done((bf16[1,288,1152]{2,1,0:T(8,128)(2,1)S(1)}, bf16[1,288,1152]{2,1,0:T(8,128)(2,1)S(1)}, u32[]{:S(2)}, u32[]{:S(2)}) %collective-permute-start.70) | collective-permute-done | bytes 663584 | tf_op jit(solution)/shard_map/ppermute | solution.py:37
  1147.5 14.7 %collective-permute-done.71 = bf16[1,144,1152]{2,1,0:T(8,128)(2,1)S(1)} collective-permute-done((bf16[1,144,1152]{2,1,0:T(8,128)(2,1)S(1)}, bf16[1,144,1152]{2,1,0:T(8,128)(2,1)S(1)}, u32[]{:S(2)}, u32[]{:S(2)}) %collective-permute-start.71) | collective-permute-done | bytes 331808 | tf_op jit(solution)/shard_map/ppermute | solution.py:37
  (627 shorter events, 376.0 us)
Async XLA Ops:
  12.8 45.5 %collective-permute-start = (bf16[144,1152]{1,0:T(8,128)(2,1)S(1)}, bf16[144,1152]{1,0:T(8,128)(2,1)}, u32[]{:S(2)}, u32[]{:S(2)}) collective-permute-start(bf16[144,1152]{1,0:T(8,128)(2,1)S(1)} %pad_maximum_fusion.25), channel_id=1, source_target_pairs={{0,16},{4,20},{8,24},{12,28},{16,0},{20,4},{24,8},{28,12},{1,17},{... | collective-permute-start | bytes 995336 | tf_op jit(solution)/shard_map/ppermute | solution.py:37
  17.6 41.9 %collective-permute-start.1 = (bf16[144,1152]{1,0:T(8,128)(2,1)}, bf16[144,1152]{1,0:T(8,128)(2,1)}, u32[]{:S(2)}, u32[]{:S(2)}) collective-permute-start(bf16[144,1152]{1,0:T(8,128)(2,1)} %get-tuple-element.1051), channel_id=1, source_target_pairs={{0,16},{4,20},{8,24},{12,28},{16,0},{20,4},{24,8},{28,12},{1,17},{... | collective-permute-start | bytes 995336 | tf_op jit(solution)/shard_map/ppermute | solution.py:37
  25.0 23.7 %collective-permute-start.4 = (f32[4,3456]{1,0:T(4,128)S(1)}, f32[4,3456]{1,0:T(4,128)S(1)}, u32[]{:S(2)}, u32[]{:S(2)}) collective-permute-start(f32[4,3456]{1,0:T(4,128)S(1)} %slice.787), channel_id=1, source_target_pairs={{0,16},{4,20},{8,24},{12,28},{16,0},{20,4},{24,8},{28,12},{1,17},{... | collective-permute-start | bytes 165896 | tf_op jit(solution)/shard_map/ppermute | solution.py:37
  65.3 55.4 %all-to-all-start.2 = ((bf16[8,2,32,1152]{3,2,1,0:T(8,128)(2,1)}), bf16[8,2,32,1152]{3,2,1,0:T(8,128)(2,1)}, u32[]{:S(2)}, u32[]{:S(2)}) async-start(bf16[8,2,32,1152]{3,2,1,0:T(8,128)(2,1)} %copy.93), calls=%async_computation.2 | async-start | bytes 2359296 | tf_op jit(solution)/shard_map/all_to_all | solution.py:585
  71.9 36.6 %collective-permute-start.3 = (bf16[288,1152]{1,0:T(8,128)(2,1)S(1)}, bf16[288,1152]{1,0:T(8,128)(2,1)S(1)}, u32[]{:S(2)}, u32[]{:S(2)}) collective-permute-start(bf16[288,1152]{1,0:T(8,128)(2,1)S(1)} %copy-done.40), channel_id=1, source_target_pairs={{0,8},{4,12},{8,0},{12,4},{16,24},{20,28},{24,16},{28,20},{1,9},{5... | collective-permute-start | bytes 1990664 | tf_op jit(solution)/shard_map/ppermute | solution.py:37
  74.7 44.9 %collective-permute-start.2 = (bf16[288,1152]{1,0:T(8,128)(2,1)S(1)}, bf16[288,1152]{1,0:T(8,128)(2,1)S(1)}, u32[]{:S(2)}, u32[]{:S(2)}) collective-permute-start(bf16[288,1152]{1,0:T(8,128)(2,1)S(1)} %pad_maximum_fusion.18), channel_id=1, source_target_pairs={{0,8},{4,12},{8,0},{12,4},{16,24},{20,28},{24,16},{28,20},{1,9},{5... | collective-permute-start | bytes 1990664 | tf_op jit(solution)/shard_map/ppermute | solution.py:37
  120.7 36.6 %collective-permute-start.8 = (bf16[576,1152]{1,0:T(8,128)(2,1)S(1)}, bf16[576,1152]{1,0:T(8,128)(2,1)S(1)}, u32[]{:S(2)}, u32[]{:S(2)}) collective-permute-start(bf16[576,1152]{1,0:T(8,128)(2,1)S(1)} %pad_maximum_fusion.11), channel_id=1, source_target_pairs={{0,2},{1,3},{2,0},{3,1},{4,6},{5,7},{6,4},{7,5},{8,10},{9,11},{10,... | collective-permute-start | bytes 3981320 | tf_op jit(solution)/shard_map/ppermute | solution.py:37
  130.0 26.4 %collective-permute-start.9 = (bf16[144,1152]{1,0:T(8,128)(2,1)S(1)}, bf16[144,1152]{1,0:T(8,128)(2,1)S(1)}, u32[]{:S(2)}, u32[]{:S(2)}) collective-permute-start(bf16[144,1152]{1,0:T(8,128)(2,1)S(1)} %copy-done.44), channel_id=1, source_target_pairs={{0,16},{4,20},{8,24},{12,28},{16,0},{20,4},{24,8},{28,12},{1,17},{... | collective-permute-start | bytes 995336 | tf_op jit(solution)/shard_map/ppermute | solution.py:37
  130.4 28.6 %collective-permute-start.7 = (bf16[576,1152]{1,0:T(8,128)(2,1)S(1)}, bf16[576,1152]{1,0:T(8,128)(2,1)S(1)}, u32[]{:S(2)}, u32[]{:S(2)}) collective-permute-start(bf16[576,1152]{1,0:T(8,128)(2,1)S(1)} %copy-done.34), channel_id=1, source_target_pairs={{0,4},{4,0},{8,12},{12,8},{16,20},{20,16},{24,28},{28,24},{1,5},{5... | collective-permute-start | bytes 3981320 | tf_op jit(solution)/shard_map/ppermute | solution.py:37
  160.7 58.9 %collective-permute-start.11 = (bf16[1152,1152]{1,0:T(8,128)(2,1)}, bf16[1152,1152]{1,0:T(8,128)(2,1)}, u32[]{:S(2)}, u32[]{:S(2)}) collective-permute-start(bf16[1152,1152]{1,0:T(8,128)(2,1)} %pad_maximum_fusion.refs_1_), channel_id=1, source_target_pairs={{0,2},{1,3},{2,0},{3,1},{4,6},{5,7},{6,4},{7,5},{8,10},{9,11},{10,... | collective-permute-start | bytes 7962632 | tf_op jit(solution)/shard_map/ppermute | solution.py:37
  161.0 60.0 %collective-permute-start.12 = (bf16[1152,1152]{1,0:T(8,128)(2,1)}, bf16[1152,1152]{1,0:T(8,128)(2,1)}, u32[]{:S(2)}, u32[]{:S(2)}) collective-permute-start(bf16[1152,1152]{1,0:T(8,128)(2,1)} %pad_maximum_fusion.1.refs_1_), channel_id=1, source_target_pairs={{0,4},{4,0},{8,12},{12,8},{16,20},{20,16},{24,28},{28,24},{1,5},{5... | collective-permute-start | bytes 7962632 | tf_op jit(solution)/shard_map/ppermute | solution.py:37
  164.3 30.4 %collective-permute-start.13 = (bf16[288,1152]{1,0:T(8,128)(2,1)}, bf16[288,1152]{1,0:T(8,128)(2,1)S(1)}, u32[]{:S(2)}, u32[]{:S(2)}) collective-permute-start(bf16[288,1152]{1,0:T(8,128)(2,1)} %pad_maximum_fusion.20), channel_id=1, source_target_pairs={{0,8},{4,12},{8,0},{12,4},{16,24},{20,28},{24,16},{28,20},{1,9},{5... | collective-permute-start | bytes 1990664 | tf_op jit(solution)/shard_map/ppermute | solution.py:37
  221.0 40.6 %collective-permute-start.20 = (bf16[576,1152]{1,0:T(8,128)(2,1)S(1)}, bf16[576,1152]{1,0:T(8,128)(2,1)}, u32[]{:S(2)}, u32[]{:S(2)}) collective-permute-start(bf16[576,1152]{1,0:T(8,128)(2,1)S(1)} %pad_maximum_fusion.13), channel_id=1, source_target_pairs={{0,2},{1,3},{2,0},{3,1},{4,6},{5,7},{6,4},{7,5},{8,10},{9,11},{10,... | collective-permute-start | bytes 3981320 | tf_op jit(solution)/shard_map/ppermute | solution.py:37
  230.9 23.6 %collective-permute-start.22 = (bf16[144,1152]{1,0:T(8,128)(2,1)S(1)}, bf16[144,1152]{1,0:T(8,128)(2,1)S(1)}, u32[]{:S(2)}, u32[]{:S(2)}) collective-permute-start(bf16[144,1152]{1,0:T(8,128)(2,1)S(1)} %copy-done.43), channel_id=1, source_target_pairs={{0,16},{4,20},{8,24},{12,28},{16,0},{20,4},{24,8},{28,12},{1,17},{... | collective-permute-start | bytes 995336 | tf_op jit(solution)/shard_map/ppermute | solution.py:37
  231.0 30.6 %collective-permute-start.21 = (bf16[144,1152]{1,0:T(8,128)(2,1)S(1)}, bf16[144,1152]{1,0:T(8,128)(2,1)S(1)}, u32[]{:S(2)}, u32[]{:S(2)}) collective-permute-start(bf16[144,1152]{1,0:T(8,128)(2,1)S(1)} %copy-done.41), channel_id=1, source_target_pairs={{0,16},{4,20},{8,24},{12,28},{16,0},{20,4},{24,8},{28,12},{1,17},{... | collective-permute-start | bytes 995336 | tf_op jit(solution)/shard_map/ppermute | solution.py:37
  235.9 59.2 %collective-permute-start.15 = (bf16[1152,1152]{1,0:T(8,128)(2,1)}, bf16[1152,1152]{1,0:T(8,128)(2,1)S(1)}, u32[]{:S(2)}, u32[]{:S(2)}) collective-permute-start(bf16[1152,1152]{1,0:T(8,128)(2,1)} %pad_maximum_fusion.refs_1_), channel_id=1, source_target_pairs={{0,1},{1,0},{2,3},{3,2},{4,5},{5,4},{6,7},{7,6},{8,9},{9,8},{10,11... | collective-permute-start | bytes 7962632 | tf_op jit(solution)/shard_map/ppermute | solution.py:37
  236.0 59.2 %collective-permute-start.16 = (bf16[1152,1152]{1,0:T(8,128)(2,1)}, bf16[1152,1152]{1,0:T(8,128)(2,1)}, u32[]{:S(2)}, u32[]{:S(2)}) collective-permute-start(bf16[1152,1152]{1,0:T(8,128)(2,1)} %collective-permute-done.11.refs_3_), channel_id=1, source_target_pairs={{0,1},{1,0},{2,3},{3,2},{4,5},{5,4},{6,7},{7,6},{8,9},{9,8},{10,11... | collective-permute-start | bytes 7962632 | tf_op jit(solution)/shard_map/ppermute | solution.py:37
  254.5 40.6 %collective-permute-start.17 = (bf16[1152,1152]{1,0:T(8,128)(2,1)}, bf16[1152,1152]{1,0:T(8,128)(2,1)S(1)}, u32[]{:S(2)}, u32[]{:S(2)}) collective-permute-start(bf16[1152,1152]{1,0:T(8,128)(2,1)} %pad_maximum_fusion.1.refs_1_), channel_id=1, source_target_pairs={{0,1},{1,0},{2,3},{3,2},{4,5},{5,4},{6,7},{7,6},{8,9},{9,8},{10,11... | collective-permute-start | bytes 7962632 | tf_op jit(solution)/shard_map/ppermute | solution.py:37
  261.6 33.6 %collective-permute-start.18 = (bf16[1152,1152]{1,0:T(8,128)(2,1)}, bf16[1152,1152]{1,0:T(8,128)(2,1)S(1)}, u32[]{:S(2)}, u32[]{:S(2)}) collective-permute-start(bf16[1152,1152]{1,0:T(8,128)(2,1)} %collective-permute-done.12.refs_3_), channel_id=1, source_target_pairs={{0,1},{1,0},{2,3},{3,2},{4,5},{5,4},{6,7},{7,6},{8,9},{9,8},{10,11... | collective-permute-start | bytes 7962632 | tf_op jit(solution)/shard_map/ppermute | solution.py:37
  261.6 31.8 %collective-permute-start.19 = (bf16[576,1152]{1,0:T(8,128)(2,1)}, bf16[576,1152]{1,0:T(8,128)(2,1)S(1)}, u32[]{:S(2)}, u32[]{:S(2)}) collective-permute-start(bf16[576,1152]{1,0:T(8,128)(2,1)} %pad_maximum_fusion.12), channel_id=1, source_target_pairs={{0,4},{4,0},{8,12},{12,8},{16,20},{20,16},{24,28},{28,24},{1,5},{5... | collective-permute-start | bytes 3981320 | tf_op jit(solution)/shard_map/ppermute | solution.py:37
  296.7 42.9 %collective-permute-start.26 = (bf16[288,1152]{1,0:T(8,128)(2,1)}, bf16[288,1152]{1,0:T(8,128)(2,1)}, u32[]{:S(2)}, u32[]{:S(2)}) collective-permute-start(bf16[288,1152]{1,0:T(8,128)(2,1)} %pad_maximum_fusion.23), channel_id=1, source_target_pairs={{0,8},{4,12},{8,0},{12,4},{16,24},{20,28},{24,16},{28,20},{1,9},{5... | collective-permute-start | bytes 1990664 | tf_op jit(solution)/shard_map/ppermute | solution.py:37
  297.5 43.5 %collective-permute-start.25 = (bf16[288,1152]{1,0:T(8,128)(2,1)S(1)}, bf16[288,1152]{1,0:T(8,128)(2,1)}, u32[]{:S(2)}, u32[]{:S(2)}) collective-permute-start(bf16[288,1152]{1,0:T(8,128)(2,1)S(1)} %pad_maximum_fusion.22), channel_id=1, source_target_pairs={{0,8},{4,12},{8,0},{12,4},{16,24},{20,28},{24,16},{28,20},{1,9},{5... | collective-permute-start | bytes 1990664 | tf_op jit(solution)/shard_map/ppermute | solution.py:37
  298.8 58.9 %collective-permute-start.23 = (bf16[1152,1152]{1,0:T(8,128)(2,1)}, bf16[1152,1152]{1,0:T(8,128)(2,1)}, u32[]{:S(2)}, u32[]{:S(2)}) collective-permute-start(bf16[1152,1152]{1,0:T(8,128)(2,1)} %pad_maximum_fusion.2.refs_1_), channel_id=1, source_target_pairs={{0,2},{1,3},{2,0},{3,1},{4,6},{5,7},{6,4},{7,5},{8,10},{9,11},{10,... | collective-permute-start | bytes 7962632 | tf_op jit(solution)/shard_map/ppermute | solution.py:37
  299.3 58.7 %collective-permute-start.24 = (bf16[1152,1152]{1,0:T(8,128)(2,1)}, bf16[1152,1152]{1,0:T(8,128)(2,1)}, u32[]{:S(2)}, u32[]{:S(2)}) collective-permute-start(bf16[1152,1152]{1,0:T(8,128)(2,1)} %pad_maximum_fusion.3.refs_1_), channel_id=1, source_target_pairs={{0,4},{4,0},{8,12},{12,8},{16,20},{20,16},{24,28},{28,24},{1,5},{5... | collective-permute-start | bytes 7962632 | tf_op jit(solution)/shard_map/ppermute | solution.py:37
  357.9 29.1 %collective-permute-start.32 = (bf16[576,1152]{1,0:T(8,128)(2,1)S(1)}, bf16[576,1152]{1,0:T(8,128)(2,1)}, u32[]{:S(2)}, u32[]{:S(2)}) collective-permute-start(bf16[576,1152]{1,0:T(8,128)(2,1)S(1)} %pad_maximum_fusion.15), channel_id=1, source_target_pairs={{0,2},{1,3},{2,0},{3,1},{4,6},{5,7},{6,4},{7,5},{8,10},{9,11},{10,... | collective-permute-start | bytes 3981320 | tf_op jit(solution)/shard_map/ppermute | solution.py:37
  360.3 58.3 %collective-permute-start.27 = (bf16[1152,1152]{1,0:T(8,128)(2,1)}, bf16[1152,1152]{1,0:T(8,128)(2,1)}, u32[]{:S(2)}, u32[]{:S(2)}) collective-permute-start(bf16[1152,1152]{1,0:T(8,128)(2,1)} %pad_maximum_fusion.2.refs_1_), channel_id=1, source_target_pairs={{0,1},{1,0},{2,3},{3,2},{4,5},{5,4},{6,7},{7,6},{8,9},{9,8},{10,11... | collective-permute-start | bytes 7962632 | tf_op jit(solution)/shard_map/ppermute | solution.py:37
  360.4 58.2 %collective-permute-start.28 = (bf16[1152,1152]{1,0:T(8,128)(2,1)}, bf16[1152,1152]{1,0:T(8,128)(2,1)}, u32[]{:S(2)}, u32[]{:S(2)}) collective-permute-start(bf16[1152,1152]{1,0:T(8,128)(2,1)} %collective-permute-done.23.refs_3_), channel_id=1, source_target_pairs={{0,1},{1,0},{2,3},{3,2},{4,5},{5,4},{6,7},{7,6},{8,9},{9,8},{10,11... | collective-permute-start | bytes 7962632 | tf_op jit(solution)/shard_map/ppermute | solution.py:37
  360.9 57.7 %collective-permute-start.29 = (bf16[1152,1152]{1,0:T(8,128)(2,1)}, bf16[1152,1152]{1,0:T(8,128)(2,1)}, u32[]{:S(2)}, u32[]{:S(2)}) collective-permute-start(bf16[1152,1152]{1,0:T(8,128)(2,1)} %pad_maximum_fusion.3.refs_1_), channel_id=1, source_target_pairs={{0,1},{1,0},{2,3},{3,2},{4,5},{5,4},{6,7},{7,6},{8,9},{9,8},{10,11... | collective-permute-start | bytes 7962632 | tf_op jit(solution)/shard_map/ppermute | solution.py:37
  361.0 57.6 %collective-permute-start.30 = (bf16[1152,1152]{1,0:T(8,128)(2,1)}, bf16[1152,1152]{1,0:T(8,128)(2,1)}, u32[]{:S(2)}, u32[]{:S(2)}) collective-permute-start(bf16[1152,1152]{1,0:T(8,128)(2,1)} %collective-permute-done.24.refs_3_), channel_id=1, source_target_pairs={{0,1},{1,0},{2,3},{3,2},{4,5},{5,4},{6,7},{7,6},{8,9},{9,8},{10,11... | collective-permute-start | bytes 7962632 | tf_op jit(solution)/shard_map/ppermute | solution.py:37
  387.1 28.4 %collective-permute-start.31 = (bf16[576,1152]{1,0:T(8,128)(2,1)}, bf16[576,1152]{1,0:T(8,128)(2,1)}, u32[]{:S(2)}, u32[]{:S(2)}) collective-permute-start(bf16[576,1152]{1,0:T(8,128)(2,1)} %pad_maximum_fusion.14), channel_id=1, source_target_pairs={{0,4},{4,0},{8,12},{12,8},{16,20},{20,16},{24,28},{28,24},{1,5},{5... | collective-permute-start | bytes 3981320 | tf_op jit(solution)/shard_map/ppermute | solution.py:37
  437.1 29.4 %all-to-all-start.4 = ((bf16[8,2,32,1152]{3,2,1,0:T(8,128)(2,1)}), bf16[8,2,32,1152]{3,2,1,0:T(8,128)(2,1)S(1)}, u32[]{:S(2)}, u32[]{:S(2)}) async-start(bf16[8,2,32,1152]{3,2,1,0:T(8,128)(2,1)} %bitcast.188), calls=%async_computation.4 | async-start | bytes 2359296 | tf_op jit(solution)/shard_map/all_to_all | solution.py:585
  441.1 56.0 %collective-permute-start.33 = (bf16[1152,1152]{1,0:T(8,128)(2,1)}, bf16[1152,1152]{1,0:T(8,128)(2,1)}, u32[]{:S(2)}, u32[]{:S(2)}) collective-permute-start(bf16[1152,1152]{1,0:T(8,128)(2,1)} %pad_maximum_fusion.4.refs_1_), channel_id=1, source_target_pairs={{0,2},{1,3},{2,0},{3,1},{4,6},{5,7},{6,4},{7,5},{8,10},{9,11},{10,... | collective-permute-start | bytes 7962632 | tf_op jit(solution)/shard_map/ppermute | solution.py:37
  442.6 67.0 %collective-permute-start.34 = (bf16[1152,1152]{1,0:T(8,128)(2,1)}, bf16[1152,1152]{1,0:T(8,128)(2,1)}, u32[]{:S(2)}, u32[]{:S(2)}) collective-permute-start(bf16[1152,1152]{1,0:T(8,128)(2,1)} %pad_maximum_fusion.5.refs_1_), channel_id=1, source_target_pairs={{0,4},{4,0},{8,12},{12,8},{16,20},{20,16},{24,28},{28,24},{1,5},{5... | collective-permute-start | bytes 7962632 | tf_op jit(solution)/shard_map/ppermute | solution.py:37
  525.7 31.5 %collective-permute-start.37 = (bf16[1152,1152]{1,0:T(8,128)(2,1)}, bf16[1152,1152]{1,0:T(8,128)(2,1)}, u32[]{:S(2)}, u32[]{:S(2)}) collective-permute-start(bf16[1152,1152]{1,0:T(8,128)(2,1)} %pad_maximum_fusion.5.refs_1_), channel_id=1, source_target_pairs={{0,1},{1,0},{2,3},{3,2},{4,5},{5,4},{6,7},{7,6},{8,9},{9,8},{10,11... | collective-permute-start | bytes 7962632 | tf_op jit(solution)/shard_map/ppermute | solution.py:37
  525.8 31.4 %collective-permute-start.38 = (bf16[1152,1152]{1,0:T(8,128)(2,1)}, bf16[1152,1152]{1,0:T(8,128)(2,1)}, u32[]{:S(2)}, u32[]{:S(2)}) collective-permute-start(bf16[1152,1152]{1,0:T(8,128)(2,1)} %collective-permute-done.34.refs_3_), channel_id=1, source_target_pairs={{0,1},{1,0},{2,3},{3,2},{4,5},{5,4},{6,7},{7,6},{8,9},{9,8},{10,11... | collective-permute-start | bytes 7962632 | tf_op jit(solution)/shard_map/ppermute | solution.py:37
  557.2 42.2 %collective-permute-start.39 = (bf16[2,1152,1152]{2,1,0:T(8,128)(2,1)}, bf16[2,1152,1152]{2,1,0:T(8,128)(2,1)}, u32[]{:S(2)}, u32[]{:S(2)}) collective-permute-start(bf16[2,1152,1152]{2,1,0:T(8,128)(2,1)} %get-tuple-element.657), channel_id=1, source_target_pairs={{0,1},{1,0},{2,3},{3,2},{4,5},{5,4},{6,7},{7,6},{8,9},{9,8},{10,11... | collective-permute-start | bytes 15925256 | tf_op jit(solution)/shard_map/ppermute | solution.py:37
  602.8 33.7 %all-to-all-start.6 = ((bf16[8,2,32,1152]{3,2,1,0:T(8,128)(2,1)}), bf16[8,2,32,1152]{3,2,1,0:T(8,128)(2,1)}, u32[]{:S(2)}, u32[]{:S(2)}) async-start(bf16[8,2,32,1152]{3,2,1,0:T(8,128)(2,1)} %bitcast.223), calls=%async_computation.6 | async-start | bytes 2359296 | tf_op jit(solution)/shard_map/all_to_all | solution.py:589
  625.1 60.9 %collective-permute-start.42 = (bf16[2,576,1152]{2,1,0:T(8,128)(2,1)}, bf16[2,576,1152]{2,1,0:T(8,128)(2,1)}, u32[]{:S(2)}, u32[]{:S(2)}) collective-permute-start(bf16[2,576,1152]{2,1,0:T(8,128)(2,1)} %pad_maximum_fusion.6), channel_id=1, source_target_pairs={{0,4},{4,0},{8,12},{12,8},{16,20},{20,16},{24,28},{28,24},{1,5},{5... | collective-permute-start | bytes 7962632 | tf_op jit(solution)/shard_map/ppermute | solution.py:37
  631.8 59.0 %collective-permute-start.41 = (bf16[1,1152,1152]{2,1,0:T(8,128)(2,1)}, bf16[1,1152,1152]{2,1,0:T(8,128)(2,1)}, u32[]{:S(2)}, u32[]{:S(2)}) collective-permute-start(bf16[1,1152,1152]{2,1,0:T(8,128)(2,1)} %add_convert_fusion.2), channel_id=1, source_target_pairs={{0,2},{1,3},{2,0},{3,1},{4,6},{5,7},{6,4},{7,5},{8,10},{9,11},{10,... | collective-permute-start | bytes 7962632 | tf_op jit(solution)/shard_map/ppermute | solution.py:37
  690.8 72.8 %collective-permute-start.43 = (bf16[2,1152,1152]{2,1,0:T(8,128)(2,1)}, bf16[2,1152,1152]{2,1,0:T(8,128)(2,1)}, u32[]{:S(2)}, u32[]{:S(2)}) collective-permute-start(bf16[2,1152,1152]{2,1,0:T(8,128)(2,1)} %get-tuple-element.752), channel_id=1, source_target_pairs={{0,1},{1,0},{2,3},{3,2},{4,5},{5,4},{6,7},{7,6},{8,9},{9,8},{10,11... | collective-permute-start | bytes 15925256 | tf_op jit(solution)/shard_map/ppermute | solution.py:37
  709.1 33.7 %all-to-all-start.5 = ((bf16[8,2,32,1152]{3,2,1,0:T(8,128)(2,1)}), bf16[8,2,32,1152]{3,2,1,0:T(8,128)(2,1)S(1)}, u32[]{:S(2)}, u32[]{:S(2)}) async-start(bf16[8,2,32,1152]{3,2,1,0:T(8,128)(2,1)} %bitcast.222), calls=%async_computation.5 | async-start | bytes 2359296 | tf_op jit(solution)/shard_map/all_to_all | solution.py:589
  717.3 46.3 %collective-permute-start.45 = (bf16[1,576,1152]{2,1,0:T(8,128)(2,1)}, bf16[1,576,1152]{2,1,0:T(8,128)(2,1)}, u32[]{:S(2)}, u32[]{:S(2)}) collective-permute-start(bf16[1,576,1152]{2,1,0:T(8,128)(2,1)} %add_convert_fusion.11), channel_id=1, source_target_pairs={{0,2},{1,3},{2,0},{3,1},{4,6},{5,7},{6,4},{7,5},{8,10},{9,11},{10,... | collective-permute-start | bytes 3981320 | tf_op jit(solution)/shard_map/ppermute | solution.py:37
  722.4 41.2 %collective-permute-start.44 = (bf16[1,576,1152]{2,1,0:T(8,128)(2,1)}, bf16[1,576,1152]{2,1,0:T(8,128)(2,1)}, u32[]{:S(2)}, u32[]{:S(2)}) collective-permute-start(bf16[1,576,1152]{2,1,0:T(8,128)(2,1)} %add_convert_fusion.12), channel_id=1, source_target_pairs={{0,4},{4,0},{8,12},{12,8},{16,20},{20,16},{24,28},{28,24},{1,5},{5... | collective-permute-start | bytes 3981320 | tf_op jit(solution)/shard_map/ppermute | solution.py:37
  766.0 64.0 %collective-permute-start.48 = (bf16[1,288,1152]{2,1,0:T(8,128)(2,1)S(1)}, bf16[1,288,1152]{2,1,0:T(8,128)(2,1)}, u32[]{:S(2)}, u32[]{:S(2)}) collective-permute-start(bf16[1,288,1152]{2,1,0:T(8,128)(2,1)S(1)} %add_convert_fusion.25), channel_id=1, source_target_pairs={{0,8},{4,12},{8,0},{12,4},{16,24},{20,28},{24,16},{28,20},{1,9},{5... | collective-permute-start | bytes 1990664 | tf_op jit(solution)/shard_map/ppermute | solution.py:37
  769.5 60.5 %collective-permute-start.46 = (bf16[2,576,1152]{2,1,0:T(8,128)(2,1)S(1)}, bf16[2,576,1152]{2,1,0:T(8,128)(2,1)}, u32[]{:S(2)}, u32[]{:S(2)}) collective-permute-start(bf16[2,576,1152]{2,1,0:T(8,128)(2,1)S(1)} %pad_maximum_fusion.7), channel_id=1, source_target_pairs={{0,4},{4,0},{8,12},{12,8},{16,20},{20,16},{24,28},{28,24},{1,5},{5... | collective-permute-start | bytes 7962632 | tf_op jit(solution)/shard_map/ppermute | solution.py:37
  773.0 57.0 %collective-permute-start.47 = (bf16[1,288,1152]{2,1,0:T(8,128)(2,1)S(1)}, bf16[1,288,1152]{2,1,0:T(8,128)(2,1)S(1)}, u32[]{:S(2)}, u32[]{:S(2)}) collective-permute-start(bf16[1,288,1152]{2,1,0:T(8,128)(2,1)S(1)} %add_convert_fusion.26), channel_id=1, source_target_pairs={{0,8},{4,12},{8,0},{12,4},{16,24},{20,28},{24,16},{28,20},{1,9},{5... | collective-permute-start | bytes 1990664 | tf_op jit(solution)/shard_map/ppermute | solution.py:37
  830.0 40.5 %collective-permute-start.49 = (bf16[2,1152,1152]{2,1,0:T(8,128)(2,1)}, bf16[2,1152,1152]{2,1,0:T(8,128)(2,1)}, u32[]{:S(2)}, u32[]{:S(2)}) collective-permute-start(bf16[2,1152,1152]{2,1,0:T(8,128)(2,1)} %get-tuple-element.818), channel_id=1, source_target_pairs={{0,1},{1,0},{2,3},{3,2},{4,5},{5,4},{6,7},{7,6},{8,9},{9,8},{10,11... | collective-permute-start | bytes 15925256 | tf_op jit(solution)/shard_map/ppermute | solution.py:37
  830.1 40.4 %collective-permute-start.50 = (bf16[2,1152,1152]{2,1,0:T(8,128)(2,1)}, bf16[2,1152,1152]{2,1,0:T(8,128)(2,1)}, u32[]{:S(2)}, u32[]{:S(2)}) collective-permute-start(bf16[2,1152,1152]{2,1,0:T(8,128)(2,1)} %get-tuple-element.820), channel_id=1, source_target_pairs={{0,1},{1,0},{2,3},{3,2},{4,5},{5,4},{6,7},{7,6},{8,9},{9,8},{10,11... | collective-permute-start | bytes 15925256 | tf_op jit(solution)/shard_map/ppermute | solution.py:37
  834.1 33.6 %collective-permute-start.53 = (bf16[1,144,1152]{2,1,0:T(8,128)(2,1)S(1)}, bf16[1,144,1152]{2,1,0:T(8,128)(2,1)S(1)}, u32[]{:S(2)}, u32[]{:S(2)}) collective-permute-start(bf16[1,144,1152]{2,1,0:T(8,128)(2,1)S(1)} %add_convert_fusion.33), channel_id=1, source_target_pairs={{0,16},{4,20},{8,24},{12,28},{16,0},{20,4},{24,8},{28,12},{1,17},{... | collective-permute-start | bytes 995336 | tf_op jit(solution)/shard_map/ppermute | solution.py:37
  839.1 31.4 %collective-permute-start.51 = (bf16[1,576,1152]{2,1,0:T(8,128)(2,1)}, bf16[1,576,1152]{2,1,0:T(8,128)(2,1)}, u32[]{:S(2)}, u32[]{:S(2)}) collective-permute-start(bf16[1,576,1152]{2,1,0:T(8,128)(2,1)} %add_convert_fusion.8), channel_id=1, source_target_pairs={{0,2},{1,3},{2,0},{3,1},{4,6},{5,7},{6,4},{7,5},{8,10},{9,11},{10,... | collective-permute-start | bytes 3981320 | tf_op jit(solution)/shard_map/ppermute | solution.py:37
  842.5 25.1 %collective-permute-start.52 = (bf16[1,144,1152]{2,1,0:T(8,128)(2,1)}, bf16[1,144,1152]{2,1,0:T(8,128)(2,1)S(1)}, u32[]{:S(2)}, u32[]{:S(2)}) collective-permute-start(bf16[1,144,1152]{2,1,0:T(8,128)(2,1)} %add_convert_fusion.34), channel_id=1, source_target_pairs={{0,16},{4,20},{8,24},{12,28},{16,0},{20,4},{24,8},{28,12},{1,17},{... | collective-permute-start | bytes 995336 | tf_op jit(solution)/shard_map/ppermute | solution.py:37
  887.8 38.5 %collective-permute-start.56 = (bf16[1,288,1152]{2,1,0:T(8,128)(2,1)}, bf16[1,288,1152]{2,1,0:T(8,128)(2,1)}, u32[]{:S(2)}, u32[]{:S(2)}) collective-permute-start(bf16[1,288,1152]{2,1,0:T(8,128)(2,1)} %add_convert_fusion.24), channel_id=1, source_target_pairs={{0,8},{4,12},{8,0},{12,4},{16,24},{20,28},{24,16},{28,20},{1,9},{5... | collective-permute-start | bytes 1990664 | tf_op jit(solution)/shard_map/ppermute | solution.py:37
  893.0 58.6 %collective-permute-start.55 = (bf16[1,1152,1152]{2,1,0:T(8,128)(2,1)}, bf16[1,1152,1152]{2,1,0:T(8,128)(2,1)}, u32[]{:S(2)}, u32[]{:S(2)}) collective-permute-start(bf16[1,1152,1152]{2,1,0:T(8,128)(2,1)} %add_convert_fusion.1), channel_id=1, source_target_pairs={{0,2},{1,3},{2,0},{3,1},{4,6},{5,7},{6,4},{7,5},{8,10},{9,11},{10,... | collective-permute-start | bytes 7962632 | tf_op jit(solution)/shard_map/ppermute | solution.py:37
  898.4 58.1 %collective-permute-start.54 = (bf16[2,576,1152]{2,1,0:T(8,128)(2,1)}, bf16[2,576,1152]{2,1,0:T(8,128)(2,1)}, u32[]{:S(2)}, u32[]{:S(2)}) collective-permute-start(bf16[2,576,1152]{2,1,0:T(8,128)(2,1)} %pad_maximum_fusion.8), channel_id=1, source_target_pairs={{0,4},{4,0},{8,12},{12,8},{16,20},{20,16},{24,28},{28,24},{1,5},{5... | collective-permute-start | bytes 7962632 | tf_op jit(solution)/shard_map/ppermute | solution.py:37
  979.3 36.0 %collective-permute-start.64 = (bf16[1,576,1152]{2,1,0:T(8,128)(2,1)}, bf16[1,576,1152]{2,1,0:T(8,128)(2,1)}, u32[]{:S(2)}, u32[]{:S(2)}) collective-permute-start(bf16[1,576,1152]{2,1,0:T(8,128)(2,1)} %add_convert_fusion.4), channel_id=1, source_target_pairs={{0,4},{4,0},{8,12},{12,8},{16,20},{20,16},{24,28},{28,24},{1,5},{5... | collective-permute-start | bytes 3981320 | tf_op jit(solution)/shard_map/ppermute | solution.py:37
  980.3 37.7 %collective-permute-start.62 = (bf16[2,1152,1152]{2,1,0:T(8,128)(2,1)}, bf16[2,1152,1152]{2,1,0:T(8,128)(2,1)}, u32[]{:S(2)}, u32[]{:S(2)}) collective-permute-start(bf16[2,1152,1152]{2,1,0:T(8,128)(2,1)} %get-tuple-element.894), channel_id=1, source_target_pairs={{0,1},{1,0},{2,3},{3,2},{4,5},{5,4},{6,7},{7,6},{8,9},{9,8},{10,11... | collective-permute-start | bytes 15925256 | tf_op jit(solution)/shard_map/ppermute | solution.py:37
  985.8 32.3 %collective-permute-start.63 = (bf16[1,576,1152]{2,1,0:T(8,128)(2,1)}, bf16[1,576,1152]{2,1,0:T(8,128)(2,1)}, u32[]{:S(2)}, u32[]{:S(2)}) collective-permute-start(bf16[1,576,1152]{2,1,0:T(8,128)(2,1)} %add_convert_fusion.5), channel_id=1, source_target_pairs={{0,2},{1,3},{2,0},{3,1},{4,6},{5,7},{6,4},{7,5},{8,10},{9,11},{10,... | collective-permute-start | bytes 3981320 | tf_op jit(solution)/shard_map/ppermute | solution.py:37
  991.0 24.2 %collective-permute-start.65 = (bf16[1,144,1152]{2,1,0:T(8,128)(2,1)}, bf16[1,144,1152]{2,1,0:T(8,128)(2,1)}, u32[]{:S(2)}, u32[]{:S(2)}) collective-permute-start(bf16[1,144,1152]{2,1,0:T(8,128)(2,1)} %add_convert_fusion.32), channel_id=1, source_target_pairs={{0,16},{4,20},{8,24},{12,28},{16,0},{20,4},{24,8},{28,12},{1,17},{... | collective-permute-start | bytes 995336 | tf_op jit(solution)/shard_map/ppermute | solution.py:37
  996.6 41.4 %all-to-all-start.8 = ((bf16[4,288,512]{2,1,0:T(8,128)(2,1)}), bf16[4,288,512]{2,1,0:T(8,128)(2,1)S(1)}, u32[]{:S(2)}, u32[]{:S(2)}) async-start(bf16[4,288,512]{2,1,0:T(8,128)(2,1)} %bitcast.220), calls=%async_computation.8 | async-start | bytes 2359296 | tf_op jit(solution)/shard_map/all_to_all | solution.py:659
  1022.7 64.3 %collective-permute-start.66 = (bf16[1,1152,1152]{2,1,0:T(8,128)(2,1)}, bf16[1,1152,1152]{2,1,0:T(8,128)(2,1)}, u32[]{:S(2)}, u32[]{:S(2)}) collective-permute-start(bf16[1,1152,1152]{2,1,0:T(8,128)(2,1)} %add_convert_fusion), channel_id=1, source_target_pairs={{0,2},{1,3},{2,0},{3,1},{4,6},{5,7},{6,4},{7,5},{8,10},{9,11},{10,... | collective-permute-start | bytes 7962632 | tf_op jit(solution)/shard_map/ppermute | solution.py:37
  1034.0 25.9 %collective-permute-start.67 = (bf16[1,288,1152]{2,1,0:T(8,128)(2,1)}, bf16[1,288,1152]{2,1,0:T(8,128)(2,1)}, u32[]{:S(2)}, u32[]{:S(2)}) collective-permute-start(bf16[1,288,1152]{2,1,0:T(8,128)(2,1)} %add_convert_fusion.23), channel_id=1, source_target_pairs={{0,8},{4,12},{8,0},{12,4},{16,24},{20,28},{24,16},{28,20},{1,9},{5... | collective-permute-start | bytes 1990664 | tf_op jit(solution)/shard_map/ppermute | solution.py:37
  1090.7 30.8 %collective-permute-start.69 = (bf16[1,576,1152]{2,1,0:T(8,128)(2,1)}, bf16[1,576,1152]{2,1,0:T(8,128)(2,1)}, u32[]{:S(2)}, u32[]{:S(2)}) collective-permute-start(bf16[1,576,1152]{2,1,0:T(8,128)(2,1)} %add_convert_fusion.3), channel_id=1, source_target_pairs={{0,4},{4,0},{8,12},{12,8},{16,20},{20,16},{24,28},{28,24},{1,5},{5... | collective-permute-start | bytes 3981320 | tf_op jit(solution)/shard_map/ppermute | solution.py:37
  1098.0 26.6 %collective-permute-start.73 = (bf16[1,144,1152]{2,1,0:T(8,128)(2,1)S(1)}, bf16[1,144,1152]{2,1,0:T(8,128)(2,1)S(1)}, u32[]{:S(2)}, u32[]{:S(2)}) collective-permute-start(bf16[1,144,1152]{2,1,0:T(8,128)(2,1)S(1)} %add_convert_fusion.29), channel_id=1, source_target_pairs={{0,16},{4,20},{8,24},{12,28},{16,0},{20,4},{24,8},{28,12},{1,17},{... | collective-permute-start | bytes 995336 | tf_op jit(solution)/shard_map/ppermute | solution.py:37
  1101.5 27.7 %collective-permute-start.72 = (bf16[1,144,1152]{2,1,0:T(8,128)(2,1)S(1)}, bf16[1,144,1152]{2,1,0:T(8,128)(2,1)S(1)}, u32[]{:S(2)}, u32[]{:S(2)}) collective-permute-start(bf16[1,144,1152]{2,1,0:T(8,128)(2,1)S(1)} %add_convert_fusion.30), channel_id=1, source_target_pairs={{0,16},{4,20},{8,24},{12,28},{16,0},{20,4},{24,8},{28,12},{1,17},{... | collective-permute-start | bytes 995336 | tf_op jit(solution)/shard_map/ppermute | solution.py:37
  (117 other events, 1707.6 us)

commit v3 on v2

--- a/solution.py
+++ b/solution.py
@@ -63,6 +63,35 @@
     return result
 
 
+def sum_rows(terms, names, first, count):
+    width = terms[0][0].shape[2]
+    rows = 576 if count % 576 == 0 else count // 2 if count % 32 == 0 else count
+    assert first % rows == 0
+
+    def body(*refs):
+        value = refs[0][...].astype(f32)
+        for ref in refs[1:-1]:
+            value = value + ref[...].astype(f32)
+        refs[-1][...] = value.astype(bf16)
+
+    def spec(lead):
+        return pl.BlockSpec((1, rows, width), lambda i, r: (lead + i, first // rows + r, 0))
+
+    return pl.pallas_call(
+        body,
+        grid=(names, count // rows),
+        in_specs=[spec(lead) for _, lead in terms],
+        out_specs=pl.BlockSpec((1, rows, width), lambda i, r: (i, r, 0)),
+        out_shape=jax.ShapeDtypeStruct((names, count, width), bf16),
+        cost_estimate=pl.CostEstimate(
+            flops=len(terms) * names * count * width,
+            transcendentals=0,
+            bytes_accessed=2 * (len(terms) + 1) * names * count * width,
+        ),
+        name="sum_rows",
+    )(*[value for value, _ in terms])
+
+
 class Gather:
     def __init__(self, shard, rows, parts, kind):
         self.rows, self.parts, self.depth = rows, parts, shard.shape[0]
@@ -71,21 +100,33 @@
         self.arrays = [shard]
         self.done = 0
 
-    def step(self):
+    def step(self, after=None):
         axis, bit = self.plan[self.done]
-        merge = self.done < len(self.plan) - 2
-        labels, arrays = [], []
-        for names, value in zip(self.labels, self.arrays):
+        last_axis, last_bit = self.plan[-1]
+        left = len(self.plan) - self.done
+
+        def behind(value):
+            return value if after is None else lax.optimization_barrier((value, after))[0]
+
+        if left == 1:
+            names, value = self.labels[1], self.arrays[1]
+            result = swap(behind(value), axis, bit)
+            self.labels.append([moved(name, axis, bit) for name in names])
+            self.arrays.append(result)
+        else:
+            (names,), (value,) = self.labels, self.arrays
+            result = after
             other = swap(value, axis, bit)
             other_names = [moved(name, axis, bit) for name in names]
-            if merge:
-                labels.append(names + other_names)
-                arrays.append(jnp.concatenate([value, other], 0))
+            if left > 2:
+                self.labels = [names + other_names]
+                self.arrays = [jnp.concatenate([value, other], 0)]
             else:
-                labels += [names, other_names]
-                arrays += [value, other]
-        self.labels, self.arrays = labels, arrays
+                result = swap(behind(value), last_axis, last_bit)
+                self.labels = [names, other_names, [moved(name, last_axis, last_bit) for name in names]]
+                self.arrays = [value, other, result]
         self.done += 1
+        return result
 
     def pieces(self):
         order, depth = row_order(self.rows), self.depth
@@ -109,44 +150,57 @@
         self.order = row_order(rows)
         self.depth = kept.shape[1] // rows
         self.span = rows
-        self.arrays = [sent, kept]
-        evens = [part for part in range(parts) if not part & 1]
-        self.live = {part: [(1, place, 0)] for place, part in enumerate(evens)}
+        assert self.plan[0] == ("m", 1)
+        self.arrays = [kept, sent]
+        self.outgoing = 1
+        self.gaining = [part for part in range(parts) if not part & 1]
+        self.live = {part: [(0, place)] for place, part in enumerate(self.gaining)}
         self.done = 0
 
     def take(self, term, first, count):
-        number, lead, start = term
-        return self.arrays[number][lead, start + first : start + first + count]
+        number, lead = term
+        return self.arrays[number][lead, first : first + count]
 
     def sums(self, names, first, count):
-        return [total([self.take(t, first, count) for t in self.live[n]]).astype(bf16) for n in names]
-
-    def step(self):
+        if self.depth % 16 == 0:
+            leads = [[term[1] for term in terms] for terms in zip(*[self.live[n] for n in names])]
+            numbers = [term[0] for term in self.live[names[0]]]
+            assert all(list(l) == list(range(l[0], l[0] + len(l))) for l in leads)
+            return sum_rows([(self.arrays[n], l[0]) for n, l in zip(numbers, leads)], len(names), first, count)
+        return jnp.stack(
+            [total([self.take(t, first, count) for t in self.live[n]]).astype(bf16) for n in names]
+        )
+
+    def step(self, after=None):
         axis, bit = self.plan[self.done]
-        if self.done == 0:
-            assert (axis, bit) == ("m", 1)
-            self.arrays.append(swap(self.arrays[0], axis, bit))
-            for place, name in enumerate(sorted(self.live)):
-                self.live[name].append((len(self.arrays) - 1, place, 0))
-        elif axis == "m":
+        got = swap(self.arrays.pop(self.outgoing), axis, bit)
+        if after is not None:
+            got, _ = lax.optimization_barrier((got, after))
+        self.arrays.append(got)
+        for place, name in enumerate(self.gaining):
+            self.live[name].append((len(self.arrays) - 1, place))
+        self.done += 1
+        self.prepare()
+
+    def prepare(self):
+        if self.done == len(self.plan):
+            return
+        axis, bit = self.plan[self.done]
+        if axis == "m":
             names = [name for name in sorted(self.live) if name & bit]
             sent = self.sums(names, 0, self.span * self.depth)
             for name in names:
                 self.live.pop(name)
-            self.arrays.append(swap(jnp.stack(sent), axis, bit))
-            for place, name in enumerate(names):
-                self.live[name ^ bit].append((len(self.arrays) - 1, place, 0))
+            self.gaining = [name ^ bit for name in names]
         else:
             half = self.span // 2
             order = self.order
             assert all(order[half + p] == order[p] ^ bit for p in range(half))
-            names = sorted(self.live)
-            sent = self.sums(names, half * self.depth, half * self.depth)
-            self.arrays.append(swap(jnp.stack(sent), axis, bit))
-            for place, name in enumerate(names):
-                self.live[name].append((len(self.arrays) - 1, place, 0))
+            self.gaining = sorted(self.live)
+            sent = self.sums(self.gaining, half * self.depth, half * self.depth)
             self.span = half
-        self.done += 1
+        self.outgoing = len(self.arrays)
+        self.arrays.append(sent)
 
     def result(self):
         return total([self.take(t, 0, self.depth) for t in self.live[0]])
@@ -284,47 +338,160 @@
     )(x, *weight.arrays, *extras)
 
 
-def contract(xs, weight, columns, name):
+def contract(xs, weight, columns, name, large=(), small=(), outs=None, finish=None):
     parts, tokens, n = xs.shape
     low, high = columns
     count = len(weight.arrays)
     height = weight.height
+    if finish is None:
+        outs = [jax.ShapeDtypeStruct((tokens, height), f32)]
 
     def body(*refs):
         x_ref, refs = refs[0], refs[1:]
-        w_refs, (out, held, sems) = refs[:count], refs[count:]
+        w_refs, refs = refs[:count], refs[count:]
+        large_refs, refs = refs[: len(large)], refs[len(large) :]
+        small_refs, refs = refs[: len(small)], refs[len(small) :]
+        out_refs, refs = refs[: len(outs)], refs[len(outs) :]
+        held, sems = refs[:2]
         step = pl.program_id(0)
+        acc = out_refs[0]
+        if finish is not None:
+            acc, local, large_sems = refs[2], refs[3:-1], refs[-1]
+            copies = [
+                pltpu.make_async_copy(ref, to, large_sems.at[place])
+                for place, (ref, to) in enumerate(zip(large_refs, local))
+            ]
         weight.arrive(step, w_refs, held, sems)
-        left = x_ref[0]
+        if finish is not None:
+
+            @pl.when(step == 0)
+            def _():
+                for copy in copies:
+                    copy.start()
+
         right = cut_last(lambda a, b: held[step, :, a:b], low, high)
-        value = dot_nt(left, right)
+        value = dot_nt(x_ref[0], right)
 
         @pl.when(step == 0)
         def _():
-            out[...] = value
+            acc[...] = value
 
         @pl.when(step > 0)
         def _():
-            out[...] += value
-
-    return pl.pallas_call(
+            acc[...] += value
+
+        if finish is not None:
+
+            @pl.when(step == parts - 1)
+            def _():
+                for copy in copies:
+                    copy.wait()
+                finish(acc, local, small_refs, out_refs)
+
+    scratch = weight.scratch()
+    if finish is not None:
+        scratch.append(pltpu.VMEM((tokens, height), f32))
+        scratch += [pltpu.VMEM(value.shape, value.dtype) for value in large]
+        scratch.append(pltpu.SemaphoreType.DMA((max(len(large), 1),)))
+    results = pl.pallas_call(
         body,
         grid=(parts,),
-        in_specs=[part_spec((tokens, n))] + [pl.BlockSpec(memory_space=pl.ANY)] * count,
-        out_specs=whole_spec((tokens, height)),
-        out_shape=jax.ShapeDtypeStruct((tokens, height), f32),
-        scratch_shapes=weight.scratch(),
+        in_specs=[part_spec((tokens, n))]
+        + [pl.BlockSpec(memory_space=pl.ANY)] * (count + len(large))
+        + [whole_spec(value.shape) for value in small],
+        out_specs=[whole_spec(out.shape) for out in outs],
+        out_shape=outs,
+        scratch_shapes=scratch,
         compiler_params=pltpu.CompilerParams(vmem_limit_bytes=LIMIT),
         cost_estimate=pl.CostEstimate(
             flops=2 * tokens * height * n * parts,
             transcendentals=0,
-            bytes_accessed=2 * parts * n * (height + tokens) + 4 * tokens * height,
+            bytes_accessed=2 * parts * n * (height + tokens) + 4 * tokens * height * (1 + len(large)),
         ),
         name=name,
-    )(xs, *weight.arrays)
-
-
-def weight_grads(pairs, name):
+    )(xs, *weight.arrays, *large, *small)
+    return results[0] if finish is None else results
+
+
+ROWS = 32
+
+
+def by_rows(tokens, work, sums=0, width=0):
+    def turn(index, carried):
+        made = work(pl.ds(pl.multiple_of(index * ROWS, ROWS), ROWS))
+        return tuple(c + jnp.sum(m, 0, keepdims=True) for c, m in zip(carried, made or ()))
+
+    return lax.fori_loop(0, tokens // ROWS, turn, (jnp.zeros((1, width), f32),) * sums)
+
+
+def finish_middle(acc, large, small, outs):
+    (stream,), (bias, gate, scale, shift) = large, small
+    branch_out, middle_out, normed_out, inverse_out, hidden_out = outs
+
+    def work(rows):
+        branch = acc[rows, :] + bias[...]
+        middle = stream[rows, :] + gate[...] * branch
+        center = middle - jnp.sum(middle, 1, keepdims=True) / D
+        inverse = lax.rsqrt(jnp.sum(center * center, 1, keepdims=True) / D + EPSILON)
+        normed = center * inverse
+        branch_out[rows, :] = branch
+        middle_out[rows, :] = middle
+        normed_out[rows, :] = normed
+        inverse_out[rows, :] = inverse
+        hidden_out[rows, :] = (normed * (1.0 + scale[...]) + shift[...]).astype(bf16)
+
+    by_rows(acc.shape[0], work)
+
+
+def finish_stream(acc, large, small, outs):
+    (middle,), (bias, gate) = large, small
+    branch_out, result_out = outs
+
+    def work(rows):
+        branch = acc[rows, :] + bias[...]
+        branch_out[rows, :] = branch
+        result_out[rows, :] = (middle[rows, :] + gate[...] * branch).astype(bf16)
+
+    by_rows(acc.shape[0], work)
+
+
+def norm_back(grad_hidden, scale, normed, inverse):
+    grad_normed = grad_hidden * (1.0 + scale)
+    first = jnp.sum(grad_normed, 1, keepdims=True) / D
+    second = jnp.sum(grad_normed * normed, 1, keepdims=True) / D
+    return inverse * (grad_normed - first - normed * second)
+
+
+def finish_middle_back(acc, large, small, outs):
+    (grad, normed, branch, inverse), (scale, gate) = large, small
+    middle_out, low_out, sums_out = outs
+
+    def work(rows):
+        grad_hidden = acc[rows, :]
+        middle = grad[rows, :] + norm_back(grad_hidden, scale[...], normed[rows, :], inverse[rows, :])
+        middle_out[rows, :] = middle
+        low_out[rows, :] = (gate[...] * middle).astype(bf16)
+        return grad_hidden, grad_hidden * normed[rows, :], middle * branch[rows, :]
+
+    made = by_rows(acc.shape[0], work, 3, acc.shape[1])
+    sums_out[...] = jnp.concatenate(made, 0)
+
+
+def finish_stream_back(acc, large, small, outs):
+    (middle, normed, inverse), (scale,) = large, small
+    stream_out, sums_out = outs
+
+    def work(rows):
+        grad_hidden = acc[rows, :]
+        back = norm_back(grad_hidden, scale[...], normed[rows, :], inverse[rows, :])
+        stream_out[rows, :] = (middle[rows, :] + back).astype(bf16)
+        return grad_hidden, grad_hidden * normed[rows, :]
+
+    made = by_rows(acc.shape[0], work, 2, acc.shape[1])
+    sums_out[...] = jnp.concatenate(made, 0)
+
+
+def weight_grads(pairs, cuts, name):
     tokens, depth = pairs[0][0].shape
     parts = pairs[0][1].shape[0]
     half = parts // 2
@@ -338,7 +505,8 @@
     def body(*refs):
         x_refs, refs = refs[:count], refs[count:]
         g_refs, refs = refs[:count], refs[count:]
-        (sent, kept), refs = refs[:2], refs[2:]
+        sent, refs = refs[: len(cuts)], refs[len(cuts) :]
+        kept, refs = refs[: len(cuts)], refs[len(cuts) :]
         x_sums, refs = refs[:count], refs[count:]
         g_sums, turned = refs[:count], refs[count:]
         step = pl.program_id(0)
@@ -354,9 +522,11 @@
         for right, g_sum in zip(rights, g_sums):
             g_sum[0] = jnp.sum(right.astype(f32), 0, keepdims=True)
 
-        def fill(out):
+        def fill(outs):
             made = [dot_nn(t_ref[...], r).astype(bf16) for t_ref, r in zip(turned, rights)]
-            out[0] = made[0] if count == 1 else jnp.concatenate(made, 1)
+            made = made[0] if count == 1 else jnp.concatenate(made, 1)
+            for out, (low, high) in zip(outs, cuts):
+                out[0] = made[:, low:high]
 
         @pl.when(step < half)
         def _():
@@ -372,12 +542,16 @@
         in_specs=[whole_spec((tokens, depth))] * count
         + [pl.BlockSpec((1, tokens, n), lambda s: (which(s), 0, 0)) for n in widths],
         out_specs=[
-            pl.BlockSpec((1, depth, full), lambda s: (jnp.minimum(s, half - 1), 0, 0)),
-            pl.BlockSpec((1, depth, full), lambda s: (jnp.maximum(s - half, 0), 0, 0)),
+            pl.BlockSpec((1, depth, high - low), lambda s: (jnp.minimum(s, half - 1), 0, 0))
+            for low, high in cuts
+        ]
+        + [
+            pl.BlockSpec((1, depth, high - low), lambda s: (jnp.maximum(s - half, 0), 0, 0))
+            for low, high in cuts
         ]
         + [whole_spec((1, depth))] * count
         + [pl.BlockSpec((1, 1, n), lambda s: (which(s), 0, 0)) for n in widths],
-        out_shape=[jax.ShapeDtypeStruct((half, depth, full), bf16)] * 2
+        out_shape=[jax.ShapeDtypeStruct((half, depth, high - low), bf16) for low, high in cuts] * 2
         + [jax.ShapeDtypeStruct((1, depth), f32)] * count
         + [jax.ShapeDtypeStruct((parts, 1, n), f32) for n in widths],
         scratch_shapes=[pltpu.VMEM((depth, tokens), bf16)] * count,
@@ -389,7 +563,10 @@
         ),
         name=name,
     )(*[x for x, _ in pairs], *[g for _, g in pairs])
-    return outs[:2], outs[2 : 2 + count], outs[2 + count :]
+    ranges = len(cuts)
+    stacks = list(zip(outs[:ranges], outs[ranges : 2 * ranges]))
+    outs = outs[2 * ranges :]
+    return stacks, outs[:count], outs[count:]
 
 
 def gelu_pair(value, bias):
@@ -585,7 +762,10 @@
         return lax.all_to_all(shaped, "row", 0, 0).reshape(tokens, span)
 
     def to_frames(value):
-        shaped = stream_plain(value.astype(bf16)).reshape(rows, frames_dev, pos_block, span)
+        return send_frames(stream_plain(value.astype(bf16)))
+
+    def send_frames(value):
+        shaped = value.reshape(rows, frames_dev, pos_block, span)
         return lax.all_to_all(shaped, "row", 0, 0).swapaxes(0, 1).reshape(tokens, span)
 
     def gathered(gather):
@@ -641,6 +821,8 @@
     bias_fc1 = [all_fc1[:, b][:, None, :] for b in range(2)]
     hidden_width = w_fc1.shape[2]
     mixed_cols, out_cols, hidden_cols = (0, 3 * width), (3 * width, 4 * width), (0, hidden_width)
+    middle_cut = 4 * width // 256 * 128 + 128
+    mixed_cuts = [(0, middle_cut), (middle_cut, 4 * width)]
     layouts = (spatial, temporal)
     groups_of = (1, lat_count)
 
@@ -676,7 +858,22 @@
         attended, logs = attention_call(forward_kernel, [qkv], None, layouts[b], width, 4, "attend")
         return {**k, "qkv": qkv, "attended": attended, "logs": logs}
 
+    fused = relative and lat_count == 1
+
+    def shaped(*kinds):
+        return [jax.ShapeDtypeStruct(shape, kind) for shape, kind in kinds]
+
+    full = (tokens, span)
+
     def middle_stage(b, k):
+        if fused:
+            made = contract(
+                k["attended"], weights[b]["mixed"], out_cols, "out",
+                [k["stream"]], [all_out[b][None], mods[b][2], mods[b][4], mods[b][3]],
+                shaped((full, f32), (full, f32), (full, f32), ((tokens, 1), f32), (full, bf16)),
+                finish_middle,
+            )
+            return {**k, **dict(zip(("branch", "middle", "normed2", "inverse2", "hidden2"), made))}
         branch = features_sum(contract(k["attended"], weights[b]["mixed"], out_cols, "out")) + all_out[b]
         middle = k["stream"] + mods[b][2] * branch
         normed, inverse = norm_forward(middle)
@@ -690,31 +887,48 @@
         return {**k, "act": act, "slope": slope}
 
     def down_stage(b, k):
+        if fused:
+            branch, result = contract(
+                k["act"], weights[b]["fc2"], hidden_cols, "down",
+                [k["middle"]], [all_fc2[b][None], mods[b][5]],
+                shaped((full, f32), (full, bf16)), finish_stream,
+            )
+            return result, {**k, "branch2": branch}
         branch = features_sum(contract(k["act"], weights[b]["fc2"], hidden_cols, "down")) + all_fc2[b]
         return k["middle"] + mods[b][5] * branch, {**k, "branch2": branch}
 
     def fc2_grads(b, k, grad):
         low = features_all((mods[b][5] * grad).astype(bf16))
-        stacks, (total_low,), _ = weight_grads([(low, k["act"])], "grad_fc2")
-        return {**k, "grad": grad, "low2": low, "sum_b2": own_share(total_low)}, scatter(stacks, KINDS[b]["fc2"])
+        stacks, (total_low,), _ = weight_grads([(low, k["act"])], [hidden_cols], "grad_fc2")
+        return {**k, "grad": grad, "low2": low, "sum_b2": own_share(total_low)}, scatter(stacks[0], KINDS[b]["fc2"])
 
     def up_back(b, k):
         grad_pre = project(
             k["low2"], weights[b]["fc2"], hidden_cols, [k["slope"]],
             lambda v, s: (v * s.astype(f32),), [bf16], "up_back",
         )[0]
-        stacks, _, (total_pre,) = weight_grads([(k["hidden2"], grad_pre)], "grad_fc1")
-        return {**k, "pre": grad_pre, "sum_b1": total_pre[:, 0]}, scatter(stacks, KINDS[b]["fc1"])
+        stacks, _, (total_pre,) = weight_grads([(k["hidden2"], grad_pre)], [hidden_cols], "grad_fc1")
+        return {**k, "pre": grad_pre, "sum_b1": total_pre[:, 0]}, scatter(stacks[0], KINDS[b]["fc1"])
 
     def hidden2_back(b, k):
+        if fused:
+            middle, low, sums = contract(
+                k["pre"], weights[b]["fc1"], hidden_cols, "hidden2_back",
+                [k["grad"], k["normed2"], k["branch"], k["inverse2"]], [mods[b][4], mods[b][2]],
+                shaped((full, f32), (full, bf16), ((3, span), f32)), finish_middle_back,
+            )
+            return {**k, "g_middle": middle, "low1": low, "sums2": sums}
         grad_hidden = features_sum(contract(k["pre"], weights[b]["fc1"], hidden_cols, "hidden2_back"))
         return {**k, "g_hidden2": grad_hidden}
 
     def attention_back(b, k):
-        grad_hidden = k["g_hidden2"]
-        back = norm_backward(grad_hidden * (1.0 + mods[b][4]), k["normed2"], k["inverse2"])
-        middle = k["grad"] + back
-        low = features_all((mods[b][2] * middle).astype(bf16))
+        if fused:
+            middle, low = k["g_middle"], k["low1"]
+        else:
+            grad_hidden = k["g_hidden2"]
+            back = norm_backward(grad_hidden * (1.0 + mods[b][4]), k["normed2"], k["inverse2"])
+            middle = k["grad"] + back
+            low = features_all((mods[b][2] * middle).astype(bf16))
         grad_att = project(low, weights[b]["mixed"], out_cols, [], lambda v: (v,), [bf16], "out_back")[0]
         grad_qkv = attention_call(
             backward_kernel, [k["qkv"], grad_att, k["attended"]], k["logs"], layouts[b], 3 * width, 10, "attend_back"
@@ -723,11 +937,23 @@
 
     def mixed_grads(b, k):
         stacks, (_, total_low), (total_qkv, _) = weight_grads(
-            [(k["hidden"], k["g_qkv"]), (k["low1"], k["attended"])], "grad_mixed"
+            [(k["hidden"], k["g_qkv"]), (k["low1"], k["attended"])], mixed_cuts, "grad_mixed"
         )
-        return {**k, "sum_bo": own_share(total_low), "sum_qkv": total_qkv[:, 0]}, scatter(stacks, KINDS[b]["mixed"])
+        return {**k, "sum_bo": own_share(total_low), "sum_qkv": total_qkv[:, 0]}, [
+            scatter(pair, kind) for kind, pair in enumerate(stacks)
+        ]
 
     def stream_back(b, k):
+        biases = (
+            k["sum_qkv"][:, :width], k["sum_qkv"][:, 2 * width :], k["sum_bo"], k["sum_b1"], k["sum_b2"],
+        )
+        if fused:
+            stream, sums = contract(
+                k["g_qkv"], weights[b]["mixed"], mixed_cols, "hidden_back",
+                [k["g_middle"], k["normed"], k["inverse"]], [mods[b][1]],
+                shaped((full, bf16), ((2, span), f32)), finish_stream_back,
+            )
+            return stream, ((sums, k["sums2"], k["grad"], k["branch2"]), biases)
         grad_hidden = features_sum(contract(k["g_qkv"], weights[b]["mixed"], mixed_cols, "hidden_back"))
         back = norm_backward(grad_hidden * (1.0 + mods[b][1]), k["normed"], k["inverse"])
         groups = groups_of[b]
@@ -742,20 +968,51 @@
             ],
             1,
         )
-        biases = (
-            k["sum_qkv"][:, :width], k["sum_qkv"][:, 2 * width :], k["sum_bo"], k["sum_b1"], k["sum_b2"],
-        )
         return k["g_middle"] + back, (modulate_grad, biases)
+
+    def modulate_sums(made):
+        if not fused:
+            return made
+        sums, sums2, grad, branch = made
+        last_sum = jnp.sum(grad * branch, 0, keepdims=True)
+        return jnp.concatenate([sums, sums2[2:], sums2[:2], last_sum], 0)[None]
+
+    def pack_small(small_space, small_time):
+        mod_grad_space, biases_space = modulate_sums(small_space[0]), small_space[1]
+        mod_grad_time, biases_time = modulate_sums(small_time[0]), small_time[1]
+        onehot = (jnp.arange(lat_count) == lat_here).astype(f32)
+        mod_grads = jnp.stack([onehot[:, None, None] * mod_grad_space, mod_grad_time], 1)
+        mod_grads = vector_plain(mod_grads).reshape(lat_count, 2, 6, parts, width)
+        mod_grads = jnp.moveaxis(mod_grads, -2, 0).reshape(parts, -1)
+
+        def by_part(value):
+            return jnp.take(value, part_ids, axis=0)
+
+        def by_stream(value):
+            return vector_plain(value).reshape(parts, width)
+
+        pieces = [mod_grads]
+        for space, time in zip(biases_space, biases_time):
+            for value in (space, time):
+                pieces.append(by_part(value) if value.shape[0] == parts else by_stream(value))
+        counts = np.cumsum([0] + [piece.shape[1] for piece in pieces])
+        packed = jnp.concatenate(pieces, 1)
+        packed = lax.all_to_all(packed, "m", split_axis=0, concat_axis=0, tiled=True)
+        return packed, counts
 
     names = ("mixed", "fc1", "fc2")
     gathers = [Gather(shard_of(b, n), rows, parts, KINDS[b][n]) for b in range(2) for n in names]
     weights = [{}, {}]
     depth_of = len(gathers[0].plan)
 
-    def move(*pairs):
+    def move(*pairs, after=None):
+        tail = None
         for item, until in pairs:
             while item.done < min(until, depth_of):
-                item.step()
+                if isinstance(item, Gather):
+                    tail = item.step(tail)
+                else:
+                    item.step(after)
 
     def ready(number):
         weights[number // 3][names[number % 3]] = gathered(gathers[number])
@@ -764,105 +1021,83 @@
     g = gathers
     first = depth_of - 3
     move((g[0], first - 1), (g[1], first - 1))
-    first_in, grad_top = fence(g, (own_batch(latents), own_batch(cotangent)))
+    fence(g, ())
     move((g[0], first), (g[1], first))
-    grad_top = send_positions(grad_top.T)
-    grad_top, mods = fence(g, (grad_top, mods))
+    first_in, top = fence(g, (own_batch(latents), own_batch(cotangent)))
     move((g[0], last - 2), (g[1], last - 2), (g[2], first - 1), (g[3], first - 1))
-    first_in, grad_top = to_stream(first_in), stream_rel(grad_top)
-    first_in, grad_top = fence(g, (first_in, grad_top))
+    first_in, mods, top = fence(g, (to_stream(first_in), mods, top.T))
     move((g[0], last - 1), (g[1], last - 1), (g[2], first), (g[3], first))
+    k0 = fence(g, open_stage(0, first_in))
+    move((g[2], last - 2), (g[3], last - 2), (g[4], first - 1), (g[5], first - 1), (g[0], last), (g[1], last))
     fence(g, ())
-    move((g[0], last), (g[1], last), (g[2], last - 2), (g[3], last - 2), (g[4], first - 1), (g[5], first - 1))
-    k0 = open_stage(0, first_in)
-    k0 = fence(g, k0)
     ready(0)
     ready(1)
     move((g[2], last - 1), (g[3], last - 1), (g[4], first), (g[5], first))
-    k0 = middle_stage(0, attention_stage(0, k0))
-    k0, grad_top = fence(g, (k0, grad_top))
-    move((g[2], last), (g[3], last), (g[4], last - 2), (g[5], last - 2))
-    k0 = up_stage(0, k0)
-    k0 = fence(g, k0)
+    k0 = fence(g, middle_stage(0, attention_stage(0, k0)))
+    move((g[4], last - 2), (g[5], last - 2), (g[2], last), (g[3], last))
+    k0, top = fence(g, (up_stage(0, k0), top))
     ready(2)
     ready(3)
     move((g[4], last - 1), (g[5], last - 1))
     first_out, k0 = down_stage(0, k0)
     k1 = open_stage(1, to_positions(first_out))
     k1 = attention_stage(1, k1)
-    k0, k1 = fence(g, (k0, k1))
-    move((g[4], last))
+    k0, k1, top = fence(g, (k0, k1, top))
+    move((g[4], last), (g[5], last))
+    grad_top = send_positions(top)
     k1 = middle_stage(1, k1)
     k0, k1 = fence(g, (k0, k1))
     ready(4)
-    move((g[5], last))
+    ready(5)
     k1 = up_stage(1, k1)
-    k1, s5 = fc2_grads(1, k1, grad_top)
-    k0, k1 = fence(g + [s5], (k0, k1))
-    ready(5)
+    k1, s5 = fc2_grads(1, k1, stream_rel(grad_top))
+    k0, k1 = fence([s5], (k0, k1))
     move((s5, 1))
     second_out, k1 = down_stage(1, k1)
+    second_out, k1 = lax.optimization_barrier((stream_plain(second_out.astype(bf16)), k1))
+    output = send_frames(second_out)
     k1, s4 = up_back(1, k1)
-    k0, k1, second_out = fence([s4, s5], (k0, k1, second_out))
+    k0, k1, output = fence([s4, s5], (k0, k1, output))
     move((s4, 1))
     k1 = hidden2_back(1, k1)
-    output = to_argument(to_frames(second_out).T)
     k0, k1 = fence([s4, s5], (k0, k1))
     move((s5, 2), (s4, 2))
     k1 = attention_back(1, k1)
     k1, s3 = mixed_grads(1, k1)
-    k0, k1 = fence([s3, s4, s5], (k0, k1))
-    move((s5, 3), (s4, 3), (s3, 1))
+    k0, k1, output = fence(s3 + [s4, s5], (k0, k1, output.T))
+    move((s5, 3), (s4, 3), *[(s, 1) for s in s3])
     grad_mid, small_time = stream_back(1, k1)
-    grad_low = to_frames(grad_mid)
-    k0, grad_low, small_time, output = fence([s3, s4, s5], (k0, grad_low, small_time, output))
-    move((s3, 2), (s5, 4), (s4, 4))
-    k0, s2 = fc2_grads(0, k0, stream_rel(grad_low))
+    grad_mid = stream_plain(grad_mid.astype(bf16))
+    k0, grad_mid, small_time, output = fence(s3 + [s4, s5], (k0, grad_mid, small_time, output))
+    k0, s2 = fc2_grads(0, k0, stream_rel(send_frames(grad_mid)))
     k0, s1 = up_back(0, k0)
-    k0 = hidden2_back(0, k0)
-    k0 = fence([s1, s2, s3, s4, s5], k0)
-    move((s3, 3), (s5, last), (s4, last), (s2, 1), (s1, 1))
-    k0 = attention_back(0, k0)
-    k0 = fence([s1, s2, s3, s4, s5], k0)
-    move((s2, 2), (s1, 2), (s3, 4))
+    move((s5, 4), (s4, 4), *[(s, 2) for s in s3], after=k0["pre"])
+    k0, small_time, output = fence([s1, s2] + s3 + [s4, s5], (k0, small_time, output))
+    move((s2, 1), (s5, last), (s4, last), *[(s, 3) for s in s3])
+    k0 = attention_back(0, hidden2_back(0, k0))
+    move((s1, 1))
+    k0, small_time, output = fence([s1, s2] + s3 + [s4, s5], (k0, small_time, output))
+    move((s2, 2), (s1, 2), *[(s, 4) for s in s3])
     k0, s0 = mixed_grads(0, k0)
     grad_first, small_space = stream_back(0, k0)
-    grad_first, small_space, small_time = fence(
-        [s0, s1, s2, s3], (grad_first, small_space, small_time)
-    )
-    move((s2, 3), (s1, 3), (s0, 1), (s3, last))
-    fence([s0, s1, s2, s3], ())
-    move((s0, 2), (s2, 4), (s1, 4))
-    fence([s0, s1, s2], ())
-    move((s0, 3), (s2, last), (s1, last))
-    for item in (s0, s1, s2, s3, s4, s5):
+    grad_first, small, output = fence(s0 + [s1, s2] + s3, (grad_first, (small_space, small_time), output))
+    move((s2, 3), (s1, 3), *[(s, last) for s in s3], *[(s, 1) for s in s0])
+    small, _ = lax.optimization_barrier((small, s0[0].arrays[1]))
+    packed, counts = pack_small(small[0], small[1])
+    grad_first, packed, output = fence(s0 + [s1, s2] + s3, (grad_first, packed, output))
+    move((s2, 4), (s1, 4), *[(s, 2) for s in s0])
+    output = to_argument(output)
+    output, grad_first = fence(s0 + [s1, s2], (output, grad_first))
+    move((s2, last), (s1, last), *[(s, 3) for s in s0])
+    fence(s0 + [s1, s2], ())
+    for item in s0 + [s1, s2] + s3 + [s4, s5]:
         move((item, last))
-    mod_grad_space, biases_space = small_space
-    mod_grad_time, biases_time = small_time
-    weights_space = [item.result() for item in (s0, s1, s2)]
-    weights_time = [item.result() for item in (s3, s4, s5)]
+    weights_space = [jnp.concatenate([s.result() for s in s0], 1), s1.result(), s2.result()]
+    weights_time = [jnp.concatenate([s.result() for s in s3], 1), s4.result(), s5.result()]
     grad_first = grad_first.astype(bf16)
     grad_first = dot_nt(exchange, grad_first).astype(bf16) if relative else grad_first.T
     grad_latents = to_argument(grad_first).astype(f32)
 
-    onehot = (jnp.arange(lat_count) == lat_here).astype(f32)
-    mod_grads = jnp.stack([onehot[:, None, None] * mod_grad_space, mod_grad_time], 1)
-    mod_grads = vector_plain(mod_grads).reshape(lat_count, 2, 6, parts, width)
-    mod_grads = jnp.moveaxis(mod_grads, -2, 0).reshape(parts, -1)
-
-    def by_part(value):
-        return jnp.take(value, part_ids, axis=0)
-
-    def by_stream(value):
-        return vector_plain(value).reshape(parts, width)
-
-    pieces = [mod_grads]
-    for space, time in zip(biases_space, biases_time):
-        for value in (space, time):
-            pieces.append(by_part(value) if value.shape[0] == parts else by_stream(value))
-    counts = np.cumsum([0] + [piece.shape[1] for piece in pieces])
-    packed = jnp.concatenate(pieces, 1)
-    packed = lax.all_to_all(packed, "m", split_axis=0, concat_axis=0, tiled=True)
     mod_part = packed[:, : counts[1]]
     bias_part = jnp.sum(packed[:, counts[1] :], 0, keepdims=True)
     flat = jnp.concatenate([mod_part.reshape(1, -1), bias_part], 1)

time: 1180 us -> 1120 us (0.949)
  Pallas kernels: 318 us -> 435 us
  other arithmetic: 183 us -> 74.1 us
  waiting for transfers between devices: 452 us -> 375 us
    pallas_call x0 -> x32, Pallas kernels: none -> 87.7 us  [sum_rows(): pl.pallas_call(body, grid=(names, count // rows), in_specs=[spec(lead) fo...]
    convert_element_type x27 -> x0, other arithmetic: 80.3 us -> none  [the longest x24 70 us: sums(): total([self.take(t, first, count) for t in self.live[n]]).astype(bf16)]
    ppermute x74 -> x84, waiting for transfers between devices: 390 us -> 311 us  [swap(): return lax.ppermute(value, axis, [(i, i ^ bit) for i in range(count)])]
    pallas_call x8, Pallas kernels: 94.4 us -> 122 us  [contract(): pl.pallas_call(body, grid=(parts,), in_specs=[part_spec((tokens, n))] + [...]
    all_to_all x2, waiting for transfers between devices: 21.2 us -> 38 us  [send_positions(): return lax.all_to_all(shaped, 'row', 0, 0).reshape(tokens, span)]
    all_to_all x2, waiting for transfers between devices: 11.9 us -> 0.01 us  [to_argument(): return lax.all_to_all(value.reshape(parts, width, tokens), 'm', 0, 0)]
    all_to_all x2 -> x3, waiting for transfers between devices: 18.8 us -> 26.5 us  [the longest x2 26.5 us: send_frames(): lax.all_to_all(shaped, 'row', 0, 0).swapaxes(0, 1).reshape(tokens, span)]
    concatenate x18 -> x20, other arithmetic: 27.8 us -> 24.6 us  [the longest x18 23.7 us: step(): self.arrays = [jnp.concatenate([value, other], 0)]]
  transfers between devices with their start and end apart: 84 -> 94, of which waited for: 40 -> 43; matrix products, arithmetic and copies ran while one was open for 18% -> 14% of each run, Pallas kernels for 25% -> 32%
where the time goes in v3:
time: 1120 us; the launch traced here: 1110 us
  Pallas kernels  435 us (39%)
  waiting for transfers between devices  375 us (33%)
  starting transfers between devices  120 us (11%)
  local copies, waits for them, and re-layouts  74.2 us (7%)
  other arithmetic  74.1 us (7%)
  matrix products  33.2 us (3%)
    ppermute x84, waiting for transfers between devices, swap(): return lax.ppermute(value, axis, [(i, i ^ bit) for i in range(count)])  311 us
    pallas_call x8, Pallas kernels, contract(): pl.pallas_call(body, grid=(parts,), in_specs=[part_spec((tokens, n))] + [...  122 us
    pallas_call x8, Pallas kernels, project(): pl.pallas_call(body, grid=(weight.parts,), in_specs=[whole_spec((tokens,...  89.4 us
    pallas_call x32, Pallas kernels, sum_rows(): pl.pallas_call(body, grid=(names, count // rows), in_specs=[spec(lead) fo...  87.7 us
    pallas_call x6, Pallas kernels, weight_grads(): pl.pallas_call(body, grid=(parts,), in_specs=[whole_spec((tokens, depth))...  81.8 us
    ppermute x84, starting transfers between devices, swap(): return lax.ppermute(value, axis, [(i, i ^ bit) for i in range(count)])  78.2 us
    pallas_call x4, Pallas kernels, attention_call(): pl.pallas_call(functools.partial(kernel, temporal, chunk), grid=grid, in_...  53.8 us
    all_to_all x2, waiting for transfers between devices, send_positions(): return lax.all_to_all(shaped, 'row', 0, 0).reshape(tokens, span)  38 us
  transfers between devices with their start and end apart: 94, of which 43 were waited for; matrix products, arithmetic and copies ran while one was open for 14% of the time, Pallas kernels for 32%

profile of v3, /device:TPU:0, one launch (start us, length us, event | category | flops | bytes accessed | tf_op | source)
XLA Modules:
  0.0 1114.5 jit_solution(2088319397648461845)
XLA Ops:
  6.6 4.2 all-to-all-start.2
  21.0 4.3 all-to-all-start
  29.3 19.7 %collective-permute-done.8 = f32[4,3456]{1,0:T(4,128)S(1)} collective-permute-done((f32[4,3456]{1,0:T(4,128)S(1)}, f32[4,3456]{1,0:T(4,128)S(1)}, u32[]{:S(2)}, u32[]{:S(2)}) %collective-permute-start.8) | collective-permute-done | bytes 55328 | tf_op jit(solution)/shard_map/ppermute | solution.py:37
  63.8 4.6 all-to-all-start.1
  68.4 10.9 collective-permute-done.2
  80.5 9.6 collective-permute-done.3
  99.6 4.6 fusion.7.refs_5_
  104.2 14.0 %collective-permute-done.6 = bf16[144,1152]{1,0:T(8,128)(2,1)S(1)} collective-permute-done((bf16[144,1152]{1,0:T(8,128)(2,1)}, bf16[144,1152]{1,0:T(8,128)(2,1)S(1)}, u32[]{:S(2)}, u32[]{:S(2)}) %collective-permute-start.6) | collective-permute-done | bytes 331808 | tf_op jit(solution)/shard_map/ppermute | solution.py:37
  118.3 6.0 collective-permute-done.7
  142.7 9.1 collective-permute-done.15
  151.9 13.6 %collective-permute-done.16 = bf16[288,1152]{1,0:T(8,128)(2,1)S(1)} collective-permute-done((bf16[288,1152]{1,0:T(8,128)(2,1)}, bf16[288,1152]{1,0:T(8,128)(2,1)S(1)}, u32[]{:S(2)}, u32[]{:S(2)}) %collective-permute-start.16) | collective-permute-done | bytes 663584 | tf_op jit(solution)/shard_map/ppermute | solution.py:37
  166.7 22.3 %collective-permute-done.11.refs_2_ = bf16[1152,1152]{1,0:T(8,128)(2,1)} collective-permute-done((bf16[1152,1152]{1,0:T(8,128)(2,1)}, bf16[1152,1152]{1,0:T(8,128)(2,1)}, u32[]{:S(2)}, u32[]{:S(2)}) %collective-permute-start.11) | collective-permute-done | bytes 2654240 | tf_op jit(solution)/shard_map/ppermute | solution.py:37
  190.3 5.3 collective-permute-done.17.refs_4_
  199.6 22.4 %collective-permute-done.21 = bf16[144,1152]{1,0:T(8,128)(2,1)S(1)} collective-permute-done((bf16[144,1152]{1,0:T(8,128)(2,1)S(1)}, bf16[144,1152]{1,0:T(8,128)(2,1)S(1)}, u32[]{:S(2)}, u32[]{:S(2)}) %collective-permute-start.21) | collective-permute-done | bytes 331808 | tf_op jit(solution)/shard_map/ppermute | solution.py:37
  222.1 6.2 collective-permute-done.22
  244.2 10.0 qkv.2
  254.2 13.3 %attend.2 = (bf16[4,2,256,288]{3,2,1,0:T(8,128)(2,1)}, f32[4,2,4,256]{3,2,1,0:T(4,128)}) custom-call(bf16[4,2,256,864]{3,2,1,0:T(8,128)(2,1)} %bitcast.199), custom_call_target="tpu_custom_call" | custom-call | flops 1073741824 | bytes 4718592 | tf_op jit(solution)/shard_map/attend/pallas_call | solution.py:670
  267.5 15.2 %out.2 = (f32[512,1152]{1,0:T(8,128)}, f32[512,1152]{1,0:T(8,128)}, f32[512,1152]{1,0:T(8,128)}, f32[512,1]{1,0:T(8,128)}, bf16[512,1152]{1,0:T(8,128)(2,1)}) custom-call(bf16[4,512,288]{2,1,0:T(8,128)(2,1)} %bitcast.203, bf16[1152,1152]{1,0:T(8,128)(2,1)} %pad_maximum_fusion.refs_1_, bf16[1152,1152]{1,0:T(8,128)(2,1)} %collective-permute-done.11.refs_2_, ...), custom_call_target="tpu_custom_call" | custom-call | flops 1358954496 | bytes 8552448 | tf_op jit(solution)/shard_map/out/pallas_call | solution.py:396
  286.3 6.6 collective-permute-done.23.refs_2_
  300.9 15.4 %up.2 = (bf16[4,512,1152]{2,1,0:T(8,128)(2,1)}, bf16[4,512,1152]{2,1,0:T(8,128)(2,1)}) custom-call(bf16[512,1152]{1,0:T(8,128)(2,1)} %get-tuple-element.1026.refs_0_, bf16[1152,1152]{1,0:T(8,128)(2,1)} %pad_maximum_fusion.1.refs_1_, bf16[1152,1152]{1,0:T(8,128)(2,1)} %collective-permute-done.13.refs_2_, bf16[1152,1152]{1,0:T(8,128)(2,1)} %collective-permute-done.14.refs_3_, ...), custom_call_target="tpu_custom_call" | custom-call | flops 5435817984 | bytes 20054016 | tf_op jit(solution)/shard_map/up/pallas_call | solution.py:322
  316.4 9.0 collective-permute-done.31
  332.7 13.7 %down.2 = (f32[512,1152]{1,0:T(8,128)}, bf16[512,1152]{1,0:T(8,128)(2,1)}) custom-call(bf16[4,512,1152]{2,1,0:T(8,128)(2,1)} %get-tuple-element.1031.refs_0_.refs_1_, bf16[1152,1152]{1,0:T(8,128)(2,1)} %pad_maximum_fusion.2.refs_1_, bf16[1152,1152]{1,0:T(8,128)(2,1)} %collective-permute-done.23.refs_2_, bf16[1152,1152]{1,0:T(8,128)(2,1)} %collective-permute-done.24.refs_3_, ...), custom_call_target="tpu_custom_call" | custom-call | flops 5435817984 | bytes 20054016 | tf_op jit(solution)/shard_map/down/pallas_call | solution.py:396
  350.8 4.6 all-to-all-start.3
  359.7 25.0 %all-to-all-done.3 = bf16[8,2,32,1152]{3,2,1,0:T(8,128)(2,1)S(1)} async-done(((bf16[8,2,32,1152]{3,2,1,0:T(8,128)(2,1)}), bf16[8,2,32,1152]{3,2,1,0:T(8,128)(2,1)S(1)}, u32[]{:S(2)}, u32[]{:S(2)}) %all-to-all-start.3) | async-done | bytes 1179680 | tf_op jit(solution)/shard_map/all_to_all | solution.py:762
  389.4 10.0 qkv.3
  399.5 13.4 %attend.3 = (bf16[4,1,16,32,288]{4,3,2,1,0:T(8,128)(2,1)}, f32[4,2,4,256]{3,2,1,0:T(4,128)}) custom-call(bf16[4,1,16,32,864]{4,3,2,1,0:T(8,128)(2,1)} %bitcast.201), custom_call_target="tpu_custom_call" | custom-call | flops 1073741824 | bytes 4718592 | tf_op jit(solution)/shard_map/attend/pallas_call | solution.py:670
  415.4 12.6 %collective-permute-done.35.refs_2_ = bf16[1152,1152]{1,0:T(8,128)(2,1)} collective-permute-done((bf16[1152,1152]{1,0:T(8,128)(2,1)}, bf16[1152,1152]{1,0:T(8,128)(2,1)}, u32[]{:S(2)}, u32[]{:S(2)}) %collective-permute-start.35) | collective-permute-done | bytes 2654240 | tf_op jit(solution)/shard_map/ppermute | solution.py:37
  428.1 5.2 collective-permute-done.37.refs_4_
  437.7 4.8 all-to-all-start.4
  443.2 15.2 %out.3 = (f32[512,1152]{1,0:T(8,128)}, f32[512,1152]{1,0:T(8,128)}, f32[512,1152]{1,0:T(8,128)}, f32[512,1]{1,0:T(8,128)}, bf16[512,1152]{1,0:T(8,128)(2,1)}) custom-call(bf16[4,512,288]{2,1,0:T(8,128)(2,1)} %bitcast.205, bf16[1152,1152]{1,0:T(8,128)(2,1)} %pad_maximum_fusion.3.refs_1_, bf16[1152,1152]{1,0:T(8,128)(2,1)} %collective-permute-done.25.refs_2_, ...), custom_call_target="tpu_custom_call" | custom-call | flops 1358954496 | bytes 8552448 | tf_op jit(solution)/shard_map/out/pallas_call | solution.py:396
  458.4 13.1 %all-to-all-done.4 = bf16[8,2,32,1152]{3,2,1,0:T(8,128)(2,1)S(1)} async-done(((bf16[8,2,32,1152]{3,2,1,0:T(8,128)(2,1)}), bf16[8,2,32,1152]{3,2,1,0:T(8,128)(2,1)S(1)}, u32[]{:S(2)}, u32[]{:S(2)}) %all-to-all-start.4) | async-done | bytes 1179680 | tf_op jit(solution)/shard_map/all_to_all | solution.py:762
  475.3 14.8 %up.3 = (bf16[4,512,1152]{2,1,0:T(8,128)(2,1)}, bf16[4,512,1152]{2,1,0:T(8,128)(2,1)}) custom-call(bf16[512,1152]{1,0:T(8,128)(2,1)} %get-tuple-element.879.refs_0_, bf16[1152,1152]{1,0:T(8,128)(2,1)} %pad_maximum_fusion.4.refs_1_, bf16[1152,1152]{1,0:T(8,128)(2,1)} %collective-permute-done.33.refs_2_, bf16[1152,1152]{1,0:T(8,128)(2,1)} %collective-permute-done.34.refs_3_, ...), custom_call_target="tpu_custom_call" | custom-call | flops 5435817984 | bytes 20054016 | tf_op jit(solution)/shard_map/up/pallas_call | solution.py:322
  490.1 12.7 %grad_fc2.2 = (bf16[2,1152,1152]{2,1,0:T(8,128)(2,1)}, bf16[2,1152,1152]{2,1,0:T(8,128)(2,1)}, f32[1,1152]{1,0:T(1,128)}, f32[4,1,1152]{2,1,0:T(1,128)}) custom-call(bf16[512,1152]{1,0:T(8,128)(2,1)} %get-tuple-element.880.refs_0_, bf16[4,512,1152]{2,1,0:T(8,128)(2,1)} %get-tuple-element.857.refs_1_.refs_0_), custom_call_target="tpu_custom_call" | custom-call | flops 5435817984 | bytes 15335424 | tf_op jit(solution)/shard_map/grad_fc2/pallas_call | solution.py:539
  503.5 13.9 %down.3 = (f32[512,1152]{1,0:T(8,128)}, bf16[512,1152]{1,0:T(8,128)(2,1)}) custom-call(bf16[4,512,1152]{2,1,0:T(8,128)(2,1)} %get-tuple-element.857.refs_1_.refs_0_, bf16[1152,1152]{1,0:T(8,128)(2,1)} %pad_maximum_fusion.5.refs_1_, bf16[1152,1152]{1,0:T(8,128)(2,1)} %collective-permute-done.35.refs_2_, bf16[1152,1152]{1,0:T(8,128)(2,1)} %collective-permute-done.36.refs_3_, ...), custom_call_target="tpu_custom_call" | custom-call | flops 5435817984 | bytes 20054016 | tf_op jit(solution)/shard_map/down/pallas_call | solution.py:396
  517.5 4.2 fusion.9
  525.4 12.0 %up_back.2.refs_1_.refs_0_ = bf16[4,512,1152]{2,1,0:T(8,128)(2,1)} custom-call(bf16[512,1152]{1,0:T(8,128)(2,1)} %get-tuple-element.880.refs_0_, bf16[1152,1152]{1,0:T(8,128)(2,1)} %pad_maximum_fusion.5.refs_1_, bf16[1152,1152]{1,0:T(8,128)(2,1)} %collective-permute-done.35.refs_2_, bf16[1152,1152]{1,0:T(8,128)(2,1)} %collective-permute-done.36.refs_3_, ...), custom_call_target="tpu_custom_call" | custom-call | flops 5435817984 | bytes 20054016 | tf_op jit(solution)/shard_map/up_back/pallas_call | solution.py:322
  537.5 12.7 %grad_fc1.2 = (bf16[2,1152,1152]{2,1,0:T(8,128)(2,1)}, bf16[2,1152,1152]{2,1,0:T(8,128)(2,1)}, f32[1,1152]{1,0:T(1,128)}, f32[4,1,1152]{2,1,0:T(1,128)}) custom-call(bf16[512,1152]{1,0:T(8,128)(2,1)} %get-tuple-element.879.refs_0_, bf16[4,512,1152]{2,1,0:T(8,128)(2,1)} %up_back.2.refs_1_.refs_0_), custom_call_target="tpu_custom_call" | custom-call | flops 5435817984 | bytes 15335424 | tf_op jit(solution)/shard_map/grad_fc1/pallas_call | solution.py:539
  559.8 17.1 %hidden2_back.2 = (f32[512,1152]{1,0:T(8,128)}, bf16[512,1152]{1,0:T(8,128)(2,1)}, f32[3,1152]{1,0:T(4,128)}) custom-call(bf16[4,512,1152]{2,1,0:T(8,128)(2,1)} %up_back.2.refs_1_.refs_0_, bf16[1152,1152]{1,0:T(8,128)(2,1)} %pad_maximum_fusion.4.refs_1_, bf16[1152,1152]{1,0:T(8,128)(2,1)} %collective-permute-done.33.refs_2_, ...), custom_call_target="tpu_custom_call" | custom-call | flops 5435817984 | bytes 27131904 | tf_op jit(solution)/shard_map/hidden2_back/pallas_call | solution.py:396
  583.9 7.5 out_back.2
  591.5 13.6 %attend_back.2 = bf16[4,1,16,32,864]{4,3,2,1,0:T(8,128)(2,1)} custom-call(bf16[4,1,16,32,864]{4,3,2,1,0:T(8,128)(2,1)} %bitcast.202, bf16[4,1,16,32,288]{4,3,2,1,0:T(8,128)(2,1)} %bitcast.207, bf16[4,1,16,32,288]{4,3,2,1,0:T(8,128)(2,1)} %get-tuple-element.785, f32[4,2,4,256]{3,2,1,0:T(4,128)} %get-tuple-element.952.logs), custom_call_target="tpu_custom_call" | custom-call | flops 2684354560 | bytes 14155776 | tf_op jit(solution)/shard_map/attend_back/pallas_call | solution.py:670
  605.1 15.3 %grad_mixed.2 = (bf16[2,1152,640]{2,1,0:T(8,128)(2,1)}, bf16[2,1152,512]{2,1,0:T(8,128)(2,1)}, bf16[2,1152,640]{2,1,0:T(8,128)(2,1)}, bf16[2,1152,512]{2,1,0:T(8...) custom-call(bf16[512,1152]{1,0:T(8,128)(2,1)} %get-tuple-element.948.refs_0_, ...), custom_call_target="tpu_custom_call" | custom-call | flops 5435817984 | bytes 15335424 | tf_op jit(solution)/shard_map/grad_mixed/pallas_call | solution.py:539
  621.1 20.0 %collective-permute-done.41.refs_2_ = bf16[1,1152,1152]{2,1,0:T(8,128)(2,1)} collective-permute-done((bf16[1,1152,1152]{2,1,0:T(8,128)(2,1)}, bf16[1,1152,1152]{2,1,0:T(8,128)(2,1)}, u32[]{:S(2)}, u32[]{:S(2)}) %collective-permute-start.41) | collective-permute-done | bytes 2654240 | tf_op jit(solution)/shard_map/ppermute | solution.py:37
  653.0 14.7 %hidden_back.2 = (bf16[512,1152]{1,0:T(8,128)(2,1)}, f32[2,1152]{1,0:T(2,128)}) custom-call(bf16[4,512,864]{2,1,0:T(8,128)(2,1)} %bitcast.198, bf16[1152,1152]{1,0:T(8,128)(2,1)} %pad_maximum_fusion.3.refs_1_, bf16[1152,1152]{1,0:T(8,128)(2,1)} %collective-permute-done.25.refs_2_, bf16[1152,1152]{1,0:T(8,128)(2,1)} %collective-permute-done.26.refs_3_, ...), custom_call_target="tpu_custom_call" | custom-call | flops 4076863488 | bytes 20938752 | tf_op jit(solution)/shard_map/hidden_back/pallas_call | solution.py:396
  667.7 4.2 fusion.10
  671.9 8.4 collective-permute-done.45.refs_3_
  692.0 4.6 all-to-all-start.6
  702.3 22.6 %all-to-all-done.6 = bf16[8,2,32,1152]{3,2,1,0:T(8,128)(2,1)} async-done(((bf16[8,2,32,1152]{3,2,1,0:T(8,128)(2,1)}), bf16[8,2,32,1152]{3,2,1,0:T(8,128)(2,1)}, u32[]{:S(2)}, u32[]{:S(2)}) %all-to-all-start.6) | async-done | bytes 1179680 | tf_op jit(solution)/shard_map/all_to_all | solution.py:769
  730.0 12.0 %up_back.3.refs_1_.refs_0_ = bf16[4,512,1152]{2,1,0:T(8,128)(2,1)} custom-call(bf16[512,1152]{1,0:T(8,128)(2,1)} %get-tuple-element.1446.refs_0_, bf16[1152,1152]{1,0:T(8,128)(2,1)} %pad_maximum_fusion.2.refs_1_, bf16[1152,1152]{1,0:T(8,128)(2,1)} %collective-permute-done.23.refs_2_, bf16[1152,1152]{1,0:T(8,128)(2,1)} %collective-permute-done.24.refs_3_, ...), custom_call_target="tpu_custom_call" | custom-call | flops 5435817984 | bytes 20054016 | tf_op jit(solution)/shard_map/up_back/pallas_call | solution.py:322
  745.8 13.4 %grad_fc1.3 = (bf16[2,1152,1152]{2,1,0:T(8,128)(2,1)}, bf16[2,1152,1152]{2,1,0:T(8,128)(2,1)}, f32[1,1152]{1,0:T(1,128)}, f32[4,1,1152]{2,1,0:T(1,128)}) custom-call(bf16[512,1152]{1,0:T(8,128)(2,1)} %get-tuple-element.1026.refs_0_, bf16[4,512,1152]{2,1,0:T(8,128)(2,1)} %up_back.3.refs_1_.refs_0_), custom_call_target="tpu_custom_call" | custom-call | flops 5435817984 | bytes 15335424 | tf_op jit(solution)/shard_map/grad_fc1/pallas_call | solution.py:539
  759.9 12.8 %grad_fc2.3 = (bf16[2,1152,1152]{2,1,0:T(8,128)(2,1)}, bf16[2,1152,1152]{2,1,0:T(8,128)(2,1)}, f32[1,1152]{1,0:T(1,128)}, f32[4,1,1152]{2,1,0:T(1,128)}) custom-call(bf16[512,1152]{1,0:T(8,128)(2,1)} %get-tuple-element.1446.refs_0_, bf16[4,512,1152]{2,1,0:T(8,128)(2,1)} %get-tuple-element.1031.refs_0_.refs_1_), custom_call_target="tpu_custom_call" | custom-call | flops 5435817984 | bytes 15335424 | tf_op jit(solution)/shard_map/grad_fc2/pallas_call | solution.py:539
  788.7 17.5 %hidden2_back.3 = (f32[512,1152]{1,0:T(8,128)}, bf16[512,1152]{1,0:T(8,128)(2,1)}, f32[3,1152]{1,0:T(4,128)}) custom-call(bf16[4,512,1152]{2,1,0:T(8,128)(2,1)} %up_back.3.refs_1_.refs_0_, bf16[1152,1152]{1,0:T(8,128)(2,1)} %pad_maximum_fusion.1.refs_1_, bf16[1152,1152]{1,0:T(8,128)(2,1)} %collective-permute-done.13.refs_2_, ...), custom_call_target="tpu_custom_call" | custom-call | flops 5435817984 | bytes 27131904 | tf_op jit(solution)/shard_map/hidden2_back/pallas_call | solution.py:396
  806.8 7.5 out_back.3
  814.3 13.4 %attend_back.3 = bf16[4,2,256,864]{3,2,1,0:T(8,128)(2,1)} custom-call(bf16[4,2,256,864]{3,2,1,0:T(8,128)(2,1)} %bitcast.200, bf16[4,2,256,288]{3,2,1,0:T(8,128)(2,1)} %bitcast.208, bf16[4,2,256,288]{3,2,1,0:T(8,128)(2,1)} %get-tuple-element.720, f32[4,2,4,256]{3,2,1,0:T(4,128)} %get-tuple-element.1110.logs), custom_call_target="tpu_custom_call" | custom-call | flops 2684354560 | bytes 14155776 | tf_op jit(solution)/shard_map/attend_back/pallas_call | solution.py:670
  844.8 14.9 %grad_mixed.3 = (bf16[2,1152,640]{2,1,0:T(8,128)(2,1)}, bf16[2,1152,512]{2,1,0:T(8,128)(2,1)}, bf16[2,1152,640]{2,1,0:T(8,128)(2,1)}, bf16[2,1152,512]{2,1,0:T(8...) custom-call(bf16[512,1152]{1,0:T(8,128)(2,1)} %get-tuple-element.1127.refs_0_, ...), custom_call_target="tpu_custom_call" | custom-call | flops 5435817984 | bytes 15335424 | tf_op jit(solution)/shard_map/grad_mixed/pallas_call | solution.py:539
  859.7 15.1 %hidden_back.3 = (bf16[512,1152]{1,0:T(8,128)(2,1)}, f32[2,1152]{1,0:T(2,128)}) custom-call(bf16[4,512,864]{2,1,0:T(8,128)(2,1)} %bitcast.196, bf16[1152,1152]{1,0:T(8,128)(2,1)} %pad_maximum_fusion.refs_1_, bf16[1152,1152]{1,0:T(8,128)(2,1)} %collective-permute-done.11.refs_2_, bf16[1152,1152]{1,0:T(8,128)(2,1)} %collective-permute-done.12.refs_3_, ...), custom_call_target="tpu_custom_call" | custom-call | flops 4076863488 | bytes 20938752 | tf_op jit(solution)/shard_map/hidden_back/pallas_call | solution.py:396
  880.4 19.2 %collective-permute-done.57.refs_2_ = bf16[2,576,1152]{2,1,0:T(8,128)(2,1)} collective-permute-done((bf16[2,576,1152]{2,1,0:T(8,128)(2,1)}, bf16[2,576,1152]{2,1,0:T(8,128)(2,1)}, u32[]{:S(2)}, u32[]{:S(2)}) %collective-permute-start.57) | collective-permute-done | bytes 2654240 | tf_op jit(solution)/shard_map/ppermute | solution.py:37
  982.3 4.6 all-to-all-start.8
  999.6 9.0 collective-permute-done.70.refs_4_
  1018.1 16.3 %collective-permute-done.67.refs_2_ = bf16[1,1152,640]{2,1,0:T(8,128)(2,1)S(1)} collective-permute-done((bf16[1,1152,640]{2,1,0:T(8,128)(2,1)}, bf16[1,1152,640]{2,1,0:T(8,128)(2,1)S(1)}, u32[]{:S(2)}, u32[]{:S(2)}) %collective-permute-start.67) | collective-permute-done | bytes 1474592 | tf_op jit(solution)/shard_map/ppermute | solution.py:37
  1044.9 4.0 fusion.11
  1052.4 5.0 collective-permute-done.77.refs_3_
  1062.5 4.6 collective-permute-done.78
  1067.1 7.0 collective-permute-done.79
  1098.9 7.7 collective-permute-done.81
  (543 shorter events, 385.9 us)
Async XLA Ops:
  13.0 45.5 %collective-permute-start = (bf16[144,1152]{1,0:T(8,128)(2,1)S(1)}, bf16[144,1152]{1,0:T(8,128)(2,1)}, u32[]{:S(2)}, u32[]{:S(2)}) collective-permute-start(bf16[144,1152]{1,0:T(8,128)(2,1)S(1)} %pad_maximum_fusion.24), channel_id=1, source_target_pairs={{0,16},{4,20},{8,24},{12,28},{16,0},{20,4},{24,8},{28,12},{1,17},{... | collective-permute-start | bytes 995336 | tf_op jit(solution)/shard_map/ppermute | solution.py:37
  18.7 40.8 %collective-permute-start.1 = (bf16[144,1152]{1,0:T(8,128)(2,1)S(1)}, bf16[144,1152]{1,0:T(8,128)(2,1)}, u32[]{:S(2)}, u32[]{:S(2)}) collective-permute-start(bf16[144,1152]{1,0:T(8,128)(2,1)S(1)} %get-tuple-element.1387), channel_id=1, source_target_pairs={{0,16},{4,20},{8,24},{12,28},{16,0},{20,4},{24,8},{28,12},{1,17},{... | collective-permute-start | bytes 995336 | tf_op jit(solution)/shard_map/ppermute | solution.py:37
  21.0 42.7 %all-to-all-start = ((bf16[4,288,512]{2,1,0:T(8,128)(2,1)}), bf16[4,288,512]{2,1,0:T(8,128)(2,1)}, u32[]{:S(2)}, u32[]{:S(2)}) async-start(bf16[4,288,512]{2,1,0:T(8,128)(2,1)} %param.25), calls=%async_computation | async-start | bytes 2359296 | tf_op jit(solution)/shard_map/all_to_all | solution.py:835
  62.4 27.7 %collective-permute-start.3 = (bf16[288,1152]{1,0:T(8,128)(2,1)}, bf16[288,1152]{1,0:T(8,128)(2,1)}, u32[]{:S(2)}, u32[]{:S(2)}) collective-permute-start(bf16[288,1152]{1,0:T(8,128)(2,1)} %pad_maximum_fusion.16), channel_id=1, source_target_pairs={{0,8},{4,12},{8,0},{12,4},{16,24},{20,28},{24,16},{28,20},{1,9},{5... | collective-permute-start | bytes 1990664 | tf_op jit(solution)/shard_map/ppermute | solution.py:37
  63.8 28.8 %all-to-all-start.1 = ((bf16[4,288,512]{2,1,0:T(8,128)(2,1)}), bf16[4,288,512]{2,1,0:T(8,128)(2,1)}, u32[]{:S(2)}, u32[]{:S(2)}) async-start(bf16[4,288,512]{2,1,0:T(8,128)(2,1)} %param.37), calls=%async_computation.1 | async-start | bytes 2359296 | tf_op jit(solution)/shard_map/all_to_all | solution.py:835
  92.6 32.6 %collective-permute-start.4 = (bf16[576,1152]{1,0:T(8,128)(2,1)S(1)}, bf16[576,1152]{1,0:T(8,128)(2,1)S(1)}, u32[]{:S(2)}, u32[]{:S(2)}) collective-permute-start(bf16[576,1152]{1,0:T(8,128)(2,1)S(1)} %pad_maximum_fusion.7), channel_id=1, source_target_pairs={{0,4},{4,0},{8,12},{12,8},{16,20},{20,16},{24,28},{28,24},{1,5},{5... | collective-permute-start | bytes 3981320 | tf_op jit(solution)/shard_map/ppermute | solution.py:37
  98.1 28.7 %collective-permute-start.5 = (bf16[576,1152]{1,0:T(8,128)(2,1)}, bf16[576,1152]{1,0:T(8,128)(2,1)S(1)}, u32[]{:S(2)}, u32[]{:S(2)}) collective-permute-start(bf16[576,1152]{1,0:T(8,128)(2,1)} %pad_maximum_fusion.8), channel_id=1, source_target_pairs={{0,2},{1,3},{2,0},{3,1},{4,6},{5,7},{6,4},{7,5},{8,10},{9,11},{10,... | collective-permute-start | bytes 3981320 | tf_op jit(solution)/shard_map/ppermute | solution.py:37
  128.6 60.3 %collective-permute-start.11 = (bf16[1152,1152]{1,0:T(8,128)(2,1)}, bf16[1152,1152]{1,0:T(8,128)(2,1)}, u32[]{:S(2)}, u32[]{:S(2)}) collective-permute-start(bf16[1152,1152]{1,0:T(8,128)(2,1)} %pad_maximum_fusion.refs_1_), channel_id=1, source_target_pairs={{0,2},{1,3},{2,0},{3,1},{4,6},{5,7},{6,4},{7,5},{8,10},{9,11},{10,... | collective-permute-start | bytes 7962632 | tf_op jit(solution)/shard_map/ppermute | solution.py:37
  130.3 60.0 %collective-permute-start.13 = (bf16[1152,1152]{1,0:T(8,128)(2,1)}, bf16[1152,1152]{1,0:T(8,128)(2,1)}, u32[]{:S(2)}, u32[]{:S(2)}) collective-permute-start(bf16[1152,1152]{1,0:T(8,128)(2,1)} %pad_maximum_fusion.1.refs_1_), channel_id=1, source_target_pairs={{0,4},{4,0},{8,12},{12,8},{16,20},{20,16},{24,28},{28,24},{1,5},{5... | collective-permute-start | bytes 7962632 | tf_op jit(solution)/shard_map/ppermute | solution.py:37
  133.9 56.3 %collective-permute-start.14 = (bf16[1152,1152]{1,0:T(8,128)(2,1)}, bf16[1152,1152]{1,0:T(8,128)(2,1)}, u32[]{:S(2)}, u32[]{:S(2)}) collective-permute-start(bf16[1152,1152]{1,0:T(8,128)(2,1)} %pad_maximum_fusion.1.refs_1_), channel_id=1, source_target_pairs={{0,1},{1,0},{2,3},{3,2},{4,5},{5,4},{6,7},{7,6},{8,9},{9,8},{10,11... | collective-permute-start | bytes 7962632 | tf_op jit(solution)/shard_map/ppermute | solution.py:37
  134.9 30.6 %collective-permute-start.16 = (bf16[288,1152]{1,0:T(8,128)(2,1)}, bf16[288,1152]{1,0:T(8,128)(2,1)S(1)}, u32[]{:S(2)}, u32[]{:S(2)}) collective-permute-start(bf16[288,1152]{1,0:T(8,128)(2,1)} %pad_maximum_fusion.18), channel_id=1, source_target_pairs={{0,8},{4,12},{8,0},{12,4},{16,24},{20,28},{24,16},{28,20},{1,9},{5... | collective-permute-start | bytes 1990664 | tf_op jit(solution)/shard_map/ppermute | solution.py:37
  195.6 37.1 %collective-permute-start.18 = (bf16[1152,1152]{1,0:T(8,128)(2,1)}, bf16[1152,1152]{1,0:T(8,128)(2,1)}, u32[]{:S(2)}, u32[]{:S(2)}) collective-permute-start(bf16[1152,1152]{1,0:T(8,128)(2,1)} %collective-permute-done.13.refs_2_), channel_id=1, source_target_pairs={{0,1},{1,0},{2,3},{3,2},{4,5},{5,4},{6,7},{7,6},{8,9},{9,8},{10,11... | collective-permute-start | bytes 7962632 | tf_op jit(solution)/shard_map/ppermute | solution.py:37
  195.7 33.4 %collective-permute-start.19 = (bf16[576,1152]{1,0:T(8,128)(2,1)S(1)}, bf16[576,1152]{1,0:T(8,128)(2,1)S(1)}, u32[]{:S(2)}, u32[]{:S(2)}) collective-permute-start(bf16[576,1152]{1,0:T(8,128)(2,1)S(1)} %pad_maximum_fusion.9), channel_id=1, source_target_pairs={{0,4},{4,0},{8,12},{12,8},{16,20},{20,16},{24,28},{28,24},{1,5},{5... | collective-permute-start | bytes 3981320 | tf_op jit(solution)/shard_map/ppermute | solution.py:37
  197.7 33.2 %collective-permute-start.20 = (bf16[576,1152]{1,0:T(8,128)(2,1)S(1)}, bf16[576,1152]{1,0:T(8,128)(2,1)S(1)}, u32[]{:S(2)}, u32[]{:S(2)}) collective-permute-start(bf16[576,1152]{1,0:T(8,128)(2,1)S(1)} %pad_maximum_fusion.10), channel_id=1, source_target_pairs={{0,2},{1,3},{2,0},{3,1},{4,6},{5,7},{6,4},{7,5},{8,10},{9,11},{10,... | collective-permute-start | bytes 3981320 | tf_op jit(solution)/shard_map/ppermute | solution.py:37
  198.1 30.1 %collective-permute-start.22 = (bf16[144,1152]{1,0:T(8,128)(2,1)S(1)}, bf16[144,1152]{1,0:T(8,128)(2,1)S(1)}, u32[]{:S(2)}, u32[]{:S(2)}) collective-permute-start(bf16[144,1152]{1,0:T(8,128)(2,1)S(1)} %copy-done.24), channel_id=1, source_target_pairs={{0,16},{4,20},{8,24},{12,28},{16,0},{20,4},{24,8},{28,12},{1,17},{... | collective-permute-start | bytes 995336 | tf_op jit(solution)/shard_map/ppermute | solution.py:37
  232.6 60.3 %collective-permute-start.23 = (bf16[1152,1152]{1,0:T(8,128)(2,1)}, bf16[1152,1152]{1,0:T(8,128)(2,1)}, u32[]{:S(2)}, u32[]{:S(2)}) collective-permute-start(bf16[1152,1152]{1,0:T(8,128)(2,1)} %pad_maximum_fusion.2.refs_1_), channel_id=1, source_target_pairs={{0,2},{1,3},{2,0},{3,1},{4,6},{5,7},{6,4},{7,5},{8,10},{9,11},{10,... | collective-permute-start | bytes 7962632 | tf_op jit(solution)/shard_map/ppermute | solution.py:37
  233.1 60.0 %collective-permute-start.25 = (bf16[1152,1152]{1,0:T(8,128)(2,1)}, bf16[1152,1152]{1,0:T(8,128)(2,1)}, u32[]{:S(2)}, u32[]{:S(2)}) collective-permute-start(bf16[1152,1152]{1,0:T(8,128)(2,1)} %pad_maximum_fusion.3.refs_1_), channel_id=1, source_target_pairs={{0,4},{4,0},{8,12},{12,8},{16,20},{20,16},{24,28},{28,24},{1,5},{5... | collective-permute-start | bytes 7962632 | tf_op jit(solution)/shard_map/ppermute | solution.py:37
  237.9 55.1 %collective-permute-start.26 = (bf16[1152,1152]{1,0:T(8,128)(2,1)}, bf16[1152,1152]{1,0:T(8,128)(2,1)}, u32[]{:S(2)}, u32[]{:S(2)}) collective-permute-start(bf16[1152,1152]{1,0:T(8,128)(2,1)} %pad_maximum_fusion.3.refs_1_), channel_id=1, source_target_pairs={{0,1},{1,0},{2,3},{3,2},{4,5},{5,4},{6,7},{7,6},{8,9},{9,8},{10,11... | collective-permute-start | bytes 7962632 | tf_op jit(solution)/shard_map/ppermute | solution.py:37
  240.7 41.9 %collective-permute-start.27 = (bf16[288,1152]{1,0:T(8,128)(2,1)S(1)}, bf16[288,1152]{1,0:T(8,128)(2,1)}, u32[]{:S(2)}, u32[]{:S(2)}) collective-permute-start(bf16[288,1152]{1,0:T(8,128)(2,1)S(1)} %pad_maximum_fusion.19), channel_id=1, source_target_pairs={{0,8},{4,12},{8,0},{12,4},{16,24},{20,28},{24,16},{28,20},{1,9},{5... | collective-permute-start | bytes 1990664 | tf_op jit(solution)/shard_map/ppermute | solution.py:37
  242.4 41.5 %collective-permute-start.28 = (bf16[288,1152]{1,0:T(8,128)(2,1)}, bf16[288,1152]{1,0:T(8,128)(2,1)}, u32[]{:S(2)}, u32[]{:S(2)}) collective-permute-start(bf16[288,1152]{1,0:T(8,128)(2,1)} %pad_maximum_fusion.20), channel_id=1, source_target_pairs={{0,8},{4,12},{8,0},{12,4},{16,24},{20,28},{24,16},{28,20},{1,9},{5... | collective-permute-start | bytes 1990664 | tf_op jit(solution)/shard_map/ppermute | solution.py:37
  293.8 31.6 %collective-permute-start.31 = (bf16[576,1152]{1,0:T(8,128)(2,1)S(1)}, bf16[576,1152]{1,0:T(8,128)(2,1)S(1)}, u32[]{:S(2)}, u32[]{:S(2)}) collective-permute-start(bf16[576,1152]{1,0:T(8,128)(2,1)S(1)} %pad_maximum_fusion.11), channel_id=1, source_target_pairs={{0,4},{4,0},{8,12},{12,8},{16,20},{20,16},{24,28},{28,24},{1,5},{5... | collective-permute-start | bytes 3981320 | tf_op jit(solution)/shard_map/ppermute | solution.py:37
  298.4 33.6 %collective-permute-start.30 = (bf16[1152,1152]{1,0:T(8,128)(2,1)}, bf16[1152,1152]{1,0:T(8,128)(2,1)}, u32[]{:S(2)}, u32[]{:S(2)}) collective-permute-start(bf16[1152,1152]{1,0:T(8,128)(2,1)} %collective-permute-done.25.refs_2_), channel_id=1, source_target_pairs={{0,1},{1,0},{2,3},{3,2},{4,5},{5,4},{6,7},{7,6},{8,9},{9,8},{10,11... | collective-permute-start | bytes 7962632 | tf_op jit(solution)/shard_map/ppermute | solution.py:37
  298.6 31.7 %collective-permute-start.32 = (bf16[576,1152]{1,0:T(8,128)(2,1)}, bf16[576,1152]{1,0:T(8,128)(2,1)S(1)}, u32[]{:S(2)}, u32[]{:S(2)}) collective-permute-start(bf16[576,1152]{1,0:T(8,128)(2,1)} %pad_maximum_fusion.12), channel_id=1, source_target_pairs={{0,2},{1,3},{2,0},{3,1},{4,6},{5,7},{6,4},{7,5},{8,10},{9,11},{10,... | collective-permute-start | bytes 3981320 | tf_op jit(solution)/shard_map/ppermute | solution.py:37
  332.0 27.1 %collective-permute-start.34 = (bf16[1152,1152]{1,0:T(8,128)(2,1)}, bf16[1152,1152]{1,0:T(8,128)(2,1)}, u32[]{:S(2)}, u32[]{:S(2)}) collective-permute-start(bf16[1152,1152]{1,0:T(8,128)(2,1)} %pad_maximum_fusion.4.refs_1_), channel_id=1, source_target_pairs={{0,1},{1,0},{2,3},{3,2},{4,5},{5,4},{6,7},{7,6},{8,9},{9,8},{10,11... | collective-permute-start | bytes 7962632 | tf_op jit(solution)/shard_map/ppermute | solution.py:37
  350.8 33.9 %all-to-all-start.3 = ((bf16[8,2,32,1152]{3,2,1,0:T(8,128)(2,1)}), bf16[8,2,32,1152]{3,2,1,0:T(8,128)(2,1)S(1)}, u32[]{:S(2)}, u32[]{:S(2)}) async-start(bf16[8,2,32,1152]{3,2,1,0:T(8,128)(2,1)} %bitcast.187), calls=%async_computation.3 | async-start | bytes 2359296 | tf_op jit(solution)/shard_map/all_to_all | solution.py:762
  355.4 60.0 %collective-permute-start.33 = (bf16[1152,1152]{1,0:T(8,128)(2,1)}, bf16[1152,1152]{1,0:T(8,128)(2,1)}, u32[]{:S(2)}, u32[]{:S(2)}) collective-permute-start(bf16[1152,1152]{1,0:T(8,128)(2,1)} %pad_maximum_fusion.4.refs_1_), channel_id=1, source_target_pairs={{0,2},{1,3},{2,0},{3,1},{4,6},{5,7},{6,4},{7,5},{8,10},{9,11},{10,... | collective-permute-start | bytes 7962632 | tf_op jit(solution)/shard_map/ppermute | solution.py:37
  357.0 71.0 %collective-permute-start.35 = (bf16[1152,1152]{1,0:T(8,128)(2,1)}, bf16[1152,1152]{1,0:T(8,128)(2,1)}, u32[]{:S(2)}, u32[]{:S(2)}) collective-permute-start(bf16[1152,1152]{1,0:T(8,128)(2,1)} %pad_maximum_fusion.5.refs_1_), channel_id=1, source_target_pairs={{0,4},{4,0},{8,12},{12,8},{16,20},{20,16},{24,28},{28,24},{1,5},{5... | collective-permute-start | bytes 7962632 | tf_op jit(solution)/shard_map/ppermute | solution.py:37
  359.1 69.0 %collective-permute-start.36 = (bf16[1152,1152]{1,0:T(8,128)(2,1)}, bf16[1152,1152]{1,0:T(8,128)(2,1)}, u32[]{:S(2)}, u32[]{:S(2)}) collective-permute-start(bf16[1152,1152]{1,0:T(8,128)(2,1)} %pad_maximum_fusion.5.refs_1_), channel_id=1, source_target_pairs={{0,1},{1,0},{2,3},{3,2},{4,5},{5,4},{6,7},{7,6},{8,9},{9,8},{10,11... | collective-permute-start | bytes 7962632 | tf_op jit(solution)/shard_map/ppermute | solution.py:37
  434.7 40.5 %collective-permute-start.38 = (bf16[1152,1152]{1,0:T(8,128)(2,1)}, bf16[1152,1152]{1,0:T(8,128)(2,1)}, u32[]{:S(2)}, u32[]{:S(2)}) collective-permute-start(bf16[1152,1152]{1,0:T(8,128)(2,1)} %collective-permute-done.35.refs_2_), channel_id=1, source_target_pairs={{0,1},{1,0},{2,3},{3,2},{4,5},{5,4},{6,7},{7,6},{8,9},{9,8},{10,11... | collective-permute-start | bytes 7962632 | tf_op jit(solution)/shard_map/ppermute | solution.py:37
  437.7 33.8 %all-to-all-start.4 = ((bf16[8,2,32,1152]{3,2,1,0:T(8,128)(2,1)}), bf16[8,2,32,1152]{3,2,1,0:T(8,128)(2,1)S(1)}, u32[]{:S(2)}, u32[]{:S(2)}) async-start(bf16[8,2,32,1152]{3,2,1,0:T(8,128)(2,1)} %copy.116), calls=%async_computation.4 | async-start | bytes 2359296 | tf_op jit(solution)/shard_map/all_to_all | solution.py:762
  502.8 53.1 %collective-permute-start.39 = (bf16[2,1152,1152]{2,1,0:T(8,128)(2,1)}, bf16[2,1152,1152]{2,1,0:T(8,128)(2,1)}, u32[]{:S(2)}, u32[]{:S(2)}) collective-permute-start(bf16[2,1152,1152]{2,1,0:T(8,128)(2,1)} %get-tuple-element.885), channel_id=1, source_target_pairs={{0,1},{1,0},{2,3},{3,2},{4,5},{5,4},{6,7},{7,6},{8,9},{9,8},{10,11... | collective-permute-start | bytes 15925256 | tf_op jit(solution)/shard_map/ppermute | solution.py:37
  521.7 33.0 %all-to-all-start.5 = ((bf16[8,2,32,1152]{3,2,1,0:T(8,128)(2,1)}), bf16[8,2,32,1152]{3,2,1,0:T(8,128)(2,1)S(1)}, u32[]{:S(2)}, u32[]{:S(2)}) async-start(bf16[8,2,32,1152]{3,2,1,0:T(8,128)(2,1)} %bitcast.217), calls=%async_computation.5 | async-start | bytes 2359296 | tf_op jit(solution)/shard_map/all_to_all | solution.py:769
  580.8 60.3 %collective-permute-start.41 = (bf16[1,1152,1152]{2,1,0:T(8,128)(2,1)}, bf16[1,1152,1152]{2,1,0:T(8,128)(2,1)}, u32[]{:S(2)}, u32[]{:S(2)}) collective-permute-start(bf16[1,1152,1152]{2,1,0:T(8,128)(2,1)} %sum_rows.33), channel_id=1, source_target_pairs={{0,2},{1,3},{2,0},{3,1},{4,6},{5,7},{6,4},{7,5},{8,10},{9,11},{10,... | collective-permute-start | bytes 7962632 | tf_op jit(solution)/shard_map/ppermute | solution.py:37
  582.5 62.3 %collective-permute-start.42 = (bf16[2,576,1152]{2,1,0:T(8,128)(2,1)}, bf16[2,576,1152]{2,1,0:T(8,128)(2,1)}, u32[]{:S(2)}, u32[]{:S(2)}) collective-permute-start(bf16[2,576,1152]{2,1,0:T(8,128)(2,1)} %sum_rows.32), channel_id=1, source_target_pairs={{0,4},{4,0},{8,12},{12,8},{16,20},{20,16},{24,28},{28,24},{1,5},{5... | collective-permute-start | bytes 7962632 | tf_op jit(solution)/shard_map/ppermute | solution.py:37
  648.4 40.7 %collective-permute-start.43 = (bf16[2,1152,640]{2,1,0:T(8,128)(2,1)}, bf16[2,1152,640]{2,1,0:T(8,128)(2,1)}, u32[]{:S(2)}, u32[]{:S(2)}) collective-permute-start(bf16[2,1152,640]{2,1,0:T(8,128)(2,1)} %get-tuple-element.988), channel_id=1, source_target_pairs={{0,1},{1,0},{2,3},{3,2},{4,5},{5,4},{6,7},{7,6},{8,9},{9,8},{10,11... | collective-permute-start | bytes 8847368 | tf_op jit(solution)/shard_map/ppermute | solution.py:37
  648.4 38.0 %collective-permute-start.44 = (bf16[2,1152,512]{2,1,0:T(8,128)(2,1)}, bf16[2,1152,512]{2,1,0:T(8,128)(2,1)}, u32[]{:S(2)}, u32[]{:S(2)}) collective-permute-start(bf16[2,1152,512]{2,1,0:T(8,128)(2,1)} %get-tuple-element.990), channel_id=1, source_target_pairs={{0,1},{1,0},{2,3},{3,2},{4,5},{5,4},{6,7},{7,6},{8,9},{9,8},{10,11... | collective-permute-start | bytes 7077896 | tf_op jit(solution)/shard_map/ppermute | solution.py:37
  649.0 31.4 %collective-permute-start.45 = (bf16[1,576,1152]{2,1,0:T(8,128)(2,1)}, bf16[1,576,1152]{2,1,0:T(8,128)(2,1)}, u32[]{:S(2)}, u32[]{:S(2)}) collective-permute-start(bf16[1,576,1152]{2,1,0:T(8,128)(2,1)} %sum_rows.34), channel_id=1, source_target_pairs={{0,4},{4,0},{8,12},{12,8},{16,20},{20,16},{24,28},{28,24},{1,5},{5... | collective-permute-start | bytes 3981320 | tf_op jit(solution)/shard_map/ppermute | solution.py:37
  650.4 32.4 %collective-permute-start.46 = (bf16[1,576,1152]{2,1,0:T(8,128)(2,1)}, bf16[1,576,1152]{2,1,0:T(8,128)(2,1)S(1)}, u32[]{:S(2)}, u32[]{:S(2)}) collective-permute-start(bf16[1,576,1152]{2,1,0:T(8,128)(2,1)} %sum_rows.35), channel_id=1, source_target_pairs={{0,2},{1,3},{2,0},{3,1},{4,6},{5,7},{6,4},{7,5},{8,10},{9,11},{10,... | collective-permute-start | bytes 3981320 | tf_op jit(solution)/shard_map/ppermute | solution.py:37
  692.0 32.9 %all-to-all-start.6 = ((bf16[8,2,32,1152]{3,2,1,0:T(8,128)(2,1)}), bf16[8,2,32,1152]{3,2,1,0:T(8,128)(2,1)}, u32[]{:S(2)}, u32[]{:S(2)}) async-start(bf16[8,2,32,1152]{3,2,1,0:T(8,128)(2,1)} %bitcast.61), calls=%async_computation.6 | async-start | bytes 2359296 | tf_op jit(solution)/shard_map/all_to_all | solution.py:769
  696.5 49.3 %collective-permute-start.47 = (bf16[1,1152,640]{2,1,0:T(8,128)(2,1)}, bf16[1,1152,640]{2,1,0:T(8,128)(2,1)S(1)}, u32[]{:S(2)}, u32[]{:S(2)}) collective-permute-start(bf16[1,1152,640]{2,1,0:T(8,128)(2,1)} %sum_rows.36), channel_id=1, source_target_pairs={{0,2},{1,3},{2,0},{3,1},{4,6},{5,7},{6,4},{7,5},{8,10},{9,11},{10,... | collective-permute-start | bytes 4423688 | tf_op jit(solution)/shard_map/ppermute | solution.py:37
  698.2 47.6 %collective-permute-start.48 = (bf16[2,576,512]{2,1,0:T(8,128)(2,1)}, bf16[2,576,512]{2,1,0:T(8,128)(2,1)}, u32[]{:S(2)}, u32[]{:S(2)}) collective-permute-start(bf16[2,576,512]{2,1,0:T(8,128)(2,1)} %sum_rows.37), channel_id=1, source_target_pairs={{0,4},{4,0},{8,12},{12,8},{16,20},{20,16},{24,28},{28,24},{1,5},{5... | collective-permute-start | bytes 3538952 | tf_op jit(solution)/shard_map/ppermute | solution.py:37
  700.2 45.6 %collective-permute-start.49 = (bf16[1,288,1152]{2,1,0:T(8,128)(2,1)}, bf16[1,288,1152]{2,1,0:T(8,128)(2,1)}, u32[]{:S(2)}, u32[]{:S(2)}) collective-permute-start(bf16[1,288,1152]{2,1,0:T(8,128)(2,1)} %sum_rows.38), channel_id=1, source_target_pairs={{0,8},{4,12},{8,0},{12,4},{16,24},{20,28},{24,16},{28,20},{1,9},{5... | collective-permute-start | bytes 1990664 | tf_op jit(solution)/shard_map/ppermute | solution.py:37
  701.7 44.1 %collective-permute-start.50 = (bf16[1,288,1152]{2,1,0:T(8,128)(2,1)}, bf16[1,288,1152]{2,1,0:T(8,128)(2,1)S(1)}, u32[]{:S(2)}, u32[]{:S(2)}) collective-permute-start(bf16[1,288,1152]{2,1,0:T(8,128)(2,1)} %sum_rows.39), channel_id=1, source_target_pairs={{0,8},{4,12},{8,0},{12,4},{16,24},{20,28},{24,16},{28,20},{1,9},{5... | collective-permute-start | bytes 1990664 | tf_op jit(solution)/shard_map/ppermute | solution.py:37
  782.7 50.2 %collective-permute-start.51 = (bf16[2,1152,1152]{2,1,0:T(8,128)(2,1)}, bf16[2,1152,1152]{2,1,0:T(8,128)(2,1)}, u32[]{:S(2)}, u32[]{:S(2)}) collective-permute-start(bf16[2,1152,1152]{2,1,0:T(8,128)(2,1)} %get-tuple-element.1077), channel_id=1, source_target_pairs={{0,1},{1,0},{2,3},{3,2},{4,5},{5,4},{6,7},{7,6},{8,9},{9,8},{10,11... | collective-permute-start | bytes 15925256 | tf_op jit(solution)/shard_map/ppermute | solution.py:37
  782.7 54.1 %collective-permute-start.52 = (bf16[2,1152,1152]{2,1,0:T(8,128)(2,1)}, bf16[2,1152,1152]{2,1,0:T(8,128)(2,1)}, u32[]{:S(2)}, u32[]{:S(2)}) collective-permute-start(bf16[2,1152,1152]{2,1,0:T(8,128)(2,1)} %get-tuple-element.1079), channel_id=1, source_target_pairs={{0,1},{1,0},{2,3},{3,2},{4,5},{5,4},{6,7},{7,6},{8,9},{9,8},{10,11... | collective-permute-start | bytes 15925256 | tf_op jit(solution)/shard_map/ppermute | solution.py:37
  784.8 56.0 %collective-permute-start.55 = (bf16[1,144,1152]{2,1,0:T(8,128)(2,1)}, bf16[1,144,1152]{2,1,0:T(8,128)(2,1)}, u32[]{:S(2)}, u32[]{:S(2)}) collective-permute-start(bf16[1,144,1152]{2,1,0:T(8,128)(2,1)} %sum_rows.42), channel_id=1, source_target_pairs={{0,16},{4,20},{8,24},{12,28},{16,0},{20,4},{24,8},{28,12},{1,17},{... | collective-permute-start | bytes 995336 | tf_op jit(solution)/shard_map/ppermute | solution.py:37
  787.2 42.6 %collective-permute-start.53 = (bf16[1,576,640]{2,1,0:T(8,128)(2,1)S(1)}, bf16[1,576,640]{2,1,0:T(8,128)(2,1)S(1)}, u32[]{:S(2)}, u32[]{:S(2)}) collective-permute-start(bf16[1,576,640]{2,1,0:T(8,128)(2,1)S(1)} %copy-done.32), channel_id=1, source_target_pairs={{0,4},{4,0},{8,12},{12,8},{16,20},{20,16},{24,28},{28,24},{1,5},{5... | collective-permute-start | bytes 2211848 | tf_op jit(solution)/shard_map/ppermute | solution.py:37
  806.2 34.6 %collective-permute-start.56 = (bf16[1,144,1152]{2,1,0:T(8,128)(2,1)}, bf16[1,144,1152]{2,1,0:T(8,128)(2,1)}, u32[]{:S(2)}, u32[]{:S(2)}) collective-permute-start(bf16[1,144,1152]{2,1,0:T(8,128)(2,1)} %sum_rows.43), channel_id=1, source_target_pairs={{0,16},{4,20},{8,24},{12,28},{16,0},{20,4},{24,8},{28,12},{1,17},{... | collective-permute-start | bytes 995336 | tf_op jit(solution)/shard_map/ppermute | solution.py:37
  840.8 58.7 %collective-permute-start.57 = (bf16[2,576,1152]{2,1,0:T(8,128)(2,1)}, bf16[2,576,1152]{2,1,0:T(8,128)(2,1)}, u32[]{:S(2)}, u32[]{:S(2)}) collective-permute-start(bf16[2,576,1152]{2,1,0:T(8,128)(2,1)} %sum_rows.44), channel_id=1, source_target_pairs={{0,4},{4,0},{8,12},{12,8},{16,20},{20,16},{24,28},{28,24},{1,5},{5... | collective-permute-start | bytes 7962632 | tf_op jit(solution)/shard_map/ppermute | solution.py:37
  841.5 61.8 %collective-permute-start.58 = (bf16[1,1152,1152]{2,1,0:T(8,128)(2,1)}, bf16[1,1152,1152]{2,1,0:T(8,128)(2,1)}, u32[]{:S(2)}, u32[]{:S(2)}) collective-permute-start(bf16[1,1152,1152]{2,1,0:T(8,128)(2,1)} %sum_rows.45), channel_id=1, source_target_pairs={{0,2},{1,3},{2,0},{3,1},{4,6},{5,7},{6,4},{7,5},{8,10},{9,11},{10,... | collective-permute-start | bytes 7962632 | tf_op jit(solution)/shard_map/ppermute | solution.py:37
  842.7 32.1 %collective-permute-start.60 = (bf16[1,288,512]{2,1,0:T(8,128)(2,1)S(1)}, bf16[1,288,512]{2,1,0:T(8,128)(2,1)S(1)}, u32[]{:S(2)}, u32[]{:S(2)}) collective-permute-start(bf16[1,288,512]{2,1,0:T(8,128)(2,1)S(1)} %copy-done.39), channel_id=1, source_target_pairs={{0,8},{4,12},{8,0},{12,4},{16,24},{20,28},{24,16},{28,20},{1,9},{5... | collective-permute-start | bytes 884744 | tf_op jit(solution)/shard_map/ppermute | solution.py:37
  843.1 34.5 %collective-permute-start.59 = (bf16[1,288,640]{2,1,0:T(8,128)(2,1)S(1)}, bf16[1,288,640]{2,1,0:T(8,128)(2,1)S(1)}, u32[]{:S(2)}, u32[]{:S(2)}) collective-permute-start(bf16[1,288,640]{2,1,0:T(8,128)(2,1)S(1)} %copy-done.37), channel_id=1, source_target_pairs={{0,8},{4,12},{8,0},{12,4},{16,24},{20,28},{24,16},{28,20},{1,9},{5... | collective-permute-start | bytes 1105928 | tf_op jit(solution)/shard_map/ppermute | solution.py:37
  911.3 52.6 %collective-permute-start.66 = (bf16[1,144,512]{2,1,0:T(8,128)(2,1)}, bf16[1,144,512]{2,1,0:T(8,128)(2,1)}, u32[]{:S(2)}, u32[]{:S(2)}) collective-permute-start(bf16[1,144,512]{2,1,0:T(8,128)(2,1)} %sum_rows.51), channel_id=1, source_target_pairs={{0,16},{4,20},{8,24},{12,28},{16,0},{20,4},{24,8},{28,12},{1,17},{... | collective-permute-start | bytes 442376 | tf_op jit(solution)/shard_map/ppermute | solution.py:37
  913.7 50.2 %collective-permute-start.65 = (bf16[1,144,640]{2,1,0:T(8,128)(2,1)}, bf16[1,144,640]{2,1,0:T(8,128)(2,1)}, u32[]{:S(2)}, u32[]{:S(2)}) collective-permute-start(bf16[1,144,640]{2,1,0:T(8,128)(2,1)} %sum_rows.50), channel_id=1, source_target_pairs={{0,16},{4,20},{8,24},{12,28},{16,0},{20,4},{24,8},{28,12},{1,17},{... | collective-permute-start | bytes 552968 | tf_op jit(solution)/shard_map/ppermute | solution.py:37
  914.2 38.0 %collective-permute-start.63 = (bf16[1,576,1152]{2,1,0:T(8,128)(2,1)}, bf16[1,576,1152]{2,1,0:T(8,128)(2,1)}, u32[]{:S(2)}, u32[]{:S(2)}) collective-permute-start(bf16[1,576,1152]{2,1,0:T(8,128)(2,1)} %sum_rows.48), channel_id=1, source_target_pairs={{0,2},{1,3},{2,0},{3,1},{4,6},{5,7},{6,4},{7,5},{8,10},{9,11},{10,... | collective-permute-start | bytes 3981320 | tf_op jit(solution)/shard_map/ppermute | solution.py:37
  914.6 40.2 %collective-permute-start.64 = (bf16[1,576,1152]{2,1,0:T(8,128)(2,1)}, bf16[1,576,1152]{2,1,0:T(8,128)(2,1)S(1)}, u32[]{:S(2)}, u32[]{:S(2)}) collective-permute-start(bf16[1,576,1152]{2,1,0:T(8,128)(2,1)} %sum_rows.49), channel_id=1, source_target_pairs={{0,4},{4,0},{8,12},{12,8},{16,20},{20,16},{24,28},{28,24},{1,5},{5... | collective-permute-start | bytes 3981320 | tf_op jit(solution)/shard_map/ppermute | solution.py:37
  915.2 43.2 %collective-permute-start.62 = (bf16[2,1152,512]{2,1,0:T(8,128)(2,1)}, bf16[2,1152,512]{2,1,0:T(8,128)(2,1)}, u32[]{:S(2)}, u32[]{:S(2)}) collective-permute-start(bf16[2,1152,512]{2,1,0:T(8,128)(2,1)} %get-tuple-element.1176), channel_id=1, source_target_pairs={{0,1},{1,0},{2,3},{3,2},{4,5},{5,4},{6,7},{7,6},{8,9},{9,8},{10,11... | collective-permute-start | bytes 7077896 | tf_op jit(solution)/shard_map/ppermute | solution.py:37
  978.9 29.7 %collective-permute-start.70 = (bf16[1,288,1152]{2,1,0:T(8,128)(2,1)}, bf16[1,288,1152]{2,1,0:T(8,128)(2,1)S(1)}, u32[]{:S(2)}, u32[]{:S(2)}) collective-permute-start(bf16[1,288,1152]{2,1,0:T(8,128)(2,1)} %sum_rows.55), channel_id=1, source_target_pairs={{0,8},{4,12},{8,0},{12,4},{16,24},{20,28},{24,16},{28,20},{1,9},{5... | collective-permute-start | bytes 1990664 | tf_op jit(solution)/shard_map/ppermute | solution.py:37
  982.3 55.9 %all-to-all-start.8 = ((bf16[4,288,512]{2,1,0:T(8,128)(2,1)}), bf16[4,288,512]{2,1,0:T(8,128)(2,1)}, u32[]{:S(2)}, u32[]{:S(2)}) async-start(bf16[4,288,512]{2,1,0:T(8,128)(2,1)} %bitcast.210), calls=%async_computation.8 | async-start | bytes 2359296 | tf_op jit(solution)/shard_map/all_to_all | solution.py:841
  986.9 28.7 %collective-permute-start.68 = (bf16[2,576,512]{2,1,0:T(8,128)(2,1)}, bf16[2,576,512]{2,1,0:T(8,128)(2,1)}, u32[]{:S(2)}, u32[]{:S(2)}) collective-permute-start(bf16[2,576,512]{2,1,0:T(8,128)(2,1)} %sum_rows.53), channel_id=1, source_target_pairs={{0,4},{4,0},{8,12},{12,8},{16,20},{20,16},{24,28},{28,24},{1,5},{5... | collective-permute-start | bytes 3538952 | tf_op jit(solution)/shard_map/ppermute | solution.py:37
  987.3 47.1 %collective-permute-start.67 = (bf16[1,1152,640]{2,1,0:T(8,128)(2,1)}, bf16[1,1152,640]{2,1,0:T(8,128)(2,1)S(1)}, u32[]{:S(2)}, u32[]{:S(2)}) collective-permute-start(bf16[1,1152,640]{2,1,0:T(8,128)(2,1)} %sum_rows.52), channel_id=1, source_target_pairs={{0,2},{1,3},{2,0},{3,1},{4,6},{5,7},{6,4},{7,5},{8,10},{9,11},{10,... | collective-permute-start | bytes 4423688 | tf_op jit(solution)/shard_map/ppermute | solution.py:37
  991.6 47.5 %collective-permute-start.74 = (f32[4,1,144]{2,0,1:T(4,128)S(1)}, f32[4,1,144]{2,0,1:T(4,128)}, u32[]{:S(2)}, u32[]{:S(2)}) collective-permute-start(f32[4,1,144]{2,0,1:T(4,128)S(1)} %convolution_bitcast_fusion.1), channel_id=1, source_target_pairs={{0,2},{1,3},{2,0},{3,1},{4,6},{5,7},{6,4},{7,5},{8,10},{9,11},{10,... | collective-permute-start | bytes 6920 | tf_op jit(solution)/shard_map/ppermute | solution.py:37
  1043.1 31.0 %collective-permute-start.79 = (bf16[1,144,1152]{2,1,0:T(8,128)(2,1)}, bf16[1,144,1152]{2,1,0:T(8,128)(2,1)}, u32[]{:S(2)}, u32[]{:S(2)}) collective-permute-start(bf16[1,144,1152]{2,1,0:T(8,128)(2,1)} %sum_rows.59), channel_id=1, source_target_pairs={{0,16},{4,20},{8,24},{12,28},{16,0},{20,4},{24,8},{28,12},{1,17},{... | collective-permute-start | bytes 995336 | tf_op jit(solution)/shard_map/ppermute | solution.py:37
  1048.9 40.5 %all-to-all-start.9 = ((bf16[4,288,512]{2,1,0:T(8,128)(2,1)}), bf16[4,288,512]{2,1,0:T(8,128)(2,1)S(1)}, u32[]{:S(2)}, u32[]{:S(2)}) async-start(bf16[4,288,512]{2,1,0:T(8,128)(2,1)} %bitcast.214), calls=%async_computation.9 | async-start | bytes 2359296 | tf_op jit(solution)/shard_map/all_to_all | solution.py:841
  (92 other events, 2407.9 us)

commit v4 on v3

--- a/solution.py
+++ b/solution.py
@@ -754,15 +754,9 @@
     def stream_rel(value):
         return dot_nn(value, exchange) if relative else value.astype(f32)
 
-    def to_positions(value):
-        return stream_rel(send_positions(stream_plain(value.astype(bf16))))
-
     def send_positions(value):
         shaped = value.reshape(frames_dev, rows, pos_block, span).swapaxes(0, 1)
         return lax.all_to_all(shaped, "row", 0, 0).reshape(tokens, span)
-
-    def to_frames(value):
-        return send_frames(stream_plain(value.astype(bf16)))
 
     def send_frames(value):
         shaped = value.reshape(rows, frames_dev, pos_block, span)
@@ -982,23 +976,23 @@
         mod_grad_time, biases_time = modulate_sums(small_time[0]), small_time[1]
         onehot = (jnp.arange(lat_count) == lat_here).astype(f32)
         mod_grads = jnp.stack([onehot[:, None, None] * mod_grad_space, mod_grad_time], 1)
-        mod_grads = vector_plain(mod_grads).reshape(lat_count, 2, 6, parts, width)
-        mod_grads = jnp.moveaxis(mod_grads, -2, 0).reshape(parts, -1)
-
-        def by_part(value):
-            return jnp.take(value, part_ids, axis=0)
-
-        def by_stream(value):
-            return vector_plain(value).reshape(parts, width)
-
-        pieces = [mod_grads]
-        for space, time in zip(biases_space, biases_time):
-            for value in (space, time):
-                pieces.append(by_part(value) if value.shape[0] == parts else by_stream(value))
-        counts = np.cumsum([0] + [piece.shape[1] for piece in pieces])
+        row_sums = [pair[place] for place in (2, 4) for pair in (biases_space, biases_time)]
+        streams = vector_plain(jnp.concatenate([mod_grads.reshape(-1, span)] + row_sums, 0))
+        streams = jnp.moveaxis(streams.reshape(-1, parts, width), 1, 0)
+        ordered = [pair[place] for place in (0, 1, 3) for pair in (biases_space, biases_time)]
+        ordered = jnp.take(jnp.concatenate(ordered, 1), part_ids, axis=0)
+        mods_count = lat_count * 12
+        pieces = [
+            streams[:, :mods_count].reshape(parts, -1),
+            ordered[:, : 4 * width],
+            streams[:, mods_count : mods_count + 2].reshape(parts, -1),
+            ordered[:, 4 * width :],
+            streams[:, mods_count + 2 :].reshape(parts, -1),
+        ]
         packed = jnp.concatenate(pieces, 1)
+        sizes = [mods_count * width] + [width] * 6 + [hidden_width] * 2 + [width] * 2
         packed = lax.all_to_all(packed, "m", split_axis=0, concat_axis=0, tiled=True)
-        return packed, counts
+        return packed, np.cumsum([0] + sizes)
 
     names = ("mixed", "fc1", "fc2")
     gathers = [Gather(shard_of(b, n), rows, parts, KINDS[b][n]) for b in range(2) for n in names]
@@ -1034,19 +1028,21 @@
     ready(1)
     move((g[2], last - 1), (g[3], last - 1), (g[4], first), (g[5], first))
     k0 = fence(g, middle_stage(0, attention_stage(0, k0)))
-    move((g[4], last - 2), (g[5], last - 2), (g[2], last), (g[3], last))
-    k0, top = fence(g, (up_stage(0, k0), top))
+    move((g[2], last), (g[3], last), (g[4], last - 2), (g[5], last - 2))
+    ready(2)
+    first_out, k0 = down_stage(0, up_stage(0, k0))
+    first_out = stream_plain(first_out.astype(bf16))
+    k0, first_out, top = fence(g, (k0, first_out, top))
     ready(2)
     ready(3)
     move((g[4], last - 1), (g[5], last - 1))
-    first_out, k0 = down_stage(0, k0)
-    k1 = open_stage(1, to_positions(first_out))
+    k1 = open_stage(1, stream_rel(send_positions(first_out)))
     k1 = attention_stage(1, k1)
     k0, k1, top = fence(g, (k0, k1, top))
     move((g[4], last), (g[5], last))
     grad_top = send_positions(top)
     k1 = middle_stage(1, k1)
-    k0, k1 = fence(g, (k0, k1))
+    k0, k1, grad_top = fence(g, (k0, k1, grad_top))
     ready(4)
     ready(5)
     k1 = up_stage(1, k1)
@@ -1065,19 +1061,24 @@
     k1 = attention_back(1, k1)
     k1, s3 = mixed_grads(1, k1)
     k0, k1, output = fence(s3 + [s4, s5], (k0, k1, output.T))
-    move((s5, 3), (s4, 3), *[(s, 1) for s in s3])
+    move((s5, 3), (s4, 3))
     grad_mid, small_time = stream_back(1, k1)
     grad_mid = stream_plain(grad_mid.astype(bf16))
     k0, grad_mid, small_time, output = fence(s3 + [s4, s5], (k0, grad_mid, small_time, output))
-    k0, s2 = fc2_grads(0, k0, stream_rel(send_frames(grad_mid)))
+    move(*[(s, 1) for s in s3])
+    grad_low = send_frames(grad_mid)
+    k0, grad_low, small_time, output = fence(s3 + [s4, s5], (k0, grad_low, small_time, output))
+    k0, s2 = fc2_grads(0, k0, stream_rel(grad_low))
+    move((s2, 1))
     k0, s1 = up_back(0, k0)
     move((s5, 4), (s4, 4), *[(s, 2) for s in s3], after=k0["pre"])
     k0, small_time, output = fence([s1, s2] + s3 + [s4, s5], (k0, small_time, output))
-    move((s2, 1), (s5, last), (s4, last), *[(s, 3) for s in s3])
-    k0 = attention_back(0, hidden2_back(0, k0))
+    move((s5, last), (s4, last), *[(s, 3) for s in s3])
+    k0 = hidden2_back(0, k0)
     move((s1, 1))
     k0, small_time, output = fence([s1, s2] + s3 + [s4, s5], (k0, small_time, output))
     move((s2, 2), (s1, 2), *[(s, 4) for s in s3])
+    k0 = attention_back(0, k0)
     k0, s0 = mixed_grads(0, k0)
     grad_first, small_space = stream_back(0, k0)
     grad_first, small, output = fence(s0 + [s1, s2] + s3, (grad_first, (small_space, small_time), output))
@@ -1086,6 +1087,7 @@
     packed, counts = pack_small(small[0], small[1])
     grad_first, packed, output = fence(s0 + [s1, s2] + s3, (grad_first, packed, output))
     move((s2, 4), (s1, 4), *[(s, 2) for s in s0])
+    packed, _ = lax.optimization_barrier((packed, s0[0].arrays[-2]))
     output = to_argument(output)
     output, grad_first = fence(s0 + [s1, s2], (output, grad_first))
     move((s2, last), (s1, last), *[(s, 3) for s in s0])

time: 1120 us -> 1080 us (0.964)
  waiting for transfers between devices: 375 us -> 354 us
  local copies, waits for them, and re-layouts: 74.2 us -> 59.6 us
    ppermute x84, waiting for transfers between devices: 311 us -> 284 us  [swap(): return lax.ppermute(value, axis, [(i, i ^ bit) for i in range(count)])]
  transfers between devices with their start and end apart: 94 -> 94, of which waited for: 43 -> 39; matrix products, arithmetic and copies ran while one was open for 14% -> 12% of each run, Pallas kernels for 32% -> 34%
where the time goes in v4:
time: 1080 us; the launch traced here: 1070 us
  Pallas kernels  434 us (40%)
  waiting for transfers between devices  354 us (33%)
  starting transfers between devices  117 us (11%)
  other arithmetic  71.3 us (7%)
  local copies, waits for them, and re-layouts  59.6 us (6%)
  matrix products  33 us (3%)
    ppermute x84, waiting for transfers between devices, swap(): return lax.ppermute(value, axis, [(i, i ^ bit) for i in range(count)])  284 us
    pallas_call x8, Pallas kernels, contract(): pl.pallas_call(body, grid=(parts,), in_specs=[part_spec((tokens, n))] + [...  123 us
    pallas_call x8, Pallas kernels, project(): pl.pallas_call(body, grid=(weight.parts,), in_specs=[whole_spec((tokens,...  89 us
    pallas_call x32, Pallas kernels, sum_rows(): pl.pallas_call(body, grid=(names, count // rows), in_specs=[spec(lead) fo...  87.9 us
    pallas_call x6, Pallas kernels, weight_grads(): pl.pallas_call(body, grid=(parts,), in_specs=[whole_spec((tokens, depth))...  81.2 us
    ppermute x84, starting transfers between devices, swap(): return lax.ppermute(value, axis, [(i, i ^ bit) for i in range(count)])  75.7 us
    pallas_call x4, Pallas kernels, attention_call(): pl.pallas_call(functools.partial(kernel, temporal, chunk), grid=grid, in_...  53.7 us
    all_to_all x2, waiting for transfers between devices, send_positions(): return lax.all_to_all(shaped, 'row', 0, 0).reshape(tokens, span)  38.1 us
  transfers between devices with their start and end apart: 94, of which 39 were waited for; matrix products, arithmetic and copies ran while one was open for 12% of the time, Pallas kernels for 34%

profile of v4, /device:TPU:0, one launch (start us, length us, event | category | flops | bytes accessed | tf_op | source)
XLA Modules:
  0.0 1072.7 jit_solution(4109612054531683781)
XLA Ops:
  6.6 4.2 all-to-all-start.2
  21.0 4.3 all-to-all-start
  29.8 19.1 %collective-permute-done.8 = f32[4,3456]{1,0:T(4,128)S(1)} collective-permute-done((f32[4,3456]{1,0:T(4,128)S(1)}, f32[4,3456]{1,0:T(4,128)S(1)}, u32[]{:S(2)}, u32[]{:S(2)}) %collective-permute-start.8) | collective-permute-done | bytes 55328 | tf_op jit(solution)/shard_map/ppermute | solution.py:37
  63.7 4.8 all-to-all-start.1
  68.5 11.0 %collective-permute-done.2 = bf16[288,1152]{1,0:T(8,128)(2,1)} collective-permute-done((bf16[288,1152]{1,0:T(8,128)(2,1)S(1)}, bf16[288,1152]{1,0:T(8,128)(2,1)}, u32[]{:S(2)}, u32[]{:S(2)}) %collective-permute-start.2) | collective-permute-done | bytes 663584 | tf_op jit(solution)/shard_map/ppermute | solution.py:37
  80.7 9.6 collective-permute-done.3
  99.2 4.6 fusion.7.refs_5_
  103.8 14.0 %collective-permute-done.6 = bf16[144,1152]{1,0:T(8,128)(2,1)S(1)} collective-permute-done((bf16[144,1152]{1,0:T(8,128)(2,1)}, bf16[144,1152]{1,0:T(8,128)(2,1)S(1)}, u32[]{:S(2)}, u32[]{:S(2)}) %collective-permute-start.6) | collective-permute-done | bytes 331808 | tf_op jit(solution)/shard_map/ppermute | solution.py:37
  117.9 6.0 collective-permute-done.7
  142.2 9.2 collective-permute-done.15
  152.7 12.4 %collective-permute-done.16 = bf16[288,1152]{1,0:T(8,128)(2,1)S(1)} collective-permute-done((bf16[288,1152]{1,0:T(8,128)(2,1)}, bf16[288,1152]{1,0:T(8,128)(2,1)S(1)}, u32[]{:S(2)}, u32[]{:S(2)}) %collective-permute-start.16) | collective-permute-done | bytes 663584 | tf_op jit(solution)/shard_map/ppermute | solution.py:37
  166.2 22.3 %collective-permute-done.11.refs_2_ = bf16[1152,1152]{1,0:T(8,128)(2,1)} collective-permute-done((bf16[1152,1152]{1,0:T(8,128)(2,1)}, bf16[1152,1152]{1,0:T(8,128)(2,1)}, u32[]{:S(2)}, u32[]{:S(2)}) %collective-permute-start.11) | collective-permute-done | bytes 2654240 | tf_op jit(solution)/shard_map/ppermute | solution.py:37
  189.8 5.3 collective-permute-done.17.refs_4_
  199.1 22.4 %collective-permute-done.21 = bf16[144,1152]{1,0:T(8,128)(2,1)S(1)} collective-permute-done((bf16[144,1152]{1,0:T(8,128)(2,1)S(1)}, bf16[144,1152]{1,0:T(8,128)(2,1)S(1)}, u32[]{:S(2)}, u32[]{:S(2)}) %collective-permute-start.21) | collective-permute-done | bytes 331808 | tf_op jit(solution)/shard_map/ppermute | solution.py:37
  221.6 6.2 collective-permute-done.22
  244.4 10.0 qkv.2
  254.4 13.3 %attend.2 = (bf16[4,2,256,288]{3,2,1,0:T(8,128)(2,1)}, f32[4,2,4,256]{3,2,1,0:T(4,128)}) custom-call(bf16[4,2,256,864]{3,2,1,0:T(8,128)(2,1)} %bitcast.188), custom_call_target="tpu_custom_call" | custom-call | flops 1073741824 | bytes 4718592 | tf_op jit(solution)/shard_map/attend/pallas_call | solution.py:670
  267.7 15.2 %out.2 = (f32[512,1152]{1,0:T(8,128)}, f32[512,1152]{1,0:T(8,128)}, f32[512,1152]{1,0:T(8,128)}, f32[512,1]{1,0:T(8,128)}, bf16[512,1152]{1,0:T(8,128)(2,1)}) custom-call(bf16[4,512,288]{2,1,0:T(8,128)(2,1)} %bitcast.192, bf16[1152,1152]{1,0:T(8,128)(2,1)} %pad_maximum_fusion.refs_1_, bf16[1152,1152]{1,0:T(8,128)(2,1)} %collective-permute-done.11.refs_2_, ...), custom_call_target="tpu_custom_call" | custom-call | flops 1358954496 | bytes 8552448 | tf_op jit(solution)/shard_map/out/pallas_call | solution.py:396
  286.5 6.7 collective-permute-done.23.refs_2_
  298.8 15.1 %up.2 = (bf16[4,512,1152]{2,1,0:T(8,128)(2,1)}, bf16[4,512,1152]{2,1,0:T(8,128)(2,1)}) custom-call(bf16[512,1152]{1,0:T(8,128)(2,1)} %get-tuple-element.1105.refs_0_, bf16[1152,1152]{1,0:T(8,128)(2,1)} %pad_maximum_fusion.1.refs_1_, bf16[1152,1152]{1,0:T(8,128)(2,1)} %collective-permute-done.13.refs_2_, bf16[1152,1152]{1,0:T(8,128)(2,1)} %collective-permute-done.14.refs_3_, ...), custom_call_target="tpu_custom_call" | custom-call | flops 5435817984 | bytes 20054016 | tf_op jit(solution)/shard_map/up/pallas_call | solution.py:322
  313.9 11.9 %collective-permute-done.31 = bf16[576,1152]{1,0:T(8,128)(2,1)} collective-permute-done((bf16[576,1152]{1,0:T(8,128)(2,1)S(1)}, bf16[576,1152]{1,0:T(8,128)(2,1)}, u32[]{:S(2)}, u32[]{:S(2)}) %collective-permute-start.31) | collective-permute-done | bytes 1327136 | tf_op jit(solution)/shard_map/ppermute | solution.py:37
  331.9 13.8 %down.2 = (f32[512,1152]{1,0:T(8,128)}, bf16[512,1152]{1,0:T(8,128)(2,1)}) custom-call(bf16[4,512,1152]{2,1,0:T(8,128)(2,1)} %get-tuple-element.1110.refs_0_.refs_1_, bf16[1152,1152]{1,0:T(8,128)(2,1)} %pad_maximum_fusion.2.refs_1_, bf16[1152,1152]{1,0:T(8,128)(2,1)} %collective-permute-done.23.refs_2_, bf16[1152,1152]{1,0:T(8,128)(2,1)} %collective-permute-done.24.refs_3_, ...), custom_call_target="tpu_custom_call" | custom-call | flops 5435817984 | bytes 20054016 | tf_op jit(solution)/shard_map/down/pallas_call | solution.py:396
  350.1 4.6 all-to-all-start.3
  359.0 25.0 %all-to-all-done.3 = bf16[8,2,32,1152]{3,2,1,0:T(8,128)(2,1)S(1)} async-done(((bf16[8,2,32,1152]{3,2,1,0:T(8,128)(2,1)}), bf16[8,2,32,1152]{3,2,1,0:T(8,128)(2,1)S(1)}, u32[]{:S(2)}, u32[]{:S(2)}) %all-to-all-start.3) | async-done | bytes 1179680 | tf_op jit(solution)/shard_map/all_to_all | solution.py:759
  388.7 10.0 qkv.3
  398.7 13.4 %attend.3 = (bf16[4,1,16,32,288]{4,3,2,1,0:T(8,128)(2,1)}, f32[4,2,4,256]{3,2,1,0:T(4,128)}) custom-call(bf16[4,1,16,32,864]{4,3,2,1,0:T(8,128)(2,1)} %bitcast.190), custom_call_target="tpu_custom_call" | custom-call | flops 1073741824 | bytes 4718592 | tf_op jit(solution)/shard_map/attend/pallas_call | solution.py:670
  414.7 12.6 %collective-permute-done.35.refs_2_ = bf16[1152,1152]{1,0:T(8,128)(2,1)} collective-permute-done((bf16[1152,1152]{1,0:T(8,128)(2,1)}, bf16[1152,1152]{1,0:T(8,128)(2,1)}, u32[]{:S(2)}, u32[]{:S(2)}) %collective-permute-start.35) | collective-permute-done | bytes 2654240 | tf_op jit(solution)/shard_map/ppermute | solution.py:37
  427.4 5.2 collective-permute-done.37.refs_4_
  436.9 4.8 all-to-all-start.4
  442.5 15.2 %out.3 = (f32[512,1152]{1,0:T(8,128)}, f32[512,1152]{1,0:T(8,128)}, f32[512,1152]{1,0:T(8,128)}, f32[512,1]{1,0:T(8,128)}, bf16[512,1152]{1,0:T(8,128)(2,1)}) custom-call(bf16[4,512,288]{2,1,0:T(8,128)(2,1)} %bitcast.194, bf16[1152,1152]{1,0:T(8,128)(2,1)} %pad_maximum_fusion.3.refs_1_, bf16[1152,1152]{1,0:T(8,128)(2,1)} %collective-permute-done.25.refs_2_, ...), custom_call_target="tpu_custom_call" | custom-call | flops 1358954496 | bytes 8552448 | tf_op jit(solution)/shard_map/out/pallas_call | solution.py:396
  457.7 13.1 %all-to-all-done.4 = bf16[8,2,32,1152]{3,2,1,0:T(8,128)(2,1)S(1)} async-done(((bf16[8,2,32,1152]{3,2,1,0:T(8,128)(2,1)}), bf16[8,2,32,1152]{3,2,1,0:T(8,128)(2,1)S(1)}, u32[]{:S(2)}, u32[]{:S(2)}) %all-to-all-start.4) | async-done | bytes 1179680 | tf_op jit(solution)/shard_map/all_to_all | solution.py:759
  474.5 14.9 %up.3 = (bf16[4,512,1152]{2,1,0:T(8,128)(2,1)}, bf16[4,512,1152]{2,1,0:T(8,128)(2,1)}) custom-call(bf16[512,1152]{1,0:T(8,128)(2,1)} %get-tuple-element.920.refs_0_, bf16[1152,1152]{1,0:T(8,128)(2,1)} %pad_maximum_fusion.4.refs_1_, bf16[1152,1152]{1,0:T(8,128)(2,1)} %collective-permute-done.33.refs_2_, bf16[1152,1152]{1,0:T(8,128)(2,1)} %collective-permute-done.34.refs_3_, ...), custom_call_target="tpu_custom_call" | custom-call | flops 5435817984 | bytes 20054016 | tf_op jit(solution)/shard_map/up/pallas_call | solution.py:322
  489.4 12.7 %grad_fc2.2 = (bf16[2,1152,1152]{2,1,0:T(8,128)(2,1)}, bf16[2,1152,1152]{2,1,0:T(8,128)(2,1)}, f32[1,1152]{1,0:T(1,128)}, f32[4,1,1152]{2,1,0:T(1,128)}) custom-call(bf16[512,1152]{1,0:T(8,128)(2,1)} %get-tuple-element.921.refs_0_, bf16[4,512,1152]{2,1,0:T(8,128)(2,1)} %get-tuple-element.898.refs_1_.refs_0_), custom_call_target="tpu_custom_call" | custom-call | flops 5435817984 | bytes 15335424 | tf_op jit(solution)/shard_map/grad_fc2/pallas_call | solution.py:539
  502.7 14.2 %down.3 = (f32[512,1152]{1,0:T(8,128)}, bf16[512,1152]{1,0:T(8,128)(2,1)}) custom-call(bf16[4,512,1152]{2,1,0:T(8,128)(2,1)} %get-tuple-element.898.refs_1_.refs_0_, bf16[1152,1152]{1,0:T(8,128)(2,1)} %pad_maximum_fusion.5.refs_1_, bf16[1152,1152]{1,0:T(8,128)(2,1)} %collective-permute-done.35.refs_2_, bf16[1152,1152]{1,0:T(8,128)(2,1)} %collective-permute-done.36.refs_3_, ...), custom_call_target="tpu_custom_call" | custom-call | flops 5435817984 | bytes 20054016 | tf_op jit(solution)/shard_map/down/pallas_call | solution.py:396
  517.0 4.2 fusion.9
  524.8 12.0 %up_back.2.refs_1_.refs_0_ = bf16[4,512,1152]{2,1,0:T(8,128)(2,1)} custom-call(bf16[512,1152]{1,0:T(8,128)(2,1)} %get-tuple-element.921.refs_0_, bf16[1152,1152]{1,0:T(8,128)(2,1)} %pad_maximum_fusion.5.refs_1_, bf16[1152,1152]{1,0:T(8,128)(2,1)} %collective-permute-done.35.refs_2_, bf16[1152,1152]{1,0:T(8,128)(2,1)} %collective-permute-done.36.refs_3_, ...), custom_call_target="tpu_custom_call" | custom-call | flops 5435817984 | bytes 20054016 | tf_op jit(solution)/shard_map/up_back/pallas_call | solution.py:322
  536.8 12.7 %grad_fc1.2 = (bf16[2,1152,1152]{2,1,0:T(8,128)(2,1)}, bf16[2,1152,1152]{2,1,0:T(8,128)(2,1)}, f32[1,1152]{1,0:T(1,128)}, f32[4,1,1152]{2,1,0:T(1,128)}) custom-call(bf16[512,1152]{1,0:T(8,128)(2,1)} %get-tuple-element.920.refs_0_, bf16[4,512,1152]{2,1,0:T(8,128)(2,1)} %up_back.2.refs_1_.refs_0_), custom_call_target="tpu_custom_call" | custom-call | flops 5435817984 | bytes 15335424 | tf_op jit(solution)/shard_map/grad_fc1/pallas_call | solution.py:539
  559.2 17.1 %hidden2_back.2 = (f32[512,1152]{1,0:T(8,128)}, bf16[512,1152]{1,0:T(8,128)(2,1)}, f32[3,1152]{1,0:T(4,128)}) custom-call(bf16[4,512,1152]{2,1,0:T(8,128)(2,1)} %up_back.2.refs_1_.refs_0_, bf16[1152,1152]{1,0:T(8,128)(2,1)} %pad_maximum_fusion.4.refs_1_, bf16[1152,1152]{1,0:T(8,128)(2,1)} %collective-permute-done.33.refs_2_, ...), custom_call_target="tpu_custom_call" | custom-call | flops 5435817984 | bytes 27131904 | tf_op jit(solution)/shard_map/hidden2_back/pallas_call | solution.py:396
  576.4 3.9 sum_rows.33
  583.4 7.5 out_back.2
  590.9 13.6 %attend_back.2 = bf16[4,1,16,32,864]{4,3,2,1,0:T(8,128)(2,1)} custom-call(bf16[4,1,16,32,864]{4,3,2,1,0:T(8,128)(2,1)} %bitcast.191, bf16[4,1,16,32,288]{4,3,2,1,0:T(8,128)(2,1)} %bitcast.196, bf16[4,1,16,32,288]{4,3,2,1,0:T(8,128)(2,1)} %get-tuple-element.825, f32[4,2,4,256]{3,2,1,0:T(4,128)} %get-tuple-element.993.logs), custom_call_target="tpu_custom_call" | custom-call | flops 2684354560 | bytes 14155776 | tf_op jit(solution)/shard_map/attend_back/pallas_call | solution.py:670
  604.5 15.1 %grad_mixed.2 = (bf16[2,1152,640]{2,1,0:T(8,128)(2,1)}, bf16[2,1152,512]{2,1,0:T(8,128)(2,1)}, bf16[2,1152,640]{2,1,0:T(8,128)(2,1)}, bf16[2,1152,512]{2,1,0:T(8...) custom-call(bf16[512,1152]{1,0:T(8,128)(2,1)} %get-tuple-element.989.refs_0_, ...), custom_call_target="tpu_custom_call" | custom-call | flops 5435817984 | bytes 15335424 | tf_op jit(solution)/shard_map/grad_mixed/pallas_call | solution.py:539
  620.3 20.3 %collective-permute-done.41.refs_2_ = bf16[1,1152,1152]{2,1,0:T(8,128)(2,1)} collective-permute-done((bf16[1,1152,1152]{2,1,0:T(8,128)(2,1)}, bf16[1,1152,1152]{2,1,0:T(8,128)(2,1)}, u32[]{:S(2)}, u32[]{:S(2)}) %collective-permute-start.41) | collective-permute-done | bytes 2654240 | tf_op jit(solution)/shard_map/ppermute | solution.py:37
  651.9 14.7 %hidden_back.2 = (bf16[512,1152]{1,0:T(8,128)(2,1)}, f32[2,1152]{1,0:T(2,128)}) custom-call(bf16[4,512,864]{2,1,0:T(8,128)(2,1)} %bitcast.185, bf16[1152,1152]{1,0:T(8,128)(2,1)} %pad_maximum_fusion.3.refs_1_, bf16[1152,1152]{1,0:T(8,128)(2,1)} %collective-permute-done.25.refs_2_, bf16[1152,1152]{1,0:T(8,128)(2,1)} %collective-permute-done.26.refs_3_, ...), custom_call_target="tpu_custom_call" | custom-call | flops 4076863488 | bytes 20938752 | tf_op jit(solution)/shard_map/hidden_back/pallas_call | solution.py:396
  666.6 4.2 fusion.10
  670.8 8.2 collective-permute-done.43.refs_3_
  689.6 29.0 %all-to-all-done.6 = bf16[8,2,32,1152]{3,2,1,0:T(8,128)(2,1)S(1)} async-done(((bf16[8,2,32,1152]{3,2,1,0:T(8,128)(2,1)}), bf16[8,2,32,1152]{3,2,1,0:T(8,128)(2,1)S(1)}, u32[]{:S(2)}, u32[]{:S(2)}) %all-to-all-start.6) | async-done | bytes 1179680 | tf_op jit(solution)/shard_map/all_to_all | solution.py:763
  728.9 12.8 %grad_fc2.3 = (bf16[2,1152,1152]{2,1,0:T(8,128)(2,1)}, bf16[2,1152,1152]{2,1,0:T(8,128)(2,1)}, f32[1,1152]{1,0:T(1,128)}, f32[4,1,1152]{2,1,0:T(1,128)}) custom-call(bf16[512,1152]{1,0:T(8,128)(2,1)} %get-tuple-element.1533.refs_0_, bf16[4,512,1152]{2,1,0:T(8,128)(2,1)} %get-tuple-element.1110.refs_0_.refs_1_), custom_call_target="tpu_custom_call" | custom-call | flops 5435817984 | bytes 15335424 | tf_op jit(solution)/shard_map/grad_fc2/pallas_call | solution.py:539
  746.7 12.0 %up_back.3.refs_1_.refs_0_ = bf16[4,512,1152]{2,1,0:T(8,128)(2,1)} custom-call(bf16[512,1152]{1,0:T(8,128)(2,1)} %get-tuple-element.1533.refs_0_, bf16[1152,1152]{1,0:T(8,128)(2,1)} %pad_maximum_fusion.2.refs_1_, bf16[1152,1152]{1,0:T(8,128)(2,1)} %collective-permute-done.23.refs_2_, bf16[1152,1152]{1,0:T(8,128)(2,1)} %collective-permute-done.24.refs_3_, ...), custom_call_target="tpu_custom_call" | custom-call | flops 5435817984 | bytes 20054016 | tf_op jit(solution)/shard_map/up_back/pallas_call | solution.py:322
  758.8 13.1 %grad_fc1.3 = (bf16[2,1152,1152]{2,1,0:T(8,128)(2,1)}, bf16[2,1152,1152]{2,1,0:T(8,128)(2,1)}, f32[1,1152]{1,0:T(1,128)}, f32[4,1,1152]{2,1,0:T(1,128)}) custom-call(bf16[512,1152]{1,0:T(8,128)(2,1)} %get-tuple-element.1105.refs_0_, bf16[4,512,1152]{2,1,0:T(8,128)(2,1)} %up_back.3.refs_1_.refs_0_), custom_call_target="tpu_custom_call" | custom-call | flops 5435817984 | bytes 15335424 | tf_op jit(solution)/shard_map/grad_fc1/pallas_call | solution.py:539
  786.7 4.0 sum_rows.40
  794.8 17.5 %hidden2_back.3 = (f32[512,1152]{1,0:T(8,128)}, bf16[512,1152]{1,0:T(8,128)(2,1)}, f32[3,1152]{1,0:T(4,128)}) custom-call(bf16[4,512,1152]{2,1,0:T(8,128)(2,1)} %up_back.3.refs_1_.refs_0_, bf16[1152,1152]{1,0:T(8,128)(2,1)} %pad_maximum_fusion.1.refs_1_, bf16[1152,1152]{1,0:T(8,128)(2,1)} %collective-permute-done.13.refs_2_, ...), custom_call_target="tpu_custom_call" | custom-call | flops 5435817984 | bytes 27131904 | tf_op jit(solution)/shard_map/hidden2_back/pallas_call | solution.py:396
  818.3 4.0 sum_rows.45
  829.6 7.5 out_back.3
  837.1 13.4 %attend_back.3 = bf16[4,2,256,864]{3,2,1,0:T(8,128)(2,1)} custom-call(bf16[4,2,256,864]{3,2,1,0:T(8,128)(2,1)} %bitcast.189, bf16[4,2,256,288]{3,2,1,0:T(8,128)(2,1)} %bitcast.197, bf16[4,2,256,288]{3,2,1,0:T(8,128)(2,1)} %get-tuple-element.759, f32[4,2,4,256]{3,2,1,0:T(4,128)} %get-tuple-element.1211.logs), custom_call_target="tpu_custom_call" | custom-call | flops 2684354560 | bytes 14155776 | tf_op jit(solution)/shard_map/attend_back/pallas_call | solution.py:670
  850.5 14.9 %grad_mixed.3 = (bf16[2,1152,640]{2,1,0:T(8,128)(2,1)}, bf16[2,1152,512]{2,1,0:T(8,128)(2,1)}, bf16[2,1152,640]{2,1,0:T(8,128)(2,1)}, bf16[2,1152,512]{2,1,0:T(8...) custom-call(bf16[512,1152]{1,0:T(8,128)(2,1)} %get-tuple-element.1207.refs_0_, ...), custom_call_target="tpu_custom_call" | custom-call | flops 5435817984 | bytes 15335424 | tf_op jit(solution)/shard_map/grad_mixed/pallas_call | solution.py:539
  865.4 14.8 %hidden_back.3 = (bf16[512,1152]{1,0:T(8,128)(2,1)}, f32[2,1152]{1,0:T(2,128)}) custom-call(bf16[4,512,864]{2,1,0:T(8,128)(2,1)} %bitcast.187, bf16[1152,1152]{1,0:T(8,128)(2,1)} %pad_maximum_fusion.refs_1_, bf16[1152,1152]{1,0:T(8,128)(2,1)} %collective-permute-done.11.refs_2_, bf16[1152,1152]{1,0:T(8,128)(2,1)} %collective-permute-done.12.refs_3_, ...), custom_call_target="tpu_custom_call" | custom-call | flops 4076863488 | bytes 20938752 | tf_op jit(solution)/shard_map/hidden_back/pallas_call | solution.py:396
  910.9 17.5 %collective-permute-done.63.refs_3_ = bf16[1,576,1152]{2,1,0:T(8,128)(2,1)} collective-permute-done((bf16[1,576,1152]{2,1,0:T(8,128)(2,1)}, bf16[1,576,1152]{2,1,0:T(8,128)(2,1)}, u32[]{:S(2)}, u32[]{:S(2)}) %collective-permute-start.63) | collective-permute-done | bytes 1327136 | tf_op jit(solution)/shard_map/ppermute | solution.py:37
  950.6 4.6 all-to-all-start.8
  958.6 17.5 %collective-permute-done.67.refs_2_ = bf16[1,1152,640]{2,1,0:T(8,128)(2,1)S(1)} collective-permute-done((bf16[1,1152,640]{2,1,0:T(8,128)(2,1)}, bf16[1,1152,640]{2,1,0:T(8,128)(2,1)S(1)}, u32[]{:S(2)}, u32[]{:S(2)}) %collective-permute-start.67) | collective-permute-done | bytes 1474592 | tf_op jit(solution)/shard_map/ppermute | solution.py:37
  976.8 5.3 collective-permute-done.71
  1000.8 4.0 fusion.11
  1008.5 3.9 collective-permute-done.73
  1056.6 8.1 collective-permute-done.81
  (563 shorter events, 345.9 us)
Async XLA Ops:
  13.0 45.7 %collective-permute-start = (bf16[144,1152]{1,0:T(8,128)(2,1)S(1)}, bf16[144,1152]{1,0:T(8,128)(2,1)}, u32[]{:S(2)}, u32[]{:S(2)}) collective-permute-start(bf16[144,1152]{1,0:T(8,128)(2,1)S(1)} %pad_maximum_fusion.24), channel_id=1, source_target_pairs={{0,16},{4,20},{8,24},{12,28},{16,0},{20,4},{24,8},{28,12},{1,17},{... | collective-permute-start | bytes 995336 | tf_op jit(solution)/shard_map/ppermute | solution.py:37
  18.7 41.0 %collective-permute-start.1 = (bf16[144,1152]{1,0:T(8,128)(2,1)S(1)}, bf16[144,1152]{1,0:T(8,128)(2,1)}, u32[]{:S(2)}, u32[]{:S(2)}) collective-permute-start(bf16[144,1152]{1,0:T(8,128)(2,1)S(1)} %get-tuple-element.1482), channel_id=1, source_target_pairs={{0,16},{4,20},{8,24},{12,28},{16,0},{20,4},{24,8},{28,12},{1,17},{... | collective-permute-start | bytes 995336 | tf_op jit(solution)/shard_map/ppermute | solution.py:37
  21.0 42.7 %all-to-all-start = ((bf16[4,288,512]{2,1,0:T(8,128)(2,1)}), bf16[4,288,512]{2,1,0:T(8,128)(2,1)}, u32[]{:S(2)}, u32[]{:S(2)}) async-start(bf16[4,288,512]{2,1,0:T(8,128)(2,1)} %param.17), calls=%async_computation | async-start | bytes 2359296 | tf_op jit(solution)/shard_map/all_to_all | solution.py:829
  63.7 29.0 %all-to-all-start.1 = ((bf16[4,288,512]{2,1,0:T(8,128)(2,1)}), bf16[4,288,512]{2,1,0:T(8,128)(2,1)}, u32[]{:S(2)}, u32[]{:S(2)}) async-start(bf16[4,288,512]{2,1,0:T(8,128)(2,1)} %param.29), calls=%async_computation.1 | async-start | bytes 2359296 | tf_op jit(solution)/shard_map/all_to_all | solution.py:829
  92.7 32.0 %collective-permute-start.4 = (bf16[576,1152]{1,0:T(8,128)(2,1)S(1)}, bf16[576,1152]{1,0:T(8,128)(2,1)S(1)}, u32[]{:S(2)}, u32[]{:S(2)}) collective-permute-start(bf16[576,1152]{1,0:T(8,128)(2,1)S(1)} %pad_maximum_fusion.7), channel_id=1, source_target_pairs={{0,4},{4,0},{8,12},{12,8},{16,20},{20,16},{24,28},{28,24},{1,5},{5... | collective-permute-start | bytes 3981320 | tf_op jit(solution)/shard_map/ppermute | solution.py:37
  97.7 28.7 %collective-permute-start.5 = (bf16[576,1152]{1,0:T(8,128)(2,1)}, bf16[576,1152]{1,0:T(8,128)(2,1)S(1)}, u32[]{:S(2)}, u32[]{:S(2)}) collective-permute-start(bf16[576,1152]{1,0:T(8,128)(2,1)} %pad_maximum_fusion.8), channel_id=1, source_target_pairs={{0,2},{1,3},{2,0},{3,1},{4,6},{5,7},{6,4},{7,5},{8,10},{9,11},{10,... | collective-permute-start | bytes 3981320 | tf_op jit(solution)/shard_map/ppermute | solution.py:37
  128.2 60.3 %collective-permute-start.11 = (bf16[1152,1152]{1,0:T(8,128)(2,1)}, bf16[1152,1152]{1,0:T(8,128)(2,1)}, u32[]{:S(2)}, u32[]{:S(2)}) collective-permute-start(bf16[1152,1152]{1,0:T(8,128)(2,1)} %pad_maximum_fusion.refs_1_), channel_id=1, source_target_pairs={{0,2},{1,3},{2,0},{3,1},{4,6},{5,7},{6,4},{7,5},{8,10},{9,11},{10,... | collective-permute-start | bytes 7962632 | tf_op jit(solution)/shard_map/ppermute | solution.py:37
  129.8 60.0 %collective-permute-start.13 = (bf16[1152,1152]{1,0:T(8,128)(2,1)}, bf16[1152,1152]{1,0:T(8,128)(2,1)}, u32[]{:S(2)}, u32[]{:S(2)}) collective-permute-start(bf16[1152,1152]{1,0:T(8,128)(2,1)} %pad_maximum_fusion.1.refs_1_), channel_id=1, source_target_pairs={{0,4},{4,0},{8,12},{12,8},{16,20},{20,16},{24,28},{28,24},{1,5},{5... | collective-permute-start | bytes 7962632 | tf_op jit(solution)/shard_map/ppermute | solution.py:37
  133.5 56.3 %collective-permute-start.14 = (bf16[1152,1152]{1,0:T(8,128)(2,1)}, bf16[1152,1152]{1,0:T(8,128)(2,1)}, u32[]{:S(2)}, u32[]{:S(2)}) collective-permute-start(bf16[1152,1152]{1,0:T(8,128)(2,1)} %pad_maximum_fusion.1.refs_1_), channel_id=1, source_target_pairs={{0,1},{1,0},{2,3},{3,2},{4,5},{5,4},{6,7},{7,6},{8,9},{9,8},{10,11... | collective-permute-start | bytes 7962632 | tf_op jit(solution)/shard_map/ppermute | solution.py:37
  134.5 30.6 %collective-permute-start.16 = (bf16[288,1152]{1,0:T(8,128)(2,1)}, bf16[288,1152]{1,0:T(8,128)(2,1)S(1)}, u32[]{:S(2)}, u32[]{:S(2)}) collective-permute-start(bf16[288,1152]{1,0:T(8,128)(2,1)} %pad_maximum_fusion.18), channel_id=1, source_target_pairs={{0,8},{4,12},{8,0},{12,4},{16,24},{20,28},{24,16},{28,20},{1,9},{5... | collective-permute-start | bytes 1990664 | tf_op jit(solution)/shard_map/ppermute | solution.py:37
  195.1 37.1 %collective-permute-start.18 = (bf16[1152,1152]{1,0:T(8,128)(2,1)}, bf16[1152,1152]{1,0:T(8,128)(2,1)}, u32[]{:S(2)}, u32[]{:S(2)}) collective-permute-start(bf16[1152,1152]{1,0:T(8,128)(2,1)} %collective-permute-done.13.refs_2_), channel_id=1, source_target_pairs={{0,1},{1,0},{2,3},{3,2},{4,5},{5,4},{6,7},{7,6},{8,9},{9,8},{10,11... | collective-permute-start | bytes 7962632 | tf_op jit(solution)/shard_map/ppermute | solution.py:37
  195.3 33.4 %collective-permute-start.19 = (bf16[576,1152]{1,0:T(8,128)(2,1)S(1)}, bf16[576,1152]{1,0:T(8,128)(2,1)S(1)}, u32[]{:S(2)}, u32[]{:S(2)}) collective-permute-start(bf16[576,1152]{1,0:T(8,128)(2,1)S(1)} %pad_maximum_fusion.9), channel_id=1, source_target_pairs={{0,4},{4,0},{8,12},{12,8},{16,20},{20,16},{24,28},{28,24},{1,5},{5... | collective-permute-start | bytes 3981320 | tf_op jit(solution)/shard_map/ppermute | solution.py:37
  197.2 33.1 %collective-permute-start.20 = (bf16[576,1152]{1,0:T(8,128)(2,1)S(1)}, bf16[576,1152]{1,0:T(8,128)(2,1)S(1)}, u32[]{:S(2)}, u32[]{:S(2)}) collective-permute-start(bf16[576,1152]{1,0:T(8,128)(2,1)S(1)} %pad_maximum_fusion.10), channel_id=1, source_target_pairs={{0,2},{1,3},{2,0},{3,1},{4,6},{5,7},{6,4},{7,5},{8,10},{9,11},{10,... | collective-permute-start | bytes 3981320 | tf_op jit(solution)/shard_map/ppermute | solution.py:37
  197.7 30.1 %collective-permute-start.22 = (bf16[144,1152]{1,0:T(8,128)(2,1)S(1)}, bf16[144,1152]{1,0:T(8,128)(2,1)S(1)}, u32[]{:S(2)}, u32[]{:S(2)}) collective-permute-start(bf16[144,1152]{1,0:T(8,128)(2,1)S(1)} %copy-done.22), channel_id=1, source_target_pairs={{0,16},{4,20},{8,24},{12,28},{16,0},{20,4},{24,8},{28,12},{1,17},{... | collective-permute-start | bytes 995336 | tf_op jit(solution)/shard_map/ppermute | solution.py:37
  232.9 60.4 %collective-permute-start.23 = (bf16[1152,1152]{1,0:T(8,128)(2,1)}, bf16[1152,1152]{1,0:T(8,128)(2,1)}, u32[]{:S(2)}, u32[]{:S(2)}) collective-permute-start(bf16[1152,1152]{1,0:T(8,128)(2,1)} %pad_maximum_fusion.2.refs_1_), channel_id=1, source_target_pairs={{0,2},{1,3},{2,0},{3,1},{4,6},{5,7},{6,4},{7,5},{8,10},{9,11},{10,... | collective-permute-start | bytes 7962632 | tf_op jit(solution)/shard_map/ppermute | solution.py:37
  233.4 60.0 %collective-permute-start.25 = (bf16[1152,1152]{1,0:T(8,128)(2,1)}, bf16[1152,1152]{1,0:T(8,128)(2,1)}, u32[]{:S(2)}, u32[]{:S(2)}) collective-permute-start(bf16[1152,1152]{1,0:T(8,128)(2,1)} %pad_maximum_fusion.3.refs_1_), channel_id=1, source_target_pairs={{0,4},{4,0},{8,12},{12,8},{16,20},{20,16},{24,28},{28,24},{1,5},{5... | collective-permute-start | bytes 7962632 | tf_op jit(solution)/shard_map/ppermute | solution.py:37
  237.5 55.9 %collective-permute-start.26 = (bf16[1152,1152]{1,0:T(8,128)(2,1)}, bf16[1152,1152]{1,0:T(8,128)(2,1)}, u32[]{:S(2)}, u32[]{:S(2)}) collective-permute-start(bf16[1152,1152]{1,0:T(8,128)(2,1)} %pad_maximum_fusion.3.refs_1_), channel_id=1, source_target_pairs={{0,1},{1,0},{2,3},{3,2},{4,5},{5,4},{6,7},{7,6},{8,9},{9,8},{10,11... | collective-permute-start | bytes 7962632 | tf_op jit(solution)/shard_map/ppermute | solution.py:37
  240.9 42.0 %collective-permute-start.27 = (bf16[288,1152]{1,0:T(8,128)(2,1)S(1)}, bf16[288,1152]{1,0:T(8,128)(2,1)}, u32[]{:S(2)}, u32[]{:S(2)}) collective-permute-start(bf16[288,1152]{1,0:T(8,128)(2,1)S(1)} %pad_maximum_fusion.19), channel_id=1, source_target_pairs={{0,8},{4,12},{8,0},{12,4},{16,24},{20,28},{24,16},{28,20},{1,9},{5... | collective-permute-start | bytes 1990664 | tf_op jit(solution)/shard_map/ppermute | solution.py:37
  242.7 41.4 %collective-permute-start.28 = (bf16[288,1152]{1,0:T(8,128)(2,1)}, bf16[288,1152]{1,0:T(8,128)(2,1)}, u32[]{:S(2)}, u32[]{:S(2)}) collective-permute-start(bf16[288,1152]{1,0:T(8,128)(2,1)} %pad_maximum_fusion.20), channel_id=1, source_target_pairs={{0,8},{4,12},{8,0},{12,4},{16,24},{20,28},{24,16},{28,20},{1,9},{5... | collective-permute-start | bytes 1990664 | tf_op jit(solution)/shard_map/ppermute | solution.py:37
  294.1 31.7 %collective-permute-start.31 = (bf16[576,1152]{1,0:T(8,128)(2,1)S(1)}, bf16[576,1152]{1,0:T(8,128)(2,1)}, u32[]{:S(2)}, u32[]{:S(2)}) collective-permute-start(bf16[576,1152]{1,0:T(8,128)(2,1)S(1)} %pad_maximum_fusion.11), channel_id=1, source_target_pairs={{0,4},{4,0},{8,12},{12,8},{16,20},{20,16},{24,28},{28,24},{1,5},{5... | collective-permute-start | bytes 3981320 | tf_op jit(solution)/shard_map/ppermute | solution.py:37
  295.8 33.1 %collective-permute-start.32 = (bf16[576,1152]{1,0:T(8,128)(2,1)}, bf16[576,1152]{1,0:T(8,128)(2,1)}, u32[]{:S(2)}, u32[]{:S(2)}) collective-permute-start(bf16[576,1152]{1,0:T(8,128)(2,1)} %pad_maximum_fusion.12), channel_id=1, source_target_pairs={{0,2},{1,3},{2,0},{3,1},{4,6},{5,7},{6,4},{7,5},{8,10},{9,11},{10,... | collective-permute-start | bytes 3981320 | tf_op jit(solution)/shard_map/ppermute | solution.py:37
  298.8 50.1 %collective-permute-start.30 = (bf16[1152,1152]{1,0:T(8,128)(2,1)}, bf16[1152,1152]{1,0:T(8,128)(2,1)}, u32[]{:S(2)}, u32[]{:S(2)}) collective-permute-start(bf16[1152,1152]{1,0:T(8,128)(2,1)} %collective-permute-done.25.refs_2_), channel_id=1, source_target_pairs={{0,1},{1,0},{2,3},{3,2},{4,5},{5,4},{6,7},{7,6},{8,9},{9,8},{10,11... | collective-permute-start | bytes 7962632 | tf_op jit(solution)/shard_map/ppermute | solution.py:37
  350.1 33.9 %all-to-all-start.3 = ((bf16[8,2,32,1152]{3,2,1,0:T(8,128)(2,1)}), bf16[8,2,32,1152]{3,2,1,0:T(8,128)(2,1)S(1)}, u32[]{:S(2)}, u32[]{:S(2)}) async-start(bf16[8,2,32,1152]{3,2,1,0:T(8,128)(2,1)} %bitcast.177), calls=%async_computation.3 | async-start | bytes 2359296 | tf_op jit(solution)/shard_map/all_to_all | solution.py:759
  354.7 60.0 %collective-permute-start.33 = (bf16[1152,1152]{1,0:T(8,128)(2,1)}, bf16[1152,1152]{1,0:T(8,128)(2,1)}, u32[]{:S(2)}, u32[]{:S(2)}) collective-permute-start(bf16[1152,1152]{1,0:T(8,128)(2,1)} %pad_maximum_fusion.4.refs_1_), channel_id=1, source_target_pairs={{0,2},{1,3},{2,0},{3,1},{4,6},{5,7},{6,4},{7,5},{8,10},{9,11},{10,... | collective-permute-start | bytes 7962632 | tf_op jit(solution)/shard_map/ppermute | solution.py:37
  356.3 71.1 %collective-permute-start.35 = (bf16[1152,1152]{1,0:T(8,128)(2,1)}, bf16[1152,1152]{1,0:T(8,128)(2,1)}, u32[]{:S(2)}, u32[]{:S(2)}) collective-permute-start(bf16[1152,1152]{1,0:T(8,128)(2,1)} %pad_maximum_fusion.5.refs_1_), channel_id=1, source_target_pairs={{0,4},{4,0},{8,12},{12,8},{16,20},{20,16},{24,28},{28,24},{1,5},{5... | collective-permute-start | bytes 7962632 | tf_op jit(solution)/shard_map/ppermute | solution.py:37
  358.3 69.0 %collective-permute-start.36 = (bf16[1152,1152]{1,0:T(8,128)(2,1)}, bf16[1152,1152]{1,0:T(8,128)(2,1)}, u32[]{:S(2)}, u32[]{:S(2)}) collective-permute-start(bf16[1152,1152]{1,0:T(8,128)(2,1)} %pad_maximum_fusion.5.refs_1_), channel_id=1, source_target_pairs={{0,1},{1,0},{2,3},{3,2},{4,5},{5,4},{6,7},{7,6},{8,9},{9,8},{10,11... | collective-permute-start | bytes 7962632 | tf_op jit(solution)/shard_map/ppermute | solution.py:37
  434.0 36.8 %collective-permute-start.38 = (bf16[1152,1152]{1,0:T(8,128)(2,1)}, bf16[1152,1152]{1,0:T(8,128)(2,1)}, u32[]{:S(2)}, u32[]{:S(2)}) collective-permute-start(bf16[1152,1152]{1,0:T(8,128)(2,1)} %collective-permute-done.35.refs_2_), channel_id=1, source_target_pairs={{0,1},{1,0},{2,3},{3,2},{4,5},{5,4},{6,7},{7,6},{8,9},{9,8},{10,11... | collective-permute-start | bytes 7962632 | tf_op jit(solution)/shard_map/ppermute | solution.py:37
  436.9 33.8 %all-to-all-start.4 = ((bf16[8,2,32,1152]{3,2,1,0:T(8,128)(2,1)}), bf16[8,2,32,1152]{3,2,1,0:T(8,128)(2,1)S(1)}, u32[]{:S(2)}, u32[]{:S(2)}) async-start(bf16[8,2,32,1152]{3,2,1,0:T(8,128)(2,1)} %copy.151), calls=%async_computation.4 | async-start | bytes 2359296 | tf_op jit(solution)/shard_map/all_to_all | solution.py:759
  502.1 53.3 %collective-permute-start.39 = (bf16[2,1152,1152]{2,1,0:T(8,128)(2,1)}, bf16[2,1152,1152]{2,1,0:T(8,128)(2,1)}, u32[]{:S(2)}, u32[]{:S(2)}) collective-permute-start(bf16[2,1152,1152]{2,1,0:T(8,128)(2,1)} %get-tuple-element.926), channel_id=1, source_target_pairs={{0,1},{1,0},{2,3},{3,2},{4,5},{5,4},{6,7},{7,6},{8,9},{9,8},{10,11... | collective-permute-start | bytes 15925256 | tf_op jit(solution)/shard_map/ppermute | solution.py:37
  521.1 33.0 %all-to-all-start.5 = ((bf16[8,2,32,1152]{3,2,1,0:T(8,128)(2,1)}), bf16[8,2,32,1152]{3,2,1,0:T(8,128)(2,1)S(1)}, u32[]{:S(2)}, u32[]{:S(2)}) async-start(bf16[8,2,32,1152]{3,2,1,0:T(8,128)(2,1)} %bitcast.205), calls=%async_computation.5 | async-start | bytes 2359296 | tf_op jit(solution)/shard_map/all_to_all | solution.py:763
  580.3 60.3 %collective-permute-start.41 = (bf16[1,1152,1152]{2,1,0:T(8,128)(2,1)}, bf16[1,1152,1152]{2,1,0:T(8,128)(2,1)}, u32[]{:S(2)}, u32[]{:S(2)}) collective-permute-start(bf16[1,1152,1152]{2,1,0:T(8,128)(2,1)} %sum_rows.33), channel_id=1, source_target_pairs={{0,2},{1,3},{2,0},{3,1},{4,6},{5,7},{6,4},{7,5},{8,10},{9,11},{10,... | collective-permute-start | bytes 7962632 | tf_op jit(solution)/shard_map/ppermute | solution.py:37
  581.9 62.4 %collective-permute-start.42 = (bf16[2,576,1152]{2,1,0:T(8,128)(2,1)}, bf16[2,576,1152]{2,1,0:T(8,128)(2,1)}, u32[]{:S(2)}, u32[]{:S(2)}) collective-permute-start(bf16[2,576,1152]{2,1,0:T(8,128)(2,1)} %sum_rows.32), channel_id=1, source_target_pairs={{0,4},{4,0},{8,12},{12,8},{16,20},{20,16},{24,28},{28,24},{1,5},{5... | collective-permute-start | bytes 7962632 | tf_op jit(solution)/shard_map/ppermute | solution.py:37
  647.9 31.1 %collective-permute-start.43 = (bf16[1,576,1152]{2,1,0:T(8,128)(2,1)}, bf16[1,576,1152]{2,1,0:T(8,128)(2,1)}, u32[]{:S(2)}, u32[]{:S(2)}) collective-permute-start(bf16[1,576,1152]{2,1,0:T(8,128)(2,1)} %sum_rows.34), channel_id=1, source_target_pairs={{0,4},{4,0},{8,12},{12,8},{16,20},{20,16},{24,28},{28,24},{1,5},{5... | collective-permute-start | bytes 3981320 | tf_op jit(solution)/shard_map/ppermute | solution.py:37
  649.4 32.2 %collective-permute-start.44 = (bf16[1,576,1152]{2,1,0:T(8,128)(2,1)}, bf16[1,576,1152]{2,1,0:T(8,128)(2,1)S(1)}, u32[]{:S(2)}, u32[]{:S(2)}) collective-permute-start(bf16[1,576,1152]{2,1,0:T(8,128)(2,1)} %sum_rows.35), channel_id=1, source_target_pairs={{0,2},{1,3},{2,0},{3,1},{4,6},{5,7},{6,4},{7,5},{8,10},{9,11},{10,... | collective-permute-start | bytes 3981320 | tf_op jit(solution)/shard_map/ppermute | solution.py:37
  685.2 37.0 %collective-permute-start.45 = (bf16[2,1152,640]{2,1,0:T(8,128)(2,1)}, bf16[2,1152,640]{2,1,0:T(8,128)(2,1)}, u32[]{:S(2)}, u32[]{:S(2)}) collective-permute-start(bf16[2,1152,640]{2,1,0:T(8,128)(2,1)} %get-tuple-element.1068), channel_id=1, source_target_pairs={{0,1},{1,0},{2,3},{3,2},{4,5},{5,4},{6,7},{7,6},{8,9},{9,8},{10,11... | collective-permute-start | bytes 8847368 | tf_op jit(solution)/shard_map/ppermute | solution.py:37
  685.2 34.4 %collective-permute-start.46 = (bf16[2,1152,512]{2,1,0:T(8,128)(2,1)}, bf16[2,1152,512]{2,1,0:T(8,128)(2,1)}, u32[]{:S(2)}, u32[]{:S(2)}) collective-permute-start(bf16[2,1152,512]{2,1,0:T(8,128)(2,1)} %get-tuple-element.1070), channel_id=1, source_target_pairs={{0,1},{1,0},{2,3},{3,2},{4,5},{5,4},{6,7},{7,6},{8,9},{9,8},{10,11... | collective-permute-start | bytes 7077896 | tf_op jit(solution)/shard_map/ppermute | solution.py:37
  685.7 32.8 %all-to-all-start.6 = ((bf16[8,2,32,1152]{3,2,1,0:T(8,128)(2,1)}), bf16[8,2,32,1152]{3,2,1,0:T(8,128)(2,1)S(1)}, u32[]{:S(2)}, u32[]{:S(2)}) async-start(bf16[8,2,32,1152]{3,2,1,0:T(8,128)(2,1)} %bitcast.204), calls=%async_computation.6 | async-start | bytes 2359296 | tf_op jit(solution)/shard_map/all_to_all | solution.py:763
  741.6 45.1 %collective-permute-start.47 = (bf16[2,1152,1152]{2,1,0:T(8,128)(2,1)}, bf16[2,1152,1152]{2,1,0:T(8,128)(2,1)}, u32[]{:S(2)}, u32[]{:S(2)}) collective-permute-start(bf16[2,1152,1152]{2,1,0:T(8,128)(2,1)} %get-tuple-element.1112), channel_id=1, source_target_pairs={{0,1},{1,0},{2,3},{3,2},{4,5},{5,4},{6,7},{7,6},{8,9},{9,8},{10,11... | collective-permute-start | bytes 15925256 | tf_op jit(solution)/shard_map/ppermute | solution.py:37
  741.6 41.3 %collective-permute-start.48 = (bf16[1,1152,640]{2,1,0:T(8,128)(2,1)}, bf16[1,1152,640]{2,1,0:T(8,128)(2,1)S(1)}, u32[]{:S(2)}, u32[]{:S(2)}) collective-permute-start(bf16[1,1152,640]{2,1,0:T(8,128)(2,1)} %sum_rows.38), channel_id=1, source_target_pairs={{0,2},{1,3},{2,0},{3,1},{4,6},{5,7},{6,4},{7,5},{8,10},{9,11},{10,... | collective-permute-start | bytes 4423688 | tf_op jit(solution)/shard_map/ppermute | solution.py:37
  743.3 37.2 %collective-permute-start.49 = (bf16[2,576,512]{2,1,0:T(8,128)(2,1)}, bf16[2,576,512]{2,1,0:T(8,128)(2,1)}, u32[]{:S(2)}, u32[]{:S(2)}) collective-permute-start(bf16[2,576,512]{2,1,0:T(8,128)(2,1)} %sum_rows.39), channel_id=1, source_target_pairs={{0,4},{4,0},{8,12},{12,8},{16,20},{20,16},{24,28},{28,24},{1,5},{5... | collective-permute-start | bytes 3538952 | tf_op jit(solution)/shard_map/ppermute | solution.py:37
  744.7 30.9 %collective-permute-start.50 = (bf16[1,288,1152]{2,1,0:T(8,128)(2,1)S(1)}, bf16[1,288,1152]{2,1,0:T(8,128)(2,1)}, u32[]{:S(2)}, u32[]{:S(2)}) collective-permute-start(bf16[1,288,1152]{2,1,0:T(8,128)(2,1)S(1)} %copy-done.29), channel_id=1, source_target_pairs={{0,8},{4,12},{8,0},{12,4},{16,24},{20,28},{24,16},{28,20},{1,9},{5... | collective-permute-start | bytes 1990664 | tf_op jit(solution)/shard_map/ppermute | solution.py:37
  744.7 30.9 %collective-permute-start.51 = (bf16[1,288,1152]{2,1,0:T(8,128)(2,1)S(1)}, bf16[1,288,1152]{2,1,0:T(8,128)(2,1)S(1)}, u32[]{:S(2)}, u32[]{:S(2)}) collective-permute-start(bf16[1,288,1152]{2,1,0:T(8,128)(2,1)S(1)} %copy-done.30), channel_id=1, source_target_pairs={{0,8},{4,12},{8,0},{12,4},{16,24},{20,28},{24,16},{28,20},{1,9},{5... | collective-permute-start | bytes 1990664 | tf_op jit(solution)/shard_map/ppermute | solution.py:37
  791.8 30.5 %collective-permute-start.55 = (bf16[1,144,1152]{2,1,0:T(8,128)(2,1)}, bf16[1,144,1152]{2,1,0:T(8,128)(2,1)}, u32[]{:S(2)}, u32[]{:S(2)}) collective-permute-start(bf16[1,144,1152]{2,1,0:T(8,128)(2,1)} %sum_rows.43), channel_id=1, source_target_pairs={{0,16},{4,20},{8,24},{12,28},{16,0},{20,4},{24,8},{28,12},{1,17},{... | collective-permute-start | bytes 995336 | tf_op jit(solution)/shard_map/ppermute | solution.py:37
  792.8 30.8 %collective-permute-start.56 = (bf16[1,144,1152]{2,1,0:T(8,128)(2,1)}, bf16[1,144,1152]{2,1,0:T(8,128)(2,1)}, u32[]{:S(2)}, u32[]{:S(2)}) collective-permute-start(bf16[1,144,1152]{2,1,0:T(8,128)(2,1)} %sum_rows.44), channel_id=1, source_target_pairs={{0,16},{4,20},{8,24},{12,28},{16,0},{20,4},{24,8},{28,12},{1,17},{... | collective-permute-start | bytes 995336 | tf_op jit(solution)/shard_map/ppermute | solution.py:37
  823.7 62.1 %collective-permute-start.57 = (bf16[2,576,1152]{2,1,0:T(8,128)(2,1)}, bf16[2,576,1152]{2,1,0:T(8,128)(2,1)}, u32[]{:S(2)}, u32[]{:S(2)}) collective-permute-start(bf16[2,576,1152]{2,1,0:T(8,128)(2,1)} %sum_rows.45), channel_id=1, source_target_pairs={{0,4},{4,0},{8,12},{12,8},{16,20},{20,16},{24,28},{28,24},{1,5},{5... | collective-permute-start | bytes 7962632 | tf_op jit(solution)/shard_map/ppermute | solution.py:37
  825.1 64.4 %collective-permute-start.58 = (bf16[1,1152,1152]{2,1,0:T(8,128)(2,1)}, bf16[1,1152,1152]{2,1,0:T(8,128)(2,1)}, u32[]{:S(2)}, u32[]{:S(2)}) collective-permute-start(bf16[1,1152,1152]{2,1,0:T(8,128)(2,1)} %sum_rows.40), channel_id=1, source_target_pairs={{0,2},{1,3},{2,0},{3,1},{4,6},{5,7},{6,4},{7,5},{8,10},{9,11},{10,... | collective-permute-start | bytes 7962632 | tf_op jit(solution)/shard_map/ppermute | solution.py:37
  827.6 52.8 %collective-permute-start.60 = (bf16[1,288,512]{2,1,0:T(8,128)(2,1)S(1)}, bf16[1,288,512]{2,1,0:T(8,128)(2,1)S(1)}, u32[]{:S(2)}, u32[]{:S(2)}) collective-permute-start(bf16[1,288,512]{2,1,0:T(8,128)(2,1)S(1)} %copy-done.37), channel_id=1, source_target_pairs={{0,8},{4,12},{8,0},{12,4},{16,24},{20,28},{24,16},{28,20},{1,9},{5... | collective-permute-start | bytes 884744 | tf_op jit(solution)/shard_map/ppermute | solution.py:37
  827.6 55.5 %collective-permute-start.59 = (bf16[1,288,640]{2,1,0:T(8,128)(2,1)S(1)}, bf16[1,288,640]{2,1,0:T(8,128)(2,1)S(1)}, u32[]{:S(2)}, u32[]{:S(2)}) collective-permute-start(bf16[1,288,640]{2,1,0:T(8,128)(2,1)S(1)} %copy-done.36), channel_id=1, source_target_pairs={{0,8},{4,12},{8,0},{12,4},{16,24},{20,28},{24,16},{28,20},{1,9},{5... | collective-permute-start | bytes 1105928 | tf_op jit(solution)/shard_map/ppermute | solution.py:37
  893.4 47.2 %collective-permute-start.66 = (bf16[1,144,512]{2,1,0:T(8,128)(2,1)}, bf16[1,144,512]{2,1,0:T(8,128)(2,1)}, u32[]{:S(2)}, u32[]{:S(2)}) collective-permute-start(bf16[1,144,512]{2,1,0:T(8,128)(2,1)} %sum_rows.51), channel_id=1, source_target_pairs={{0,16},{4,20},{8,24},{12,28},{16,0},{20,4},{24,8},{28,12},{1,17},{... | collective-permute-start | bytes 442376 | tf_op jit(solution)/shard_map/ppermute | solution.py:37
  893.5 47.1 %collective-permute-start.65 = (bf16[1,144,640]{2,1,0:T(8,128)(2,1)}, bf16[1,144,640]{2,1,0:T(8,128)(2,1)}, u32[]{:S(2)}, u32[]{:S(2)}) collective-permute-start(bf16[1,144,640]{2,1,0:T(8,128)(2,1)} %sum_rows.50), channel_id=1, source_target_pairs={{0,16},{4,20},{8,24},{12,28},{16,0},{20,4},{24,8},{28,12},{1,17},{... | collective-permute-start | bytes 552968 | tf_op jit(solution)/shard_map/ppermute | solution.py:37
  896.4 32.0 %collective-permute-start.63 = (bf16[1,576,1152]{2,1,0:T(8,128)(2,1)}, bf16[1,576,1152]{2,1,0:T(8,128)(2,1)}, u32[]{:S(2)}, u32[]{:S(2)}) collective-permute-start(bf16[1,576,1152]{2,1,0:T(8,128)(2,1)} %sum_rows.48), channel_id=1, source_target_pairs={{0,2},{1,3},{2,0},{3,1},{4,6},{5,7},{6,4},{7,5},{8,10},{9,11},{10,... | collective-permute-start | bytes 3981320 | tf_op jit(solution)/shard_map/ppermute | solution.py:37
  896.8 34.1 %collective-permute-start.64 = (bf16[1,576,1152]{2,1,0:T(8,128)(2,1)}, bf16[1,576,1152]{2,1,0:T(8,128)(2,1)S(1)}, u32[]{:S(2)}, u32[]{:S(2)}) collective-permute-start(bf16[1,576,1152]{2,1,0:T(8,128)(2,1)} %sum_rows.49), channel_id=1, source_target_pairs={{0,4},{4,0},{8,12},{12,8},{16,20},{20,16},{24,28},{28,24},{1,5},{5... | collective-permute-start | bytes 3981320 | tf_op jit(solution)/shard_map/ppermute | solution.py:37
  898.9 35.7 %collective-permute-start.62 = (bf16[2,1152,512]{2,1,0:T(8,128)(2,1)}, bf16[2,1152,512]{2,1,0:T(8,128)(2,1)}, u32[]{:S(2)}, u32[]{:S(2)}) collective-permute-start(bf16[2,1152,512]{2,1,0:T(8,128)(2,1)} %get-tuple-element.1257), channel_id=1, source_target_pairs={{0,1},{1,0},{2,3},{3,2},{4,5},{5,4},{6,7},{7,6},{8,9},{9,8},{10,11... | collective-permute-start | bytes 7077896 | tf_op jit(solution)/shard_map/ppermute | solution.py:37
  907.6 32.4 %all-to-all-start.7 = ((f32[4,1,8064]{2,1,0:T(1,128)}), f32[4,1,8064]{2,1,0:T(1,128)S(1)}, u32[]{:S(2)}, u32[]{:S(2)}) async-start(f32[4,1,8064]{2,1,0:T(1,128)} %copy.166), calls=%async_computation.7 | async-start | bytes 258048 | tf_op jit(solution)/shard_map/all_to_all | solution.py:994
  940.7 35.4 %collective-permute-start.67 = (bf16[1,1152,640]{2,1,0:T(8,128)(2,1)}, bf16[1,1152,640]{2,1,0:T(8,128)(2,1)S(1)}, u32[]{:S(2)}, u32[]{:S(2)}) collective-permute-start(bf16[1,1152,640]{2,1,0:T(8,128)(2,1)} %sum_rows.52), channel_id=1, source_target_pairs={{0,2},{1,3},{2,0},{3,1},{4,6},{5,7},{6,4},{7,5},{8,10},{9,11},{10,... | collective-permute-start | bytes 4423688 | tf_op jit(solution)/shard_map/ppermute | solution.py:37
  946.2 38.4 %collective-permute-start.69 = (bf16[1,288,1152]{2,1,0:T(8,128)(2,1)}, bf16[1,288,1152]{2,1,0:T(8,128)(2,1)}, u32[]{:S(2)}, u32[]{:S(2)}) collective-permute-start(bf16[1,288,1152]{2,1,0:T(8,128)(2,1)} %sum_rows.54), channel_id=1, source_target_pairs={{0,8},{4,12},{8,0},{12,4},{16,24},{20,28},{24,16},{28,20},{1,9},{5... | collective-permute-start | bytes 1990664 | tf_op jit(solution)/shard_map/ppermute | solution.py:37
  946.2 40.6 %collective-permute-start.70 = (bf16[1,288,1152]{2,1,0:T(8,128)(2,1)}, bf16[1,288,1152]{2,1,0:T(8,128)(2,1)}, u32[]{:S(2)}, u32[]{:S(2)}) collective-permute-start(bf16[1,288,1152]{2,1,0:T(8,128)(2,1)} %sum_rows.55), channel_id=1, source_target_pairs={{0,8},{4,12},{8,0},{12,4},{16,24},{20,28},{24,16},{28,20},{1,9},{5... | collective-permute-start | bytes 1990664 | tf_op jit(solution)/shard_map/ppermute | solution.py:37
  950.6 43.8 %all-to-all-start.8 = ((bf16[4,288,512]{2,1,0:T(8,128)(2,1)}), bf16[4,288,512]{2,1,0:T(8,128)(2,1)}, u32[]{:S(2)}, u32[]{:S(2)}) async-start(bf16[4,288,512]{2,1,0:T(8,128)(2,1)} %bitcast.199), calls=%async_computation.8 | async-start | bytes 2359296 | tf_op jit(solution)/shard_map/all_to_all | solution.py:835
  955.2 34.0 %collective-permute-start.68 = (bf16[2,576,512]{2,1,0:T(8,128)(2,1)}, bf16[2,576,512]{2,1,0:T(8,128)(2,1)}, u32[]{:S(2)}, u32[]{:S(2)}) collective-permute-start(bf16[2,576,512]{2,1,0:T(8,128)(2,1)} %sum_rows.53), channel_id=1, source_target_pairs={{0,4},{4,0},{8,12},{12,8},{16,20},{20,16},{24,28},{28,24},{1,5},{5... | collective-permute-start | bytes 3538952 | tf_op jit(solution)/shard_map/ppermute | solution.py:37
  994.3 37.1 %collective-permute-start.78 = (bf16[1,144,1152]{2,1,0:T(8,128)(2,1)}, bf16[1,144,1152]{2,1,0:T(8,128)(2,1)}, u32[]{:S(2)}, u32[]{:S(2)}) collective-permute-start(bf16[1,144,1152]{2,1,0:T(8,128)(2,1)} %sum_rows.58), channel_id=1, source_target_pairs={{0,16},{4,20},{8,24},{12,28},{16,0},{20,4},{24,8},{28,12},{1,17},{... | collective-permute-start | bytes 995336 | tf_op jit(solution)/shard_map/ppermute | solution.py:37
  996.2 35.2 %collective-permute-start.79 = (bf16[1,144,1152]{2,1,0:T(8,128)(2,1)}, bf16[1,144,1152]{2,1,0:T(8,128)(2,1)}, u32[]{:S(2)}, u32[]{:S(2)}) collective-permute-start(bf16[1,144,1152]{2,1,0:T(8,128)(2,1)} %sum_rows.59), channel_id=1, source_target_pairs={{0,16},{4,20},{8,24},{12,28},{16,0},{20,4},{24,8},{28,12},{1,17},{... | collective-permute-start | bytes 995336 | tf_op jit(solution)/shard_map/ppermute | solution.py:37
  997.3 29.0 %collective-permute-start.77 = (bf16[1,576,512]{2,1,0:T(8,128)(2,1)}, bf16[1,576,512]{2,1,0:T(8,128)(2,1)}, u32[]{:S(2)}, u32[]{:S(2)}) collective-permute-start(bf16[1,576,512]{2,1,0:T(8,128)(2,1)} %sum_rows.57), channel_id=1, source_target_pairs={{0,2},{1,3},{2,0},{3,1},{4,6},{5,7},{6,4},{7,5},{8,10},{9,11},{10,... | collective-permute-start | bytes 1769480 | tf_op jit(solution)/shard_map/ppermute | solution.py:37
  997.7 30.6 %collective-permute-start.76 = (bf16[1,576,640]{2,1,0:T(8,128)(2,1)}, bf16[1,576,640]{2,1,0:T(8,128)(2,1)S(1)}, u32[]{:S(2)}, u32[]{:S(2)}) collective-permute-start(bf16[1,576,640]{2,1,0:T(8,128)(2,1)} %sum_rows.56), channel_id=1, source_target_pairs={{0,4},{4,0},{8,12},{12,8},{16,20},{20,16},{24,28},{28,24},{1,5},{5... | collective-permute-start | bytes 2211848 | tf_op jit(solution)/shard_map/ppermute | solution.py:37
  1004.8 42.8 %all-to-all-start.9 = ((bf16[4,288,512]{2,1,0:T(8,128)(2,1)}), bf16[4,288,512]{2,1,0:T(8,128)(2,1)S(1)}, u32[]{:S(2)}, u32[]{:S(2)}) async-start(bf16[4,288,512]{2,1,0:T(8,128)(2,1)} %bitcast.201), calls=%async_computation.9 | async-start | bytes 2359296 | tf_op jit(solution)/shard_map/all_to_all | solution.py:835
  (105 other events, 1750.6 us)

commit v5 on v4

--- a/solution.py
+++ b/solution.py
@@ -162,7 +162,7 @@
         return self.arrays[number][lead, first : first + count]
 
     def sums(self, names, first, count):
-        if self.depth % 16 == 0:
+        if self.depth % 16 == 0 and len(names) * count >= 4 * self.depth:
             leads = [[term[1] for term in terms] for terms in zip(*[self.live[n] for n in names])]
             numbers = [term[0] for term in self.live[names[0]]]
             assert all(list(l) == list(range(l[0], l[0] + len(l))) for l in leads)
@@ -783,6 +783,11 @@
             ]
         return Scatter(stacks[0], stacks[1], rows, parts, kind)
 
+    def scatters(stacks, kind):
+        if len(stacks) == 1:
+            return [scatter(stacks[0], kind)]
+        return [scatter(pair, place) for place, pair in enumerate(stacks)]
+
     def own_share(value):
         return value if relative else lax.dynamic_slice_in_dim(value, lax.axis_index("u") * span, span, 1)
 
@@ -817,6 +822,8 @@
     mixed_cols, out_cols, hidden_cols = (0, 3 * width), (3 * width, 4 * width), (0, hidden_width)
     middle_cut = 4 * width // 256 * 128 + 128
     mixed_cuts = [(0, middle_cut), (middle_cut, 4 * width)]
+    hidden_cut = hidden_width // 256 * 128 + 128
+    fc_cuts = ([hidden_cols], [(0, hidden_cut), (hidden_cut, hidden_width)])
     layouts = (spatial, temporal)
     groups_of = (1, lat_count)
 
@@ -893,16 +900,16 @@
 
     def fc2_grads(b, k, grad):
         low = features_all((mods[b][5] * grad).astype(bf16))
-        stacks, (total_low,), _ = weight_grads([(low, k["act"])], [hidden_cols], "grad_fc2")
-        return {**k, "grad": grad, "low2": low, "sum_b2": own_share(total_low)}, scatter(stacks[0], KINDS[b]["fc2"])
+        stacks, (total_low,), _ = weight_grads([(low, k["act"])], fc_cuts[b], "grad_fc2")
+        return {**k, "grad": grad, "low2": low, "sum_b2": own_share(total_low)}, scatters(stacks, KINDS[b]["fc2"])
 
     def up_back(b, k):
         grad_pre = project(
             k["low2"], weights[b]["fc2"], hidden_cols, [k["slope"]],
             lambda v, s: (v * s.astype(f32),), [bf16], "up_back",
         )[0]
-        stacks, _, (total_pre,) = weight_grads([(k["hidden2"], grad_pre)], [hidden_cols], "grad_fc1")
-        return {**k, "pre": grad_pre, "sum_b1": total_pre[:, 0]}, scatter(stacks[0], KINDS[b]["fc1"])
+        stacks, _, (total_pre,) = weight_grads([(k["hidden2"], grad_pre)], fc_cuts[b], "grad_fc1")
+        return {**k, "pre": grad_pre, "sum_b1": total_pre[:, 0]}, scatters(stacks, KINDS[b]["fc1"])
 
     def hidden2_back(b, k):
         if fused:
@@ -991,8 +998,8 @@
         ]
         packed = jnp.concatenate(pieces, 1)
         sizes = [mods_count * width] + [width] * 6 + [hidden_width] * 2 + [width] * 2
-        packed = lax.all_to_all(packed, "m", split_axis=0, concat_axis=0, tiled=True)
-        return packed, np.cumsum([0] + sizes)
+        sent = lax.all_to_all(packed, "m", split_axis=0, concat_axis=0, tiled=True)
+        return packed, sent, np.cumsum([0] + sizes)
 
     names = ("mixed", "fc1", "fc2")
     gathers = [Gather(shard_of(b, n), rows, parts, KINDS[b][n]) for b in range(2) for n in names]
@@ -1042,60 +1049,77 @@
     move((g[4], last), (g[5], last))
     grad_top = send_positions(top)
     k1 = middle_stage(1, k1)
-    k0, k1, grad_top = fence(g, (k0, k1, grad_top))
+    k0, k1 = fence(g, (k0, k1))
     ready(4)
     ready(5)
     k1 = up_stage(1, k1)
+    grad_top, _ = lax.optimization_barrier((grad_top, k1["act"]))
     k1, s5 = fc2_grads(1, k1, stream_rel(grad_top))
-    k0, k1 = fence([s5], (k0, k1))
-    move((s5, 1))
+
+    def to(count, *lists, after=None):
+        move(*[(s, count) for items in lists for s in items], after=after)
+
+    k0, k1 = fence(s5, (k0, k1))
+    to(1, s5)
     second_out, k1 = down_stage(1, k1)
-    second_out, k1 = lax.optimization_barrier((stream_plain(second_out.astype(bf16)), k1))
+    second_out = stream_plain(second_out.astype(bf16))
+    k0, k1, second_out = fence(s5, (k0, k1, second_out))
+    to(2, s5)
     output = send_frames(second_out)
     k1, s4 = up_back(1, k1)
-    k0, k1, output = fence([s4, s5], (k0, k1, output))
-    move((s4, 1))
+    k0, k1, output = fence(s4 + s5, (k0, k1, output))
+    to(1, s4)
+    to(3, s5)
     k1 = hidden2_back(1, k1)
-    k0, k1 = fence([s4, s5], (k0, k1))
-    move((s5, 2), (s4, 2))
+    k0, k1 = fence(s4 + s5, (k0, k1))
+    to(2, s4)
+    to(4, s5)
     k1 = attention_back(1, k1)
     k1, s3 = mixed_grads(1, k1)
-    k0, k1, output = fence(s3 + [s4, s5], (k0, k1, output.T))
-    move((s5, 3), (s4, 3))
+    k0, k1, output = fence(s3 + s4 + s5, (k0, k1, output.T))
+    to(3, s4)
+    to(last, s5)
     grad_mid, small_time = stream_back(1, k1)
     grad_mid = stream_plain(grad_mid.astype(bf16))
-    k0, grad_mid, small_time, output = fence(s3 + [s4, s5], (k0, grad_mid, small_time, output))
-    move(*[(s, 1) for s in s3])
+    k0, grad_mid, small_time, output = fence(s3 + s4 + s5, (k0, grad_mid, small_time, output))
+    to(1, s3)
     grad_low = send_frames(grad_mid)
-    k0, grad_low, small_time, output = fence(s3 + [s4, s5], (k0, grad_low, small_time, output))
+    k0, grad_low, small_time, output = fence(s3 + s4 + s5, (k0, grad_low, small_time, output))
     k0, s2 = fc2_grads(0, k0, stream_rel(grad_low))
-    move((s2, 1))
+    to(1, s2)
     k0, s1 = up_back(0, k0)
-    move((s5, 4), (s4, 4), *[(s, 2) for s in s3], after=k0["pre"])
-    k0, small_time, output = fence([s1, s2] + s3 + [s4, s5], (k0, small_time, output))
-    move((s5, last), (s4, last), *[(s, 3) for s in s3])
+    to(2, s3, after=k0["pre"])
+    to(4, s4, after=k0["pre"])
+    k0, small_time, output = fence(s1 + s2 + s3 + s4 + s5, (k0, small_time, output))
+    to(last, s4)
+    to(3, s3)
     k0 = hidden2_back(0, k0)
-    move((s1, 1))
-    k0, small_time, output = fence([s1, s2] + s3 + [s4, s5], (k0, small_time, output))
-    move((s2, 2), (s1, 2), *[(s, 4) for s in s3])
+    to(1, s1)
+    k0, small_time, output = fence(s1 + s2 + s3 + s4 + s5, (k0, small_time, output))
+    to(2, s2, s1)
+    to(4, s3)
     k0 = attention_back(0, k0)
     k0, s0 = mixed_grads(0, k0)
     grad_first, small_space = stream_back(0, k0)
-    grad_first, small, output = fence(s0 + [s1, s2] + s3, (grad_first, (small_space, small_time), output))
-    move((s2, 3), (s1, 3), *[(s, last) for s in s3], *[(s, 1) for s in s0])
+    grad_first, small, output = fence(s0 + s1 + s2 + s3, (grad_first, (small_space, small_time), output))
+    to(1, s0)
     small, _ = lax.optimization_barrier((small, s0[0].arrays[1]))
-    packed, counts = pack_small(small[0], small[1])
-    grad_first, packed, output = fence(s0 + [s1, s2] + s3, (grad_first, packed, output))
-    move((s2, 4), (s1, 4), *[(s, 2) for s in s0])
+    made, packed, counts = pack_small(small[0], small[1])
+    to(3, s2, s1, after=made)
+    to(last, s3)
+    grad_first, packed, output = fence(s0 + s1 + s2 + s3, (grad_first, packed, output))
+    to(4, s2, s1)
+    to(2, s0)
     packed, _ = lax.optimization_barrier((packed, s0[0].arrays[-2]))
     output = to_argument(output)
-    output, grad_first = fence(s0 + [s1, s2], (output, grad_first))
-    move((s2, last), (s1, last), *[(s, 3) for s in s0])
-    fence(s0 + [s1, s2], ())
-    for item in s0 + [s1, s2] + s3 + [s4, s5]:
-        move((item, last))
-    weights_space = [jnp.concatenate([s.result() for s in s0], 1), s1.result(), s2.result()]
-    weights_time = [jnp.concatenate([s.result() for s in s3], 1), s4.result(), s5.result()]
+    output, grad_first = fence(s0 + s1 + s2, (output, grad_first))
+    to(last, s2, s1)
+    to(3, s0)
+    fence(s0 + s1 + s2, ())
+    to(last, s0, s1, s2, s3, s4, s5)
+    joined = lambda items: jnp.concatenate([item.result() for item in items], 1)
+    weights_space = [joined(items) for items in (s0, s1, s2)]
+    weights_time = [joined(items) for items in (s3, s4, s5)]
     grad_first = grad_first.astype(bf16)
     grad_first = dot_nt(exchange, grad_first).astype(bf16) if relative else grad_first.T
     grad_latents = to_argument(grad_first).astype(f32)

time: 1080 us -> 1070 us (level)
  other arithmetic: 71.3 us -> 116 us
  waiting for transfers between devices: 354 us -> 317 us
  Pallas kernels: 434 us -> 404 us
  starting transfers between devices: 117 us -> 128 us
    convert_element_type x0 -> x20, other arithmetic: none -> 42.3 us  [sums(): total([self.take(t, first, count) for t in self.live[n]]).astype(bf16)]
    pallas_call x32 -> x20, Pallas kernels: 87.9 us -> 57.5 us  [sum_rows(): pl.pallas_call(body, grid=(names, count // rows), in_specs=[spec(lead) fo...]
    ppermute x84 -> x94, waiting for transfers between devices: 284 us -> 260 us  [swap(): return lax.ppermute(value, axis, [(i, i ^ bit) for i in range(count)])]
    all_to_all x2, waiting for transfers between devices: 38.1 us -> 26.3 us  [send_positions(): return lax.all_to_all(shaped, 'row', 0, 0).reshape(tokens, span)]
    ppermute x84 -> x94, starting transfers between devices: 75.7 us -> 83.7 us  [swap(): return lax.ppermute(value, axis, [(i, i ^ bit) for i in range(count)])]
  transfers between devices with their start and end apart: 94 -> 104, of which waited for: 39 -> 38; matrix products, arithmetic and copies ran while one was open for 12% -> 17% of each run, Pallas kernels for 34% -> 34%
where the time goes in v5:
time: 1070 us; the launch traced here: 1060 us
  Pallas kernels  404 us (38%)
  waiting for transfers between devices  317 us (30%)
  starting transfers between devices  128 us (12%)
  other arithmetic  116 us (11%)
  local copies, waits for them, and re-layouts  56.6 us (5%)
  matrix products  33.7 us (3%)
    ppermute x94, waiting for transfers between devices, swap(): return lax.ppermute(value, axis, [(i, i ^ bit) for i in range(count)])  260 us
    pallas_call x8, Pallas kernels, contract(): pl.pallas_call(body, grid=(parts,), in_specs=[part_spec((tokens, n))] + [...  122 us
    pallas_call x8, Pallas kernels, project(): pl.pallas_call(body, grid=(weight.parts,), in_specs=[whole_spec((tokens,...  89.2 us
    ppermute x94, starting transfers between devices, swap(): return lax.ppermute(value, axis, [(i, i ^ bit) for i in range(count)])  83.7 us
    pallas_call x6, Pallas kernels, weight_grads(): pl.pallas_call(body, grid=(parts,), in_specs=[whole_spec((tokens, depth))...  81.1 us
    pallas_call x20, Pallas kernels, sum_rows(): pl.pallas_call(body, grid=(names, count // rows), in_specs=[spec(lead) fo...  57.5 us
    pallas_call x4, Pallas kernels, attention_call(): pl.pallas_call(functools.partial(kernel, temporal, chunk), grid=grid, in_...  53.7 us
    convert_element_type x20, other arithmetic, sums(): total([self.take(t, first, count) for t in self.live[n]]).astype(bf16)  42.3 us
  transfers between devices with their start and end apart: 104, of which 38 were waited for; matrix products, arithmetic and copies ran while one was open for 17% of the time, Pallas kernels for 34%

profile of v5, /device:TPU:0, one launch (start us, length us, event | category | flops | bytes accessed | tf_op | source)
XLA Modules:
  0.0 1057.6 jit_solution(15315931875783096335)
XLA Ops:
  5.1 4.1 collective-permute-start
  12.4 3.9 all-to-all-start.2
  21.0 4.3 all-to-all-start
  29.8 10.9 %collective-permute-done.8 = f32[4,3456]{1,0:T(4,128)S(1)} collective-permute-done((f32[4,3456]{1,0:T(4,128)S(1)}, f32[4,3456]{1,0:T(4,128)S(1)}, u32[]{:S(2)}, u32[]{:S(2)}) %collective-permute-start.8) | collective-permute-done | bytes 55328 | tf_op jit(solution)/shard_map/ppermute | solution.py:37
  55.4 4.4 all-to-all-start.1
  59.9 11.3 %collective-permute-done.2 = bf16[288,1152]{1,0:T(8,128)(2,1)} collective-permute-done((bf16[288,1152]{1,0:T(8,128)(2,1)S(1)}, bf16[288,1152]{1,0:T(8,128)(2,1)}, u32[]{:S(2)}, u32[]{:S(2)}) %collective-permute-start.2) | collective-permute-done | bytes 663584 | tf_op jit(solution)/shard_map/ppermute | solution.py:37
  72.4 9.1 collective-permute-done.3
  90.7 4.6 fusion.7.refs_5_
  95.3 15.3 %collective-permute-done.6 = bf16[144,1152]{1,0:T(8,128)(2,1)S(1)} collective-permute-done((bf16[144,1152]{1,0:T(8,128)(2,1)}, bf16[144,1152]{1,0:T(8,128)(2,1)S(1)}, u32[]{:S(2)}, u32[]{:S(2)}) %collective-permute-start.6) | collective-permute-done | bytes 331808 | tf_op jit(solution)/shard_map/ppermute | solution.py:37
  110.7 6.0 collective-permute-done.7
  122.1 4.3 collective-permute-done.12.refs_3_
  135.1 9.2 collective-permute-done.15
  145.6 12.4 %collective-permute-done.16 = bf16[288,1152]{1,0:T(8,128)(2,1)S(1)} collective-permute-done((bf16[288,1152]{1,0:T(8,128)(2,1)}, bf16[288,1152]{1,0:T(8,128)(2,1)S(1)}, u32[]{:S(2)}, u32[]{:S(2)}) %collective-permute-start.16) | collective-permute-done | bytes 663584 | tf_op jit(solution)/shard_map/ppermute | solution.py:37
  159.1 22.3 %collective-permute-done.11.refs_2_ = bf16[1152,1152]{1,0:T(8,128)(2,1)} collective-permute-done((bf16[1152,1152]{1,0:T(8,128)(2,1)}, bf16[1152,1152]{1,0:T(8,128)(2,1)}, u32[]{:S(2)}, u32[]{:S(2)}) %collective-permute-start.11) | collective-permute-done | bytes 2654240 | tf_op jit(solution)/shard_map/ppermute | solution.py:37
  181.6 5.3 collective-permute-done.17.refs_4_
  192.0 21.4 %collective-permute-done.21 = bf16[144,1152]{1,0:T(8,128)(2,1)S(1)} collective-permute-done((bf16[144,1152]{1,0:T(8,128)(2,1)S(1)}, bf16[144,1152]{1,0:T(8,128)(2,1)S(1)}, u32[]{:S(2)}, u32[]{:S(2)}) %collective-permute-start.21) | collective-permute-done | bytes 331808 | tf_op jit(solution)/shard_map/ppermute | solution.py:37
  213.4 6.2 collective-permute-done.22
  236.2 10.0 qkv.2
  246.2 13.3 %attend.2 = (bf16[4,2,256,288]{3,2,1,0:T(8,128)(2,1)}, f32[4,2,4,256]{3,2,1,0:T(4,128)}) custom-call(bf16[4,2,256,864]{3,2,1,0:T(8,128)(2,1)} %bitcast.200), custom_call_target="tpu_custom_call" | custom-call | flops 1073741824 | bytes 4718592 | tf_op jit(solution)/shard_map/attend/pallas_call | solution.py:670
  259.5 15.2 %out.2 = (f32[512,1152]{1,0:T(8,128)}, f32[512,1152]{1,0:T(8,128)}, f32[512,1152]{1,0:T(8,128)}, f32[512,1]{1,0:T(8,128)}, bf16[512,1152]{1,0:T(8,128)(2,1)}) custom-call(bf16[4,512,288]{2,1,0:T(8,128)(2,1)} %bitcast.204, bf16[1152,1152]{1,0:T(8,128)(2,1)} %pad_maximum_fusion.refs_1_, bf16[1152,1152]{1,0:T(8,128)(2,1)} %collective-permute-done.11.refs_2_, ...), custom_call_target="tpu_custom_call" | custom-call | flops 1358954496 | bytes 8552448 | tf_op jit(solution)/shard_map/out/pallas_call | solution.py:396
  278.3 6.7 collective-permute-done.23.refs_2_
  291.7 15.3 %up.2 = (bf16[4,512,1152]{2,1,0:T(8,128)(2,1)}, bf16[4,512,1152]{2,1,0:T(8,128)(2,1)}) custom-call(bf16[512,1152]{1,0:T(8,128)(2,1)} %get-tuple-element.1275.refs_0_, bf16[1152,1152]{1,0:T(8,128)(2,1)} %pad_maximum_fusion.1.refs_1_, bf16[1152,1152]{1,0:T(8,128)(2,1)} %collective-permute-done.13.refs_2_, bf16[1152,1152]{1,0:T(8,128)(2,1)} %collective-permute-done.14.refs_3_, ...), custom_call_target="tpu_custom_call" | custom-call | flops 5435817984 | bytes 20054016 | tf_op jit(solution)/shard_map/up/pallas_call | solution.py:322
  307.0 11.7 %collective-permute-done.31 = bf16[576,1152]{1,0:T(8,128)(2,1)} collective-permute-done((bf16[576,1152]{1,0:T(8,128)(2,1)S(1)}, bf16[576,1152]{1,0:T(8,128)(2,1)}, u32[]{:S(2)}, u32[]{:S(2)}) %collective-permute-start.31) | collective-permute-done | bytes 1327136 | tf_op jit(solution)/shard_map/ppermute | solution.py:37
  324.7 13.8 %down.2 = (f32[512,1152]{1,0:T(8,128)}, bf16[512,1152]{1,0:T(8,128)(2,1)}) custom-call(bf16[4,512,1152]{2,1,0:T(8,128)(2,1)} %get-tuple-element.1280.refs_0_.refs_1_, bf16[1152,1152]{1,0:T(8,128)(2,1)} %pad_maximum_fusion.2.refs_1_, bf16[1152,1152]{1,0:T(8,128)(2,1)} %collective-permute-done.23.refs_2_, bf16[1152,1152]{1,0:T(8,128)(2,1)} %collective-permute-done.24.refs_3_, ...), custom_call_target="tpu_custom_call" | custom-call | flops 5435817984 | bytes 20054016 | tf_op jit(solution)/shard_map/down/pallas_call | solution.py:396
  349.6 26.3 %all-to-all-done.3 = bf16[8,2,32,1152]{3,2,1,0:T(8,128)(2,1)S(1)} async-done(((bf16[8,2,32,1152]{3,2,1,0:T(8,128)(2,1)}), bf16[8,2,32,1152]{3,2,1,0:T(8,128)(2,1)S(1)}, u32[]{:S(2)}, u32[]{:S(2)}) %all-to-all-start.3) | async-done | bytes 1179680 | tf_op jit(solution)/shard_map/all_to_all | solution.py:759
  380.7 10.1 qkv.3
  390.8 13.4 %attend.3 = (bf16[4,1,16,32,288]{4,3,2,1,0:T(8,128)(2,1)}, f32[4,2,4,256]{3,2,1,0:T(4,128)}) custom-call(bf16[4,1,16,32,864]{4,3,2,1,0:T(8,128)(2,1)} %bitcast.202), custom_call_target="tpu_custom_call" | custom-call | flops 1073741824 | bytes 4718592 | tf_op jit(solution)/shard_map/attend/pallas_call | solution.py:670
  406.8 12.5 %collective-permute-done.35.refs_2_ = bf16[1152,1152]{1,0:T(8,128)(2,1)} collective-permute-done((bf16[1152,1152]{1,0:T(8,128)(2,1)}, bf16[1152,1152]{1,0:T(8,128)(2,1)}, u32[]{:S(2)}, u32[]{:S(2)}) %collective-permute-start.35) | collective-permute-done | bytes 2654240 | tf_op jit(solution)/shard_map/ppermute | solution.py:37
  419.3 5.2 collective-permute-done.37.refs_4_
  428.9 4.8 all-to-all-start.4
  434.4 15.2 %out.3 = (f32[512,1152]{1,0:T(8,128)}, f32[512,1152]{1,0:T(8,128)}, f32[512,1152]{1,0:T(8,128)}, f32[512,1]{1,0:T(8,128)}, bf16[512,1152]{1,0:T(8,128)(2,1)}) custom-call(bf16[4,512,288]{2,1,0:T(8,128)(2,1)} %bitcast.206, bf16[1152,1152]{1,0:T(8,128)(2,1)} %pad_maximum_fusion.3.refs_1_, bf16[1152,1152]{1,0:T(8,128)(2,1)} %collective-permute-done.25.refs_2_, ...), custom_call_target="tpu_custom_call" | custom-call | flops 1358954496 | bytes 8552448 | tf_op jit(solution)/shard_map/out/pallas_call | solution.py:396
  449.7 14.9 %up.3 = (bf16[4,512,1152]{2,1,0:T(8,128)(2,1)}, bf16[4,512,1152]{2,1,0:T(8,128)(2,1)}) custom-call(bf16[512,1152]{1,0:T(8,128)(2,1)} %get-tuple-element.1043.refs_0_, bf16[1152,1152]{1,0:T(8,128)(2,1)} %pad_maximum_fusion.4.refs_1_, bf16[1152,1152]{1,0:T(8,128)(2,1)} %collective-permute-done.33.refs_2_, bf16[1152,1152]{1,0:T(8,128)(2,1)} %collective-permute-done.34.refs_3_, ...), custom_call_target="tpu_custom_call" | custom-call | flops 5435817984 | bytes 20054016 | tf_op jit(solution)/shard_map/up/pallas_call | solution.py:322
  468.2 12.6 %grad_fc2.2 = (bf16[2,1152,640]{2,1,0:T(8,128)(2,1)}, bf16[2,1152,512]{2,1,0:T(8,128)(2,1)}, bf16[2,1152,640]{2,1,0:T(8,128)(2,1)}, bf16[2,1152,512]{2,1,0:T(8,1...) custom-call(bf16[512,1152]{1,0:T(8,128)(2,1)} %get-tuple-element.1044.refs_0_, ...), custom_call_target="tpu_custom_call" | custom-call | flops 5435817984 | bytes 15335424 | tf_op jit(solution)/shard_map/grad_fc2/pallas_call | solution.py:539
  482.1 13.7 %down.3 = (f32[512,1152]{1,0:T(8,128)}, bf16[512,1152]{1,0:T(8,128)(2,1)}) custom-call(bf16[4,512,1152]{2,1,0:T(8,128)(2,1)} %get-tuple-element.1021.refs_1_.refs_0_, bf16[1152,1152]{1,0:T(8,128)(2,1)} %pad_maximum_fusion.5.refs_1_, bf16[1152,1152]{1,0:T(8,128)(2,1)} %collective-permute-done.35.refs_2_, bf16[1152,1152]{1,0:T(8,128)(2,1)} %collective-permute-done.36.refs_3_, ...), custom_call_target="tpu_custom_call" | custom-call | flops 5435817984 | bytes 20054016 | tf_op jit(solution)/shard_map/down/pallas_call | solution.py:396
  495.8 4.2 fusion.9
  505.5 6.2 all-to-all-start.5
  514.4 12.0 %up_back.2.refs_1_.refs_0_ = bf16[4,512,1152]{2,1,0:T(8,128)(2,1)} custom-call(bf16[512,1152]{1,0:T(8,128)(2,1)} %get-tuple-element.1044.refs_0_, bf16[1152,1152]{1,0:T(8,128)(2,1)} %pad_maximum_fusion.5.refs_1_, bf16[1152,1152]{1,0:T(8,128)(2,1)} %collective-permute-done.35.refs_2_, bf16[1152,1152]{1,0:T(8,128)(2,1)} %collective-permute-done.36.refs_3_, ...), custom_call_target="tpu_custom_call" | custom-call | flops 5435817984 | bytes 20054016 | tf_op jit(solution)/shard_map/up_back/pallas_call | solution.py:322
  526.5 12.7 %grad_fc1.2 = (bf16[2,1152,640]{2,1,0:T(8,128)(2,1)}, bf16[2,1152,512]{2,1,0:T(8,128)(2,1)}, bf16[2,1152,640]{2,1,0:T(8,128)(2,1)}, bf16[2,1152,512]{2,1,0:T(8,1...) custom-call(bf16[512,1152]{1,0:T(8,128)(2,1)} %get-tuple-element.1043.refs_0_, ...), custom_call_target="tpu_custom_call" | custom-call | flops 5435817984 | bytes 15335424 | tf_op jit(solution)/shard_map/grad_fc1/pallas_call | solution.py:539
  539.9 12.4 %collective-permute-done.42.refs_2_ = bf16[2,576,512]{2,1,0:T(8,128)(2,1)} collective-permute-done((bf16[2,576,512]{2,1,0:T(8,128)(2,1)}, bf16[2,576,512]{2,1,0:T(8,128)(2,1)}, u32[]{:S(2)}, u32[]{:S(2)}) %collective-permute-start.42) | collective-permute-done | bytes 1179680 | tf_op jit(solution)/shard_map/ppermute | solution.py:37
  561.6 17.2 %hidden2_back.2 = (f32[512,1152]{1,0:T(8,128)}, bf16[512,1152]{1,0:T(8,128)(2,1)}, f32[3,1152]{1,0:T(4,128)}) custom-call(bf16[4,512,1152]{2,1,0:T(8,128)(2,1)} %up_back.2.refs_1_.refs_0_, bf16[1152,1152]{1,0:T(8,128)(2,1)} %pad_maximum_fusion.4.refs_1_, bf16[1152,1152]{1,0:T(8,128)(2,1)} %collective-permute-done.33.refs_2_, ...), custom_call_target="tpu_custom_call" | custom-call | flops 5435817984 | bytes 27131904 | tf_op jit(solution)/shard_map/hidden2_back/pallas_call | solution.py:396
  593.7 7.5 out_back.2
  601.2 13.6 %attend_back.2 = bf16[4,1,16,32,864]{4,3,2,1,0:T(8,128)(2,1)} custom-call(bf16[4,1,16,32,864]{4,3,2,1,0:T(8,128)(2,1)} %bitcast.203, bf16[4,1,16,32,288]{4,3,2,1,0:T(8,128)(2,1)} %bitcast.208, bf16[4,1,16,32,288]{4,3,2,1,0:T(8,128)(2,1)} %get-tuple-element.929, f32[4,2,4,256]{3,2,1,0:T(4,128)} %get-tuple-element.1129.logs), custom_call_target="tpu_custom_call" | custom-call | flops 2684354560 | bytes 14155776 | tf_op jit(solution)/shard_map/attend_back/pallas_call | solution.py:670
  614.9 15.3 %grad_mixed.2 = (bf16[2,1152,640]{2,1,0:T(8,128)(2,1)}, bf16[2,1152,512]{2,1,0:T(8,128)(2,1)}, bf16[2,1152,640]{2,1,0:T(8,128)(2,1)}, bf16[2,1152,512]{2,1,0:T(8...) custom-call(bf16[512,1152]{1,0:T(8,128)(2,1)} %get-tuple-element.1125.refs_0_, ...), custom_call_target="tpu_custom_call" | custom-call | flops 5435817984 | bytes 15335424 | tf_op jit(solution)/shard_map/grad_mixed/pallas_call | solution.py:539
  644.7 14.7 %hidden_back.2 = (bf16[512,1152]{1,0:T(8,128)(2,1)}, f32[2,1152]{1,0:T(2,128)}) custom-call(bf16[4,512,864]{2,1,0:T(8,128)(2,1)} %bitcast.197, bf16[1152,1152]{1,0:T(8,128)(2,1)} %pad_maximum_fusion.3.refs_1_, bf16[1152,1152]{1,0:T(8,128)(2,1)} %collective-permute-done.25.refs_2_, bf16[1152,1152]{1,0:T(8,128)(2,1)} %collective-permute-done.26.refs_3_, ...), custom_call_target="tpu_custom_call" | custom-call | flops 4076863488 | bytes 20938752 | tf_op jit(solution)/shard_map/hidden_back/pallas_call | solution.py:396
  659.5 4.2 fusion.10
  668.6 5.9 all-to-all-start.6
  674.6 28.8 %all-to-all-done.6 = bf16[8,2,32,1152]{3,2,1,0:T(8,128)(2,1)} async-done(((bf16[8,2,32,1152]{3,2,1,0:T(8,128)(2,1)}), bf16[8,2,32,1152]{3,2,1,0:T(8,128)(2,1)}, u32[]{:S(2)}, u32[]{:S(2)}) %all-to-all-start.6) | async-done | bytes 1179680 | tf_op jit(solution)/shard_map/all_to_all | solution.py:763
  711.2 5.0 multiply_convert_fusion
  716.2 12.7 %grad_fc2.3 = (bf16[2,1152,1152]{2,1,0:T(8,128)(2,1)}, bf16[2,1152,1152]{2,1,0:T(8,128)(2,1)}, f32[1,1152]{1,0:T(1,128)}, f32[4,1,1152]{2,1,0:T(1,128)}) custom-call(bf16[512,1152]{1,0:T(8,128)(2,1)} %get-tuple-element.1741.refs_0_, bf16[4,512,1152]{2,1,0:T(8,128)(2,1)} %get-tuple-element.1280.refs_0_.refs_1_), custom_call_target="tpu_custom_call" | custom-call | flops 5435817984 | bytes 15335424 | tf_op jit(solution)/shard_map/grad_fc2/pallas_call | solution.py:539
  731.9 12.0 %up_back.3.refs_1_.refs_0_ = bf16[4,512,1152]{2,1,0:T(8,128)(2,1)} custom-call(bf16[512,1152]{1,0:T(8,128)(2,1)} %get-tuple-element.1741.refs_0_, bf16[1152,1152]{1,0:T(8,128)(2,1)} %pad_maximum_fusion.2.refs_1_, bf16[1152,1152]{1,0:T(8,128)(2,1)} %collective-permute-done.23.refs_2_, bf16[1152,1152]{1,0:T(8,128)(2,1)} %collective-permute-done.24.refs_3_, ...), custom_call_target="tpu_custom_call" | custom-call | flops 5435817984 | bytes 20054016 | tf_op jit(solution)/shard_map/up_back/pallas_call | solution.py:322
  746.0 12.8 %grad_fc1.3 = (bf16[2,1152,1152]{2,1,0:T(8,128)(2,1)}, bf16[2,1152,1152]{2,1,0:T(8,128)(2,1)}, f32[1,1152]{1,0:T(1,128)}, f32[4,1,1152]{2,1,0:T(1,128)}) custom-call(bf16[512,1152]{1,0:T(8,128)(2,1)} %get-tuple-element.1275.refs_0_, bf16[4,512,1152]{2,1,0:T(8,128)(2,1)} %up_back.3.refs_1_.refs_0_), custom_call_target="tpu_custom_call" | custom-call | flops 5435817984 | bytes 15335424 | tf_op jit(solution)/shard_map/grad_fc1/pallas_call | solution.py:539
  770.6 4.0 sum_rows.30
  778.6 17.5 %hidden2_back.3 = (f32[512,1152]{1,0:T(8,128)}, bf16[512,1152]{1,0:T(8,128)(2,1)}, f32[3,1152]{1,0:T(4,128)}) custom-call(bf16[4,512,1152]{2,1,0:T(8,128)(2,1)} %up_back.3.refs_1_.refs_0_, bf16[1152,1152]{1,0:T(8,128)(2,1)} %pad_maximum_fusion.1.refs_1_, bf16[1152,1152]{1,0:T(8,128)(2,1)} %collective-permute-done.13.refs_2_, ...), custom_call_target="tpu_custom_call" | custom-call | flops 5435817984 | bytes 27131904 | tf_op jit(solution)/shard_map/hidden2_back/pallas_call | solution.py:396
  811.1 7.5 out_back.3
  818.6 13.4 %attend_back.3 = bf16[4,2,256,864]{3,2,1,0:T(8,128)(2,1)} custom-call(bf16[4,2,256,864]{3,2,1,0:T(8,128)(2,1)} %bitcast.201, bf16[4,2,256,288]{3,2,1,0:T(8,128)(2,1)} %bitcast.209, bf16[4,2,256,288]{3,2,1,0:T(8,128)(2,1)} %get-tuple-element.863, f32[4,2,4,256]{3,2,1,0:T(4,128)} %get-tuple-element.1405.logs), custom_call_target="tpu_custom_call" | custom-call | flops 2684354560 | bytes 14155776 | tf_op jit(solution)/shard_map/attend_back/pallas_call | solution.py:670
  832.1 14.9 %grad_mixed.3 = (bf16[2,1152,640]{2,1,0:T(8,128)(2,1)}, bf16[2,1152,512]{2,1,0:T(8,128)(2,1)}, bf16[2,1152,640]{2,1,0:T(8,128)(2,1)}, bf16[2,1152,512]{2,1,0:T(8...) custom-call(bf16[512,1152]{1,0:T(8,128)(2,1)} %get-tuple-element.1401.refs_0_, ...), custom_call_target="tpu_custom_call" | custom-call | flops 5435817984 | bytes 15335424 | tf_op jit(solution)/shard_map/grad_mixed/pallas_call | solution.py:539
  847.0 15.1 %hidden_back.3 = (bf16[512,1152]{1,0:T(8,128)(2,1)}, f32[2,1152]{1,0:T(2,128)}) custom-call(bf16[4,512,864]{2,1,0:T(8,128)(2,1)} %bitcast.199, bf16[1152,1152]{1,0:T(8,128)(2,1)} %pad_maximum_fusion.refs_1_, bf16[1152,1152]{1,0:T(8,128)(2,1)} %collective-permute-done.11.refs_2_, bf16[1152,1152]{1,0:T(8,128)(2,1)} %collective-permute-done.12.refs_3_, ...), custom_call_target="tpu_custom_call" | custom-call | flops 4076863488 | bytes 20938752 | tf_op jit(solution)/shard_map/hidden_back/pallas_call | solution.py:396
  899.6 10.1 collective-permute-done.73
  910.9 3.9 all-to-all-start.7
  944.9 14.9 %collective-permute-done.77.refs_2_ = bf16[1,1152,640]{2,1,0:T(8,128)(2,1)} collective-permute-done((bf16[1,1152,640]{2,1,0:T(8,128)(2,1)}, bf16[1,1152,640]{2,1,0:T(8,128)(2,1)}, u32[]{:S(2)}, u32[]{:S(2)}) %collective-permute-start.77) | collective-permute-done | bytes 1474592 | tf_op jit(solution)/shard_map/ppermute | solution.py:37
  975.1 4.0 fusion.11
  995.1 16.3 %collective-permute-done.84 = f32[4,1,144]{2,0,1:T(4,128)S(1)} collective-permute-done((f32[4,1,144]{2,0,1:T(4,128)S(1)}, f32[4,1,144]{2,0,1:T(4,128)S(1)}, u32[]{:S(2)}, u32[]{:S(2)}) %collective-permute-start.84) | collective-permute-done | bytes 2336 | tf_op jit(solution)/shard_map/ppermute | solution.py:37
  1031.5 7.3 collective-permute-done.90
  1042.4 7.9 collective-permute-done.91
  (573 shorter events, 351.6 us)
Async XLA Ops:
  5.1 45.3 %collective-permute-start = (bf16[144,1152]{1,0:T(8,128)(2,1)S(1)}, bf16[144,1152]{1,0:T(8,128)(2,1)}, u32[]{:S(2)}, u32[]{:S(2)}) collective-permute-start(bf16[144,1152]{1,0:T(8,128)(2,1)S(1)} %pad_maximum_fusion.24), channel_id=1, source_target_pairs={{0,16},{4,20},{8,24},{12,28},{16,0},{20,4},{24,8},{28,12},{1,17},{... | collective-permute-start | bytes 995336 | tf_op jit(solution)/shard_map/ppermute | solution.py:37
  10.0 41.4 %collective-permute-start.1 = (bf16[144,1152]{1,0:T(8,128)(2,1)S(1)}, bf16[144,1152]{1,0:T(8,128)(2,1)}, u32[]{:S(2)}, u32[]{:S(2)}) collective-permute-start(bf16[144,1152]{1,0:T(8,128)(2,1)S(1)} %get-tuple-element.1690), channel_id=1, source_target_pairs={{0,16},{4,20},{8,24},{12,28},{16,0},{20,4},{24,8},{28,12},{1,17},{... | collective-permute-start | bytes 995336 | tf_op jit(solution)/shard_map/ppermute | solution.py:37
  21.0 34.4 %all-to-all-start = ((bf16[4,288,512]{2,1,0:T(8,128)(2,1)}), bf16[4,288,512]{2,1,0:T(8,128)(2,1)}, u32[]{:S(2)}, u32[]{:S(2)}) async-start(bf16[4,288,512]{2,1,0:T(8,128)(2,1)} %param.17), calls=%async_computation | async-start | bytes 2359296 | tf_op jit(solution)/shard_map/all_to_all | solution.py:836
  54.0 27.5 %collective-permute-start.3 = (bf16[288,1152]{1,0:T(8,128)(2,1)}, bf16[288,1152]{1,0:T(8,128)(2,1)}, u32[]{:S(2)}, u32[]{:S(2)}) collective-permute-start(bf16[288,1152]{1,0:T(8,128)(2,1)} %pad_maximum_fusion.16), channel_id=1, source_target_pairs={{0,8},{4,12},{8,0},{12,4},{16,24},{20,28},{24,16},{28,20},{1,9},{5... | collective-permute-start | bytes 1990664 | tf_op jit(solution)/shard_map/ppermute | solution.py:37
  55.4 28.6 %all-to-all-start.1 = ((bf16[4,288,512]{2,1,0:T(8,128)(2,1)}), bf16[4,288,512]{2,1,0:T(8,128)(2,1)}, u32[]{:S(2)}, u32[]{:S(2)}) async-start(bf16[4,288,512]{2,1,0:T(8,128)(2,1)} %param.29), calls=%async_computation.1 | async-start | bytes 2359296 | tf_op jit(solution)/shard_map/all_to_all | solution.py:836
  84.0 33.6 %collective-permute-start.4 = (bf16[576,1152]{1,0:T(8,128)(2,1)S(1)}, bf16[576,1152]{1,0:T(8,128)(2,1)S(1)}, u32[]{:S(2)}, u32[]{:S(2)}) collective-permute-start(bf16[576,1152]{1,0:T(8,128)(2,1)S(1)} %pad_maximum_fusion.7), channel_id=1, source_target_pairs={{0,4},{4,0},{8,12},{12,8},{16,20},{20,16},{24,28},{28,24},{1,5},{5... | collective-permute-start | bytes 3981320 | tf_op jit(solution)/shard_map/ppermute | solution.py:37
  85.9 33.4 %collective-permute-start.5 = (bf16[576,1152]{1,0:T(8,128)(2,1)}, bf16[576,1152]{1,0:T(8,128)(2,1)S(1)}, u32[]{:S(2)}, u32[]{:S(2)}) collective-permute-start(bf16[576,1152]{1,0:T(8,128)(2,1)} %pad_maximum_fusion.8), channel_id=1, source_target_pairs={{0,2},{1,3},{2,0},{3,1},{4,6},{5,7},{6,4},{7,5},{8,10},{9,11},{10,... | collective-permute-start | bytes 3981320 | tf_op jit(solution)/shard_map/ppermute | solution.py:37
  90.7 26.0 %collective-permute-start.7 = (bf16[144,1152]{1,0:T(8,128)(2,1)}, bf16[144,1152]{1,0:T(8,128)(2,1)S(1)}, u32[]{:S(2)}, u32[]{:S(2)}) collective-permute-start(bf16[144,1152]{1,0:T(8,128)(2,1)} %pad_maximum_fusion.25), channel_id=1, source_target_pairs={{0,16},{4,20},{8,24},{12,28},{16,0},{20,4},{24,8},{28,12},{1,17},{... | collective-permute-start | bytes 995336 | tf_op jit(solution)/shard_map/ppermute | solution.py:37
  121.1 60.3 %collective-permute-start.11 = (bf16[1152,1152]{1,0:T(8,128)(2,1)}, bf16[1152,1152]{1,0:T(8,128)(2,1)}, u32[]{:S(2)}, u32[]{:S(2)}) collective-permute-start(bf16[1152,1152]{1,0:T(8,128)(2,1)} %pad_maximum_fusion.refs_1_), channel_id=1, source_target_pairs={{0,2},{1,3},{2,0},{3,1},{4,6},{5,7},{6,4},{7,5},{8,10},{9,11},{10,... | collective-permute-start | bytes 7962632 | tf_op jit(solution)/shard_map/ppermute | solution.py:37
  121.6 60.0 %collective-permute-start.13 = (bf16[1152,1152]{1,0:T(8,128)(2,1)}, bf16[1152,1152]{1,0:T(8,128)(2,1)}, u32[]{:S(2)}, u32[]{:S(2)}) collective-permute-start(bf16[1152,1152]{1,0:T(8,128)(2,1)} %pad_maximum_fusion.1.refs_1_), channel_id=1, source_target_pairs={{0,4},{4,0},{8,12},{12,8},{16,20},{20,16},{24,28},{28,24},{1,5},{5... | collective-permute-start | bytes 7962632 | tf_op jit(solution)/shard_map/ppermute | solution.py:37
  126.4 55.3 %collective-permute-start.14 = (bf16[1152,1152]{1,0:T(8,128)(2,1)}, bf16[1152,1152]{1,0:T(8,128)(2,1)}, u32[]{:S(2)}, u32[]{:S(2)}) collective-permute-start(bf16[1152,1152]{1,0:T(8,128)(2,1)} %pad_maximum_fusion.1.refs_1_), channel_id=1, source_target_pairs={{0,1},{1,0},{2,3},{3,2},{4,5},{5,4},{6,7},{7,6},{8,9},{9,8},{10,11... | collective-permute-start | bytes 7962632 | tf_op jit(solution)/shard_map/ppermute | solution.py:37
  127.4 30.6 %collective-permute-start.16 = (bf16[288,1152]{1,0:T(8,128)(2,1)}, bf16[288,1152]{1,0:T(8,128)(2,1)S(1)}, u32[]{:S(2)}, u32[]{:S(2)}) collective-permute-start(bf16[288,1152]{1,0:T(8,128)(2,1)} %pad_maximum_fusion.18), channel_id=1, source_target_pairs={{0,8},{4,12},{8,0},{12,4},{16,24},{20,28},{24,16},{28,20},{1,9},{5... | collective-permute-start | bytes 1990664 | tf_op jit(solution)/shard_map/ppermute | solution.py:37
  186.9 37.0 %collective-permute-start.18 = (bf16[1152,1152]{1,0:T(8,128)(2,1)}, bf16[1152,1152]{1,0:T(8,128)(2,1)}, u32[]{:S(2)}, u32[]{:S(2)}) collective-permute-start(bf16[1152,1152]{1,0:T(8,128)(2,1)} %collective-permute-done.13.refs_2_), channel_id=1, source_target_pairs={{0,1},{1,0},{2,3},{3,2},{4,5},{5,4},{6,7},{7,6},{8,9},{9,8},{10,11... | collective-permute-start | bytes 7962632 | tf_op jit(solution)/shard_map/ppermute | solution.py:37
  187.1 33.4 %collective-permute-start.19 = (bf16[576,1152]{1,0:T(8,128)(2,1)S(1)}, bf16[576,1152]{1,0:T(8,128)(2,1)S(1)}, u32[]{:S(2)}, u32[]{:S(2)}) collective-permute-start(bf16[576,1152]{1,0:T(8,128)(2,1)S(1)} %pad_maximum_fusion.9), channel_id=1, source_target_pairs={{0,4},{4,0},{8,12},{12,8},{16,20},{20,16},{24,28},{28,24},{1,5},{5... | collective-permute-start | bytes 3981320 | tf_op jit(solution)/shard_map/ppermute | solution.py:37
  187.6 34.6 %collective-permute-start.20 = (bf16[576,1152]{1,0:T(8,128)(2,1)S(1)}, bf16[576,1152]{1,0:T(8,128)(2,1)S(1)}, u32[]{:S(2)}, u32[]{:S(2)}) collective-permute-start(bf16[576,1152]{1,0:T(8,128)(2,1)S(1)} %pad_maximum_fusion.10), channel_id=1, source_target_pairs={{0,2},{1,3},{2,0},{3,1},{4,6},{5,7},{6,4},{7,5},{8,10},{9,11},{10,... | collective-permute-start | bytes 3981320 | tf_op jit(solution)/shard_map/ppermute | solution.py:37
  189.1 30.5 %collective-permute-start.22 = (bf16[144,1152]{1,0:T(8,128)(2,1)S(1)}, bf16[144,1152]{1,0:T(8,128)(2,1)S(1)}, u32[]{:S(2)}, u32[]{:S(2)}) collective-permute-start(bf16[144,1152]{1,0:T(8,128)(2,1)S(1)} %copy-done.16), channel_id=1, source_target_pairs={{0,16},{4,20},{8,24},{12,28},{16,0},{20,4},{24,8},{28,12},{1,17},{... | collective-permute-start | bytes 995336 | tf_op jit(solution)/shard_map/ppermute | solution.py:37
  224.7 60.4 %collective-permute-start.23 = (bf16[1152,1152]{1,0:T(8,128)(2,1)}, bf16[1152,1152]{1,0:T(8,128)(2,1)}, u32[]{:S(2)}, u32[]{:S(2)}) collective-permute-start(bf16[1152,1152]{1,0:T(8,128)(2,1)} %pad_maximum_fusion.2.refs_1_), channel_id=1, source_target_pairs={{0,2},{1,3},{2,0},{3,1},{4,6},{5,7},{6,4},{7,5},{8,10},{9,11},{10,... | collective-permute-start | bytes 7962632 | tf_op jit(solution)/shard_map/ppermute | solution.py:37
  226.2 60.0 %collective-permute-start.25 = (bf16[1152,1152]{1,0:T(8,128)(2,1)}, bf16[1152,1152]{1,0:T(8,128)(2,1)}, u32[]{:S(2)}, u32[]{:S(2)}) collective-permute-start(bf16[1152,1152]{1,0:T(8,128)(2,1)} %pad_maximum_fusion.3.refs_1_), channel_id=1, source_target_pairs={{0,4},{4,0},{8,12},{12,8},{16,20},{20,16},{24,28},{28,24},{1,5},{5... | collective-permute-start | bytes 7962632 | tf_op jit(solution)/shard_map/ppermute | solution.py:37
  229.3 57.0 %collective-permute-start.26 = (bf16[1152,1152]{1,0:T(8,128)(2,1)}, bf16[1152,1152]{1,0:T(8,128)(2,1)}, u32[]{:S(2)}, u32[]{:S(2)}) collective-permute-start(bf16[1152,1152]{1,0:T(8,128)(2,1)} %pad_maximum_fusion.3.refs_1_), channel_id=1, source_target_pairs={{0,1},{1,0},{2,3},{3,2},{4,5},{5,4},{6,7},{7,6},{8,9},{9,8},{10,11... | collective-permute-start | bytes 7962632 | tf_op jit(solution)/shard_map/ppermute | solution.py:37
  232.7 41.9 %collective-permute-start.27 = (bf16[288,1152]{1,0:T(8,128)(2,1)S(1)}, bf16[288,1152]{1,0:T(8,128)(2,1)}, u32[]{:S(2)}, u32[]{:S(2)}) collective-permute-start(bf16[288,1152]{1,0:T(8,128)(2,1)S(1)} %pad_maximum_fusion.19), channel_id=1, source_target_pairs={{0,8},{4,12},{8,0},{12,4},{16,24},{20,28},{24,16},{28,20},{1,9},{5... | collective-permute-start | bytes 1990664 | tf_op jit(solution)/shard_map/ppermute | solution.py:37
  234.5 41.4 %collective-permute-start.28 = (bf16[288,1152]{1,0:T(8,128)(2,1)}, bf16[288,1152]{1,0:T(8,128)(2,1)}, u32[]{:S(2)}, u32[]{:S(2)}) collective-permute-start(bf16[288,1152]{1,0:T(8,128)(2,1)} %pad_maximum_fusion.20), channel_id=1, source_target_pairs={{0,8},{4,12},{8,0},{12,4},{16,24},{20,28},{24,16},{28,20},{1,9},{5... | collective-permute-start | bytes 1990664 | tf_op jit(solution)/shard_map/ppermute | solution.py:37
  287.0 31.7 %collective-permute-start.31 = (bf16[576,1152]{1,0:T(8,128)(2,1)S(1)}, bf16[576,1152]{1,0:T(8,128)(2,1)}, u32[]{:S(2)}, u32[]{:S(2)}) collective-permute-start(bf16[576,1152]{1,0:T(8,128)(2,1)S(1)} %pad_maximum_fusion.11), channel_id=1, source_target_pairs={{0,4},{4,0},{8,12},{12,8},{16,20},{20,16},{24,28},{28,24},{1,5},{5... | collective-permute-start | bytes 3981320 | tf_op jit(solution)/shard_map/ppermute | solution.py:37
  288.7 33.0 %collective-permute-start.32 = (bf16[576,1152]{1,0:T(8,128)(2,1)}, bf16[576,1152]{1,0:T(8,128)(2,1)}, u32[]{:S(2)}, u32[]{:S(2)}) collective-permute-start(bf16[576,1152]{1,0:T(8,128)(2,1)} %pad_maximum_fusion.12), channel_id=1, source_target_pairs={{0,2},{1,3},{2,0},{3,1},{4,6},{5,7},{6,4},{7,5},{8,10},{9,11},{10,... | collective-permute-start | bytes 3981320 | tf_op jit(solution)/shard_map/ppermute | solution.py:37
  291.5 50.1 %collective-permute-start.30 = (bf16[1152,1152]{1,0:T(8,128)(2,1)}, bf16[1152,1152]{1,0:T(8,128)(2,1)}, u32[]{:S(2)}, u32[]{:S(2)}) collective-permute-start(bf16[1152,1152]{1,0:T(8,128)(2,1)} %collective-permute-done.25.refs_2_), channel_id=1, source_target_pairs={{0,1},{1,0},{2,3},{3,2},{4,5},{5,4},{6,7},{7,6},{8,9},{9,8},{10,11... | collective-permute-start | bytes 7962632 | tf_op jit(solution)/shard_map/ppermute | solution.py:37
  342.9 33.0 %all-to-all-start.3 = ((bf16[8,2,32,1152]{3,2,1,0:T(8,128)(2,1)}), bf16[8,2,32,1152]{3,2,1,0:T(8,128)(2,1)S(1)}, u32[]{:S(2)}, u32[]{:S(2)}) async-start(bf16[8,2,32,1152]{3,2,1,0:T(8,128)(2,1)} %bitcast.189), calls=%async_computation.3 | async-start | bytes 2359296 | tf_op jit(solution)/shard_map/all_to_all | solution.py:759
  346.5 60.3 %collective-permute-start.33 = (bf16[1152,1152]{1,0:T(8,128)(2,1)}, bf16[1152,1152]{1,0:T(8,128)(2,1)}, u32[]{:S(2)}, u32[]{:S(2)}) collective-permute-start(bf16[1152,1152]{1,0:T(8,128)(2,1)} %pad_maximum_fusion.4.refs_1_), channel_id=1, source_target_pairs={{0,2},{1,3},{2,0},{3,1},{4,6},{5,7},{6,4},{7,5},{8,10},{9,11},{10,... | collective-permute-start | bytes 7962632 | tf_op jit(solution)/shard_map/ppermute | solution.py:37
  347.1 72.2 %collective-permute-start.35 = (bf16[1152,1152]{1,0:T(8,128)(2,1)}, bf16[1152,1152]{1,0:T(8,128)(2,1)}, u32[]{:S(2)}, u32[]{:S(2)}) collective-permute-start(bf16[1152,1152]{1,0:T(8,128)(2,1)} %pad_maximum_fusion.5.refs_1_), channel_id=1, source_target_pairs={{0,4},{4,0},{8,12},{12,8},{16,20},{20,16},{24,28},{28,24},{1,5},{5... | collective-permute-start | bytes 7962632 | tf_op jit(solution)/shard_map/ppermute | solution.py:37
  348.9 70.3 %collective-permute-start.36 = (bf16[1152,1152]{1,0:T(8,128)(2,1)}, bf16[1152,1152]{1,0:T(8,128)(2,1)}, u32[]{:S(2)}, u32[]{:S(2)}) collective-permute-start(bf16[1152,1152]{1,0:T(8,128)(2,1)} %pad_maximum_fusion.5.refs_1_), channel_id=1, source_target_pairs={{0,1},{1,0},{2,3},{3,2},{4,5},{5,4},{6,7},{7,6},{8,9},{9,8},{10,11... | collective-permute-start | bytes 7962632 | tf_op jit(solution)/shard_map/ppermute | solution.py:37
  428.9 35.6 %all-to-all-start.4 = ((bf16[8,2,32,1152]{3,2,1,0:T(8,128)(2,1)}), bf16[8,2,32,1152]{3,2,1,0:T(8,128)(2,1)S(1)}, u32[]{:S(2)}, u32[]{:S(2)}) async-start(bf16[8,2,32,1152]{3,2,1,0:T(8,128)(2,1)} %copy.151), calls=%async_computation.4 | async-start | bytes 2359296 | tf_op jit(solution)/shard_map/all_to_all | solution.py:759
  505.5 53.1 %all-to-all-start.5 = ((bf16[8,2,32,1152]{3,2,1,0:T(8,128)(2,1)}), bf16[8,2,32,1152]{3,2,1,0:T(8,128)(2,1)}, u32[]{:S(2)}, u32[]{:S(2)}) async-start(bf16[8,2,32,1152]{3,2,1,0:T(8,128)(2,1)} %bitcast.50), calls=%async_computation.5 | async-start | bytes 2359296 | tf_op jit(solution)/shard_map/all_to_all | solution.py:763
  511.8 43.0 %collective-permute-start.41 = (bf16[1,1152,640]{2,1,0:T(8,128)(2,1)}, bf16[1,1152,640]{2,1,0:T(8,128)(2,1)S(1)}, u32[]{:S(2)}, u32[]{:S(2)}) collective-permute-start(bf16[1,1152,640]{2,1,0:T(8,128)(2,1)} %sum_rows.20), channel_id=1, source_target_pairs={{0,2},{1,3},{2,0},{3,1},{4,6},{5,7},{6,4},{7,5},{8,10},{9,11},{10,... | collective-permute-start | bytes 4423688 | tf_op jit(solution)/shard_map/ppermute | solution.py:37
  512.4 39.9 %collective-permute-start.42 = (bf16[2,576,512]{2,1,0:T(8,128)(2,1)}, bf16[2,576,512]{2,1,0:T(8,128)(2,1)}, u32[]{:S(2)}, u32[]{:S(2)}) collective-permute-start(bf16[2,576,512]{2,1,0:T(8,128)(2,1)} %sum_rows.21), channel_id=1, source_target_pairs={{0,4},{4,0},{8,12},{12,8},{16,20},{20,16},{24,28},{28,24},{1,5},{5... | collective-permute-start | bytes 3538952 | tf_op jit(solution)/shard_map/ppermute | solution.py:37
  588.6 48.7 %collective-permute-start.47 = (bf16[1,1152,640]{2,1,0:T(8,128)(2,1)}, bf16[1,1152,640]{2,1,0:T(8,128)(2,1)}, u32[]{:S(2)}, u32[]{:S(2)}) collective-permute-start(bf16[1,1152,640]{2,1,0:T(8,128)(2,1)} %sum_rows.24), channel_id=1, source_target_pairs={{0,2},{1,3},{2,0},{3,1},{4,6},{5,7},{6,4},{7,5},{8,10},{9,11},{10,... | collective-permute-start | bytes 4423688 | tf_op jit(solution)/shard_map/ppermute | solution.py:37
  590.0 44.8 %collective-permute-start.48 = (bf16[2,576,512]{2,1,0:T(8,128)(2,1)}, bf16[2,576,512]{2,1,0:T(8,128)(2,1)}, u32[]{:S(2)}, u32[]{:S(2)}) collective-permute-start(bf16[2,576,512]{2,1,0:T(8,128)(2,1)} %sum_rows.25), channel_id=1, source_target_pairs={{0,4},{4,0},{8,12},{12,8},{16,20},{20,16},{24,28},{28,24},{1,5},{5... | collective-permute-start | bytes 3538952 | tf_op jit(solution)/shard_map/ppermute | solution.py:37
  591.7 41.1 %collective-permute-start.49 = (bf16[1,288,640]{2,1,0:T(8,128)(2,1)}, bf16[1,288,640]{2,1,0:T(8,128)(2,1)}, u32[]{:S(2)}, u32[]{:S(2)}) collective-permute-start(bf16[1,288,640]{2,1,0:T(8,128)(2,1)} %add_convert_fusion.7), channel_id=1, source_target_pairs={{0,8},{4,12},{8,0},{12,4},{16,24},{20,28},{24,16},{28,20},{1,9},{5... | collective-permute-start | bytes 1105928 | tf_op jit(solution)/shard_map/ppermute | solution.py:37
  593.2 37.7 %collective-permute-start.50 = (bf16[1,288,512]{2,1,0:T(8,128)(2,1)}, bf16[1,288,512]{2,1,0:T(8,128)(2,1)}, u32[]{:S(2)}, u32[]{:S(2)}) collective-permute-start(bf16[1,288,512]{2,1,0:T(8,128)(2,1)} %add_convert_fusion.13), channel_id=1, source_target_pairs={{0,8},{4,12},{8,0},{12,4},{16,24},{20,28},{24,16},{28,20},{1,9},{5... | collective-permute-start | bytes 884744 | tf_op jit(solution)/shard_map/ppermute | solution.py:37
  640.9 27.1 %collective-permute-start.53 = (bf16[1,144,640]{2,1,0:T(8,128)(2,1)}, bf16[1,144,640]{2,1,0:T(8,128)(2,1)S(1)}, u32[]{:S(2)}, u32[]{:S(2)}) collective-permute-start(bf16[1,144,640]{2,1,0:T(8,128)(2,1)} %add_convert_fusion.17), channel_id=1, source_target_pairs={{0,16},{4,20},{8,24},{12,28},{16,0},{20,4},{24,8},{28,12},{1,17},{... | collective-permute-start | bytes 552968 | tf_op jit(solution)/shard_map/ppermute | solution.py:37
  668.0 40.3 %collective-permute-start.55 = (bf16[2,1152,640]{2,1,0:T(8,128)(2,1)}, bf16[2,1152,640]{2,1,0:T(8,128)(2,1)}, u32[]{:S(2)}, u32[]{:S(2)}) collective-permute-start(bf16[2,1152,640]{2,1,0:T(8,128)(2,1)} %get-tuple-element.1226), channel_id=1, source_target_pairs={{0,1},{1,0},{2,3},{3,2},{4,5},{5,4},{6,7},{7,6},{8,9},{9,8},{10,11... | collective-permute-start | bytes 8847368 | tf_op jit(solution)/shard_map/ppermute | solution.py:37
  668.1 37.6 %collective-permute-start.56 = (bf16[2,1152,512]{2,1,0:T(8,128)(2,1)}, bf16[2,1152,512]{2,1,0:T(8,128)(2,1)}, u32[]{:S(2)}, u32[]{:S(2)}) collective-permute-start(bf16[2,1152,512]{2,1,0:T(8,128)(2,1)} %get-tuple-element.1228), channel_id=1, source_target_pairs={{0,1},{1,0},{2,3},{3,2},{4,5},{5,4},{6,7},{7,6},{8,9},{9,8},{10,11... | collective-permute-start | bytes 7077896 | tf_op jit(solution)/shard_map/ppermute | solution.py:37
  668.6 34.8 %all-to-all-start.6 = ((bf16[8,2,32,1152]{3,2,1,0:T(8,128)(2,1)}), bf16[8,2,32,1152]{3,2,1,0:T(8,128)(2,1)}, u32[]{:S(2)}, u32[]{:S(2)}) async-start(bf16[8,2,32,1152]{3,2,1,0:T(8,128)(2,1)} %bitcast.214), calls=%async_computation.6 | async-start | bytes 2359296 | tf_op jit(solution)/shard_map/all_to_all | solution.py:763
  728.9 41.6 %collective-permute-start.57 = (bf16[2,1152,1152]{2,1,0:T(8,128)(2,1)}, bf16[2,1152,1152]{2,1,0:T(8,128)(2,1)}, u32[]{:S(2)}, u32[]{:S(2)}) collective-permute-start(bf16[2,1152,1152]{2,1,0:T(8,128)(2,1)} %get-tuple-element.1282), channel_id=1, source_target_pairs={{0,1},{1,0},{2,3},{3,2},{4,5},{5,4},{6,7},{7,6},{8,9},{9,8},{10,11... | collective-permute-start | bytes 15925256 | tf_op jit(solution)/shard_map/ppermute | solution.py:37
  729.0 38.9 %collective-permute-start.58 = (bf16[1,1152,640]{2,1,0:T(8,128)(2,1)}, bf16[1,1152,640]{2,1,0:T(8,128)(2,1)}, u32[]{:S(2)}, u32[]{:S(2)}) collective-permute-start(bf16[1,1152,640]{2,1,0:T(8,128)(2,1)} %sum_rows.28), channel_id=1, source_target_pairs={{0,2},{1,3},{2,0},{3,1},{4,6},{5,7},{6,4},{7,5},{8,10},{9,11},{10,... | collective-permute-start | bytes 4423688 | tf_op jit(solution)/shard_map/ppermute | solution.py:37
  730.5 34.9 %collective-permute-start.59 = (bf16[2,576,512]{2,1,0:T(8,128)(2,1)S(1)}, bf16[2,576,512]{2,1,0:T(8,128)(2,1)}, u32[]{:S(2)}, u32[]{:S(2)}) collective-permute-start(bf16[2,576,512]{2,1,0:T(8,128)(2,1)S(1)} %copy-done.19), channel_id=1, source_target_pairs={{0,4},{4,0},{8,12},{12,8},{16,20},{20,16},{24,28},{28,24},{1,5},{5... | collective-permute-start | bytes 3538952 | tf_op jit(solution)/shard_map/ppermute | solution.py:37
  774.5 26.9 %collective-permute-start.62 = (bf16[2,1152,1152]{2,1,0:T(8,128)(2,1)}, bf16[2,1152,1152]{2,1,0:T(8,128)(2,1)}, u32[]{:S(2)}, u32[]{:S(2)}) collective-permute-start(bf16[2,1152,1152]{2,1,0:T(8,128)(2,1)} %get-tuple-element.1338), channel_id=1, source_target_pairs={{0,1},{1,0},{2,3},{3,2},{4,5},{5,4},{6,7},{7,6},{8,9},{9,8},{10,11... | collective-permute-start | bytes 15925256 | tf_op jit(solution)/shard_map/ppermute | solution.py:37
  775.7 29.6 %collective-permute-start.65 = (bf16[1,144,640]{2,1,0:T(8,128)(2,1)}, bf16[1,144,640]{2,1,0:T(8,128)(2,1)S(1)}, u32[]{:S(2)}, u32[]{:S(2)}) collective-permute-start(bf16[1,144,640]{2,1,0:T(8,128)(2,1)} %add_convert_fusion.16), channel_id=1, source_target_pairs={{0,16},{4,20},{8,24},{12,28},{16,0},{20,4},{24,8},{28,12},{1,17},{... | collective-permute-start | bytes 552968 | tf_op jit(solution)/shard_map/ppermute | solution.py:37
  776.3 29.0 %collective-permute-start.66 = (bf16[1,144,512]{2,1,0:T(8,128)(2,1)}, bf16[1,144,512]{2,1,0:T(8,128)(2,1)}, u32[]{:S(2)}, u32[]{:S(2)}) collective-permute-start(bf16[1,144,512]{2,1,0:T(8,128)(2,1)} %add_convert_fusion.20), channel_id=1, source_target_pairs={{0,16},{4,20},{8,24},{12,28},{16,0},{20,4},{24,8},{28,12},{1,17},{... | collective-permute-start | bytes 442376 | tf_op jit(solution)/shard_map/ppermute | solution.py:37
  805.3 61.3 %collective-permute-start.67 = (bf16[2,576,1152]{2,1,0:T(8,128)(2,1)}, bf16[2,576,1152]{2,1,0:T(8,128)(2,1)}, u32[]{:S(2)}, u32[]{:S(2)}) collective-permute-start(bf16[2,576,1152]{2,1,0:T(8,128)(2,1)} %sum_rows.33), channel_id=1, source_target_pairs={{0,4},{4,0},{8,12},{12,8},{16,20},{20,16},{24,28},{28,24},{1,5},{5... | collective-permute-start | bytes 7962632 | tf_op jit(solution)/shard_map/ppermute | solution.py:37
  806.8 63.5 %collective-permute-start.68 = (bf16[1,1152,1152]{2,1,0:T(8,128)(2,1)}, bf16[1,1152,1152]{2,1,0:T(8,128)(2,1)}, u32[]{:S(2)}, u32[]{:S(2)}) collective-permute-start(bf16[1,1152,1152]{2,1,0:T(8,128)(2,1)} %sum_rows.30), channel_id=1, source_target_pairs={{0,2},{1,3},{2,0},{3,1},{4,6},{5,7},{6,4},{7,5},{8,10},{9,11},{10,... | collective-permute-start | bytes 7962632 | tf_op jit(solution)/shard_map/ppermute | solution.py:37
  808.2 56.4 %collective-permute-start.69 = (bf16[1,288,640]{2,1,0:T(8,128)(2,1)}, bf16[1,288,640]{2,1,0:T(8,128)(2,1)}, u32[]{:S(2)}, u32[]{:S(2)}) collective-permute-start(bf16[1,288,640]{2,1,0:T(8,128)(2,1)} %add_convert_fusion.5), channel_id=1, source_target_pairs={{0,8},{4,12},{8,0},{12,4},{16,24},{20,28},{24,16},{28,20},{1,9},{5... | collective-permute-start | bytes 1105928 | tf_op jit(solution)/shard_map/ppermute | solution.py:37
  808.5 54.1 %collective-permute-start.70 = (bf16[1,288,512]{2,1,0:T(8,128)(2,1)}, bf16[1,288,512]{2,1,0:T(8,128)(2,1)}, u32[]{:S(2)}, u32[]{:S(2)}) collective-permute-start(bf16[1,288,512]{2,1,0:T(8,128)(2,1)} %add_convert_fusion.11), channel_id=1, source_target_pairs={{0,8},{4,12},{8,0},{12,4},{16,24},{20,28},{24,16},{28,20},{1,9},{5... | collective-permute-start | bytes 884744 | tf_op jit(solution)/shard_map/ppermute | solution.py:37
  878.4 31.4 %collective-permute-start.73 = (bf16[1,576,1152]{2,1,0:T(8,128)(2,1)}, bf16[1,576,1152]{2,1,0:T(8,128)(2,1)}, u32[]{:S(2)}, u32[]{:S(2)}) collective-permute-start(bf16[1,576,1152]{2,1,0:T(8,128)(2,1)} %sum_rows.34), channel_id=1, source_target_pairs={{0,2},{1,3},{2,0},{3,1},{4,6},{5,7},{6,4},{7,5},{8,10},{9,11},{10,... | collective-permute-start | bytes 3981320 | tf_op jit(solution)/shard_map/ppermute | solution.py:37
  879.0 31.1 %collective-permute-start.74 = (bf16[1,576,1152]{2,1,0:T(8,128)(2,1)}, bf16[1,576,1152]{2,1,0:T(8,128)(2,1)}, u32[]{:S(2)}, u32[]{:S(2)}) collective-permute-start(bf16[1,576,1152]{2,1,0:T(8,128)(2,1)} %sum_rows.35), channel_id=1, source_target_pairs={{0,4},{4,0},{8,12},{12,8},{16,20},{20,16},{24,28},{28,24},{1,5},{5... | collective-permute-start | bytes 3981320 | tf_op jit(solution)/shard_map/ppermute | solution.py:37
  879.6 44.7 %collective-permute-start.75 = (bf16[1,144,640]{2,1,0:T(8,128)(2,1)}, bf16[1,144,640]{2,1,0:T(8,128)(2,1)}, u32[]{:S(2)}, u32[]{:S(2)}) collective-permute-start(bf16[1,144,640]{2,1,0:T(8,128)(2,1)} %add_convert_fusion.15), channel_id=1, source_target_pairs={{0,16},{4,20},{8,24},{12,28},{16,0},{20,4},{24,8},{28,12},{1,17},{... | collective-permute-start | bytes 552968 | tf_op jit(solution)/shard_map/ppermute | solution.py:37
  883.1 41.2 %collective-permute-start.76 = (bf16[1,144,512]{2,1,0:T(8,128)(2,1)}, bf16[1,144,512]{2,1,0:T(8,128)(2,1)}, u32[]{:S(2)}, u32[]{:S(2)}) collective-permute-start(bf16[1,144,512]{2,1,0:T(8,128)(2,1)} %add_convert_fusion.19), channel_id=1, source_target_pairs={{0,16},{4,20},{8,24},{12,28},{16,0},{20,4},{24,8},{28,12},{1,17},{... | collective-permute-start | bytes 442376 | tf_op jit(solution)/shard_map/ppermute | solution.py:37
  924.3 35.5 %collective-permute-start.77 = (bf16[1,1152,640]{2,1,0:T(8,128)(2,1)}, bf16[1,1152,640]{2,1,0:T(8,128)(2,1)}, u32[]{:S(2)}, u32[]{:S(2)}) collective-permute-start(bf16[1,1152,640]{2,1,0:T(8,128)(2,1)} %sum_rows.36), channel_id=1, source_target_pairs={{0,2},{1,3},{2,0},{3,1},{4,6},{5,7},{6,4},{7,5},{8,10},{9,11},{10,... | collective-permute-start | bytes 4423688 | tf_op jit(solution)/shard_map/ppermute | solution.py:37
  930.0 38.2 %collective-permute-start.78 = (bf16[2,576,512]{2,1,0:T(8,128)(2,1)}, bf16[2,576,512]{2,1,0:T(8,128)(2,1)}, u32[]{:S(2)}, u32[]{:S(2)}) collective-permute-start(bf16[2,576,512]{2,1,0:T(8,128)(2,1)} %sum_rows.37), channel_id=1, source_target_pairs={{0,4},{4,0},{8,12},{12,8},{16,20},{20,16},{24,28},{28,24},{1,5},{5... | collective-permute-start | bytes 3538952 | tf_op jit(solution)/shard_map/ppermute | solution.py:37
  930.6 29.7 %collective-permute-start.79 = (bf16[1,288,1152]{2,1,0:T(8,128)(2,1)}, bf16[1,288,1152]{2,1,0:T(8,128)(2,1)}, u32[]{:S(2)}, u32[]{:S(2)}) collective-permute-start(bf16[1,288,1152]{2,1,0:T(8,128)(2,1)} %add_convert_fusion.3), channel_id=1, source_target_pairs={{0,8},{4,12},{8,0},{12,4},{16,24},{20,28},{24,16},{28,20},{1,9},{5... | collective-permute-start | bytes 1990664 | tf_op jit(solution)/shard_map/ppermute | solution.py:37
  930.9 35.0 %collective-permute-start.80 = (bf16[1,288,1152]{2,1,0:T(8,128)(2,1)}, bf16[1,288,1152]{2,1,0:T(8,128)(2,1)}, u32[]{:S(2)}, u32[]{:S(2)}) collective-permute-start(bf16[1,288,1152]{2,1,0:T(8,128)(2,1)} %add_convert_fusion.2), channel_id=1, source_target_pairs={{0,8},{4,12},{8,0},{12,4},{16,24},{20,28},{24,16},{28,20},{1,9},{5... | collective-permute-start | bytes 1990664 | tf_op jit(solution)/shard_map/ppermute | solution.py:37
  934.1 39.3 %all-to-all-start.8 = ((bf16[4,288,512]{2,1,0:T(8,128)(2,1)}), bf16[4,288,512]{2,1,0:T(8,128)(2,1)S(1)}, u32[]{:S(2)}, u32[]{:S(2)}) async-start(bf16[4,288,512]{2,1,0:T(8,128)(2,1)} %bitcast.211), calls=%async_computation.8 | async-start | bytes 2359296 | tf_op jit(solution)/shard_map/all_to_all | solution.py:842
  979.1 46.8 %all-to-all-start.9 = ((bf16[4,288,512]{2,1,0:T(8,128)(2,1)}), bf16[4,288,512]{2,1,0:T(8,128)(2,1)S(1)}, u32[]{:S(2)}, u32[]{:S(2)}) async-start(bf16[4,288,512]{2,1,0:T(8,128)(2,1)} %bitcast.213), calls=%async_computation.9 | async-start | bytes 2359296 | tf_op jit(solution)/shard_map/all_to_all | solution.py:842
  982.8 32.6 %collective-permute-start.86 = (bf16[1,576,640]{2,1,0:T(8,128)(2,1)}, bf16[1,576,640]{2,1,0:T(8,128)(2,1)}, u32[]{:S(2)}, u32[]{:S(2)}) collective-permute-start(bf16[1,576,640]{2,1,0:T(8,128)(2,1)} %sum_rows.38), channel_id=1, source_target_pairs={{0,4},{4,0},{8,12},{12,8},{16,20},{20,16},{24,28},{28,24},{1,5},{5... | collective-permute-start | bytes 2211848 | tf_op jit(solution)/shard_map/ppermute | solution.py:37
  984.3 29.0 %collective-permute-start.87 = (bf16[1,576,512]{2,1,0:T(8,128)(2,1)}, bf16[1,576,512]{2,1,0:T(8,128)(2,1)}, u32[]{:S(2)}, u32[]{:S(2)}) collective-permute-start(bf16[1,576,512]{2,1,0:T(8,128)(2,1)} %sum_rows.39), channel_id=1, source_target_pairs={{0,2},{1,3},{2,0},{3,1},{4,6},{5,7},{6,4},{7,5},{8,10},{9,11},{10,... | collective-permute-start | bytes 1769480 | tf_op jit(solution)/shard_map/ppermute | solution.py:37
  986.3 31.3 %collective-permute-start.88 = (bf16[1,144,1152]{2,1,0:T(8,128)(2,1)}, bf16[1,144,1152]{2,1,0:T(8,128)(2,1)}, u32[]{:S(2)}, u32[]{:S(2)}) collective-permute-start(bf16[1,144,1152]{2,1,0:T(8,128)(2,1)} %add_convert_fusion.9), channel_id=1, source_target_pairs={{0,16},{4,20},{8,24},{12,28},{16,0},{20,4},{24,8},{28,12},{1,17},{... | collective-permute-start | bytes 995336 | tf_op jit(solution)/shard_map/ppermute | solution.py:37
  988.4 29.7 %collective-permute-start.89 = (bf16[1,144,1152]{2,1,0:T(8,128)(2,1)}, bf16[1,144,1152]{2,1,0:T(8,128)(2,1)}, u32[]{:S(2)}, u32[]{:S(2)}) collective-permute-start(bf16[1,144,1152]{2,1,0:T(8,128)(2,1)} %add_convert_fusion.8), channel_id=1, source_target_pairs={{0,16},{4,20},{8,24},{12,28},{16,0},{20,4},{24,8},{28,12},{1,17},{... | collective-permute-start | bytes 995336 | tf_op jit(solution)/shard_map/ppermute | solution.py:37
  (105 other events, 1922.3 us)

commit v6 on v5

--- a/solution.py
+++ b/solution.py
@@ -413,7 +413,7 @@
     return results[0] if finish is None else results
 
 
-ROWS = 32
+ROWS = 16
 
 
 def by_rows(tokens, work, sums=0, width=0):

time: 1070 us -> 1080 us (level)
  Pallas kernels: 404 us -> 417 us
    pallas_call x8, Pallas kernels: 122 us -> 135 us  [contract(): pl.pallas_call(body, grid=(parts,), in_specs=[part_spec((tokens, n))] + [...]
  transfers between devices with their start and end apart: 104 -> 104, of which waited for: 38 -> 38; matrix products, arithmetic and copies ran while one was open for 17% -> 16% of each run, Pallas kernels for 34% -> 35%
where the time goes in v6:
time: 1080 us; the launch traced here: 1070 us
  Pallas kernels  417 us (39%)
  waiting for transfers between devices  314 us (29%)
  starting transfers between devices  128 us (12%)
  other arithmetic  116 us (11%)
  local copies, waits for them, and re-layouts  56.6 us (5%)
  matrix products  33.7 us (3%)
    ppermute x94, waiting for transfers between devices, swap(): return lax.ppermute(value, axis, [(i, i ^ bit) for i in range(count)])  257 us
    pallas_call x8, Pallas kernels, contract(): pl.pallas_call(body, grid=(parts,), in_specs=[part_spec((tokens, n))] + [...  135 us
    pallas_call x8, Pallas kernels, project(): pl.pallas_call(body, grid=(weight.parts,), in_specs=[whole_spec((tokens,...  89.2 us
    ppermute x94, starting transfers between devices, swap(): return lax.ppermute(value, axis, [(i, i ^ bit) for i in range(count)])  83.6 us
    pallas_call x6, Pallas kernels, weight_grads(): pl.pallas_call(body, grid=(parts,), in_specs=[whole_spec((tokens, depth))...  81.1 us
    pallas_call x20, Pallas kernels, sum_rows(): pl.pallas_call(body, grid=(names, count // rows), in_specs=[spec(lead) fo...  57.5 us
    pallas_call x4, Pallas kernels, attention_call(): pl.pallas_call(functools.partial(kernel, temporal, chunk), grid=grid, in_...  53.7 us
    convert_element_type x20, other arithmetic, sums(): total([self.take(t, first, count) for t in self.live[n]]).astype(bf16)  42.3 us
  transfers between devices with their start and end apart: 104, of which 38 were waited for; matrix products, arithmetic and copies ran while one was open for 16% of the time, Pallas kernels for 35%

profile of v6, /device:TPU:0, one launch (start us, length us, event | category | flops | bytes accessed | tf_op | source)
XLA Modules:
  0.0 1067.6 jit_solution(14031636286289101278)
XLA Ops:
  5.1 4.1 collective-permute-start
  12.4 3.9 all-to-all-start.2
  21.0 4.3 all-to-all-start
  29.8 10.9 %collective-permute-done.8 = f32[4,3456]{1,0:T(4,128)S(1)} collective-permute-done((f32[4,3456]{1,0:T(4,128)S(1)}, f32[4,3456]{1,0:T(4,128)S(1)}, u32[]{:S(2)}, u32[]{:S(2)}) %collective-permute-start.8) | collective-permute-done | bytes 55328 | tf_op jit(solution)/shard_map/ppermute | solution.py:37
  55.4 4.4 all-to-all-start.1
  59.9 11.3 %collective-permute-done.2 = bf16[288,1152]{1,0:T(8,128)(2,1)} collective-permute-done((bf16[288,1152]{1,0:T(8,128)(2,1)S(1)}, bf16[288,1152]{1,0:T(8,128)(2,1)}, u32[]{:S(2)}, u32[]{:S(2)}) %collective-permute-start.2) | collective-permute-done | bytes 663584 | tf_op jit(solution)/shard_map/ppermute | solution.py:37
  72.4 9.1 collective-permute-done.3
  90.7 4.6 fusion.7.refs_5_
  95.3 15.3 %collective-permute-done.6 = bf16[144,1152]{1,0:T(8,128)(2,1)S(1)} collective-permute-done((bf16[144,1152]{1,0:T(8,128)(2,1)}, bf16[144,1152]{1,0:T(8,128)(2,1)S(1)}, u32[]{:S(2)}, u32[]{:S(2)}) %collective-permute-start.6) | collective-permute-done | bytes 331808 | tf_op jit(solution)/shard_map/ppermute | solution.py:37
  110.7 6.0 collective-permute-done.7
  122.1 4.3 collective-permute-done.12.refs_3_
  135.1 9.2 collective-permute-done.15
  145.6 12.4 %collective-permute-done.16 = bf16[288,1152]{1,0:T(8,128)(2,1)S(1)} collective-permute-done((bf16[288,1152]{1,0:T(8,128)(2,1)}, bf16[288,1152]{1,0:T(8,128)(2,1)S(1)}, u32[]{:S(2)}, u32[]{:S(2)}) %collective-permute-start.16) | collective-permute-done | bytes 663584 | tf_op jit(solution)/shard_map/ppermute | solution.py:37
  159.1 22.3 %collective-permute-done.11.refs_2_ = bf16[1152,1152]{1,0:T(8,128)(2,1)} collective-permute-done((bf16[1152,1152]{1,0:T(8,128)(2,1)}, bf16[1152,1152]{1,0:T(8,128)(2,1)}, u32[]{:S(2)}, u32[]{:S(2)}) %collective-permute-start.11) | collective-permute-done | bytes 2654240 | tf_op jit(solution)/shard_map/ppermute | solution.py:37
  181.6 5.3 collective-permute-done.17.refs_4_
  192.0 21.4 %collective-permute-done.21 = bf16[144,1152]{1,0:T(8,128)(2,1)S(1)} collective-permute-done((bf16[144,1152]{1,0:T(8,128)(2,1)S(1)}, bf16[144,1152]{1,0:T(8,128)(2,1)S(1)}, u32[]{:S(2)}, u32[]{:S(2)}) %collective-permute-start.21) | collective-permute-done | bytes 331808 | tf_op jit(solution)/shard_map/ppermute | solution.py:37
  213.4 6.2 collective-permute-done.22
  236.2 10.0 qkv.2
  246.2 13.3 %attend.2 = (bf16[4,2,256,288]{3,2,1,0:T(8,128)(2,1)}, f32[4,2,4,256]{3,2,1,0:T(4,128)}) custom-call(bf16[4,2,256,864]{3,2,1,0:T(8,128)(2,1)} %bitcast.200), custom_call_target="tpu_custom_call" | custom-call | flops 1073741824 | bytes 4718592 | tf_op jit(solution)/shard_map/attend/pallas_call | solution.py:670
  259.5 18.0 %out.2 = (f32[512,1152]{1,0:T(8,128)}, f32[512,1152]{1,0:T(8,128)}, f32[512,1152]{1,0:T(8,128)}, f32[512,1]{1,0:T(8,128)}, bf16[512,1152]{1,0:T(8,128)(2,1)}) custom-call(bf16[4,512,288]{2,1,0:T(8,128)(2,1)} %bitcast.204, bf16[1152,1152]{1,0:T(8,128)(2,1)} %pad_maximum_fusion.refs_1_, bf16[1152,1152]{1,0:T(8,128)(2,1)} %collective-permute-done.11.refs_2_, ...), custom_call_target="tpu_custom_call" | custom-call | flops 1358954496 | bytes 8552448 | tf_op jit(solution)/shard_map/out/pallas_call | solution.py:396
  291.7 15.3 %up.2 = (bf16[4,512,1152]{2,1,0:T(8,128)(2,1)}, bf16[4,512,1152]{2,1,0:T(8,128)(2,1)}) custom-call(bf16[512,1152]{1,0:T(8,128)(2,1)} %get-tuple-element.1275.refs_0_, bf16[1152,1152]{1,0:T(8,128)(2,1)} %pad_maximum_fusion.1.refs_1_, bf16[1152,1152]{1,0:T(8,128)(2,1)} %collective-permute-done.13.refs_2_, bf16[1152,1152]{1,0:T(8,128)(2,1)} %collective-permute-done.14.refs_3_, ...), custom_call_target="tpu_custom_call" | custom-call | flops 5435817984 | bytes 20054016 | tf_op jit(solution)/shard_map/up/pallas_call | solution.py:322
  307.0 11.7 %collective-permute-done.31 = bf16[576,1152]{1,0:T(8,128)(2,1)} collective-permute-done((bf16[576,1152]{1,0:T(8,128)(2,1)S(1)}, bf16[576,1152]{1,0:T(8,128)(2,1)}, u32[]{:S(2)}, u32[]{:S(2)}) %collective-permute-start.31) | collective-permute-done | bytes 1327136 | tf_op jit(solution)/shard_map/ppermute | solution.py:37
  324.7 13.9 %down.2 = (f32[512,1152]{1,0:T(8,128)}, bf16[512,1152]{1,0:T(8,128)(2,1)}) custom-call(bf16[4,512,1152]{2,1,0:T(8,128)(2,1)} %get-tuple-element.1280.refs_0_.refs_1_, bf16[1152,1152]{1,0:T(8,128)(2,1)} %pad_maximum_fusion.2.refs_1_, bf16[1152,1152]{1,0:T(8,128)(2,1)} %collective-permute-done.23.refs_2_, bf16[1152,1152]{1,0:T(8,128)(2,1)} %collective-permute-done.24.refs_3_, ...), custom_call_target="tpu_custom_call" | custom-call | flops 5435817984 | bytes 20054016 | tf_op jit(solution)/shard_map/down/pallas_call | solution.py:396
  349.7 26.3 %all-to-all-done.3 = bf16[8,2,32,1152]{3,2,1,0:T(8,128)(2,1)S(1)} async-done(((bf16[8,2,32,1152]{3,2,1,0:T(8,128)(2,1)}), bf16[8,2,32,1152]{3,2,1,0:T(8,128)(2,1)S(1)}, u32[]{:S(2)}, u32[]{:S(2)}) %all-to-all-start.3) | async-done | bytes 1179680 | tf_op jit(solution)/shard_map/all_to_all | solution.py:759
  380.8 10.1 qkv.3
  390.9 13.4 %attend.3 = (bf16[4,1,16,32,288]{4,3,2,1,0:T(8,128)(2,1)}, f32[4,2,4,256]{3,2,1,0:T(4,128)}) custom-call(bf16[4,1,16,32,864]{4,3,2,1,0:T(8,128)(2,1)} %bitcast.202), custom_call_target="tpu_custom_call" | custom-call | flops 1073741824 | bytes 4718592 | tf_op jit(solution)/shard_map/attend/pallas_call | solution.py:670
  406.9 12.5 %collective-permute-done.35.refs_2_ = bf16[1152,1152]{1,0:T(8,128)(2,1)} collective-permute-done((bf16[1152,1152]{1,0:T(8,128)(2,1)}, bf16[1152,1152]{1,0:T(8,128)(2,1)}, u32[]{:S(2)}, u32[]{:S(2)}) %collective-permute-start.35) | collective-permute-done | bytes 2654240 | tf_op jit(solution)/shard_map/ppermute | solution.py:37
  419.4 5.2 collective-permute-done.37.refs_4_
  429.0 4.8 all-to-all-start.4
  434.5 18.1 %out.3 = (f32[512,1152]{1,0:T(8,128)}, f32[512,1152]{1,0:T(8,128)}, f32[512,1152]{1,0:T(8,128)}, f32[512,1]{1,0:T(8,128)}, bf16[512,1152]{1,0:T(8,128)(2,1)}) custom-call(bf16[4,512,288]{2,1,0:T(8,128)(2,1)} %bitcast.206, bf16[1152,1152]{1,0:T(8,128)(2,1)} %pad_maximum_fusion.3.refs_1_, bf16[1152,1152]{1,0:T(8,128)(2,1)} %collective-permute-done.25.refs_2_, ...), custom_call_target="tpu_custom_call" | custom-call | flops 1358954496 | bytes 8552448 | tf_op jit(solution)/shard_map/out/pallas_call | solution.py:396
  452.6 14.9 %up.3 = (bf16[4,512,1152]{2,1,0:T(8,128)(2,1)}, bf16[4,512,1152]{2,1,0:T(8,128)(2,1)}) custom-call(bf16[512,1152]{1,0:T(8,128)(2,1)} %get-tuple-element.1043.refs_0_, bf16[1152,1152]{1,0:T(8,128)(2,1)} %pad_maximum_fusion.4.refs_1_, bf16[1152,1152]{1,0:T(8,128)(2,1)} %collective-permute-done.33.refs_2_, bf16[1152,1152]{1,0:T(8,128)(2,1)} %collective-permute-done.34.refs_3_, ...), custom_call_target="tpu_custom_call" | custom-call | flops 5435817984 | bytes 20054016 | tf_op jit(solution)/shard_map/up/pallas_call | solution.py:322
  471.2 12.6 %grad_fc2.2 = (bf16[2,1152,640]{2,1,0:T(8,128)(2,1)}, bf16[2,1152,512]{2,1,0:T(8,128)(2,1)}, bf16[2,1152,640]{2,1,0:T(8,128)(2,1)}, bf16[2,1152,512]{2,1,0:T(8,1...) custom-call(bf16[512,1152]{1,0:T(8,128)(2,1)} %get-tuple-element.1044.refs_0_, ...), custom_call_target="tpu_custom_call" | custom-call | flops 5435817984 | bytes 15335424 | tf_op jit(solution)/shard_map/grad_fc2/pallas_call | solution.py:539
  485.1 13.8 %down.3 = (f32[512,1152]{1,0:T(8,128)}, bf16[512,1152]{1,0:T(8,128)(2,1)}) custom-call(bf16[4,512,1152]{2,1,0:T(8,128)(2,1)} %get-tuple-element.1021.refs_1_.refs_0_, bf16[1152,1152]{1,0:T(8,128)(2,1)} %pad_maximum_fusion.5.refs_1_, bf16[1152,1152]{1,0:T(8,128)(2,1)} %collective-permute-done.35.refs_2_, bf16[1152,1152]{1,0:T(8,128)(2,1)} %collective-permute-done.36.refs_3_, ...), custom_call_target="tpu_custom_call" | custom-call | flops 5435817984 | bytes 20054016 | tf_op jit(solution)/shard_map/down/pallas_call | solution.py:396
  498.9 4.2 fusion.9
  508.6 6.2 all-to-all-start.5
  517.5 12.0 %up_back.2.refs_1_.refs_0_ = bf16[4,512,1152]{2,1,0:T(8,128)(2,1)} custom-call(bf16[512,1152]{1,0:T(8,128)(2,1)} %get-tuple-element.1044.refs_0_, bf16[1152,1152]{1,0:T(8,128)(2,1)} %pad_maximum_fusion.5.refs_1_, bf16[1152,1152]{1,0:T(8,128)(2,1)} %collective-permute-done.35.refs_2_, bf16[1152,1152]{1,0:T(8,128)(2,1)} %collective-permute-done.36.refs_3_, ...), custom_call_target="tpu_custom_call" | custom-call | flops 5435817984 | bytes 20054016 | tf_op jit(solution)/shard_map/up_back/pallas_call | solution.py:322
  529.6 12.7 %grad_fc1.2 = (bf16[2,1152,640]{2,1,0:T(8,128)(2,1)}, bf16[2,1152,512]{2,1,0:T(8,128)(2,1)}, bf16[2,1152,640]{2,1,0:T(8,128)(2,1)}, bf16[2,1152,512]{2,1,0:T(8,1...) custom-call(bf16[512,1152]{1,0:T(8,128)(2,1)} %get-tuple-element.1043.refs_0_, ...), custom_call_target="tpu_custom_call" | custom-call | flops 5435817984 | bytes 15335424 | tf_op jit(solution)/shard_map/grad_fc1/pallas_call | solution.py:539
  543.0 12.4 %collective-permute-done.42.refs_2_ = bf16[2,576,512]{2,1,0:T(8,128)(2,1)} collective-permute-done((bf16[2,576,512]{2,1,0:T(8,128)(2,1)}, bf16[2,576,512]{2,1,0:T(8,128)(2,1)}, u32[]{:S(2)}, u32[]{:S(2)}) %collective-permute-start.42) | collective-permute-done | bytes 1179680 | tf_op jit(solution)/shard_map/ppermute | solution.py:37
  564.6 19.0 %hidden2_back.2 = (f32[512,1152]{1,0:T(8,128)}, bf16[512,1152]{1,0:T(8,128)(2,1)}, f32[3,1152]{1,0:T(4,128)}) custom-call(bf16[4,512,1152]{2,1,0:T(8,128)(2,1)} %up_back.2.refs_1_.refs_0_, bf16[1152,1152]{1,0:T(8,128)(2,1)} %pad_maximum_fusion.4.refs_1_, bf16[1152,1152]{1,0:T(8,128)(2,1)} %collective-permute-done.33.refs_2_, ...), custom_call_target="tpu_custom_call" | custom-call | flops 5435817984 | bytes 27131904 | tf_op jit(solution)/shard_map/hidden2_back/pallas_call | solution.py:396
  598.7 7.5 out_back.2
  606.2 13.6 %attend_back.2 = bf16[4,1,16,32,864]{4,3,2,1,0:T(8,128)(2,1)} custom-call(bf16[4,1,16,32,864]{4,3,2,1,0:T(8,128)(2,1)} %bitcast.203, bf16[4,1,16,32,288]{4,3,2,1,0:T(8,128)(2,1)} %bitcast.208, bf16[4,1,16,32,288]{4,3,2,1,0:T(8,128)(2,1)} %get-tuple-element.929, f32[4,2,4,256]{3,2,1,0:T(4,128)} %get-tuple-element.1129.logs), custom_call_target="tpu_custom_call" | custom-call | flops 2684354560 | bytes 14155776 | tf_op jit(solution)/shard_map/attend_back/pallas_call | solution.py:670
  619.8 15.3 %grad_mixed.2 = (bf16[2,1152,640]{2,1,0:T(8,128)(2,1)}, bf16[2,1152,512]{2,1,0:T(8,128)(2,1)}, bf16[2,1152,640]{2,1,0:T(8,128)(2,1)}, bf16[2,1152,512]{2,1,0:T(8...) custom-call(bf16[512,1152]{1,0:T(8,128)(2,1)} %get-tuple-element.1125.refs_0_, ...), custom_call_target="tpu_custom_call" | custom-call | flops 5435817984 | bytes 15335424 | tf_op jit(solution)/shard_map/grad_mixed/pallas_call | solution.py:539
  649.7 16.3 %hidden_back.2 = (bf16[512,1152]{1,0:T(8,128)(2,1)}, f32[2,1152]{1,0:T(2,128)}) custom-call(bf16[4,512,864]{2,1,0:T(8,128)(2,1)} %bitcast.197, bf16[1152,1152]{1,0:T(8,128)(2,1)} %pad_maximum_fusion.3.refs_1_, bf16[1152,1152]{1,0:T(8,128)(2,1)} %collective-permute-done.25.refs_2_, bf16[1152,1152]{1,0:T(8,128)(2,1)} %collective-permute-done.26.refs_3_, ...), custom_call_target="tpu_custom_call" | custom-call | flops 4076863488 | bytes 20938752 | tf_op jit(solution)/shard_map/hidden_back/pallas_call | solution.py:396
  666.0 4.2 fusion.10
  675.2 5.9 all-to-all-start.6
  681.1 28.8 %all-to-all-done.6 = bf16[8,2,32,1152]{3,2,1,0:T(8,128)(2,1)} async-done(((bf16[8,2,32,1152]{3,2,1,0:T(8,128)(2,1)}), bf16[8,2,32,1152]{3,2,1,0:T(8,128)(2,1)}, u32[]{:S(2)}, u32[]{:S(2)}) %all-to-all-start.6) | async-done | bytes 1179680 | tf_op jit(solution)/shard_map/all_to_all | solution.py:763
  717.8 5.0 multiply_convert_fusion
  722.7 12.7 %grad_fc2.3 = (bf16[2,1152,1152]{2,1,0:T(8,128)(2,1)}, bf16[2,1152,1152]{2,1,0:T(8,128)(2,1)}, f32[1,1152]{1,0:T(1,128)}, f32[4,1,1152]{2,1,0:T(1,128)}) custom-call(bf16[512,1152]{1,0:T(8,128)(2,1)} %get-tuple-element.1741.refs_0_, bf16[4,512,1152]{2,1,0:T(8,128)(2,1)} %get-tuple-element.1280.refs_0_.refs_1_), custom_call_target="tpu_custom_call" | custom-call | flops 5435817984 | bytes 15335424 | tf_op jit(solution)/shard_map/grad_fc2/pallas_call | solution.py:539
  738.5 12.0 %up_back.3.refs_1_.refs_0_ = bf16[4,512,1152]{2,1,0:T(8,128)(2,1)} custom-call(bf16[512,1152]{1,0:T(8,128)(2,1)} %get-tuple-element.1741.refs_0_, bf16[1152,1152]{1,0:T(8,128)(2,1)} %pad_maximum_fusion.2.refs_1_, bf16[1152,1152]{1,0:T(8,128)(2,1)} %collective-permute-done.23.refs_2_, bf16[1152,1152]{1,0:T(8,128)(2,1)} %collective-permute-done.24.refs_3_, ...), custom_call_target="tpu_custom_call" | custom-call | flops 5435817984 | bytes 20054016 | tf_op jit(solution)/shard_map/up_back/pallas_call | solution.py:322
  752.6 12.8 %grad_fc1.3 = (bf16[2,1152,1152]{2,1,0:T(8,128)(2,1)}, bf16[2,1152,1152]{2,1,0:T(8,128)(2,1)}, f32[1,1152]{1,0:T(1,128)}, f32[4,1,1152]{2,1,0:T(1,128)}) custom-call(bf16[512,1152]{1,0:T(8,128)(2,1)} %get-tuple-element.1275.refs_0_, bf16[4,512,1152]{2,1,0:T(8,128)(2,1)} %up_back.3.refs_1_.refs_0_), custom_call_target="tpu_custom_call" | custom-call | flops 5435817984 | bytes 15335424 | tf_op jit(solution)/shard_map/grad_fc1/pallas_call | solution.py:539
  777.1 4.0 sum_rows.30
  785.2 19.4 %hidden2_back.3 = (f32[512,1152]{1,0:T(8,128)}, bf16[512,1152]{1,0:T(8,128)(2,1)}, f32[3,1152]{1,0:T(4,128)}) custom-call(bf16[4,512,1152]{2,1,0:T(8,128)(2,1)} %up_back.3.refs_1_.refs_0_, bf16[1152,1152]{1,0:T(8,128)(2,1)} %pad_maximum_fusion.1.refs_1_, bf16[1152,1152]{1,0:T(8,128)(2,1)} %collective-permute-done.13.refs_2_, ...), custom_call_target="tpu_custom_call" | custom-call | flops 5435817984 | bytes 27131904 | tf_op jit(solution)/shard_map/hidden2_back/pallas_call | solution.py:396
  809.8 3.9 sum_rows.33
  819.6 7.5 out_back.3
  827.1 13.4 %attend_back.3 = bf16[4,2,256,864]{3,2,1,0:T(8,128)(2,1)} custom-call(bf16[4,2,256,864]{3,2,1,0:T(8,128)(2,1)} %bitcast.201, bf16[4,2,256,288]{3,2,1,0:T(8,128)(2,1)} %bitcast.209, bf16[4,2,256,288]{3,2,1,0:T(8,128)(2,1)} %get-tuple-element.863, f32[4,2,4,256]{3,2,1,0:T(4,128)} %get-tuple-element.1405.logs), custom_call_target="tpu_custom_call" | custom-call | flops 2684354560 | bytes 14155776 | tf_op jit(solution)/shard_map/attend_back/pallas_call | solution.py:670
  840.5 14.9 %grad_mixed.3 = (bf16[2,1152,640]{2,1,0:T(8,128)(2,1)}, bf16[2,1152,512]{2,1,0:T(8,128)(2,1)}, bf16[2,1152,640]{2,1,0:T(8,128)(2,1)}, bf16[2,1152,512]{2,1,0:T(8...) custom-call(bf16[512,1152]{1,0:T(8,128)(2,1)} %get-tuple-element.1401.refs_0_, ...), custom_call_target="tpu_custom_call" | custom-call | flops 5435817984 | bytes 15335424 | tf_op jit(solution)/shard_map/grad_mixed/pallas_call | solution.py:539
  855.4 16.7 %hidden_back.3 = (bf16[512,1152]{1,0:T(8,128)(2,1)}, f32[2,1152]{1,0:T(2,128)}) custom-call(bf16[4,512,864]{2,1,0:T(8,128)(2,1)} %bitcast.199, bf16[1152,1152]{1,0:T(8,128)(2,1)} %pad_maximum_fusion.refs_1_, bf16[1152,1152]{1,0:T(8,128)(2,1)} %collective-permute-done.11.refs_2_, bf16[1152,1152]{1,0:T(8,128)(2,1)} %collective-permute-done.12.refs_3_, ...), custom_call_target="tpu_custom_call" | custom-call | flops 4076863488 | bytes 20938752 | tf_op jit(solution)/shard_map/hidden_back/pallas_call | solution.py:396
  909.7 10.2 collective-permute-done.73
  920.9 3.9 all-to-all-start.7
  954.9 14.9 %collective-permute-done.77.refs_2_ = bf16[1,1152,640]{2,1,0:T(8,128)(2,1)} collective-permute-done((bf16[1,1152,640]{2,1,0:T(8,128)(2,1)}, bf16[1,1152,640]{2,1,0:T(8,128)(2,1)}, u32[]{:S(2)}, u32[]{:S(2)}) %collective-permute-start.77) | collective-permute-done | bytes 1474592 | tf_op jit(solution)/shard_map/ppermute | solution.py:37
  985.1 4.0 fusion.11
  1005.2 16.3 %collective-permute-done.84 = f32[4,1,144]{2,0,1:T(4,128)S(1)} collective-permute-done((f32[4,1,144]{2,0,1:T(4,128)S(1)}, f32[4,1,144]{2,0,1:T(4,128)S(1)}, u32[]{:S(2)}, u32[]{:S(2)}) %collective-permute-start.84) | collective-permute-done | bytes 2336 | tf_op jit(solution)/shard_map/ppermute | solution.py:37
  1041.5 7.3 collective-permute-done.90
  1052.5 7.9 collective-permute-done.91
  (573 shorter events, 351.5 us)
Async XLA Ops:
  5.1 45.3 %collective-permute-start = (bf16[144,1152]{1,0:T(8,128)(2,1)S(1)}, bf16[144,1152]{1,0:T(8,128)(2,1)}, u32[]{:S(2)}, u32[]{:S(2)}) collective-permute-start(bf16[144,1152]{1,0:T(8,128)(2,1)S(1)} %pad_maximum_fusion.24), channel_id=1, source_target_pairs={{0,16},{4,20},{8,24},{12,28},{16,0},{20,4},{24,8},{28,12},{1,17},{... | collective-permute-start | bytes 995336 | tf_op jit(solution)/shard_map/ppermute | solution.py:37
  10.0 41.4 %collective-permute-start.1 = (bf16[144,1152]{1,0:T(8,128)(2,1)S(1)}, bf16[144,1152]{1,0:T(8,128)(2,1)}, u32[]{:S(2)}, u32[]{:S(2)}) collective-permute-start(bf16[144,1152]{1,0:T(8,128)(2,1)S(1)} %get-tuple-element.1690), channel_id=1, source_target_pairs={{0,16},{4,20},{8,24},{12,28},{16,0},{20,4},{24,8},{28,12},{1,17},{... | collective-permute-start | bytes 995336 | tf_op jit(solution)/shard_map/ppermute | solution.py:37
  21.0 34.4 %all-to-all-start = ((bf16[4,288,512]{2,1,0:T(8,128)(2,1)}), bf16[4,288,512]{2,1,0:T(8,128)(2,1)}, u32[]{:S(2)}, u32[]{:S(2)}) async-start(bf16[4,288,512]{2,1,0:T(8,128)(2,1)} %param.17), calls=%async_computation | async-start | bytes 2359296 | tf_op jit(solution)/shard_map/all_to_all | solution.py:836
  54.0 27.5 %collective-permute-start.3 = (bf16[288,1152]{1,0:T(8,128)(2,1)}, bf16[288,1152]{1,0:T(8,128)(2,1)}, u32[]{:S(2)}, u32[]{:S(2)}) collective-permute-start(bf16[288,1152]{1,0:T(8,128)(2,1)} %pad_maximum_fusion.16), channel_id=1, source_target_pairs={{0,8},{4,12},{8,0},{12,4},{16,24},{20,28},{24,16},{28,20},{1,9},{5... | collective-permute-start | bytes 1990664 | tf_op jit(solution)/shard_map/ppermute | solution.py:37
  55.4 28.6 %all-to-all-start.1 = ((bf16[4,288,512]{2,1,0:T(8,128)(2,1)}), bf16[4,288,512]{2,1,0:T(8,128)(2,1)}, u32[]{:S(2)}, u32[]{:S(2)}) async-start(bf16[4,288,512]{2,1,0:T(8,128)(2,1)} %param.29), calls=%async_computation.1 | async-start | bytes 2359296 | tf_op jit(solution)/shard_map/all_to_all | solution.py:836
  84.0 33.6 %collective-permute-start.4 = (bf16[576,1152]{1,0:T(8,128)(2,1)S(1)}, bf16[576,1152]{1,0:T(8,128)(2,1)S(1)}, u32[]{:S(2)}, u32[]{:S(2)}) collective-permute-start(bf16[576,1152]{1,0:T(8,128)(2,1)S(1)} %pad_maximum_fusion.7), channel_id=1, source_target_pairs={{0,4},{4,0},{8,12},{12,8},{16,20},{20,16},{24,28},{28,24},{1,5},{5... | collective-permute-start | bytes 3981320 | tf_op jit(solution)/shard_map/ppermute | solution.py:37
  85.9 33.4 %collective-permute-start.5 = (bf16[576,1152]{1,0:T(8,128)(2,1)}, bf16[576,1152]{1,0:T(8,128)(2,1)S(1)}, u32[]{:S(2)}, u32[]{:S(2)}) collective-permute-start(bf16[576,1152]{1,0:T(8,128)(2,1)} %pad_maximum_fusion.8), channel_id=1, source_target_pairs={{0,2},{1,3},{2,0},{3,1},{4,6},{5,7},{6,4},{7,5},{8,10},{9,11},{10,... | collective-permute-start | bytes 3981320 | tf_op jit(solution)/shard_map/ppermute | solution.py:37
  121.1 60.3 %collective-permute-start.11 = (bf16[1152,1152]{1,0:T(8,128)(2,1)}, bf16[1152,1152]{1,0:T(8,128)(2,1)}, u32[]{:S(2)}, u32[]{:S(2)}) collective-permute-start(bf16[1152,1152]{1,0:T(8,128)(2,1)} %pad_maximum_fusion.refs_1_), channel_id=1, source_target_pairs={{0,2},{1,3},{2,0},{3,1},{4,6},{5,7},{6,4},{7,5},{8,10},{9,11},{10,... | collective-permute-start | bytes 7962632 | tf_op jit(solution)/shard_map/ppermute | solution.py:37
  121.6 60.0 %collective-permute-start.13 = (bf16[1152,1152]{1,0:T(8,128)(2,1)}, bf16[1152,1152]{1,0:T(8,128)(2,1)}, u32[]{:S(2)}, u32[]{:S(2)}) collective-permute-start(bf16[1152,1152]{1,0:T(8,128)(2,1)} %pad_maximum_fusion.1.refs_1_), channel_id=1, source_target_pairs={{0,4},{4,0},{8,12},{12,8},{16,20},{20,16},{24,28},{28,24},{1,5},{5... | collective-permute-start | bytes 7962632 | tf_op jit(solution)/shard_map/ppermute | solution.py:37
  126.4 55.3 %collective-permute-start.14 = (bf16[1152,1152]{1,0:T(8,128)(2,1)}, bf16[1152,1152]{1,0:T(8,128)(2,1)}, u32[]{:S(2)}, u32[]{:S(2)}) collective-permute-start(bf16[1152,1152]{1,0:T(8,128)(2,1)} %pad_maximum_fusion.1.refs_1_), channel_id=1, source_target_pairs={{0,1},{1,0},{2,3},{3,2},{4,5},{5,4},{6,7},{7,6},{8,9},{9,8},{10,11... | collective-permute-start | bytes 7962632 | tf_op jit(solution)/shard_map/ppermute | solution.py:37
  127.4 30.6 %collective-permute-start.16 = (bf16[288,1152]{1,0:T(8,128)(2,1)}, bf16[288,1152]{1,0:T(8,128)(2,1)S(1)}, u32[]{:S(2)}, u32[]{:S(2)}) collective-permute-start(bf16[288,1152]{1,0:T(8,128)(2,1)} %pad_maximum_fusion.18), channel_id=1, source_target_pairs={{0,8},{4,12},{8,0},{12,4},{16,24},{20,28},{24,16},{28,20},{1,9},{5... | collective-permute-start | bytes 1990664 | tf_op jit(solution)/shard_map/ppermute | solution.py:37
  186.9 37.0 %collective-permute-start.18 = (bf16[1152,1152]{1,0:T(8,128)(2,1)}, bf16[1152,1152]{1,0:T(8,128)(2,1)}, u32[]{:S(2)}, u32[]{:S(2)}) collective-permute-start(bf16[1152,1152]{1,0:T(8,128)(2,1)} %collective-permute-done.13.refs_2_), channel_id=1, source_target_pairs={{0,1},{1,0},{2,3},{3,2},{4,5},{5,4},{6,7},{7,6},{8,9},{9,8},{10,11... | collective-permute-start | bytes 7962632 | tf_op jit(solution)/shard_map/ppermute | solution.py:37
  187.1 33.4 %collective-permute-start.19 = (bf16[576,1152]{1,0:T(8,128)(2,1)S(1)}, bf16[576,1152]{1,0:T(8,128)(2,1)S(1)}, u32[]{:S(2)}, u32[]{:S(2)}) collective-permute-start(bf16[576,1152]{1,0:T(8,128)(2,1)S(1)} %pad_maximum_fusion.9), channel_id=1, source_target_pairs={{0,4},{4,0},{8,12},{12,8},{16,20},{20,16},{24,28},{28,24},{1,5},{5... | collective-permute-start | bytes 3981320 | tf_op jit(solution)/shard_map/ppermute | solution.py:37
  187.6 34.6 %collective-permute-start.20 = (bf16[576,1152]{1,0:T(8,128)(2,1)S(1)}, bf16[576,1152]{1,0:T(8,128)(2,1)S(1)}, u32[]{:S(2)}, u32[]{:S(2)}) collective-permute-start(bf16[576,1152]{1,0:T(8,128)(2,1)S(1)} %pad_maximum_fusion.10), channel_id=1, source_target_pairs={{0,2},{1,3},{2,0},{3,1},{4,6},{5,7},{6,4},{7,5},{8,10},{9,11},{10,... | collective-permute-start | bytes 3981320 | tf_op jit(solution)/shard_map/ppermute | solution.py:37
  189.1 30.5 %collective-permute-start.22 = (bf16[144,1152]{1,0:T(8,128)(2,1)S(1)}, bf16[144,1152]{1,0:T(8,128)(2,1)S(1)}, u32[]{:S(2)}, u32[]{:S(2)}) collective-permute-start(bf16[144,1152]{1,0:T(8,128)(2,1)S(1)} %copy-done.16), channel_id=1, source_target_pairs={{0,16},{4,20},{8,24},{12,28},{16,0},{20,4},{24,8},{28,12},{1,17},{... | collective-permute-start | bytes 995336 | tf_op jit(solution)/shard_map/ppermute | solution.py:37
  224.7 60.4 %collective-permute-start.23 = (bf16[1152,1152]{1,0:T(8,128)(2,1)}, bf16[1152,1152]{1,0:T(8,128)(2,1)}, u32[]{:S(2)}, u32[]{:S(2)}) collective-permute-start(bf16[1152,1152]{1,0:T(8,128)(2,1)} %pad_maximum_fusion.2.refs_1_), channel_id=1, source_target_pairs={{0,2},{1,3},{2,0},{3,1},{4,6},{5,7},{6,4},{7,5},{8,10},{9,11},{10,... | collective-permute-start | bytes 7962632 | tf_op jit(solution)/shard_map/ppermute | solution.py:37
  226.2 60.0 %collective-permute-start.25 = (bf16[1152,1152]{1,0:T(8,128)(2,1)}, bf16[1152,1152]{1,0:T(8,128)(2,1)}, u32[]{:S(2)}, u32[]{:S(2)}) collective-permute-start(bf16[1152,1152]{1,0:T(8,128)(2,1)} %pad_maximum_fusion.3.refs_1_), channel_id=1, source_target_pairs={{0,4},{4,0},{8,12},{12,8},{16,20},{20,16},{24,28},{28,24},{1,5},{5... | collective-permute-start | bytes 7962632 | tf_op jit(solution)/shard_map/ppermute | solution.py:37
  229.3 57.0 %collective-permute-start.26 = (bf16[1152,1152]{1,0:T(8,128)(2,1)}, bf16[1152,1152]{1,0:T(8,128)(2,1)}, u32[]{:S(2)}, u32[]{:S(2)}) collective-permute-start(bf16[1152,1152]{1,0:T(8,128)(2,1)} %pad_maximum_fusion.3.refs_1_), channel_id=1, source_target_pairs={{0,1},{1,0},{2,3},{3,2},{4,5},{5,4},{6,7},{7,6},{8,9},{9,8},{10,11... | collective-permute-start | bytes 7962632 | tf_op jit(solution)/shard_map/ppermute | solution.py:37
  232.7 44.8 %collective-permute-start.27 = (bf16[288,1152]{1,0:T(8,128)(2,1)S(1)}, bf16[288,1152]{1,0:T(8,128)(2,1)}, u32[]{:S(2)}, u32[]{:S(2)}) collective-permute-start(bf16[288,1152]{1,0:T(8,128)(2,1)S(1)} %pad_maximum_fusion.19), channel_id=1, source_target_pairs={{0,8},{4,12},{8,0},{12,4},{16,24},{20,28},{24,16},{28,20},{1,9},{5... | collective-permute-start | bytes 1990664 | tf_op jit(solution)/shard_map/ppermute | solution.py:37
  234.5 44.3 %collective-permute-start.28 = (bf16[288,1152]{1,0:T(8,128)(2,1)}, bf16[288,1152]{1,0:T(8,128)(2,1)}, u32[]{:S(2)}, u32[]{:S(2)}) collective-permute-start(bf16[288,1152]{1,0:T(8,128)(2,1)} %pad_maximum_fusion.20), channel_id=1, source_target_pairs={{0,8},{4,12},{8,0},{12,4},{16,24},{20,28},{24,16},{28,20},{1,9},{5... | collective-permute-start | bytes 1990664 | tf_op jit(solution)/shard_map/ppermute | solution.py:37
  287.0 31.7 %collective-permute-start.31 = (bf16[576,1152]{1,0:T(8,128)(2,1)S(1)}, bf16[576,1152]{1,0:T(8,128)(2,1)}, u32[]{:S(2)}, u32[]{:S(2)}) collective-permute-start(bf16[576,1152]{1,0:T(8,128)(2,1)S(1)} %pad_maximum_fusion.11), channel_id=1, source_target_pairs={{0,4},{4,0},{8,12},{12,8},{16,20},{20,16},{24,28},{28,24},{1,5},{5... | collective-permute-start | bytes 3981320 | tf_op jit(solution)/shard_map/ppermute | solution.py:37
  288.7 33.0 %collective-permute-start.32 = (bf16[576,1152]{1,0:T(8,128)(2,1)}, bf16[576,1152]{1,0:T(8,128)(2,1)}, u32[]{:S(2)}, u32[]{:S(2)}) collective-permute-start(bf16[576,1152]{1,0:T(8,128)(2,1)} %pad_maximum_fusion.12), channel_id=1, source_target_pairs={{0,2},{1,3},{2,0},{3,1},{4,6},{5,7},{6,4},{7,5},{8,10},{9,11},{10,... | collective-permute-start | bytes 3981320 | tf_op jit(solution)/shard_map/ppermute | solution.py:37
  291.5 50.2 %collective-permute-start.30 = (bf16[1152,1152]{1,0:T(8,128)(2,1)}, bf16[1152,1152]{1,0:T(8,128)(2,1)}, u32[]{:S(2)}, u32[]{:S(2)}) collective-permute-start(bf16[1152,1152]{1,0:T(8,128)(2,1)} %collective-permute-done.25.refs_2_), channel_id=1, source_target_pairs={{0,1},{1,0},{2,3},{3,2},{4,5},{5,4},{6,7},{7,6},{8,9},{9,8},{10,11... | collective-permute-start | bytes 7962632 | tf_op jit(solution)/shard_map/ppermute | solution.py:37
  343.0 33.0 %all-to-all-start.3 = ((bf16[8,2,32,1152]{3,2,1,0:T(8,128)(2,1)}), bf16[8,2,32,1152]{3,2,1,0:T(8,128)(2,1)S(1)}, u32[]{:S(2)}, u32[]{:S(2)}) async-start(bf16[8,2,32,1152]{3,2,1,0:T(8,128)(2,1)} %bitcast.189), calls=%async_computation.3 | async-start | bytes 2359296 | tf_op jit(solution)/shard_map/all_to_all | solution.py:759
  346.6 60.3 %collective-permute-start.33 = (bf16[1152,1152]{1,0:T(8,128)(2,1)}, bf16[1152,1152]{1,0:T(8,128)(2,1)}, u32[]{:S(2)}, u32[]{:S(2)}) collective-permute-start(bf16[1152,1152]{1,0:T(8,128)(2,1)} %pad_maximum_fusion.4.refs_1_), channel_id=1, source_target_pairs={{0,2},{1,3},{2,0},{3,1},{4,6},{5,7},{6,4},{7,5},{8,10},{9,11},{10,... | collective-permute-start | bytes 7962632 | tf_op jit(solution)/shard_map/ppermute | solution.py:37
  347.2 72.2 %collective-permute-start.35 = (bf16[1152,1152]{1,0:T(8,128)(2,1)}, bf16[1152,1152]{1,0:T(8,128)(2,1)}, u32[]{:S(2)}, u32[]{:S(2)}) collective-permute-start(bf16[1152,1152]{1,0:T(8,128)(2,1)} %pad_maximum_fusion.5.refs_1_), channel_id=1, source_target_pairs={{0,4},{4,0},{8,12},{12,8},{16,20},{20,16},{24,28},{28,24},{1,5},{5... | collective-permute-start | bytes 7962632 | tf_op jit(solution)/shard_map/ppermute | solution.py:37
  349.0 70.3 %collective-permute-start.36 = (bf16[1152,1152]{1,0:T(8,128)(2,1)}, bf16[1152,1152]{1,0:T(8,128)(2,1)}, u32[]{:S(2)}, u32[]{:S(2)}) collective-permute-start(bf16[1152,1152]{1,0:T(8,128)(2,1)} %pad_maximum_fusion.5.refs_1_), channel_id=1, source_target_pairs={{0,1},{1,0},{2,3},{3,2},{4,5},{5,4},{6,7},{7,6},{8,9},{9,8},{10,11... | collective-permute-start | bytes 7962632 | tf_op jit(solution)/shard_map/ppermute | solution.py:37
  429.0 38.5 %all-to-all-start.4 = ((bf16[8,2,32,1152]{3,2,1,0:T(8,128)(2,1)}), bf16[8,2,32,1152]{3,2,1,0:T(8,128)(2,1)S(1)}, u32[]{:S(2)}, u32[]{:S(2)}) async-start(bf16[8,2,32,1152]{3,2,1,0:T(8,128)(2,1)} %copy.151), calls=%async_computation.4 | async-start | bytes 2359296 | tf_op jit(solution)/shard_map/all_to_all | solution.py:759
  508.6 53.1 %all-to-all-start.5 = ((bf16[8,2,32,1152]{3,2,1,0:T(8,128)(2,1)}), bf16[8,2,32,1152]{3,2,1,0:T(8,128)(2,1)}, u32[]{:S(2)}, u32[]{:S(2)}) async-start(bf16[8,2,32,1152]{3,2,1,0:T(8,128)(2,1)} %bitcast.50), calls=%async_computation.5 | async-start | bytes 2359296 | tf_op jit(solution)/shard_map/all_to_all | solution.py:763
  514.8 43.0 %collective-permute-start.41 = (bf16[1,1152,640]{2,1,0:T(8,128)(2,1)}, bf16[1,1152,640]{2,1,0:T(8,128)(2,1)S(1)}, u32[]{:S(2)}, u32[]{:S(2)}) collective-permute-start(bf16[1,1152,640]{2,1,0:T(8,128)(2,1)} %sum_rows.20), channel_id=1, source_target_pairs={{0,2},{1,3},{2,0},{3,1},{4,6},{5,7},{6,4},{7,5},{8,10},{9,11},{10,... | collective-permute-start | bytes 4423688 | tf_op jit(solution)/shard_map/ppermute | solution.py:37
  515.5 39.9 %collective-permute-start.42 = (bf16[2,576,512]{2,1,0:T(8,128)(2,1)}, bf16[2,576,512]{2,1,0:T(8,128)(2,1)}, u32[]{:S(2)}, u32[]{:S(2)}) collective-permute-start(bf16[2,576,512]{2,1,0:T(8,128)(2,1)} %sum_rows.21), channel_id=1, source_target_pairs={{0,4},{4,0},{8,12},{12,8},{16,20},{20,16},{24,28},{28,24},{1,5},{5... | collective-permute-start | bytes 3538952 | tf_op jit(solution)/shard_map/ppermute | solution.py:37
  563.1 27.5 %collective-permute-start.43 = (bf16[2,1152,640]{2,1,0:T(8,128)(2,1)}, bf16[2,1152,640]{2,1,0:T(8,128)(2,1)}, u32[]{:S(2)}, u32[]{:S(2)}) collective-permute-start(bf16[2,1152,640]{2,1,0:T(8,128)(2,1)} %get-tuple-element.1084), channel_id=1, source_target_pairs={{0,1},{1,0},{2,3},{3,2},{4,5},{5,4},{6,7},{7,6},{8,9},{9,8},{10,11... | collective-permute-start | bytes 8847368 | tf_op jit(solution)/shard_map/ppermute | solution.py:37
  593.5 48.7 %collective-permute-start.47 = (bf16[1,1152,640]{2,1,0:T(8,128)(2,1)}, bf16[1,1152,640]{2,1,0:T(8,128)(2,1)}, u32[]{:S(2)}, u32[]{:S(2)}) collective-permute-start(bf16[1,1152,640]{2,1,0:T(8,128)(2,1)} %sum_rows.24), channel_id=1, source_target_pairs={{0,2},{1,3},{2,0},{3,1},{4,6},{5,7},{6,4},{7,5},{8,10},{9,11},{10,... | collective-permute-start | bytes 4423688 | tf_op jit(solution)/shard_map/ppermute | solution.py:37
  595.0 44.8 %collective-permute-start.48 = (bf16[2,576,512]{2,1,0:T(8,128)(2,1)}, bf16[2,576,512]{2,1,0:T(8,128)(2,1)}, u32[]{:S(2)}, u32[]{:S(2)}) collective-permute-start(bf16[2,576,512]{2,1,0:T(8,128)(2,1)} %sum_rows.25), channel_id=1, source_target_pairs={{0,4},{4,0},{8,12},{12,8},{16,20},{20,16},{24,28},{28,24},{1,5},{5... | collective-permute-start | bytes 3538952 | tf_op jit(solution)/shard_map/ppermute | solution.py:37
  596.6 41.1 %collective-permute-start.49 = (bf16[1,288,640]{2,1,0:T(8,128)(2,1)}, bf16[1,288,640]{2,1,0:T(8,128)(2,1)}, u32[]{:S(2)}, u32[]{:S(2)}) collective-permute-start(bf16[1,288,640]{2,1,0:T(8,128)(2,1)} %add_convert_fusion.7), channel_id=1, source_target_pairs={{0,8},{4,12},{8,0},{12,4},{16,24},{20,28},{24,16},{28,20},{1,9},{5... | collective-permute-start | bytes 1105928 | tf_op jit(solution)/shard_map/ppermute | solution.py:37
  598.1 37.7 %collective-permute-start.50 = (bf16[1,288,512]{2,1,0:T(8,128)(2,1)}, bf16[1,288,512]{2,1,0:T(8,128)(2,1)}, u32[]{:S(2)}, u32[]{:S(2)}) collective-permute-start(bf16[1,288,512]{2,1,0:T(8,128)(2,1)} %add_convert_fusion.13), channel_id=1, source_target_pairs={{0,8},{4,12},{8,0},{12,4},{16,24},{20,28},{24,16},{28,20},{1,9},{5... | collective-permute-start | bytes 884744 | tf_op jit(solution)/shard_map/ppermute | solution.py:37
  645.9 28.7 %collective-permute-start.53 = (bf16[1,144,640]{2,1,0:T(8,128)(2,1)}, bf16[1,144,640]{2,1,0:T(8,128)(2,1)S(1)}, u32[]{:S(2)}, u32[]{:S(2)}) collective-permute-start(bf16[1,144,640]{2,1,0:T(8,128)(2,1)} %add_convert_fusion.17), channel_id=1, source_target_pairs={{0,16},{4,20},{8,24},{12,28},{16,0},{20,4},{24,8},{28,12},{1,17},{... | collective-permute-start | bytes 552968 | tf_op jit(solution)/shard_map/ppermute | solution.py:37
  674.6 40.3 %collective-permute-start.55 = (bf16[2,1152,640]{2,1,0:T(8,128)(2,1)}, bf16[2,1152,640]{2,1,0:T(8,128)(2,1)}, u32[]{:S(2)}, u32[]{:S(2)}) collective-permute-start(bf16[2,1152,640]{2,1,0:T(8,128)(2,1)} %get-tuple-element.1226), channel_id=1, source_target_pairs={{0,1},{1,0},{2,3},{3,2},{4,5},{5,4},{6,7},{7,6},{8,9},{9,8},{10,11... | collective-permute-start | bytes 8847368 | tf_op jit(solution)/shard_map/ppermute | solution.py:37
  674.7 37.6 %collective-permute-start.56 = (bf16[2,1152,512]{2,1,0:T(8,128)(2,1)}, bf16[2,1152,512]{2,1,0:T(8,128)(2,1)}, u32[]{:S(2)}, u32[]{:S(2)}) collective-permute-start(bf16[2,1152,512]{2,1,0:T(8,128)(2,1)} %get-tuple-element.1228), channel_id=1, source_target_pairs={{0,1},{1,0},{2,3},{3,2},{4,5},{5,4},{6,7},{7,6},{8,9},{9,8},{10,11... | collective-permute-start | bytes 7077896 | tf_op jit(solution)/shard_map/ppermute | solution.py:37
  675.2 34.7 %all-to-all-start.6 = ((bf16[8,2,32,1152]{3,2,1,0:T(8,128)(2,1)}), bf16[8,2,32,1152]{3,2,1,0:T(8,128)(2,1)}, u32[]{:S(2)}, u32[]{:S(2)}) async-start(bf16[8,2,32,1152]{3,2,1,0:T(8,128)(2,1)} %bitcast.214), calls=%async_computation.6 | async-start | bytes 2359296 | tf_op jit(solution)/shard_map/all_to_all | solution.py:763
  735.5 41.6 %collective-permute-start.57 = (bf16[2,1152,1152]{2,1,0:T(8,128)(2,1)}, bf16[2,1152,1152]{2,1,0:T(8,128)(2,1)}, u32[]{:S(2)}, u32[]{:S(2)}) collective-permute-start(bf16[2,1152,1152]{2,1,0:T(8,128)(2,1)} %get-tuple-element.1282), channel_id=1, source_target_pairs={{0,1},{1,0},{2,3},{3,2},{4,5},{5,4},{6,7},{7,6},{8,9},{9,8},{10,11... | collective-permute-start | bytes 15925256 | tf_op jit(solution)/shard_map/ppermute | solution.py:37
  735.6 38.9 %collective-permute-start.58 = (bf16[1,1152,640]{2,1,0:T(8,128)(2,1)}, bf16[1,1152,640]{2,1,0:T(8,128)(2,1)}, u32[]{:S(2)}, u32[]{:S(2)}) collective-permute-start(bf16[1,1152,640]{2,1,0:T(8,128)(2,1)} %sum_rows.28), channel_id=1, source_target_pairs={{0,2},{1,3},{2,0},{3,1},{4,6},{5,7},{6,4},{7,5},{8,10},{9,11},{10,... | collective-permute-start | bytes 4423688 | tf_op jit(solution)/shard_map/ppermute | solution.py:37
  737.1 34.9 %collective-permute-start.59 = (bf16[2,576,512]{2,1,0:T(8,128)(2,1)S(1)}, bf16[2,576,512]{2,1,0:T(8,128)(2,1)}, u32[]{:S(2)}, u32[]{:S(2)}) collective-permute-start(bf16[2,576,512]{2,1,0:T(8,128)(2,1)S(1)} %copy-done.19), channel_id=1, source_target_pairs={{0,4},{4,0},{8,12},{12,8},{16,20},{20,16},{24,28},{28,24},{1,5},{5... | collective-permute-start | bytes 3538952 | tf_op jit(solution)/shard_map/ppermute | solution.py:37
  781.1 28.7 %collective-permute-start.62 = (bf16[2,1152,1152]{2,1,0:T(8,128)(2,1)}, bf16[2,1152,1152]{2,1,0:T(8,128)(2,1)}, u32[]{:S(2)}, u32[]{:S(2)}) collective-permute-start(bf16[2,1152,1152]{2,1,0:T(8,128)(2,1)} %get-tuple-element.1338), channel_id=1, source_target_pairs={{0,1},{1,0},{2,3},{3,2},{4,5},{5,4},{6,7},{7,6},{8,9},{9,8},{10,11... | collective-permute-start | bytes 15925256 | tf_op jit(solution)/shard_map/ppermute | solution.py:37
  782.3 31.5 %collective-permute-start.65 = (bf16[1,144,640]{2,1,0:T(8,128)(2,1)}, bf16[1,144,640]{2,1,0:T(8,128)(2,1)S(1)}, u32[]{:S(2)}, u32[]{:S(2)}) collective-permute-start(bf16[1,144,640]{2,1,0:T(8,128)(2,1)} %add_convert_fusion.16), channel_id=1, source_target_pairs={{0,16},{4,20},{8,24},{12,28},{16,0},{20,4},{24,8},{28,12},{1,17},{... | collective-permute-start | bytes 552968 | tf_op jit(solution)/shard_map/ppermute | solution.py:37
  782.8 30.9 %collective-permute-start.66 = (bf16[1,144,512]{2,1,0:T(8,128)(2,1)}, bf16[1,144,512]{2,1,0:T(8,128)(2,1)}, u32[]{:S(2)}, u32[]{:S(2)}) collective-permute-start(bf16[1,144,512]{2,1,0:T(8,128)(2,1)} %add_convert_fusion.20), channel_id=1, source_target_pairs={{0,16},{4,20},{8,24},{12,28},{16,0},{20,4},{24,8},{28,12},{1,17},{... | collective-permute-start | bytes 442376 | tf_op jit(solution)/shard_map/ppermute | solution.py:37
  813.8 63.0 %collective-permute-start.67 = (bf16[2,576,1152]{2,1,0:T(8,128)(2,1)}, bf16[2,576,1152]{2,1,0:T(8,128)(2,1)}, u32[]{:S(2)}, u32[]{:S(2)}) collective-permute-start(bf16[2,576,1152]{2,1,0:T(8,128)(2,1)} %sum_rows.33), channel_id=1, source_target_pairs={{0,4},{4,0},{8,12},{12,8},{16,20},{20,16},{24,28},{28,24},{1,5},{5... | collective-permute-start | bytes 7962632 | tf_op jit(solution)/shard_map/ppermute | solution.py:37
  815.2 65.2 %collective-permute-start.68 = (bf16[1,1152,1152]{2,1,0:T(8,128)(2,1)}, bf16[1,1152,1152]{2,1,0:T(8,128)(2,1)}, u32[]{:S(2)}, u32[]{:S(2)}) collective-permute-start(bf16[1,1152,1152]{2,1,0:T(8,128)(2,1)} %sum_rows.30), channel_id=1, source_target_pairs={{0,2},{1,3},{2,0},{3,1},{4,6},{5,7},{6,4},{7,5},{8,10},{9,11},{10,... | collective-permute-start | bytes 7962632 | tf_op jit(solution)/shard_map/ppermute | solution.py:37
  816.7 58.0 %collective-permute-start.69 = (bf16[1,288,640]{2,1,0:T(8,128)(2,1)}, bf16[1,288,640]{2,1,0:T(8,128)(2,1)}, u32[]{:S(2)}, u32[]{:S(2)}) collective-permute-start(bf16[1,288,640]{2,1,0:T(8,128)(2,1)} %add_convert_fusion.5), channel_id=1, source_target_pairs={{0,8},{4,12},{8,0},{12,4},{16,24},{20,28},{24,16},{28,20},{1,9},{5... | collective-permute-start | bytes 1105928 | tf_op jit(solution)/shard_map/ppermute | solution.py:37
  817.0 55.8 %collective-permute-start.70 = (bf16[1,288,512]{2,1,0:T(8,128)(2,1)}, bf16[1,288,512]{2,1,0:T(8,128)(2,1)}, u32[]{:S(2)}, u32[]{:S(2)}) collective-permute-start(bf16[1,288,512]{2,1,0:T(8,128)(2,1)} %add_convert_fusion.11), channel_id=1, source_target_pairs={{0,8},{4,12},{8,0},{12,4},{16,24},{20,28},{24,16},{28,20},{1,9},{5... | collective-permute-start | bytes 884744 | tf_op jit(solution)/shard_map/ppermute | solution.py:37
  888.5 31.4 %collective-permute-start.73 = (bf16[1,576,1152]{2,1,0:T(8,128)(2,1)}, bf16[1,576,1152]{2,1,0:T(8,128)(2,1)}, u32[]{:S(2)}, u32[]{:S(2)}) collective-permute-start(bf16[1,576,1152]{2,1,0:T(8,128)(2,1)} %sum_rows.34), channel_id=1, source_target_pairs={{0,2},{1,3},{2,0},{3,1},{4,6},{5,7},{6,4},{7,5},{8,10},{9,11},{10,... | collective-permute-start | bytes 3981320 | tf_op jit(solution)/shard_map/ppermute | solution.py:37
  889.0 31.1 %collective-permute-start.74 = (bf16[1,576,1152]{2,1,0:T(8,128)(2,1)}, bf16[1,576,1152]{2,1,0:T(8,128)(2,1)}, u32[]{:S(2)}, u32[]{:S(2)}) collective-permute-start(bf16[1,576,1152]{2,1,0:T(8,128)(2,1)} %sum_rows.35), channel_id=1, source_target_pairs={{0,4},{4,0},{8,12},{12,8},{16,20},{20,16},{24,28},{28,24},{1,5},{5... | collective-permute-start | bytes 3981320 | tf_op jit(solution)/shard_map/ppermute | solution.py:37
  889.6 44.7 %collective-permute-start.75 = (bf16[1,144,640]{2,1,0:T(8,128)(2,1)}, bf16[1,144,640]{2,1,0:T(8,128)(2,1)}, u32[]{:S(2)}, u32[]{:S(2)}) collective-permute-start(bf16[1,144,640]{2,1,0:T(8,128)(2,1)} %add_convert_fusion.15), channel_id=1, source_target_pairs={{0,16},{4,20},{8,24},{12,28},{16,0},{20,4},{24,8},{28,12},{1,17},{... | collective-permute-start | bytes 552968 | tf_op jit(solution)/shard_map/ppermute | solution.py:37
  893.2 41.2 %collective-permute-start.76 = (bf16[1,144,512]{2,1,0:T(8,128)(2,1)}, bf16[1,144,512]{2,1,0:T(8,128)(2,1)}, u32[]{:S(2)}, u32[]{:S(2)}) collective-permute-start(bf16[1,144,512]{2,1,0:T(8,128)(2,1)} %add_convert_fusion.19), channel_id=1, source_target_pairs={{0,16},{4,20},{8,24},{12,28},{16,0},{20,4},{24,8},{28,12},{1,17},{... | collective-permute-start | bytes 442376 | tf_op jit(solution)/shard_map/ppermute | solution.py:37
  934.3 35.5 %collective-permute-start.77 = (bf16[1,1152,640]{2,1,0:T(8,128)(2,1)}, bf16[1,1152,640]{2,1,0:T(8,128)(2,1)}, u32[]{:S(2)}, u32[]{:S(2)}) collective-permute-start(bf16[1,1152,640]{2,1,0:T(8,128)(2,1)} %sum_rows.36), channel_id=1, source_target_pairs={{0,2},{1,3},{2,0},{3,1},{4,6},{5,7},{6,4},{7,5},{8,10},{9,11},{10,... | collective-permute-start | bytes 4423688 | tf_op jit(solution)/shard_map/ppermute | solution.py:37
  940.0 38.2 %collective-permute-start.78 = (bf16[2,576,512]{2,1,0:T(8,128)(2,1)}, bf16[2,576,512]{2,1,0:T(8,128)(2,1)}, u32[]{:S(2)}, u32[]{:S(2)}) collective-permute-start(bf16[2,576,512]{2,1,0:T(8,128)(2,1)} %sum_rows.37), channel_id=1, source_target_pairs={{0,4},{4,0},{8,12},{12,8},{16,20},{20,16},{24,28},{28,24},{1,5},{5... | collective-permute-start | bytes 3538952 | tf_op jit(solution)/shard_map/ppermute | solution.py:37
  940.6 29.7 %collective-permute-start.79 = (bf16[1,288,1152]{2,1,0:T(8,128)(2,1)}, bf16[1,288,1152]{2,1,0:T(8,128)(2,1)}, u32[]{:S(2)}, u32[]{:S(2)}) collective-permute-start(bf16[1,288,1152]{2,1,0:T(8,128)(2,1)} %add_convert_fusion.3), channel_id=1, source_target_pairs={{0,8},{4,12},{8,0},{12,4},{16,24},{20,28},{24,16},{28,20},{1,9},{5... | collective-permute-start | bytes 1990664 | tf_op jit(solution)/shard_map/ppermute | solution.py:37
  940.9 35.0 %collective-permute-start.80 = (bf16[1,288,1152]{2,1,0:T(8,128)(2,1)}, bf16[1,288,1152]{2,1,0:T(8,128)(2,1)}, u32[]{:S(2)}, u32[]{:S(2)}) collective-permute-start(bf16[1,288,1152]{2,1,0:T(8,128)(2,1)} %add_convert_fusion.2), channel_id=1, source_target_pairs={{0,8},{4,12},{8,0},{12,4},{16,24},{20,28},{24,16},{28,20},{1,9},{5... | collective-permute-start | bytes 1990664 | tf_op jit(solution)/shard_map/ppermute | solution.py:37
  944.1 39.3 %all-to-all-start.8 = ((bf16[4,288,512]{2,1,0:T(8,128)(2,1)}), bf16[4,288,512]{2,1,0:T(8,128)(2,1)S(1)}, u32[]{:S(2)}, u32[]{:S(2)}) async-start(bf16[4,288,512]{2,1,0:T(8,128)(2,1)} %bitcast.211), calls=%async_computation.8 | async-start | bytes 2359296 | tf_op jit(solution)/shard_map/all_to_all | solution.py:842
  989.2 46.8 %all-to-all-start.9 = ((bf16[4,288,512]{2,1,0:T(8,128)(2,1)}), bf16[4,288,512]{2,1,0:T(8,128)(2,1)S(1)}, u32[]{:S(2)}, u32[]{:S(2)}) async-start(bf16[4,288,512]{2,1,0:T(8,128)(2,1)} %bitcast.213), calls=%async_computation.9 | async-start | bytes 2359296 | tf_op jit(solution)/shard_map/all_to_all | solution.py:842
  992.8 32.6 %collective-permute-start.86 = (bf16[1,576,640]{2,1,0:T(8,128)(2,1)}, bf16[1,576,640]{2,1,0:T(8,128)(2,1)}, u32[]{:S(2)}, u32[]{:S(2)}) collective-permute-start(bf16[1,576,640]{2,1,0:T(8,128)(2,1)} %sum_rows.38), channel_id=1, source_target_pairs={{0,4},{4,0},{8,12},{12,8},{16,20},{20,16},{24,28},{28,24},{1,5},{5... | collective-permute-start | bytes 2211848 | tf_op jit(solution)/shard_map/ppermute | solution.py:37
  994.3 29.0 %collective-permute-start.87 = (bf16[1,576,512]{2,1,0:T(8,128)(2,1)}, bf16[1,576,512]{2,1,0:T(8,128)(2,1)}, u32[]{:S(2)}, u32[]{:S(2)}) collective-permute-start(bf16[1,576,512]{2,1,0:T(8,128)(2,1)} %sum_rows.39), channel_id=1, source_target_pairs={{0,2},{1,3},{2,0},{3,1},{4,6},{5,7},{6,4},{7,5},{8,10},{9,11},{10,... | collective-permute-start | bytes 1769480 | tf_op jit(solution)/shard_map/ppermute | solution.py:37
  996.3 31.3 %collective-permute-start.88 = (bf16[1,144,1152]{2,1,0:T(8,128)(2,1)}, bf16[1,144,1152]{2,1,0:T(8,128)(2,1)}, u32[]{:S(2)}, u32[]{:S(2)}) collective-permute-start(bf16[1,144,1152]{2,1,0:T(8,128)(2,1)} %add_convert_fusion.9), channel_id=1, source_target_pairs={{0,16},{4,20},{8,24},{12,28},{16,0},{20,4},{24,8},{28,12},{1,17},{... | collective-permute-start | bytes 995336 | tf_op jit(solution)/shard_map/ppermute | solution.py:37
  998.4 29.7 %collective-permute-start.89 = (bf16[1,144,1152]{2,1,0:T(8,128)(2,1)}, bf16[1,144,1152]{2,1,0:T(8,128)(2,1)}, u32[]{:S(2)}, u32[]{:S(2)}) collective-permute-start(bf16[1,144,1152]{2,1,0:T(8,128)(2,1)} %add_convert_fusion.8), channel_id=1, source_target_pairs={{0,16},{4,20},{8,24},{12,28},{16,0},{20,4},{24,8},{28,12},{1,17},{... | collective-permute-start | bytes 995336 | tf_op jit(solution)/shard_map/ppermute | solution.py:37
  (105 other events, 1941.8 us)
